TPU v7x, 256 devices: a whole 4x4x8 slice. The times are simulated.
256 devices in a mesh: comp: 2 (over x_hi), lat: 4 (over y), lon: 32 (over z, x_lo, core).
Axes of the slice: x: 4 (x_hi: 2, x_lo: 2; x = x_hi * 2 + x_lo), y: 4, z: 8, core: 2. Of those that a mesh axis runs over, the one named last changes fastest.
Arguments:
- state: bfloat16 [2, 80, 8, 8192], P('comp', None, 'lat', 'lon'), may hold values from -6 to 6
- direction: bfloat16 [2, 80, 8, 8192], P('comp', None, 'lat', 'lon'), may hold values from -6 to 6
- air_first: bfloat16 [9, 512, 80], replicated, may hold values from -0.21875 to 0.21875
- air_bias: float32 [512], replicated, may hold values from -4 to 4
- air_second: bfloat16 [9, 80, 512], replicated, may hold values from -0.09375 to 0.09375
- air_flux: bfloat16 [2, 80], replicated, may hold values from -1.25 to 1.25
- aloft_reaction_to_seawarmth: float32 [80], replicated, may hold values from -4 to 4
- sea_first: bfloat16 [9, 256, 40], replicated, may hold values from -0.3125 to 0.3125
- sea_bias: float32 [256], replicated, may hold values from -4 to 4
- sea_second: bfloat16 [9, 40, 256], replicated, may hold values from -0.125 to 0.125
- sea_forcing: bfloat16 [40, 2], replicated, may hold values from -4 to 4
- regrid_index: int32 [2, 8, 8, 8192], P('comp', None, 'lat', 'lon'), may hold values from 0 to 2047, as said below
- regrid_weight: int32 [2, 8, 8, 8192], P('comp', None, 'lat', 'lon'), may hold values from 1 to 255
- land_mask: int32 [2, 8, 8192], P(None, 'lat', 'lon'), may hold values 0 or 1
Outputs:
- image: bfloat16 [2, 80, 8, 8192], P('comp', None, 'lat', 'lon')
- product: bfloat16 [2, 80, 8, 8192], P('comp', None, 'lat', 'lon')
Inputs may be any that keep to these rules, and one draw needn't show every extreme that they name: `regrid_index`: in block 0, entries number cells of the fine window of the tile that holds the cell (below 2048); in block 1 they number cells of its coarse window (below 1024); the sources of a cell lie near it.
All inputs are finite; a program needn't handle non-finite values. No bound on the sum of `land_mask` on one device may be relied on, other than what follows from the above.
Results may differ from a plain program's by a relative error of at most 0.0064.
Values may be sent and summed in bfloat16 or wider, within the bound.
No kernel may reach another device: no remote copies, remote signals or barrier semaphores. Data moves between devices by JAX's collectives and lax.ppermute only.
A program may use at most 64 MiB of HBM per device.

v0:
```python
import functools

import jax
import jax.numpy as jnp
from jax import lax
from jax.experimental import pallas as pl
from jax.experimental.pallas import tpu as pltpu
from jax.sharding import PartitionSpec as P

F32 = jnp.float32
BF16 = jnp.bfloat16
ROWS = 2
COLS = 256
PITCH = COLS + 128
CELLS = ROWS * COLS
SLOTS = 8


def lane_iota(shape):
    return lax.broadcasted_iota(jnp.int32, shape, 1)


def split_parts(values):
    high = values.astype(BF16)
    low = (values - high.astype(F32)).astype(BF16)
    return jnp.concatenate([high, low], axis=0)


def dot(left, right):
    return lax.dot_general(left, right, (((1,), (0,)), ((), ())), preferred_element_type=F32)


def sources(own, above, below):
    return [(ref, r) for ref in (above, own, below) for r in range(ROWS)]


def prepare_kernel(
    flags, first_a, second_a, first_o, second_o, index, weight, fwd1, fwd2, bwd1, bwd2, hot, share
):
    def weights(first, second, channels):
        padded = -(-3 * channels // 16) * 16
        hidden = first.shape[2]
        fill = jnp.zeros((padded - 3 * channels, hidden), F32)

        def to_hidden(source, flip, target):
            pieces = []
            for a in range(3):
                for e in range(3):
                    tap = 3 * a + e
                    pieces.append(source[8 - tap if flip else tap].astype(F32))
                if padded > 3 * channels:
                    pieces.append(fill)
            stacked = jnp.concatenate(pieces, axis=0)
            target[:hidden, : 3 * padded] = stacked.T.astype(BF16)

        def from_hidden(source, flip, target):
            for a in range(3):
                pieces = []
                for e in range(3):
                    tap = 3 * a + e
                    pieces.append(source[8 - tap if flip else tap].astype(F32))
                stacked = jnp.concatenate(pieces, axis=0)
                target[: 3 * channels, a * hidden : (a + 1) * hidden] = stacked.astype(BF16)

        to_hidden(first, False, fwd1)
        from_hidden(second, False, fwd2)
        to_hidden(second, True, bwd1)
        from_hidden(first, True, bwd2)

    table = weight[...].astype(F32)

    @pl.when(flags[0] == 0)
    def _():
        weights(first_a, second_a, first_a.shape[1])
        share[...] = table / jnp.sum(table, axis=0, keepdims=True)

    @pl.when(flags[0] != 0)
    def _():
        weights(first_o, second_o, first_o.shape[1])
        upper = jnp.sum(table[:4], axis=0, keepdims=True)
        lower = jnp.sum(table[4:], axis=0, keepdims=True)
        place = lax.broadcasted_iota(jnp.int32, table.shape, 0)
        share[...] = table / jnp.where(place < 4, upper, lower)

    lanes = lax.broadcasted_iota(jnp.int32, (128, CELLS), 0)
    for slot in range(SLOTS):
        low = index[slot : slot + 1, :] & 127
        hot[:, slot * CELLS : (slot + 1) * CELLS] = jnp.where(lanes == low, 1.0, 0.0).astype(BF16)


def edge_kernel(own, above, below, to_left, to_right):
    channels = own.shape[0]
    lanes = lane_iota((channels, 128))
    left = jnp.zeros((channels, 128), F32)
    right = jnp.zeros((channels, 128), F32)
    for place, (ref, r) in enumerate(sources(own, above, below)):
        initial = ref[:, r * COLS : r * COLS + 128].astype(F32)
        last = ref[:, r * COLS + 128 : (r + 1) * COLS].astype(F32)
        here = (lanes >> 1) == place
        if place:
            initial = pltpu.roll(initial, 2 * place, 1)
        left = jnp.where(here, initial, left)
        right = jnp.where(here, pltpu.roll(last, 2 * place + 2, 1), right)
    to_left[...] = left.astype(BF16)
    to_right[...] = right.astype(BF16)


def shifted_rows(main, place, from_left, from_right, fill):
    lanes = lane_iota(from_left.shape)
    after = pltpu.roll(from_right, (128 - 2 * place) % 128, 1) if place else from_right
    before = pltpu.roll(from_left, 126 - 2 * place, 1)
    edge = jnp.where(lanes < 2, after, jnp.where(lanes >= 126, before, 0.0))
    full = jnp.concatenate([main, edge], axis=1)
    pieces = [pltpu.roll(full, 1, 1), full, pltpu.roll(full, PITCH - 1, 1)]
    if fill:
        pieces.append(jnp.zeros((fill, PITCH), F32))
    return jnp.concatenate(pieces, axis=0).astype(BF16)


def air_rows(own, above, below, from_left, from_right, fields, store):
    for field in range(fields):
        part = slice(field * 80, (field + 1) * 80)
        left = from_left[part, :].astype(F32)
        right = from_right[part, :].astype(F32)
        for place, (ref, r) in enumerate(sources(own, above, below)):
            main = ref[part, r * COLS : (r + 1) * COLS].astype(F32)
            store(field, place, shifted_rows(main, place, left, right, 0))


def sea_rows(own, above, below, from_left, from_right, fields, store):
    for field in range(fields):
        part = slice(field * 80, (field + 1) * 80)
        left = from_left[part, :].astype(F32)
        right = from_right[part, :].astype(F32)
        for place, (ref, r) in enumerate(sources(own, above, below)):
            main = ref[part, r * COLS : (r + 1) * COLS].astype(F32)
            for half in range(2):
                fine = 2 * (2 * (place // 2) + half - 1) + r
                if 0 <= fine < 8:
                    cut = slice(half * 40, half * 40 + 40)
                    rows = shifted_rows(main[cut], place, left[cut], right[cut], 8)
                    store(field, fine, rows)


def row_span(place):
    return pl.ds(pl.multiple_of(place * PITCH, 128), PITCH)


def tap_stack(ref, first_row, depth, place):
    pieces = [ref[first_row : first_row + depth, row_span(place + a)] for a in range(3)]
    return jnp.concatenate(pieces, axis=0)


def joined_taps(product, channels):
    total = pltpu.roll(product[:channels], 1, 1) + product[channels : 2 * channels]
    total = total + pltpu.roll(product[2 * channels : 3 * channels], PITCH - 1, 1)
    return total[:, :COLS]


def pole_scale(flags, place, count):
    outside = ((flags[1] == 0) & (place == 0)) | ((flags[1] == flags[2] - 1) & (place == count - 1))
    return jnp.where(outside, 0.0, 1.0).astype(F32)


def tangent_kernel(
    flags, own, above, below, from_left, from_right, fwd1, fwd2, bias, flux_weight,
    y, slope, payload, stack, hidden,
):
    def run(channels, width, depth, count, slope_slice):
        padded = depth // 3

        def one_row(place, unused):
            scale = pole_scale(flags, place, count)
            base = dot(fwd1[:width, :depth], tap_stack(stack, 0, padded, place))
            tangent = dot(fwd1[:width, :depth], tap_stack(stack, padded, padded, place))
            steep = 1.0 - jnp.tanh(base + bias[:width, :]) ** 2
            hidden[:width, row_span(place)] = (steep * tangent * scale).astype(BF16)
            slope_slice(place, steep.astype(BF16))
            return unused

        lax.fori_loop(0, count, one_row, 0)

    def second(channels, width, place):
        taps = tap_stack(hidden, 0, width, place)
        return joined_taps(dot(fwd2[: 3 * channels, : 3 * width], taps), channels)

    @pl.when(flags[0] == 0)
    def _():
        def store(field, place, rows):
            stack[field * 240 : field * 240 + 240, place * PITCH : (place + 1) * PITCH] = rows

        air_rows(own, above, below, from_left, from_right, 2, store)

        def keep(place, rows):
            slope[:, row_span(place)] = rows

        run(80, 512, 720, 4, keep)
        for r in range(ROWS):
            result = second(80, 512, r)
            y[:, r * COLS : (r + 1) * COLS] = result
            for f in range(2):
                flux = jnp.sum(flux_weight[:, f : f + 1] * result, axis=0, keepdims=True)
                for part in range(2):
                    line = f * 4 + r * 2 + part
                    payload[line : line + 1, :] = flux[:, part * 128 : (part + 1) * 128]

    @pl.when(flags[0] != 0)
    def _():
        def store(field, place, rows):
            stack[field * 128 : field * 128 + 128, place * PITCH : (place + 1) * PITCH] = rows

        sea_rows(own, above, below, from_left, from_right, 2, store)

        def keep(place, rows):
            @pl.when(place < 4)
            def _():
                slope[:256, row_span(place)] = rows

            @pl.when(place >= 4)
            def _():
                slope[256:, row_span(place - 4)] = rows

        run(40, 256, 384, 6, keep)
        for fine in range(2 * ROWS):
            y[:40, fine * COLS : (fine + 1) * COLS] = second(40, 256, fine)
            half, r = divmod(fine, 2)
            line = own[80 + 40 * half : 88 + 40 * half, r * COLS : (r + 1) * COLS].astype(F32)
            for part in range(2):
                place = fine * 2 + part
                payload[place : place + 1, :] = line[:1, part * 128 : (part + 1) * 128]


def couple_kernel(
    flags, y, near, far, hot, index, share, mask, aloft, forcing_weight, image, back_near, back_far
):
    window = jnp.concatenate([near[...], far[...]], axis=0)
    parts = dot(split_parts(window), hot[...])
    gathered = parts[:16] + parts[16:]
    lines = lax.broadcasted_iota(jnp.int32, (16, CELLS), 0)

    def span(slot):
        return slice(slot * CELLS, (slot + 1) * CELLS)

    def line_of(slot):
        place = index[slot : slot + 1, :]
        return ((place >> 8) & 1) * 8 + (place >> 9) * 2 + ((place >> 7) & 1)

    def scatter(pieces):
        spread = split_parts(jnp.concatenate(pieces, axis=1))
        total = lax.dot_general(
            spread, hot[...], (((1,), (1,)), ((), ())), preferred_element_type=F32
        )
        total = total[:16] + total[16:]
        back_near[...] = total[:8]
        back_far[...] = total[8:]

    def pick(slot, offset):
        chosen = jnp.where(lines == line_of(slot) + offset, gathered[:, span(slot)], 0.0)
        return share[slot : slot + 1, :] * jnp.sum(chosen, axis=0, keepdims=True)

    @pl.when(flags[0] == 0)
    def _():
        lifted = pick(0, 0)
        for slot in range(1, SLOTS):
            lifted = lifted + pick(slot, 0)
        rounded = (y[:, :CELLS] + aloft[...] * lifted).astype(BF16)
        image[...] = rounded
        surface = jnp.sum(aloft[...] * rounded.astype(F32), axis=0, keepdims=True)
        pieces = []
        for slot in range(SLOTS):
            value = share[slot : slot + 1, :] * surface
            pieces.append(jnp.where(lines == line_of(slot), value, 0.0))
        scatter(pieces)

    @pl.when(flags[0] != 0)
    def _():
        halves = []
        pulled = []
        for half in range(2):
            forcing = []
            for f in range(2):
                total = pick(4 * half, 4 * f)
                for k in range(1, 4):
                    total = total + pick(4 * half + k, 4 * f)
                forcing.append(total)
            added = forcing_weight[:, :1] * forcing[0] + forcing_weight[:, 1:] * forcing[1]
            fine = mask[half : half + 1, :] * (y[:40, span(half)] + added)
            rounded = fine.astype(BF16).astype(F32)
            halves.append(rounded)
            pulled.append(
                [jnp.sum(forcing_weight[:, f : f + 1] * rounded, axis=0, keepdims=True) for f in range(2)]
            )
        image[...] = jnp.concatenate(halves, axis=0).astype(BF16)
        pieces = []
        for slot in range(SLOTS):
            line = line_of(slot)
            part = share[slot : slot + 1, :]
            first = jnp.where(lines == line, part * pulled[slot // 4][0], 0.0)
            other = jnp.where(lines == line + 4, part * pulled[slot // 4][1], 0.0)
            pieces.append(first + other)
        scatter(pieces)


def cotangent_kernel(flags, image, near, far, flux_weight, cotangent):
    @pl.when(flags[0] == 0)
    def _():
        arrived = near[...] + far[...]
        total = image[...].astype(F32)
        for f in range(2):
            row = jnp.concatenate([arrived[f * 4 + q : f * 4 + q + 1, :] for q in range(4)], axis=1)
            total = total + flux_weight[:, f : f + 1] * row
        cotangent[...] = total.astype(BF16)

    @pl.when(flags[0] != 0)
    def _():
        cotangent[...] = image[...]


def adjoint_kernel(
    flags, own, above, below, from_left, from_right, bwd1, bwd2, slope, near, far,
    product, stack, hidden,
):
    def run(width, depth, count, slope_slice):
        padded = depth // 3

        def one_row(place, unused):
            scale = pole_scale(flags, place, count)
            back = dot(bwd1[:width, :depth], tap_stack(stack, 0, padded, place))
            back = back * slope_slice(place).astype(F32) * scale
            hidden[:width, row_span(place)] = back.astype(BF16)
            return unused

        lax.fori_loop(0, count, one_row, 0)

    def second(channels, width, place):
        taps = tap_stack(hidden, 0, width, place)
        return joined_taps(dot(bwd2[: 3 * channels, : 3 * width], taps), channels)

    @pl.when(flags[0] == 0)
    def _():
        def store(field, place, rows):
            stack[:240, place * PITCH : (place + 1) * PITCH] = rows

        air_rows(own, above, below, from_left, from_right, 1, store)
        run(512, 720, 4, lambda place: slope[:, row_span(place)])
        for r in range(ROWS):
            product[:, r * COLS : (r + 1) * COLS] = second(80, 512, r).astype(BF16)

    @pl.when(flags[0] != 0)
    def _():
        def store(field, place, rows):
            stack[:128, place * PITCH : (place + 1) * PITCH] = rows

        sea_rows(own, above, below, from_left, from_right, 1, store)

        def slope_slice(place):
            upper = slope[:256, row_span(jnp.minimum(place, 3))]
            lower = slope[256:, row_span(jnp.maximum(place - 4, 0))]
            return jnp.where(place < 4, upper, lower)

        run(256, 384, 6, slope_slice)
        arrived = near[...] + far[...]
        channel = lax.broadcasted_iota(jnp.int32, (40, COLS), 0)
        for r in range(ROWS):
            halves = []
            for half in range(2):
                fine = 2 * half + r
                row = jnp.concatenate(
                    [arrived[2 * fine + q : 2 * fine + q + 1, :] for q in range(2)], axis=1
                )
                halves.append(second(40, 256, fine) + jnp.where(channel == 0, row, 0.0))
            rows = jnp.concatenate(halves, axis=0)
            product[:, r * COLS : (r + 1) * COLS] = rows.astype(BF16)


def call(kernel, name, out_shape, inputs, scratch=()):
    smem = pl.BlockSpec(memory_space=pltpu.SMEM)
    vmem = pl.BlockSpec(memory_space=pltpu.VMEM)
    flagged = inputs[0].ndim == 1
    specs = [smem if flagged and i == 0 else vmem for i in range(len(inputs))]
    out_specs = tuple(vmem for _ in out_shape)
    return pl.pallas_call(
        kernel,
        name=name,
        out_shape=tuple(jax.ShapeDtypeStruct(shape, dtype) for shape, dtype in out_shape),
        in_specs=specs,
        out_specs=out_specs,
        scratch_shapes=[pltpu.VMEM(shape, dtype) for shape, dtype in scratch],
        compiler_params=pltpu.CompilerParams(vmem_limit_bytes=48 << 20),
    )(*inputs)


def lat_pair(block):
    count = lax.axis_size("lat")
    above = lax.ppermute(block, "lat", [(i, i + 1) for i in range(count - 1)])
    below = lax.ppermute(block, "lat", [(i + 1, i) for i in range(count - 1)])
    return above, below


def lon_pair(to_left, to_right):
    count = lax.axis_size("lon")
    from_left = lax.ppermute(to_right, "lon", [(i, (i + 1) % count) for i in range(count)])
    from_right = lax.ppermute(to_left, "lon", [((i + 1) % count, i) for i in range(count)])
    return from_left, from_right


def across(near, far, shift):
    count = lax.axis_size("lon")
    same = lax.ppermute(near, "comp", [(0, 1), (1, 0)])
    route = []
    for part in range(2):
        for i in range(count):
            route.append((part * count + i, (1 - part) * count + (i + shift) % count))
    return same, lax.ppermute(far, ("comp", "lon"), route)


def shards(
    state,
    direction,
    air_first,
    air_bias,
    air_second,
    air_flux,
    aloft_reaction_to_seawarmth,
    sea_first,
    sea_bias,
    sea_second,
    sea_forcing,
    regrid_index,
    regrid_weight,
    land_mask,
):
    comp = lax.axis_index("comp")
    flags = jnp.stack([comp, lax.axis_index("lat"), jnp.int32(lax.axis_size("lat"))]).astype(jnp.int32)
    own = jnp.concatenate([state[0].reshape(80, CELLS), direction[0].reshape(80, CELLS)], axis=0)
    index = regrid_index[0].reshape(SLOTS, CELLS)
    weight = regrid_weight[0].reshape(SLOTS, CELLS)
    mask = land_mask.reshape(2, CELLS).astype(F32)
    bias = jnp.where(comp == 0, air_bias, jnp.concatenate([sea_bias, sea_bias])).reshape(512, 1)
    flux_weight = air_flux.astype(F32).T
    forcing_weight = sea_forcing.astype(F32)
    aloft = aloft_reaction_to_seawarmth.reshape(80, 1)

    above, below = lat_pair(own)
    fwd1, fwd2, bwd1, bwd2, hot, share = call(
        prepare_kernel,
        "prepare",
        [
            ((512, 720), BF16), ((240, 1536), BF16), ((512, 720), BF16), ((240, 1536), BF16),
            ((128, SLOTS * CELLS), BF16), ((SLOTS, CELLS), F32),
        ],
        [
            flags, air_first.transpose(0, 2, 1), air_second, sea_first.transpose(0, 2, 1),
            sea_second, index, weight,
        ],
    )
    to_left, to_right = call(
        edge_kernel, "edges", [((160, 128), BF16)] * 2, [own, above, below]
    )
    from_left, from_right = lon_pair(to_left, to_right)
    y, slope, payload = call(
        tangent_kernel,
        "tangent",
        [((80, 2 * CELLS), F32), ((512, 4 * PITCH), BF16), ((8, 128), F32)],
        [flags, own, above, below, from_left, from_right, fwd1, fwd2, bias, flux_weight],
        [((480, 8 * PITCH), BF16), ((512, 6 * PITCH), BF16)],
    )
    near, far = across(payload, payload, -1)
    image, back_near, back_far = call(
        couple_kernel,
        "couple",
        [((80, CELLS), BF16), ((8, 128), F32), ((8, 128), F32)],
        [flags, y, near, far, hot, index, share, mask, aloft, forcing_weight],
    )
    back_near, back_far = across(back_near, back_far, 1)
    (cotangent,) = call(
        cotangent_kernel, "cotangent", [((80, CELLS), BF16)],
        [flags, image, back_near, back_far, flux_weight],
    )
    above, below = lat_pair(cotangent)
    to_left, to_right = call(
        edge_kernel, "edges_back", [((80, 128), BF16)] * 2, [cotangent, above, below]
    )
    from_left, from_right = lon_pair(to_left, to_right)
    (product,) = call(
        adjoint_kernel,
        "adjoint",
        [((80, CELLS), BF16)],
        [
            flags, cotangent, above, below, from_left, from_right, bwd1, bwd2, slope,
            back_near, back_far,
        ],
        [((240, 8 * PITCH), BF16), ((512, 6 * PITCH), BF16)],
    )
    return image.reshape(1, 80, ROWS, COLS), product.reshape(1, 80, ROWS, COLS)


def solution(mesh):
    return jax.shard_map(
        shards,
        mesh=mesh,
        in_specs=(
            P("comp", None, "lat", "lon"),
            P("comp", None, "lat", "lon"),
            P(),
            P(),
            P(),
            P(),
            P(),
            P(),
            P(),
            P(),
            P(),
            P("comp", None, "lat", "lon"),
            P("comp", None, "lat", "lon"),
            P(None, "lat", "lon"),
        ),
        out_specs=(P("comp", None, "lat", "lon"), P("comp", None, "lat", "lon")),
        check_vma=False,
    )
```

profile of v0, /device:TPU:99, one launch (start us, length us, event | category | flops | bytes accessed | tf_op | source)
XLA Modules:
  0.0 77.3 jit_solution(16829689904059037447)
XLA Ops:
  0.6 0.0 copy-start.2
  0.6 0.0 copy-start.3
  0.7 1.0 %copy.27 = bf16[10,8,2,256]{3,1,2,0:T(8,128)(2,1)S(1)} copy(bf16[10,8,2,256]{3,2,1,0:T(2,128)(2,1)} %bitcast.32) | data formatting | bytes 163840
  1.7 0.9 %copy.28 = bf16[10,8,2,256]{3,1,2,0:T(8,128)(2,1)S(1)} copy(bf16[10,8,2,256]{3,2,1,0:T(2,128)(2,1)} %bitcast.33) | data formatting | bytes 163840
  2.6 3.2 %collective-permute-start = (bf16[160,512]{1,0:T(8,128)(2,1)S(1)}, bf16[160,512]{1,0:T(8,128)(2,1)S(1)}, u32[]{:S(2)}, u32[]{:S(2)}) collective-permute-start(bf16[160,512]{1,0:T(8,128)(2,1)S(1)} %constant_dynamic-update-slice_fusion.own), channel_id=1, source_target_pairs={{0,32},{32,64},{64,96},{1,33},{33,65},{65,97},{2,34},{34,66},{66,9... | collective-permute-start | bytes 491528 | tf_op jit(solution)/shard_map/ppermute | solution.py:395
  5.8 1.3 %collective-permute-start.1 = (bf16[160,512]{1,0:T(8,128)(2,1)S(1)}, bf16[160,512]{1,0:T(8,128)(2,1)S(1)}, u32[]{:S(2)}, u32[]{:S(2)}) collective-permute-start(bf16[160,512]{1,0:T(8,128)(2,1)S(1)} %constant_dynamic-update-slice_fusion.own), channel_id=1, source_target_pairs={{32,0},{64,32},{96,64},{33,1},{65,33},{97,65},{34,2},{66,34},{98,6... | collective-permute-start | bytes 491528 | tf_op jit(solution)/shard_map/ppermute | solution.py:396
  7.1 0.8 maximum_select_fusion
  7.9 0.8 %collective-permute-done.above = bf16[160,512]{1,0:T(8,128)(2,1)S(1)} collective-permute-done((bf16[160,512]{1,0:T(8,128)(2,1)S(1)}, bf16[160,512]{1,0:T(8,128)(2,1)S(1)}, u32[]{:S(2)}, u32[]{:S(2)}) %collective-permute-start) | collective-permute-done | bytes 163872 | tf_op jit(solution)/shard_map/ppermute | solution.py:395
  8.7 3.8 %collective-permute-done.1.below = bf16[160,512]{1,0:T(8,128)(2,1)S(1)} collective-permute-done((bf16[160,512]{1,0:T(8,128)(2,1)S(1)}, bf16[160,512]{1,0:T(8,128)(2,1)S(1)}, u32[]{:S(2)}, u32[]{:S(2)}) %collective-permute-start.1) | collective-permute-done | bytes 163872 | tf_op jit(solution)/shard_map/ppermute | solution.py:396
  12.5 0.2 edges.1
  12.7 4.6 %collective-permute-start.2 = (bf16[160,128]{1,0:T(8,128)(2,1)S(1)}, bf16[160,128]{1,0:T(8,128)(2,1)S(1)}, u32[]{:S(2)}, u32[]{:S(2)}) collective-permute-start(bf16[160,128]{1,0:T(8,128)(2,1)S(1)} %get-tuple-element.18), channel_id=1, source_target_pairs={{0,1},{1,2},{2,3},{3,4},{4,5},{5,6},{6,7},{7,8},{8,9},{9,10},{10,1... | collective-permute-start | bytes 122888 | tf_op jit(solution)/shard_map/ppermute | solution.py:402
  17.3 0.0 collective-permute-start.3
  17.3 0.1 pad_add_fusion.flags
  17.4 0.7 copy.29
  18.1 0.7 copy.30
  18.8 0.1 copy.24.bias
  19.0 0.8 copy.23
  19.7 0.0 copy-done.2
  19.7 0.0 copy-done.3
  19.7 0.0 copy-start.9
  19.8 0.9 %copy-done.9 = bf16[9,256,40]{1,2,0:T(8,128)(2,1)S(1)} copy-done((bf16[9,256,40]{1,2,0:T(8,128)(2,1)S(1)}, bf16[9,256,40]{1,2,0:T(8,128)(2,1)}, u32[]{:S(2)}) %copy-start.9) | copy-done | bytes 184344
  20.7 0.0 copy-start.10
  20.7 0.9 %copy-done.10 = bf16[9,40,256]{2,1,0:T(8,128)(2,1)S(1)} copy-done((bf16[9,40,256]{2,1,0:T(8,128)(2,1)S(1)}, bf16[9,40,256]{2,1,0:T(8,128)(2,1)}, u32[]{:S(2)}) %copy-start.10) | copy-done | bytes 184344
  21.6 1.2 %prepare.1 = (bf16[512,720]{1,0:T(8,128)(2,1)S(1)}, bf16[240,1536]{1,0:T(8,128)(2,1)S(1)}, bf16[512,720]{1,0:T(8,128)(2,1)S(1)}, bf16[240,1536]{1,0:T(8,128)(2,1...) custom-call(s32[3]{0:T(128)S(1)} %pad_add_fusion.flags, bf16[9,80,512]{2,1,0:T(8,128)(2,1)S(1)} %bitcast.22, ...), custom_call_target="tpu_custom_call" | custom-call | tf_op jit(solution)/shard_map/prepare/pallas_call | solution.py:382
  22.8 0.0 copy-start.4
  22.9 0.9 %copy-done.4 = bf16[240,1536]{1,0:T(8,128)(2,1)} copy-done((bf16[240,1536]{1,0:T(8,128)(2,1)}, bf16[240,1536]{1,0:T(8,128)(2,1)S(1)}, u32[]{:S(2)}) %copy-start.4) | copy-done | bytes 737304
  23.8 0.0 collective-permute-done.2.from_left
  23.8 0.0 collective-permute-done.3.from_right
  23.8 7.6 %tangent.1 = (f32[80,1024]{1,0:T(8,128)S(1)}, bf16[512,1536]{1,0:T(8,128)(2,1)S(1)}, f32[8,128]{1,0:T(8,128)}) custom-call(s32[3]{0:T(128)S(1)} %pad_add_fusion.flags, bf16[160,512]{1,0:T(8,128)(2,1)S(1)} %constant_dynamic-update-slice_fusion.own, bf16[160,512]{1,0:T(8,128)(2,1)S(1)} %collective-permute-done.above, ...), custom_call_target="tpu_custom_call" | custom-call | tf_op jit(solution)/shard_map/tangent/pallas_call | solution.py:382
  31.4 0.0 copy-done
  31.4 0.0 copy-done.11
  31.4 0.8 copy-done.7
  32.2 0.0 collective-permute-start.4
  32.2 2.2 %collective-permute-start.5 = (f32[8,128]{1,0:T(8,128)}, f32[8,128]{1,0:T(8,128)S(1)}, u32[]{:S(2)}, u32[]{:S(2)}) collective-permute-start(f32[8,128]{1,0:T(8,128)} %get-tuple-element.23), channel_id=1, source_target_pairs={{0,159},{1,128},{2,129},{3,130},{4,131},{5,132},{6,133},{7,134},{8... | collective-permute-start | bytes 12296 | tf_op jit(solution)/shard_map/ppermute | solution.py:414
  34.3 0.0 copy-done.15
  34.3 0.7 copy.25.aloft
  35.1 0.7 copy.26.forcing_weight
  35.8 0.5 collective-permute-done.4.near
  36.3 2.7 %collective-permute-done.5.far = f32[8,128]{1,0:T(8,128)S(1)} collective-permute-done((f32[8,128]{1,0:T(8,128)}, f32[8,128]{1,0:T(8,128)S(1)}, u32[]{:S(2)}, u32[]{:S(2)}) %collective-permute-start.5) | collective-permute-done | bytes 4128 | tf_op jit(solution)/shard_map/ppermute | solution.py:414
  39.0 0.6 copy-done.13
  39.6 1.0 %copy-done.8 = f32[80,1024]{1,0:T(8,128)S(1)} copy-done((f32[80,1024]{1,0:T(8,128)S(1)}, f32[80,1024]{1,0:T(8,128)}, u32[]{:S(2)}) %copy-start.8) | copy-done | bytes 327704
  40.6 0.7 copy-done.12
  41.3 0.7 copy-done.14
  42.0 1.3 %couple.1 = (bf16[80,512]{1,0:T(8,128)(2,1)S(1)}, f32[8,128]{1,0:T(8,128)S(1)}, f32[8,128]{1,0:T(8,128)S(1)}) custom-call(s32[3]{0:T(128)S(1)} %pad_add_fusion.flags, f32[80,1024]{1,0:T(8,128)S(1)} %copy-done.8, f32[8,128]{1,0:T(8,128)S(1)} %collective-permute-done.4.near, f32[8,128]{1,0:T(8,128)S(1)} %copy-done.14, ...), custom_call_target="tpu_custom_call" | custom-call | tf_op jit(solution)/shard_map/couple/pallas_call | solution.py:382
  43.3 2.8 %collective-permute-start.6 = (f32[8,128]{1,0:T(8,128)S(1)}, f32[8,128]{1,0:T(8,128)S(1)}, u32[]{:S(2)}, u32[]{:S(2)}) collective-permute-start(f32[8,128]{1,0:T(8,128)S(1)} %get-tuple-element.27), channel_id=1, source_target_pairs={{0,128},{128,0},{1,129},{129,1},{2,130},{130,2},{3,131},{131,3},{4... | collective-permute-start | bytes 12296 | tf_op jit(solution)/shard_map/ppermute | solution.py:409
  46.1 1.2 %collective-permute-start.7 = (f32[8,128]{1,0:T(8,128)S(1)}, f32[8,128]{1,0:T(8,128)S(1)}, u32[]{:S(2)}, u32[]{:S(2)}) collective-permute-start(f32[8,128]{1,0:T(8,128)S(1)} %get-tuple-element.28), channel_id=1, source_target_pairs={{0,129},{1,130},{2,131},{3,132},{4,133},{5,134},{6,135},{7,136},{8... | collective-permute-start | bytes 12296 | tf_op jit(solution)/shard_map/ppermute | solution.py:414
  47.2 0.1 collective-permute-done.6.near
  47.3 3.3 %collective-permute-done.7.far = f32[8,128]{1,0:T(8,128)S(1)} collective-permute-done((f32[8,128]{1,0:T(8,128)S(1)}, f32[8,128]{1,0:T(8,128)S(1)}, u32[]{:S(2)}, u32[]{:S(2)}) %collective-permute-start.7) | collective-permute-done | bytes 4128 | tf_op jit(solution)/shard_map/ppermute | solution.py:414
  50.6 0.6 cotangent.1.own
  51.3 3.2 %collective-permute-start.8 = (bf16[80,512]{1,0:T(8,128)(2,1)S(1)}, bf16[80,512]{1,0:T(8,128)(2,1)S(1)}, u32[]{:S(2)}, u32[]{:S(2)}) collective-permute-start(bf16[80,512]{1,0:T(8,128)(2,1)S(1)} %cotangent.1.own), channel_id=1, source_target_pairs={{0,32},{32,64},{64,96},{1,33},{33,65},{65,97},{2,34},{34,66},{66,9... | collective-permute-start | bytes 245768 | tf_op jit(solution)/shard_map/ppermute | solution.py:395
  54.5 1.3 %collective-permute-start.9 = (bf16[80,512]{1,0:T(8,128)(2,1)S(1)}, bf16[80,512]{1,0:T(8,128)(2,1)S(1)}, u32[]{:S(2)}, u32[]{:S(2)}) collective-permute-start(bf16[80,512]{1,0:T(8,128)(2,1)S(1)} %cotangent.1.own), channel_id=1, source_target_pairs={{32,0},{64,32},{96,64},{33,1},{65,33},{97,65},{34,2},{66,34},{98,6... | collective-permute-start | bytes 245768 | tf_op jit(solution)/shard_map/ppermute | solution.py:396
  55.8 0.2 collective-permute-done.8.above
  55.9 3.7 %collective-permute-done.9.below = bf16[80,512]{1,0:T(8,128)(2,1)S(1)} collective-permute-done((bf16[80,512]{1,0:T(8,128)(2,1)S(1)}, bf16[80,512]{1,0:T(8,128)(2,1)S(1)}, u32[]{:S(2)}, u32[]{:S(2)}) %collective-permute-start.9) | collective-permute-done | bytes 81952 | tf_op jit(solution)/shard_map/ppermute | solution.py:396
  59.7 0.0 copy-done.6
  59.7 0.1 edges_back.1
  59.8 5.9 %collective-permute-start.10 = (bf16[80,128]{1,0:T(8,128)(2,1)S(1)}, bf16[80,128]{1,0:T(8,128)(2,1)S(1)}, u32[]{:S(2)}, u32[]{:S(2)}) collective-permute-start(bf16[80,128]{1,0:T(8,128)(2,1)S(1)} %get-tuple-element.29), channel_id=1, source_target_pairs={{0,1},{1,2},{2,3},{3,4},{4,5},{5,6},{6,7},{7,8},{8,9},{9,10},{10,1... | collective-permute-start | bytes 61448 | tf_op jit(solution)/shard_map/ppermute | solution.py:402
  65.7 0.0 collective-permute-start.11
  65.7 1.5 %reshape.20 = bf16[1,80,2,256]{3,2,1,0:T(2,128)(2,1)} reshape(bf16[80,512]{1,0:T(8,128)(2,1)} %copy-done.6) | data formatting | bytes 163840 | tf_op jit(solution)/shard_map/reshape | solution.py:495
  67.3 0.0 collective-permute-done.10.from_left
  67.3 3.8 %collective-permute-done.11.from_right = bf16[80,128]{1,0:T(8,128)(2,1)S(1)} collective-permute-done((bf16[80,128]{1,0:T(8,128)(2,1)S(1)}, bf16[80,128]{1,0:T(8,128)(2,1)S(1)}, u32[]{:S(2)}, u32[]{:S(2)}) %collective-permute-start.11) | collective-permute-done | bytes 20512 | tf_op jit(solution)/shard_map/ppermute | solution.py:403
  71.0 0.0 copy-done.1
  71.0 1.1 %copy-done.5 = bf16[240,1536]{1,0:T(8,128)(2,1)S(1)} copy-done((bf16[240,1536]{1,0:T(8,128)(2,1)S(1)}, bf16[240,1536]{1,0:T(8,128)(2,1)}, u32[]{:S(2)}) %copy-start.5) | copy-done | bytes 737304
  72.2 4.5 %adjoint.1 = bf16[80,512]{1,0:T(8,128)(2,1)S(1)} custom-call(s32[3]{0:T(128)S(1)} %pad_add_fusion.flags, bf16[80,512]{1,0:T(8,128)(2,1)S(1)} %cotangent.1.own, bf16[80,512]{1,0:T(8,128)(2,1)S(1)} %collective-permute-done.8.above, bf16[80,512]{1,0:T(8,128)(2,1)S(1)} %collective-permute-done.9.below, bf16[80,128]{1,0:T(8,128)(2,1)S(1)} %collective-permute-done.10.from_left, ...), custom_call_target="tpu_custom_call" | custom-call | tf_op jit(solution)/shard_map/adjoint/pallas_call | solution.py:382
  76.6 0.7 reshape.21
  (15 shorter events, 0.0 us)
Async XLA Ops:
  0.6 19.1 %copy-start.2 = (bf16[9,512,80]{1,2,0:T(8,128)(2,1)S(1)}, bf16[9,512,80]{1,2,0:T(8,128)(2,1)}, u32[]{:S(2)}) copy-start(bf16[9,512,80]{1,2,0:T(8,128)(2,1)} %param.16) | copy-start | bytes 2211844
  0.6 19.1 %copy-start.3 = (bf16[9,80,512]{2,1,0:T(8,128)(2,1)S(1)}, bf16[9,80,512]{2,1,0:T(8,128)(2,1)}, u32[]{:S(2)}) copy-start(bf16[9,80,512]{2,1,0:T(8,128)(2,1)} %second_a.1) | copy-start | bytes 2211844
  2.6 6.1 %collective-permute-start = (bf16[160,512]{1,0:T(8,128)(2,1)S(1)}, bf16[160,512]{1,0:T(8,128)(2,1)S(1)}, u32[]{:S(2)}, u32[]{:S(2)}) collective-permute-start(bf16[160,512]{1,0:T(8,128)(2,1)S(1)} %constant_dynamic-update-slice_fusion.own), channel_id=1, source_target_pairs={{0,32},{32,64},{64,96},{1,33},{33,65},{65,97},{2,34},{34,66},{66,9... | collective-permute-start | bytes 491528 | tf_op jit(solution)/shard_map/ppermute | solution.py:395
  5.8 6.7 %collective-permute-start.1 = (bf16[160,512]{1,0:T(8,128)(2,1)S(1)}, bf16[160,512]{1,0:T(8,128)(2,1)S(1)}, u32[]{:S(2)}, u32[]{:S(2)}) collective-permute-start(bf16[160,512]{1,0:T(8,128)(2,1)S(1)} %constant_dynamic-update-slice_fusion.own), channel_id=1, source_target_pairs={{32,0},{64,32},{96,64},{33,1},{65,33},{97,65},{34,2},{66,34},{98,6... | collective-permute-start | bytes 491528 | tf_op jit(solution)/shard_map/ppermute | solution.py:396
  12.7 11.1 %collective-permute-start.2 = (bf16[160,128]{1,0:T(8,128)(2,1)S(1)}, bf16[160,128]{1,0:T(8,128)(2,1)S(1)}, u32[]{:S(2)}, u32[]{:S(2)}) collective-permute-start(bf16[160,128]{1,0:T(8,128)(2,1)S(1)} %get-tuple-element.18), channel_id=1, source_target_pairs={{0,1},{1,2},{2,3},{3,4},{4,5},{5,6},{6,7},{7,8},{8,9},{9,10},{10,1... | collective-permute-start | bytes 122888 | tf_op jit(solution)/shard_map/ppermute | solution.py:402
  17.3 6.5 %collective-permute-start.3 = (bf16[160,128]{1,0:T(8,128)(2,1)S(1)}, bf16[160,128]{1,0:T(8,128)(2,1)S(1)}, u32[]{:S(2)}, u32[]{:S(2)}) collective-permute-start(bf16[160,128]{1,0:T(8,128)(2,1)S(1)} %get-tuple-element.19), channel_id=1, source_target_pairs={{1,0},{2,1},{3,2},{4,3},{5,4},{6,5},{7,6},{8,7},{9,8},{10,9},{11,1... | collective-permute-start | bytes 122888 | tf_op jit(solution)/shard_map/ppermute | solution.py:403
  19.7 0.9 %copy-start.9 = (bf16[9,256,40]{1,2,0:T(8,128)(2,1)S(1)}, bf16[9,256,40]{1,2,0:T(8,128)(2,1)}, u32[]{:S(2)}) copy-start(bf16[9,256,40]{1,2,0:T(8,128)(2,1)} %param.21) | copy-start | bytes 552964
  20.7 0.9 %copy-start.10 = (bf16[9,40,256]{2,1,0:T(8,128)(2,1)S(1)}, bf16[9,40,256]{2,1,0:T(8,128)(2,1)}, u32[]{:S(2)}) copy-start(bf16[9,40,256]{2,1,0:T(8,128)(2,1)} %second_o.1) | copy-start | bytes 552964
  22.8 0.9 %copy-start.4 = (bf16[240,1536]{1,0:T(8,128)(2,1)}, bf16[240,1536]{1,0:T(8,128)(2,1)S(1)}, u32[]{:S(2)}) copy-start(bf16[240,1536]{1,0:T(8,128)(2,1)S(1)} %get-tuple-element.32.bwd2) | copy-start | bytes 2211844
  23.8 7.6 %copy-start = (bf16[512,720]{1,0:T(8,128)(2,1)}, bf16[512,720]{1,0:T(8,128)(2,1)S(1)}, u32[]{:S(2)}) copy-start(bf16[512,720]{1,0:T(8,128)(2,1)S(1)} %get-tuple-element.31.bwd1) | copy-start | bytes 2211844
  23.8 7.6 %copy-start.11 = (f32[8,512]{1,0:T(8,128)}, f32[8,512]{1,0:T(8,128)S(1)}, u32[]{:S(2)}) copy-start(f32[8,512]{1,0:T(8,128)S(1)} %get-tuple-element.25.share) | copy-start | bytes 49156
  23.8 10.6 %copy-start.15 = (s32[2,2,256]{2,1,0:T(2,128)S(1)}, s32[2,2,256]{2,1,0:T(2,128)}, u32[]{:S(2)}) copy-start(s32[2,2,256]{2,1,0:T(2,128)} %param.27) | copy-start | bytes 12292
  31.4 0.8 copy-start.7
  32.2 38.9 %copy-start.1 = (bf16[512,720]{1,0:T(8,128)(2,1)S(1)}, bf16[512,720]{1,0:T(8,128)(2,1)}, u32[]{:S(2)}) copy-start(bf16[512,720]{1,0:T(8,128)(2,1)} %copy-done) | copy-start | bytes 2211844
  32.2 4.2 %collective-permute-start.4 = (f32[8,128]{1,0:T(8,128)}, f32[8,128]{1,0:T(8,128)S(1)}, u32[]{:S(2)}, u32[]{:S(2)}) collective-permute-start(f32[8,128]{1,0:T(8,128)} %get-tuple-element.23), channel_id=1, source_target_pairs={{0,128},{128,0},{1,129},{129,1},{2,130},{130,2},{3,131},{131,3},{4... | collective-permute-start | bytes 12296 | tf_op jit(solution)/shard_map/ppermute | solution.py:409
  32.2 6.8 %collective-permute-start.5 = (f32[8,128]{1,0:T(8,128)}, f32[8,128]{1,0:T(8,128)S(1)}, u32[]{:S(2)}, u32[]{:S(2)}) collective-permute-start(f32[8,128]{1,0:T(8,128)} %get-tuple-element.23), channel_id=1, source_target_pairs={{0,159},{1,128},{2,129},{3,130},{4,131},{5,132},{6,133},{7,134},{8... | collective-permute-start | bytes 12296 | tf_op jit(solution)/shard_map/ppermute | solution.py:414
  39.0 0.6 copy-start.13
  39.6 1.0 %copy-start.8 = (f32[80,1024]{1,0:T(8,128)S(1)}, f32[80,1024]{1,0:T(8,128)}, u32[]{:S(2)}) copy-start(f32[80,1024]{1,0:T(8,128)} %copy-done.7) | copy-start | bytes 983044
  40.6 0.7 copy-start.12
  41.3 0.7 copy-start.14
  43.3 16.4 %copy-start.6 = (bf16[80,512]{1,0:T(8,128)(2,1)}, bf16[80,512]{1,0:T(8,128)(2,1)S(1)}, u32[]{:S(2)}) copy-start(bf16[80,512]{1,0:T(8,128)(2,1)S(1)} %get-tuple-element.26.image) | copy-start | bytes 245764
  43.3 4.0 %collective-permute-start.6 = (f32[8,128]{1,0:T(8,128)S(1)}, f32[8,128]{1,0:T(8,128)S(1)}, u32[]{:S(2)}, u32[]{:S(2)}) collective-permute-start(f32[8,128]{1,0:T(8,128)S(1)} %get-tuple-element.27), channel_id=1, source_target_pairs={{0,128},{128,0},{1,129},{129,1},{2,130},{130,2},{3,131},{131,3},{4... | collective-permute-start | bytes 12296 | tf_op jit(solution)/shard_map/ppermute | solution.py:409
  46.1 4.5 %collective-permute-start.7 = (f32[8,128]{1,0:T(8,128)S(1)}, f32[8,128]{1,0:T(8,128)S(1)}, u32[]{:S(2)}, u32[]{:S(2)}) collective-permute-start(f32[8,128]{1,0:T(8,128)S(1)} %get-tuple-element.28), channel_id=1, source_target_pairs={{0,129},{1,130},{2,131},{3,132},{4,133},{5,134},{6,135},{7,136},{8... | collective-permute-start | bytes 12296 | tf_op jit(solution)/shard_map/ppermute | solution.py:414
  51.3 4.7 %collective-permute-start.8 = (bf16[80,512]{1,0:T(8,128)(2,1)S(1)}, bf16[80,512]{1,0:T(8,128)(2,1)S(1)}, u32[]{:S(2)}, u32[]{:S(2)}) collective-permute-start(bf16[80,512]{1,0:T(8,128)(2,1)S(1)} %cotangent.1.own), channel_id=1, source_target_pairs={{0,32},{32,64},{64,96},{1,33},{33,65},{65,97},{2,34},{34,66},{66,9... | collective-permute-start | bytes 245768 | tf_op jit(solution)/shard_map/ppermute | solution.py:395
  54.5 5.2 %collective-permute-start.9 = (bf16[80,512]{1,0:T(8,128)(2,1)S(1)}, bf16[80,512]{1,0:T(8,128)(2,1)S(1)}, u32[]{:S(2)}, u32[]{:S(2)}) collective-permute-start(bf16[80,512]{1,0:T(8,128)(2,1)S(1)} %cotangent.1.own), channel_id=1, source_target_pairs={{32,0},{64,32},{96,64},{33,1},{65,33},{97,65},{34,2},{66,34},{98,6... | collective-permute-start | bytes 245768 | tf_op jit(solution)/shard_map/ppermute | solution.py:396
  59.8 7.5 %collective-permute-start.10 = (bf16[80,128]{1,0:T(8,128)(2,1)S(1)}, bf16[80,128]{1,0:T(8,128)(2,1)S(1)}, u32[]{:S(2)}, u32[]{:S(2)}) collective-permute-start(bf16[80,128]{1,0:T(8,128)(2,1)S(1)} %get-tuple-element.29), channel_id=1, source_target_pairs={{0,1},{1,2},{2,3},{3,4},{4,5},{5,6},{6,7},{7,8},{8,9},{9,10},{10,1... | collective-permute-start | bytes 61448 | tf_op jit(solution)/shard_map/ppermute | solution.py:402
  65.7 5.3 %collective-permute-start.11 = (bf16[80,128]{1,0:T(8,128)(2,1)S(1)}, bf16[80,128]{1,0:T(8,128)(2,1)S(1)}, u32[]{:S(2)}, u32[]{:S(2)}) collective-permute-start(bf16[80,128]{1,0:T(8,128)(2,1)S(1)} %get-tuple-element.30), channel_id=1, source_target_pairs={{1,0},{2,1},{3,2},{4,3},{5,4},{6,5},{7,6},{8,7},{9,8},{10,9},{11,1... | collective-permute-start | bytes 61448 | tf_op jit(solution)/shard_map/ppermute | solution.py:403
  71.0 1.1 %copy-start.5 = (bf16[240,1536]{1,0:T(8,128)(2,1)S(1)}, bf16[240,1536]{1,0:T(8,128)(2,1)}, u32[]{:S(2)}) copy-start(bf16[240,1536]{1,0:T(8,128)(2,1)} %copy-done.4) | copy-start | bytes 2211844
where the time goes:
time: 77.9 us; the launch traced here: 77.3 us
  starting transfers between devices  25.6 us (33%)
  waiting for transfers between devices  18.8 us (24%)
  local copies, waits for them, and re-layouts  15.6 us (20%)
  Pallas kernels  15.6 us (20%)
  other arithmetic  0.85 us (1%)
  between operations  0.82 us (1%)
    pallas_call x7, Pallas kernels, call(): pl.pallas_call(kernel, name=name, out_shape=tuple((jax.ShapeDtypeStruct(s...  15.6 us
    unnamed x38, local copies, waits for them, and re-layouts  11 us
    ppermute x2, starting transfers between devices, lon_pair(): lax.ppermute(to_right, 'lon', [(i, (i + 1) % count) for i in range(count)])  10.5 us
    ppermute x2, waiting for transfers between devices, lat_pair(): below = lax.ppermute(block, 'lat', [(i + 1, i) for i in range(count - 1)])  7.56 us
    ppermute x2, starting transfers between devices, lat_pair(): above = lax.ppermute(block, 'lat', [(i, i + 1) for i in range(count - 1)])  6.41 us
    ppermute x2, waiting for transfers between devices, across(): return (same, lax.ppermute(far, ('comp', 'lon'), route))  5.99 us
    ppermute x2, waiting for transfers between devices, lon_pair(): lax.ppermute(to_left, 'lon', [((i + 1) % count, i) for i in range(count)])  3.77 us
    ppermute x2, starting transfers between devices, across(): return (same, lax.ppermute(far, ('comp', 'lon'), route))  3.33 us
  transfers between devices with their start and end apart: 12, of which 9 were waited for; matrix products, arithmetic and copies ran while one was open for 8% of the time, Pallas kernels for 2%

commit v1 on v0

--- a/solution.py
+++ b/solution.py
@@ -30,13 +30,35 @@
     return lax.dot_general(left, right, (((1,), (0,)), ((), ())), preferred_element_type=F32)
 
 
-def sources(own, above, below):
-    return [(ref, r) for ref in (above, own, below) for r in range(ROWS)]
+def sources(flags, own, above, below):
+    upper = jnp.where(flags[1] == 0, 0.0, 1.0).astype(F32)
+    lower = jnp.where(flags[1] == flags[2] - 1, 0.0, 1.0).astype(F32)
+    chosen = []
+    for ref, scale in ((above, upper), (own, None), (below, lower)):
+        for r in range(ROWS):
+
+            def read(part, start, stop, ref=ref, scale=scale, r=r):
+                rows = ref[part, r * COLS + start : r * COLS + stop].astype(F32)
+                return rows if scale is None else rows * scale
+
+            chosen.append((read, r))
+    return chosen
+
+
+def pack_kernel(state, direction, packed):
+    for field, ref in enumerate((state, direction)):
+        block = ref[0].astype(F32)
+        for r in range(ROWS):
+            packed[field * 80 : field * 80 + 80, r * COLS : (r + 1) * COLS] = block[:, r, :].astype(BF16)
 
 
 def prepare_kernel(
-    flags, first_a, second_a, first_o, second_o, index, weight, fwd1, fwd2, bwd1, bwd2, hot, share
+    flags, first_a, second_a, first_o, second_o, index, weight, land, bias_a, bias_o, flux, aloft,
+    forcing, fwd1, fwd2, bwd1, bwd2, hot, share, line, mask, columns,
 ):
+    def flat(rows):
+        return jnp.concatenate([rows[r : r + 1] for r in range(ROWS)], axis=1)
+
     def weights(first, second, channels):
         padded = -(-3 * channels // 16) * 16
         hidden = first.shape[2]
@@ -67,7 +89,18 @@
         to_hidden(second, True, bwd1)
         from_hidden(first, True, bwd2)
 
-    table = weight[...].astype(F32)
+    table = jnp.concatenate([flat(weight[0, s]) for s in range(SLOTS)], axis=0).astype(F32)
+    place = jnp.concatenate([flat(index[0, s]) for s in range(SLOTS)], axis=0)
+    line[...] = ((place >> 8) & 1) * 8 + (place >> 9) * 2 + ((place >> 7) & 1)
+    mask[...] = jnp.concatenate([flat(land[s]) for s in range(2)], axis=0).astype(F32)
+    pad = jnp.zeros((1, 512 - 80), F32)
+    bias = jnp.where(flags[0] == 0, bias_a[...], jnp.concatenate([bias_o[...]] * 2, axis=1))
+    rows = [bias] + [jnp.concatenate([flux[f : f + 1, :].astype(F32), pad], axis=1) for f in range(2)]
+    rows.append(jnp.concatenate([aloft[...], pad], axis=1))
+    pad = jnp.zeros((1, 512 - 40), F32)
+    rows += [jnp.concatenate([forcing[f : f + 1, :].astype(F32), pad], axis=1) for f in range(2)]
+    rows.append(jnp.zeros((2, 512), F32))
+    columns[...] = jnp.concatenate(rows, axis=0).T
 
     @pl.when(flags[0] == 0)
     def _():
@@ -79,23 +112,23 @@
         weights(first_o, second_o, first_o.shape[1])
         upper = jnp.sum(table[:4], axis=0, keepdims=True)
         lower = jnp.sum(table[4:], axis=0, keepdims=True)
-        place = lax.broadcasted_iota(jnp.int32, table.shape, 0)
-        share[...] = table / jnp.where(place < 4, upper, lower)
+        slot = lax.broadcasted_iota(jnp.int32, table.shape, 0)
+        share[...] = table / jnp.where(slot < 4, upper, lower)
 
     lanes = lax.broadcasted_iota(jnp.int32, (128, CELLS), 0)
     for slot in range(SLOTS):
-        low = index[slot : slot + 1, :] & 127
+        low = place[slot : slot + 1, :] & 127
         hot[:, slot * CELLS : (slot + 1) * CELLS] = jnp.where(lanes == low, 1.0, 0.0).astype(BF16)
 
 
-def edge_kernel(own, above, below, to_left, to_right):
+def edge_kernel(flags, own, above, below, after, to_left, to_right):
     channels = own.shape[0]
     lanes = lane_iota((channels, 128))
     left = jnp.zeros((channels, 128), F32)
     right = jnp.zeros((channels, 128), F32)
-    for place, (ref, r) in enumerate(sources(own, above, below)):
-        initial = ref[:, r * COLS : r * COLS + 128].astype(F32)
-        last = ref[:, r * COLS + 128 : (r + 1) * COLS].astype(F32)
+    for place, (read, r) in enumerate(sources(flags, own, above, below)):
+        initial = read(slice(0, channels), 0, 128)
+        last = read(slice(0, channels), 128, COLS)
         here = (lanes >> 1) == place
         if place:
             initial = pltpu.roll(initial, 2 * place, 1)
@@ -117,23 +150,23 @@
     return jnp.concatenate(pieces, axis=0).astype(BF16)
 
 
-def air_rows(own, above, below, from_left, from_right, fields, store):
+def air_rows(flags, own, above, below, from_left, from_right, fields, store):
     for field in range(fields):
         part = slice(field * 80, (field + 1) * 80)
         left = from_left[part, :].astype(F32)
         right = from_right[part, :].astype(F32)
-        for place, (ref, r) in enumerate(sources(own, above, below)):
-            main = ref[part, r * COLS : (r + 1) * COLS].astype(F32)
+        for place, (read, r) in enumerate(sources(flags, own, above, below)):
+            main = read(part, 0, COLS)
             store(field, place, shifted_rows(main, place, left, right, 0))
 
 
-def sea_rows(own, above, below, from_left, from_right, fields, store):
+def sea_rows(flags, own, above, below, from_left, from_right, fields, store):
     for field in range(fields):
         part = slice(field * 80, (field + 1) * 80)
         left = from_left[part, :].astype(F32)
         right = from_right[part, :].astype(F32)
-        for place, (ref, r) in enumerate(sources(own, above, below)):
-            main = ref[part, r * COLS : (r + 1) * COLS].astype(F32)
+        for place, (read, r) in enumerate(sources(flags, own, above, below)):
+            main = read(part, 0, COLS)
             for half in range(2):
                 fine = 2 * (2 * (place // 2) + half - 1) + r
                 if 0 <= fine < 8:
@@ -163,7 +196,7 @@
 
 
 def tangent_kernel(
-    flags, own, above, below, from_left, from_right, fwd1, fwd2, bias, flux_weight,
+    flags, own, above, below, from_left, from_right, fwd1, fwd2, columns,
     y, slope, payload, stack, hidden,
 ):
     def run(channels, width, depth, count, slope_slice):
@@ -173,7 +206,7 @@
             scale = pole_scale(flags, place, count)
             base = dot(fwd1[:width, :depth], tap_stack(stack, 0, padded, place))
             tangent = dot(fwd1[:width, :depth], tap_stack(stack, padded, padded, place))
-            steep = 1.0 - jnp.tanh(base + bias[:width, :]) ** 2
+            steep = 1.0 - jnp.tanh(base + columns[:width, 0:1]) ** 2
             hidden[:width, row_span(place)] = (steep * tangent * scale).astype(BF16)
             slope_slice(place, steep.astype(BF16))
             return unused
@@ -189,7 +222,7 @@
         def store(field, place, rows):
             stack[field * 240 : field * 240 + 240, place * PITCH : (place + 1) * PITCH] = rows
 
-        air_rows(own, above, below, from_left, from_right, 2, store)
+        air_rows(flags, own, above, below, from_left, from_right, 2, store)
 
         def keep(place, rows):
             slope[:, row_span(place)] = rows
@@ -199,7 +232,7 @@
             result = second(80, 512, r)
             y[:, r * COLS : (r + 1) * COLS] = result
             for f in range(2):
-                flux = jnp.sum(flux_weight[:, f : f + 1] * result, axis=0, keepdims=True)
+                flux = jnp.sum(columns[:80, 1 + f : 2 + f] * result, axis=0, keepdims=True)
                 for part in range(2):
                     line = f * 4 + r * 2 + part
                     payload[line : line + 1, :] = flux[:, part * 128 : (part + 1) * 128]
@@ -209,7 +242,7 @@
         def store(field, place, rows):
             stack[field * 128 : field * 128 + 128, place * PITCH : (place + 1) * PITCH] = rows
 
-        sea_rows(own, above, below, from_left, from_right, 2, store)
+        sea_rows(flags, own, above, below, from_left, from_right, 2, store)
 
         def keep(place, rows):
             @pl.when(place < 4)
@@ -231,7 +264,7 @@
 
 
 def couple_kernel(
-    flags, y, near, far, hot, index, share, mask, aloft, forcing_weight, image, back_near, back_far
+    flags, y, near, far, hot, line, share, mask, columns, image, back_near, back_far
 ):
     window = jnp.concatenate([near[...], far[...]], axis=0)
     parts = dot(split_parts(window), hot[...])
@@ -242,8 +275,7 @@
         return slice(slot * CELLS, (slot + 1) * CELLS)
 
     def line_of(slot):
-        place = index[slot : slot + 1, :]
-        return ((place >> 8) & 1) * 8 + (place >> 9) * 2 + ((place >> 7) & 1)
+        return line[slot : slot + 1, :]
 
     def scatter(pieces):
         spread = split_parts(jnp.concatenate(pieces, axis=1))
@@ -260,12 +292,13 @@
 
     @pl.when(flags[0] == 0)
     def _():
+        aloft = columns[:80, 3:4]
         lifted = pick(0, 0)
         for slot in range(1, SLOTS):
             lifted = lifted + pick(slot, 0)
-        rounded = (y[:, :CELLS] + aloft[...] * lifted).astype(BF16)
+        rounded = (y[:, :CELLS] + aloft * lifted).astype(BF16)
         image[...] = rounded
-        surface = jnp.sum(aloft[...] * rounded.astype(F32), axis=0, keepdims=True)
+        surface = jnp.sum(aloft * rounded.astype(F32), axis=0, keepdims=True)
         pieces = []
         for slot in range(SLOTS):
             value = share[slot : slot + 1, :] * surface
@@ -274,6 +307,7 @@
 
     @pl.when(flags[0] != 0)
     def _():
+        forcing_weight = columns[:40, 4:6]
         halves = []
         pulled = []
         for half in range(2):
@@ -293,27 +327,31 @@
         image[...] = jnp.concatenate(halves, axis=0).astype(BF16)
         pieces = []
         for slot in range(SLOTS):
-            line = line_of(slot)
+            lead = line_of(slot)
             part = share[slot : slot + 1, :]
-            first = jnp.where(lines == line, part * pulled[slot // 4][0], 0.0)
-            other = jnp.where(lines == line + 4, part * pulled[slot // 4][1], 0.0)
+            first = jnp.where(lines == lead, part * pulled[slot // 4][0], 0.0)
+            other = jnp.where(lines == lead + 4, part * pulled[slot // 4][1], 0.0)
             pieces.append(first + other)
         scatter(pieces)
 
 
-def cotangent_kernel(flags, image, near, far, flux_weight, cotangent):
+def cotangent_kernel(flags, image, near, far, columns, cotangent):
     @pl.when(flags[0] == 0)
     def _():
         arrived = near[...] + far[...]
         total = image[...].astype(F32)
         for f in range(2):
             row = jnp.concatenate([arrived[f * 4 + q : f * 4 + q + 1, :] for q in range(4)], axis=1)
-            total = total + flux_weight[:, f : f + 1] * row
+            total = total + columns[:80, 1 + f : 2 + f] * row
         cotangent[...] = total.astype(BF16)
 
     @pl.when(flags[0] != 0)
     def _():
         cotangent[...] = image[...]
+
+
+def spread_rows(target, rows):
+    target[0] = jnp.stack(rows, axis=1).astype(BF16)
 
 
 def adjoint_kernel(
@@ -341,17 +379,19 @@
         def store(field, place, rows):
             stack[:240, place * PITCH : (place + 1) * PITCH] = rows
 
-        air_rows(own, above, below, from_left, from_right, 1, store)
+        air_rows(flags, own, above, below, from_left, from_right, 1, store)
         run(512, 720, 4, lambda place: slope[:, row_span(place)])
+        rows = []
         for r in range(ROWS):
-            product[:, r * COLS : (r + 1) * COLS] = second(80, 512, r).astype(BF16)
+            rows.append(second(80, 512, r))
+        spread_rows(product, rows)
 
     @pl.when(flags[0] != 0)
     def _():
         def store(field, place, rows):
             stack[:128, place * PITCH : (place + 1) * PITCH] = rows
 
-        sea_rows(own, above, below, from_left, from_right, 1, store)
+        sea_rows(flags, own, above, below, from_left, from_right, 1, store)
 
         def slope_slice(place):
             upper = slope[:256, row_span(jnp.minimum(place, 3))]
@@ -361,6 +401,7 @@
         run(256, 384, 6, slope_slice)
         arrived = near[...] + far[...]
         channel = lax.broadcasted_iota(jnp.int32, (40, COLS), 0)
+        rows = []
         for r in range(ROWS):
             halves = []
             for half in range(2):
@@ -369,11 +410,11 @@
                     [arrived[2 * fine + q : 2 * fine + q + 1, :] for q in range(2)], axis=1
                 )
                 halves.append(second(40, 256, fine) + jnp.where(channel == 0, row, 0.0))
-            rows = jnp.concatenate(halves, axis=0)
-            product[:, r * COLS : (r + 1) * COLS] = rows.astype(BF16)
-
-
-def call(kernel, name, out_shape, inputs, scratch=()):
+            rows.append(jnp.concatenate(halves, axis=0))
+        spread_rows(product, rows)
+
+
+def call(kernel, name, out_shape, inputs, scratch=(), limit=8):
     smem = pl.BlockSpec(memory_space=pltpu.SMEM)
     vmem = pl.BlockSpec(memory_space=pltpu.VMEM)
     flagged = inputs[0].ndim == 1
@@ -386,14 +427,14 @@
         in_specs=specs,
         out_specs=out_specs,
         scratch_shapes=[pltpu.VMEM(shape, dtype) for shape, dtype in scratch],
-        compiler_params=pltpu.CompilerParams(vmem_limit_bytes=48 << 20),
+        compiler_params=pltpu.CompilerParams(vmem_limit_bytes=limit << 20),
     )(*inputs)
 
 
 def lat_pair(block):
     count = lax.axis_size("lat")
-    above = lax.ppermute(block, "lat", [(i, i + 1) for i in range(count - 1)])
-    below = lax.ppermute(block, "lat", [(i + 1, i) for i in range(count - 1)])
+    above = lax.ppermute(block, "lat", [(i, (i + 1) % count) for i in range(count)])
+    below = lax.ppermute(block, "lat", [((i + 1) % count, i) for i in range(count)])
     return above, below
 
 
@@ -432,67 +473,66 @@
 ):
     comp = lax.axis_index("comp")
     flags = jnp.stack([comp, lax.axis_index("lat"), jnp.int32(lax.axis_size("lat"))]).astype(jnp.int32)
-    own = jnp.concatenate([state[0].reshape(80, CELLS), direction[0].reshape(80, CELLS)], axis=0)
-    index = regrid_index[0].reshape(SLOTS, CELLS)
-    weight = regrid_weight[0].reshape(SLOTS, CELLS)
-    mask = land_mask.reshape(2, CELLS).astype(F32)
-    bias = jnp.where(comp == 0, air_bias, jnp.concatenate([sea_bias, sea_bias])).reshape(512, 1)
-    flux_weight = air_flux.astype(F32).T
-    forcing_weight = sea_forcing.astype(F32)
-    aloft = aloft_reaction_to_seawarmth.reshape(80, 1)
-
+    (own,) = call(pack_kernel, "pack", [((160, CELLS), BF16)], [state, direction])
     above, below = lat_pair(own)
-    fwd1, fwd2, bwd1, bwd2, hot, share = call(
+    fwd1, fwd2, bwd1, bwd2, hot, share, line, mask, columns = call(
         prepare_kernel,
         "prepare",
         [
             ((512, 720), BF16), ((240, 1536), BF16), ((512, 720), BF16), ((240, 1536), BF16),
-            ((128, SLOTS * CELLS), BF16), ((SLOTS, CELLS), F32),
+            ((128, SLOTS * CELLS), BF16), ((SLOTS, CELLS), F32), ((SLOTS, CELLS), jnp.int32),
+            ((2, CELLS), F32), ((512, 8), F32),
         ],
         [
             flags, air_first.transpose(0, 2, 1), air_second, sea_first.transpose(0, 2, 1),
-            sea_second, index, weight,
+            sea_second, regrid_index, regrid_weight, land_mask, air_bias.reshape(1, 512),
+            sea_bias.reshape(1, 256), air_flux, aloft_reaction_to_seawarmth.reshape(1, 80),
+            sea_forcing.T,
         ],
+        limit=16,
     )
     to_left, to_right = call(
-        edge_kernel, "edges", [((160, 128), BF16)] * 2, [own, above, below]
+        edge_kernel, "edges", [((160, 128), BF16)] * 2, [flags, own, above, below, columns]
     )
     from_left, from_right = lon_pair(to_left, to_right)
     y, slope, payload = call(
         tangent_kernel,
         "tangent",
         [((80, 2 * CELLS), F32), ((512, 4 * PITCH), BF16), ((8, 128), F32)],
-        [flags, own, above, below, from_left, from_right, fwd1, fwd2, bias, flux_weight],
+        [flags, own, above, below, from_left, from_right, fwd1, fwd2, columns],
         [((480, 8 * PITCH), BF16), ((512, 6 * PITCH), BF16)],
+        limit=20,
     )
     near, far = across(payload, payload, -1)
     image, back_near, back_far = call(
         couple_kernel,
         "couple",
         [((80, CELLS), BF16), ((8, 128), F32), ((8, 128), F32)],
-        [flags, y, near, far, hot, index, share, mask, aloft, forcing_weight],
+        [flags, y, near, far, hot, line, share, mask, columns],
     )
     back_near, back_far = across(back_near, back_far, 1)
     (cotangent,) = call(
         cotangent_kernel, "cotangent", [((80, CELLS), BF16)],
-        [flags, image, back_near, back_far, flux_weight],
+        [flags, image, back_near, back_far, columns],
     )
     above, below = lat_pair(cotangent)
     to_left, to_right = call(
-        edge_kernel, "edges_back", [((80, 128), BF16)] * 2, [cotangent, above, below]
+        edge_kernel, "edges_back", [((80, 128), BF16)] * 2,
+        [flags, cotangent, above, below, columns],
     )
     from_left, from_right = lon_pair(to_left, to_right)
     (product,) = call(
         adjoint_kernel,
         "adjoint",
-        [((80, CELLS), BF16)],
+        [((1, 80, ROWS, COLS), BF16)],
         [
             flags, cotangent, above, below, from_left, from_right, bwd1, bwd2, slope,
             back_near, back_far,
         ],
         [((240, 8 * PITCH), BF16), ((512, 6 * PITCH), BF16)],
-    )
-    return image.reshape(1, 80, ROWS, COLS), product.reshape(1, 80, ROWS, COLS)
+        limit=16,
+    )
+    return image.reshape(1, 80, ROWS, COLS), product
 
 
 def solution(mesh):

time: 77.9 us -> 75 us (0.963)
  starting transfers between devices: 25.6 us -> 21.7 us
  waiting for transfers between devices: 18.8 us -> 21.7 us
  local copies, waits for them, and re-layouts: 15.6 us -> 12.9 us
  Pallas kernels: 15.6 us -> 17.4 us
    ppermute x2, waiting for transfers between devices: 3.77 us -> 8.84 us  [lon_pair(): lax.ppermute(to_left, 'lon', [((i + 1) % count, i) for i in range(count)])]
    ppermute x4, waiting for transfers between devices: 8.5 us -> 5.34 us  [the longest x2 3.52 us: lat_pair(): lax.ppermute(block, 'lat', [(i, (i + 1) % count) for i in range(count)])]
    ppermute x4, starting transfers between devices: 8.99 us -> 5.84 us  [the longest x2 5.83 us: lat_pair(): lax.ppermute(block, 'lat', [((i + 1) % count, i) for i in range(count)])]
    reshape x4 -> x1, local copies, waits for them, and re-layouts: 3.1 us -> 0.66 us  [shards(): return (image.reshape(1, 80, ROWS, COLS), product)]
    pallas_call x7 -> x8, Pallas kernels: 15.6 us -> 17.4 us  [call(): pl.pallas_call(kernel, name=name, out_shape=tuple((jax.ShapeDtypeStruct(s...]
    ppermute x2, starting transfers between devices: 2.77 us -> 1.19 us  [across(): same = lax.ppermute(near, 'comp', [(0, 1), (1, 0)])]
    ppermute x2, waiting for transfers between devices: 0.01 us -> 1.34 us  [lon_pair(): lax.ppermute(to_right, 'lon', [(i, (i + 1) % count) for i in range(count)])]
    unnamed x38 -> x32, local copies, waits for them, and re-layouts: 11 us -> 12.2 us
  transfers between devices with their start and end apart: 12 -> 12, of which waited for: 9 -> 8; matrix products, arithmetic and copies ran while one was open for 8% -> 1% of each run, Pallas kernels for 2% -> 2%
where the time goes in v1:
time: 75 us; the launch traced here: 74.4 us
  starting transfers between devices  21.7 us (29%)
  waiting for transfers between devices  21.7 us (29%)
  Pallas kernels  17.4 us (23%)
  local copies, waits for them, and re-layouts  12.9 us (17%)
  between operations  0.75 us (1%)
    pallas_call x8, Pallas kernels, call(): pl.pallas_call(kernel, name=name, out_shape=tuple((jax.ShapeDtypeStruct(s...  17.4 us
    unnamed x32, local copies, waits for them, and re-layouts  12.2 us
    ppermute x2, starting transfers between devices, lon_pair(): lax.ppermute(to_right, 'lon', [(i, (i + 1) % count) for i in range(count)])  11.1 us
    ppermute x2, waiting for transfers between devices, lon_pair(): lax.ppermute(to_left, 'lon', [((i + 1) % count, i) for i in range(count)])  8.84 us
    ppermute x2, waiting for transfers between devices, across(): return (same, lax.ppermute(far, ('comp', 'lon'), route))  6.13 us
    ppermute x2, starting transfers between devices, lat_pair(): lax.ppermute(block, 'lat', [((i + 1) % count, i) for i in range(count)])  5.83 us
    ppermute x2, waiting for transfers between devices, lat_pair(): lax.ppermute(block, 'lat', [(i, (i + 1) % count) for i in range(count)])  3.52 us
    ppermute x2, starting transfers between devices, across(): return (same, lax.ppermute(far, ('comp', 'lon'), route))  3.51 us
  transfers between devices with their start and end apart: 12, of which 8 were waited for; matrix products, arithmetic and copies ran while one was open for 1% of the time, Pallas kernels for 2%

profile of v1, /device:TPU:99, one launch (start us, length us, event | category | flops | bytes accessed | tf_op | source)
XLA Modules:
  0.0 74.4 jit_solution(1454667713861946110)
XLA Ops:
  0.6 0.0 copy-start.6
  0.6 0.9 %copy-done.6 = bf16[1,80,2,256]{3,2,1,0:T(2,128)(2,1)S(1)} copy-done((bf16[1,80,2,256]{3,2,1,0:T(2,128)(2,1)S(1)}, bf16[1,80,2,256]{3,2,1,0:T(2,128)(2,1)}, u32[]{:S(2)}) %copy-start.6) | copy-done | bytes 81944
  1.5 0.0 copy-start.7
  1.5 0.9 %copy-done.7 = bf16[1,80,2,256]{3,2,1,0:T(2,128)(2,1)S(1)} copy-done((bf16[1,80,2,256]{3,2,1,0:T(2,128)(2,1)S(1)}, bf16[1,80,2,256]{3,2,1,0:T(2,128)(2,1)}, u32[]{:S(2)}) %copy-start.7) | copy-done | bytes 81944
  2.4 0.4 pack.1.own
  2.8 2.8 %collective-permute-start.1 = (bf16[160,512]{1,0:T(8,128)(2,1)S(1)}, bf16[160,512]{1,0:T(8,128)(2,1)S(1)}, u32[]{:S(2)}, u32[]{:S(2)}) collective-permute-start(bf16[160,512]{1,0:T(8,128)(2,1)S(1)} %pack.1.own), channel_id=1, source_target_pairs={{32,0},{64,32},{96,64},{0,96},{33,1},{65,33},{97,65},{1,97},{34,2}... | collective-permute-start | bytes 491528 | tf_op jit(solution)/shard_map/ppermute | solution.py:437
  5.7 0.0 collective-permute-start
  5.7 0.1 pad_add_fusion.flags
  5.7 0.0 copy-start
  5.7 1.1 %copy-done = bf16[9,512,80]{1,2,0:T(8,128)(2,1)S(1)} copy-done((bf16[9,512,80]{1,2,0:T(8,128)(2,1)S(1)}, bf16[9,512,80]{1,2,0:T(8,128)(2,1)}, u32[]{:S(2)}) %copy-start) | copy-done | bytes 737304
  6.8 0.0 copy-start.1
  6.9 1.1 %copy-done.1 = bf16[9,80,512]{2,1,0:T(8,128)(2,1)S(1)} copy-done((bf16[9,80,512]{2,1,0:T(8,128)(2,1)S(1)}, bf16[9,80,512]{2,1,0:T(8,128)(2,1)}, u32[]{:S(2)}) %copy-start.1) | copy-done | bytes 737304
  8.0 0.0 copy-start.4
  8.0 0.9 %copy-done.4 = bf16[9,256,40]{1,2,0:T(8,128)(2,1)S(1)} copy-done((bf16[9,256,40]{1,2,0:T(8,128)(2,1)S(1)}, bf16[9,256,40]{1,2,0:T(8,128)(2,1)}, u32[]{:S(2)}) %copy-start.4) | copy-done | bytes 184344
  8.9 0.0 copy-start.5
  8.9 0.9 %copy-done.5 = bf16[9,40,256]{2,1,0:T(8,128)(2,1)S(1)} copy-done((bf16[9,40,256]{2,1,0:T(8,128)(2,1)S(1)}, bf16[9,40,256]{2,1,0:T(8,128)(2,1)}, u32[]{:S(2)}) %copy-start.5) | copy-done | bytes 184344
  9.8 0.0 copy-start.8
  9.8 0.7 copy-done.8
  10.5 0.0 copy-start.9
  10.5 0.7 copy-done.9
  11.2 0.0 copy-start.10
  11.2 0.7 copy-done.10
  11.9 0.0 copy-start.11
  11.9 0.7 copy-done.11
  12.6 0.0 copy-start.12
  12.6 0.7 copy-done.12
  13.3 0.0 copy-start.13
  13.3 0.7 copy-done.13
  14.0 0.0 copy-start.14
  14.0 0.7 copy-done.14
  14.6 0.7 copy-done.15
  15.3 1.4 %prepare.1 = (bf16[512,720]{1,0:T(8,128)(2,1)S(1)}, bf16[240,1536]{1,0:T(8,128)(2,1)S(1)}, bf16[512,720]{1,0:T(8,128)(2,1)S(1)}, bf16[240,1536]{1,0:T(8,128)(2,1...) custom-call(s32[3]{0:T(128)S(1)} %pad_add_fusion.flags, ...), custom_call_target="tpu_custom_call" | custom-call | tf_op jit(solution)/shard_map/prepare/pallas_call | solution.py:423
  16.7 0.0 collective-permute-done.1.below
  16.7 0.0 collective-permute-done.above
  16.7 0.0 copy-start.2
  16.7 0.7 edges.1
  17.5 3.7 %collective-permute-start.2 = (bf16[160,128]{1,0:T(8,128)(2,1)S(1)}, bf16[160,128]{1,0:T(8,128)(2,1)S(1)}, u32[]{:S(2)}, u32[]{:S(2)}) collective-permute-start(bf16[160,128]{1,0:T(8,128)(2,1)S(1)} %get-tuple-element.22), channel_id=1, source_target_pairs={{0,1},{1,2},{2,3},{3,4},{4,5},{5,6},{6,7},{7,8},{8,9},{9,10},{10,1... | collective-permute-start | bytes 122888 | tf_op jit(solution)/shard_map/ppermute | solution.py:443
  21.2 0.0 collective-permute-start.3
  21.2 1.1 %collective-permute-done.2.from_left = bf16[160,128]{1,0:T(8,128)(2,1)S(1)} collective-permute-done((bf16[160,128]{1,0:T(8,128)(2,1)S(1)}, bf16[160,128]{1,0:T(8,128)(2,1)S(1)}, u32[]{:S(2)}, u32[]{:S(2)}) %collective-permute-start.2) | collective-permute-done | bytes 40992 | tf_op jit(solution)/shard_map/ppermute | solution.py:443
  22.3 4.4 %collective-permute-done.3.from_right = bf16[160,128]{1,0:T(8,128)(2,1)S(1)} collective-permute-done((bf16[160,128]{1,0:T(8,128)(2,1)S(1)}, bf16[160,128]{1,0:T(8,128)(2,1)S(1)}, u32[]{:S(2)}, u32[]{:S(2)}) %collective-permute-start.3) | collective-permute-done | bytes 40992 | tf_op jit(solution)/shard_map/ppermute | solution.py:444
  26.7 0.0 copy-done.2
  26.7 0.9 %copy-done.3 = bf16[160,512]{1,0:T(8,128)(2,1)S(1)} copy-done((bf16[160,512]{1,0:T(8,128)(2,1)S(1)}, bf16[160,512]{1,0:T(8,128)(2,1)}, u32[]{:S(2)}) %copy-start.3) | copy-done | bytes 163864
  27.7 7.0 %tangent.1 = (f32[80,1024]{1,0:T(8,128)S(1)}, bf16[512,1536]{1,0:T(8,128)(2,1)S(1)}, f32[8,128]{1,0:T(8,128)S(1)}) custom-call(s32[3]{0:T(128)S(1)} %pad_add_fusion.flags, bf16[160,512]{1,0:T(8,128)(2,1)S(1)} %pack.1.own, bf16[160,512]{1,0:T(8,128)(2,1)S(1)} %copy-done.3, bf16[160,512]{1,0:T(8,128)(2,1)S(1)} %collective-permute-done.1.below, ...), custom_call_target="tpu_custom_call" | custom-call | tf_op jit(solution)/shard_map/tangent/pallas_call | solution.py:423
  34.7 0.1 collective-permute-start.5
  34.7 0.1 collective-permute-start.4
  34.8 5.0 %collective-permute-done.5.far = f32[8,128]{1,0:T(8,128)S(1)} collective-permute-done((f32[8,128]{1,0:T(8,128)S(1)}, f32[8,128]{1,0:T(8,128)S(1)}, u32[]{:S(2)}, u32[]{:S(2)}) %collective-permute-start.5) | collective-permute-done | bytes 4128 | tf_op jit(solution)/shard_map/ppermute | solution.py:455
  39.9 0.0 collective-permute-done.4.near
  39.9 1.3 %couple.1 = (bf16[80,512]{1,0:T(8,128)(2,1)S(1)}, f32[8,128]{1,0:T(8,128)S(1)}, f32[8,128]{1,0:T(8,128)S(1)}) custom-call(s32[3]{0:T(128)S(1)} %pad_add_fusion.flags, f32[80,1024]{1,0:T(8,128)S(1)} %get-tuple-element.26.y, f32[8,128]{1,0:T(8,128)S(1)} %collective-permute-done.4.near, f32[8,128]{1,0:T(8,128)S(1)} %collective-permute-done.5.far, ...), custom_call_target="tpu_custom_call" | custom-call | tf_op jit(solution)/shard_map/couple/pallas_call | solution.py:423
  41.2 1.1 %collective-permute-start.6 = (f32[8,128]{1,0:T(8,128)S(1)}, f32[8,128]{1,0:T(8,128)S(1)}, u32[]{:S(2)}, u32[]{:S(2)}) collective-permute-start(f32[8,128]{1,0:T(8,128)S(1)} %get-tuple-element.33), channel_id=1, source_target_pairs={{0,128},{128,0},{1,129},{129,1},{2,130},{130,2},{3,131},{131,3},{4... | collective-permute-start | bytes 12296 | tf_op jit(solution)/shard_map/ppermute | solution.py:450
  42.3 3.4 %collective-permute-start.7 = (f32[8,128]{1,0:T(8,128)S(1)}, f32[8,128]{1,0:T(8,128)S(1)}, u32[]{:S(2)}, u32[]{:S(2)}) collective-permute-start(f32[8,128]{1,0:T(8,128)S(1)} %get-tuple-element.34), channel_id=1, source_target_pairs={{0,129},{1,130},{2,131},{3,132},{4,133},{5,134},{6,135},{7,136},{8... | collective-permute-start | bytes 12296 | tf_op jit(solution)/shard_map/ppermute | solution.py:455
  45.7 0.0 collective-permute-done.6.near
  45.7 1.1 %collective-permute-done.7.far = f32[8,128]{1,0:T(8,128)S(1)} collective-permute-done((f32[8,128]{1,0:T(8,128)S(1)}, f32[8,128]{1,0:T(8,128)S(1)}, u32[]{:S(2)}, u32[]{:S(2)}) %collective-permute-start.7) | collective-permute-done | bytes 4128 | tf_op jit(solution)/shard_map/ppermute | solution.py:455
  46.8 0.6 cotangent.1.own
  47.5 3.0 %collective-permute-start.9 = (bf16[80,512]{1,0:T(8,128)(2,1)S(1)}, bf16[80,512]{1,0:T(8,128)(2,1)S(1)}, u32[]{:S(2)}, u32[]{:S(2)}) collective-permute-start(bf16[80,512]{1,0:T(8,128)(2,1)S(1)} %cotangent.1.own), channel_id=1, source_target_pairs={{32,0},{64,32},{96,64},{0,96},{33,1},{65,33},{97,65},{1,97},{34,2}... | collective-permute-start | bytes 245768 | tf_op jit(solution)/shard_map/ppermute | solution.py:437
  50.5 0.0 collective-permute-start.8
  50.5 1.8 %collective-permute-done.9.below = bf16[80,512]{1,0:T(8,128)(2,1)S(1)} collective-permute-done((bf16[80,512]{1,0:T(8,128)(2,1)S(1)}, bf16[80,512]{1,0:T(8,128)(2,1)S(1)}, u32[]{:S(2)}, u32[]{:S(2)}) %collective-permute-start.9) | collective-permute-done | bytes 81952 | tf_op jit(solution)/shard_map/ppermute | solution.py:437
  52.3 3.5 %collective-permute-done.8.above = bf16[80,512]{1,0:T(8,128)(2,1)S(1)} collective-permute-done((bf16[80,512]{1,0:T(8,128)(2,1)S(1)}, bf16[80,512]{1,0:T(8,128)(2,1)S(1)}, u32[]{:S(2)}, u32[]{:S(2)}) %collective-permute-start.8) | collective-permute-done | bytes 81952 | tf_op jit(solution)/shard_map/ppermute | solution.py:436
  55.9 0.7 edges_back.1
  56.5 7.4 %collective-permute-start.10 = (bf16[80,128]{1,0:T(8,128)(2,1)S(1)}, bf16[80,128]{1,0:T(8,128)(2,1)S(1)}, u32[]{:S(2)}, u32[]{:S(2)}) collective-permute-start(bf16[80,128]{1,0:T(8,128)(2,1)S(1)} %get-tuple-element.35), channel_id=1, source_target_pairs={{0,1},{1,2},{2,3},{3,4},{4,5},{5,6},{6,7},{7,8},{8,9},{9,10},{10,1... | collective-permute-start | bytes 61448 | tf_op jit(solution)/shard_map/ppermute | solution.py:443
  63.9 0.0 collective-permute-start.11
  63.9 0.7 reshape.19
  64.6 0.2 collective-permute-done.10.from_left
  64.8 4.4 %collective-permute-done.11.from_right = bf16[80,128]{1,0:T(8,128)(2,1)S(1)} collective-permute-done((bf16[80,128]{1,0:T(8,128)(2,1)S(1)}, bf16[80,128]{1,0:T(8,128)(2,1)S(1)}, u32[]{:S(2)}, u32[]{:S(2)}) %collective-permute-start.11) | collective-permute-done | bytes 20512 | tf_op jit(solution)/shard_map/ppermute | solution.py:444
  69.2 5.2 %adjoint.1 = bf16[1,80,2,256]{3,2,1,0:T(2,128)(2,1)} custom-call(s32[3]{0:T(128)S(1)} %pad_add_fusion.flags, bf16[80,512]{1,0:T(8,128)(2,1)S(1)} %cotangent.1.own, bf16[80,512]{1,0:T(8,128)(2,1)S(1)} %collective-permute-done.8.above, bf16[80,512]{1,0:T(8,128)(2,1)S(1)} %collective-permute-done.9.below, ...), custom_call_target="tpu_custom_call" | custom-call | tf_op jit(solution)/shard_map/adjoint/pallas_call | solution.py:423
  (2 shorter events, 0.0 us)
Async XLA Ops:
  0.6 0.9 %copy-start.6 = (bf16[1,80,2,256]{3,2,1,0:T(2,128)(2,1)S(1)}, bf16[1,80,2,256]{3,2,1,0:T(2,128)(2,1)}, u32[]{:S(2)}) copy-start(bf16[1,80,2,256]{3,2,1,0:T(2,128)(2,1)} %state.1) | copy-start | bytes 245764
  1.5 0.9 %copy-start.7 = (bf16[1,80,2,256]{3,2,1,0:T(2,128)(2,1)S(1)}, bf16[1,80,2,256]{3,2,1,0:T(2,128)(2,1)}, u32[]{:S(2)}) copy-start(bf16[1,80,2,256]{3,2,1,0:T(2,128)(2,1)} %direction.1) | copy-start | bytes 245764
  2.8 13.8 %collective-permute-start.1 = (bf16[160,512]{1,0:T(8,128)(2,1)S(1)}, bf16[160,512]{1,0:T(8,128)(2,1)S(1)}, u32[]{:S(2)}, u32[]{:S(2)}) collective-permute-start(bf16[160,512]{1,0:T(8,128)(2,1)S(1)} %pack.1.own), channel_id=1, source_target_pairs={{32,0},{64,32},{96,64},{0,96},{33,1},{65,33},{97,65},{1,97},{34,2}... | collective-permute-start | bytes 491528 | tf_op jit(solution)/shard_map/ppermute | solution.py:437
  5.7 11.0 %collective-permute-start = (bf16[160,512]{1,0:T(8,128)(2,1)S(1)}, bf16[160,512]{1,0:T(8,128)(2,1)S(1)}, u32[]{:S(2)}, u32[]{:S(2)}) collective-permute-start(bf16[160,512]{1,0:T(8,128)(2,1)S(1)} %pack.1.own), channel_id=1, source_target_pairs={{0,32},{32,64},{64,96},{96,0},{1,33},{33,65},{65,97},{97,1},{2,34}... | collective-permute-start | bytes 491528 | tf_op jit(solution)/shard_map/ppermute | solution.py:436
  5.7 1.1 %copy-start = (bf16[9,512,80]{1,2,0:T(8,128)(2,1)S(1)}, bf16[9,512,80]{1,2,0:T(8,128)(2,1)}, u32[]{:S(2)}) copy-start(bf16[9,512,80]{1,2,0:T(8,128)(2,1)} %param.16) | copy-start | bytes 2211844
  6.8 1.1 %copy-start.1 = (bf16[9,80,512]{2,1,0:T(8,128)(2,1)S(1)}, bf16[9,80,512]{2,1,0:T(8,128)(2,1)}, u32[]{:S(2)}) copy-start(bf16[9,80,512]{2,1,0:T(8,128)(2,1)} %second_a.1) | copy-start | bytes 2211844
  8.0 0.9 %copy-start.4 = (bf16[9,256,40]{1,2,0:T(8,128)(2,1)S(1)}, bf16[9,256,40]{1,2,0:T(8,128)(2,1)}, u32[]{:S(2)}) copy-start(bf16[9,256,40]{1,2,0:T(8,128)(2,1)} %param.21) | copy-start | bytes 552964
  8.9 0.9 %copy-start.5 = (bf16[9,40,256]{2,1,0:T(8,128)(2,1)S(1)}, bf16[9,40,256]{2,1,0:T(8,128)(2,1)}, u32[]{:S(2)}) copy-start(bf16[9,40,256]{2,1,0:T(8,128)(2,1)} %second_o.1) | copy-start | bytes 552964
  9.8 0.7 copy-start.8
  10.5 0.7 copy-start.9
  11.2 0.7 copy-start.10
  11.9 0.7 copy-start.11
  12.6 0.7 copy-start.12
  13.3 0.7 copy-start.13
  14.0 0.7 copy-start.14
  14.6 0.7 copy-start.15
  16.7 10.0 %copy-start.2 = (bf16[160,512]{1,0:T(8,128)(2,1)}, bf16[160,512]{1,0:T(8,128)(2,1)S(1)}, u32[]{:S(2)}) copy-start(bf16[160,512]{1,0:T(8,128)(2,1)S(1)} %collective-permute-done.above) | copy-start | bytes 491524
  17.5 4.8 %collective-permute-start.2 = (bf16[160,128]{1,0:T(8,128)(2,1)S(1)}, bf16[160,128]{1,0:T(8,128)(2,1)S(1)}, u32[]{:S(2)}, u32[]{:S(2)}) collective-permute-start(bf16[160,128]{1,0:T(8,128)(2,1)S(1)} %get-tuple-element.22), channel_id=1, source_target_pairs={{0,1},{1,2},{2,3},{3,4},{4,5},{5,6},{6,7},{7,8},{8,9},{9,10},{10,1... | collective-permute-start | bytes 122888 | tf_op jit(solution)/shard_map/ppermute | solution.py:443
  21.2 5.5 %collective-permute-start.3 = (bf16[160,128]{1,0:T(8,128)(2,1)S(1)}, bf16[160,128]{1,0:T(8,128)(2,1)S(1)}, u32[]{:S(2)}, u32[]{:S(2)}) collective-permute-start(bf16[160,128]{1,0:T(8,128)(2,1)S(1)} %get-tuple-element.23), channel_id=1, source_target_pairs={{1,0},{2,1},{3,2},{4,3},{5,4},{6,5},{7,6},{8,7},{9,8},{10,9},{11,1... | collective-permute-start | bytes 122888 | tf_op jit(solution)/shard_map/ppermute | solution.py:444
  26.7 0.9 %copy-start.3 = (bf16[160,512]{1,0:T(8,128)(2,1)S(1)}, bf16[160,512]{1,0:T(8,128)(2,1)}, u32[]{:S(2)}) copy-start(bf16[160,512]{1,0:T(8,128)(2,1)} %copy-done.2) | copy-start | bytes 491524
  34.7 5.2 %collective-permute-start.5 = (f32[8,128]{1,0:T(8,128)S(1)}, f32[8,128]{1,0:T(8,128)S(1)}, u32[]{:S(2)}, u32[]{:S(2)}) collective-permute-start(f32[8,128]{1,0:T(8,128)S(1)} %get-tuple-element.27), channel_id=1, source_target_pairs={{0,159},{1,128},{2,129},{3,130},{4,131},{5,132},{6,133},{7,134},{8... | collective-permute-start | bytes 12296 | tf_op jit(solution)/shard_map/ppermute | solution.py:455
  34.7 5.1 %collective-permute-start.4 = (f32[8,128]{1,0:T(8,128)S(1)}, f32[8,128]{1,0:T(8,128)S(1)}, u32[]{:S(2)}, u32[]{:S(2)}) collective-permute-start(f32[8,128]{1,0:T(8,128)S(1)} %get-tuple-element.27), channel_id=1, source_target_pairs={{0,128},{128,0},{1,129},{129,1},{2,130},{130,2},{3,131},{131,3},{4... | collective-permute-start | bytes 12296 | tf_op jit(solution)/shard_map/ppermute | solution.py:450
  41.2 4.5 %collective-permute-start.6 = (f32[8,128]{1,0:T(8,128)S(1)}, f32[8,128]{1,0:T(8,128)S(1)}, u32[]{:S(2)}, u32[]{:S(2)}) collective-permute-start(f32[8,128]{1,0:T(8,128)S(1)} %get-tuple-element.33), channel_id=1, source_target_pairs={{0,128},{128,0},{1,129},{129,1},{2,130},{130,2},{3,131},{131,3},{4... | collective-permute-start | bytes 12296 | tf_op jit(solution)/shard_map/ppermute | solution.py:450
  42.3 4.5 %collective-permute-start.7 = (f32[8,128]{1,0:T(8,128)S(1)}, f32[8,128]{1,0:T(8,128)S(1)}, u32[]{:S(2)}, u32[]{:S(2)}) collective-permute-start(f32[8,128]{1,0:T(8,128)S(1)} %get-tuple-element.34), channel_id=1, source_target_pairs={{0,129},{1,130},{2,131},{3,132},{4,133},{5,134},{6,135},{7,136},{8... | collective-permute-start | bytes 12296 | tf_op jit(solution)/shard_map/ppermute | solution.py:455
  47.5 4.8 %collective-permute-start.9 = (bf16[80,512]{1,0:T(8,128)(2,1)S(1)}, bf16[80,512]{1,0:T(8,128)(2,1)S(1)}, u32[]{:S(2)}, u32[]{:S(2)}) collective-permute-start(bf16[80,512]{1,0:T(8,128)(2,1)S(1)} %cotangent.1.own), channel_id=1, source_target_pairs={{32,0},{64,32},{96,64},{0,96},{33,1},{65,33},{97,65},{1,97},{34,2}... | collective-permute-start | bytes 245768 | tf_op jit(solution)/shard_map/ppermute | solution.py:437
  50.5 5.3 %collective-permute-start.8 = (bf16[80,512]{1,0:T(8,128)(2,1)S(1)}, bf16[80,512]{1,0:T(8,128)(2,1)S(1)}, u32[]{:S(2)}, u32[]{:S(2)}) collective-permute-start(bf16[80,512]{1,0:T(8,128)(2,1)S(1)} %cotangent.1.own), channel_id=1, source_target_pairs={{0,32},{32,64},{64,96},{96,0},{1,33},{33,65},{65,97},{97,1},{2,34}... | collective-permute-start | bytes 245768 | tf_op jit(solution)/shard_map/ppermute | solution.py:436
  56.5 8.3 %collective-permute-start.10 = (bf16[80,128]{1,0:T(8,128)(2,1)S(1)}, bf16[80,128]{1,0:T(8,128)(2,1)S(1)}, u32[]{:S(2)}, u32[]{:S(2)}) collective-permute-start(bf16[80,128]{1,0:T(8,128)(2,1)S(1)} %get-tuple-element.35), channel_id=1, source_target_pairs={{0,1},{1,2},{2,3},{3,4},{4,5},{5,6},{6,7},{7,8},{8,9},{9,10},{10,1... | collective-permute-start | bytes 61448 | tf_op jit(solution)/shard_map/ppermute | solution.py:443
  63.9 5.3 %collective-permute-start.11 = (bf16[80,128]{1,0:T(8,128)(2,1)S(1)}, bf16[80,128]{1,0:T(8,128)(2,1)S(1)}, u32[]{:S(2)}, u32[]{:S(2)}) collective-permute-start(bf16[80,128]{1,0:T(8,128)(2,1)S(1)} %get-tuple-element.36), channel_id=1, source_target_pairs={{1,0},{2,1},{3,2},{4,3},{5,4},{6,5},{7,6},{8,7},{9,8},{10,9},{11,1... | collective-permute-start | bytes 61448 | tf_op jit(solution)/shard_map/ppermute | solution.py:444

commit v2 on v1

--- a/solution.py
+++ b/solution.py
@@ -16,6 +16,22 @@
 SLOTS = 8
 
 
+def is_air():
+    return lax.axis_index("comp") == 0
+
+
+def is_sea():
+    return lax.axis_index("comp") != 0
+
+
+def at_top():
+    return lax.axis_index("lat") == 0
+
+
+def at_bottom():
+    return lax.axis_index("lat") == lax.axis_size("lat") - 1
+
+
 def lane_iota(shape):
     return lax.broadcasted_iota(jnp.int32, shape, 1)
 
@@ -30,9 +46,9 @@
     return lax.dot_general(left, right, (((1,), (0,)), ((), ())), preferred_element_type=F32)
 
 
-def sources(flags, own, above, below):
-    upper = jnp.where(flags[1] == 0, 0.0, 1.0).astype(F32)
-    lower = jnp.where(flags[1] == flags[2] - 1, 0.0, 1.0).astype(F32)
+def sources(own, above, below):
+    upper = jnp.where(at_top(), 0.0, 1.0).astype(F32)
+    lower = jnp.where(at_bottom(), 0.0, 1.0).astype(F32)
     chosen = []
     for ref, scale in ((above, upper), (own, None), (below, lower)):
         for r in range(ROWS):
@@ -45,17 +61,44 @@
     return chosen
 
 
-def pack_kernel(state, direction, packed):
+def pack_kernel(state, direction, packed, rows, sems):
+    copies = []
     for field, ref in enumerate((state, direction)):
-        block = ref[0].astype(F32)
+        copies.append(pltpu.make_async_copy(ref.at[0], rows.at[field], sems.at[field]))
+        copies[-1].start()
+    for field, copy in enumerate(copies):
+        copy.wait()
+        block = rows[field].astype(F32)
         for r in range(ROWS):
             packed[field * 80 : field * 80 + 80, r * COLS : (r + 1) * COLS] = block[:, r, :].astype(BF16)
 
 
-def prepare_kernel(
-    flags, first_a, second_a, first_o, second_o, index, weight, land, bias_a, bias_o, flux, aloft,
-    forcing, fwd1, fwd2, bwd1, bwd2, hot, share, line, mask, columns,
-):
+def prepare_kernel(*refs):
+    sources = refs[:12]
+    fwd1, fwd2, bwd1, bwd2, hot, share, line, mask, columns = refs[12:21]
+    held = refs[21:33]
+    sems = refs[33]
+    copies = [
+        pltpu.make_async_copy(source, target, sems.at[i])
+        for i, (source, target) in enumerate(zip(sources, held))
+    ]
+    first_a, second_a, first_o, second_o, index, weight, land, bias_a, bias_o, flux, aloft, forcing = held
+    for copy in copies[4:]:
+        copy.start()
+
+    @pl.when(is_air())
+    def _():
+        for copy in copies[:2]:
+            copy.start()
+
+    @pl.when(is_sea())
+    def _():
+        for copy in copies[2:4]:
+            copy.start()
+
+    for copy in copies[4:]:
+        copy.wait()
+
     def flat(rows):
         return jnp.concatenate([rows[r : r + 1] for r in range(ROWS)], axis=1)
 
@@ -94,7 +137,7 @@
     line[...] = ((place >> 8) & 1) * 8 + (place >> 9) * 2 + ((place >> 7) & 1)
     mask[...] = jnp.concatenate([flat(land[s]) for s in range(2)], axis=0).astype(F32)
     pad = jnp.zeros((1, 512 - 80), F32)
-    bias = jnp.where(flags[0] == 0, bias_a[...], jnp.concatenate([bias_o[...]] * 2, axis=1))
+    bias = jnp.where(is_air(), bias_a[...], jnp.concatenate([bias_o[...]] * 2, axis=1))
     rows = [bias] + [jnp.concatenate([flux[f : f + 1, :].astype(F32), pad], axis=1) for f in range(2)]
     rows.append(jnp.concatenate([aloft[...], pad], axis=1))
     pad = jnp.zeros((1, 512 - 40), F32)
@@ -102,13 +145,17 @@
     rows.append(jnp.zeros((2, 512), F32))
     columns[...] = jnp.concatenate(rows, axis=0).T
 
-    @pl.when(flags[0] == 0)
-    def _():
+    @pl.when(is_air())
+    def _():
+        for copy in copies[:2]:
+            copy.wait()
         weights(first_a, second_a, first_a.shape[1])
         share[...] = table / jnp.sum(table, axis=0, keepdims=True)
 
-    @pl.when(flags[0] != 0)
-    def _():
+    @pl.when(is_sea())
+    def _():
+        for copy in copies[2:4]:
+            copy.wait()
         weights(first_o, second_o, first_o.shape[1])
         upper = jnp.sum(table[:4], axis=0, keepdims=True)
         lower = jnp.sum(table[4:], axis=0, keepdims=True)
@@ -121,12 +168,12 @@
         hot[:, slot * CELLS : (slot + 1) * CELLS] = jnp.where(lanes == low, 1.0, 0.0).astype(BF16)
 
 
-def edge_kernel(flags, own, above, below, after, to_left, to_right):
+def edge_kernel(own, above, below, after, to_left, to_right):
     channels = own.shape[0]
     lanes = lane_iota((channels, 128))
     left = jnp.zeros((channels, 128), F32)
     right = jnp.zeros((channels, 128), F32)
-    for place, (read, r) in enumerate(sources(flags, own, above, below)):
+    for place, (read, r) in enumerate(sources(own, above, below)):
         initial = read(slice(0, channels), 0, 128)
         last = read(slice(0, channels), 128, COLS)
         here = (lanes >> 1) == place
@@ -150,22 +197,22 @@
     return jnp.concatenate(pieces, axis=0).astype(BF16)
 
 
-def air_rows(flags, own, above, below, from_left, from_right, fields, store):
+def air_rows(own, above, below, from_left, from_right, fields, store):
     for field in range(fields):
         part = slice(field * 80, (field + 1) * 80)
         left = from_left[part, :].astype(F32)
         right = from_right[part, :].astype(F32)
-        for place, (read, r) in enumerate(sources(flags, own, above, below)):
+        for place, (read, r) in enumerate(sources(own, above, below)):
             main = read(part, 0, COLS)
             store(field, place, shifted_rows(main, place, left, right, 0))
 
 
-def sea_rows(flags, own, above, below, from_left, from_right, fields, store):
+def sea_rows(own, above, below, from_left, from_right, fields, store):
     for field in range(fields):
         part = slice(field * 80, (field + 1) * 80)
         left = from_left[part, :].astype(F32)
         right = from_right[part, :].astype(F32)
-        for place, (read, r) in enumerate(sources(flags, own, above, below)):
+        for place, (read, r) in enumerate(sources(own, above, below)):
             main = read(part, 0, COLS)
             for half in range(2):
                 fine = 2 * (2 * (place // 2) + half - 1) + r
@@ -190,20 +237,20 @@
     return total[:, :COLS]
 
 
-def pole_scale(flags, place, count):
-    outside = ((flags[1] == 0) & (place == 0)) | ((flags[1] == flags[2] - 1) & (place == count - 1))
+def pole_scale(place, count):
+    outside = (at_top() & (place == 0)) | (at_bottom() & (place == count - 1))
     return jnp.where(outside, 0.0, 1.0).astype(F32)
 
 
 def tangent_kernel(
-    flags, own, above, below, from_left, from_right, fwd1, fwd2, columns,
+    own, above, below, from_left, from_right, fwd1, fwd2, columns,
     y, slope, payload, stack, hidden,
 ):
     def run(channels, width, depth, count, slope_slice):
         padded = depth // 3
 
         def one_row(place, unused):
-            scale = pole_scale(flags, place, count)
+            scale = pole_scale(place, count)
             base = dot(fwd1[:width, :depth], tap_stack(stack, 0, padded, place))
             tangent = dot(fwd1[:width, :depth], tap_stack(stack, padded, padded, place))
             steep = 1.0 - jnp.tanh(base + columns[:width, 0:1]) ** 2
@@ -217,12 +264,12 @@
         taps = tap_stack(hidden, 0, width, place)
         return joined_taps(dot(fwd2[: 3 * channels, : 3 * width], taps), channels)
 
-    @pl.when(flags[0] == 0)
+    @pl.when(is_air())
     def _():
         def store(field, place, rows):
             stack[field * 240 : field * 240 + 240, place * PITCH : (place + 1) * PITCH] = rows
 
-        air_rows(flags, own, above, below, from_left, from_right, 2, store)
+        air_rows(own, above, below, from_left, from_right, 2, store)
 
         def keep(place, rows):
             slope[:, row_span(place)] = rows
@@ -237,12 +284,12 @@
                     line = f * 4 + r * 2 + part
                     payload[line : line + 1, :] = flux[:, part * 128 : (part + 1) * 128]
 
-    @pl.when(flags[0] != 0)
+    @pl.when(is_sea())
     def _():
         def store(field, place, rows):
             stack[field * 128 : field * 128 + 128, place * PITCH : (place + 1) * PITCH] = rows
 
-        sea_rows(flags, own, above, below, from_left, from_right, 2, store)
+        sea_rows(own, above, below, from_left, from_right, 2, store)
 
         def keep(place, rows):
             @pl.when(place < 4)
@@ -264,7 +311,7 @@
 
 
 def couple_kernel(
-    flags, y, near, far, hot, line, share, mask, columns, image, back_near, back_far
+    y, near, far, hot, line, share, mask, columns, image, back_near, back_far
 ):
     window = jnp.concatenate([near[...], far[...]], axis=0)
     parts = dot(split_parts(window), hot[...])
@@ -290,7 +337,7 @@
         chosen = jnp.where(lines == line_of(slot) + offset, gathered[:, span(slot)], 0.0)
         return share[slot : slot + 1, :] * jnp.sum(chosen, axis=0, keepdims=True)
 
-    @pl.when(flags[0] == 0)
+    @pl.when(is_air())
     def _():
         aloft = columns[:80, 3:4]
         lifted = pick(0, 0)
@@ -305,7 +352,7 @@
             pieces.append(jnp.where(lines == line_of(slot), value, 0.0))
         scatter(pieces)
 
-    @pl.when(flags[0] != 0)
+    @pl.when(is_sea())
     def _():
         forcing_weight = columns[:40, 4:6]
         halves = []
@@ -335,8 +382,8 @@
         scatter(pieces)
 
 
-def cotangent_kernel(flags, image, near, far, columns, cotangent):
-    @pl.when(flags[0] == 0)
+def cotangent_kernel(image, near, far, columns, cotangent):
+    @pl.when(is_air())
     def _():
         arrived = near[...] + far[...]
         total = image[...].astype(F32)
@@ -345,7 +392,7 @@
             total = total + columns[:80, 1 + f : 2 + f] * row
         cotangent[...] = total.astype(BF16)
 
-    @pl.when(flags[0] != 0)
+    @pl.when(is_sea())
     def _():
         cotangent[...] = image[...]
 
@@ -355,14 +402,14 @@
 
 
 def adjoint_kernel(
-    flags, own, above, below, from_left, from_right, bwd1, bwd2, slope, near, far,
+    own, above, below, from_left, from_right, bwd1, bwd2, slope, near, far,
     product, stack, hidden,
 ):
     def run(width, depth, count, slope_slice):
         padded = depth // 3
 
         def one_row(place, unused):
-            scale = pole_scale(flags, place, count)
+            scale = pole_scale(place, count)
             back = dot(bwd1[:width, :depth], tap_stack(stack, 0, padded, place))
             back = back * slope_slice(place).astype(F32) * scale
             hidden[:width, row_span(place)] = back.astype(BF16)
@@ -374,24 +421,24 @@
         taps = tap_stack(hidden, 0, width, place)
         return joined_taps(dot(bwd2[: 3 * channels, : 3 * width], taps), channels)
 
-    @pl.when(flags[0] == 0)
+    @pl.when(is_air())
     def _():
         def store(field, place, rows):
             stack[:240, place * PITCH : (place + 1) * PITCH] = rows
 
-        air_rows(flags, own, above, below, from_left, from_right, 1, store)
+        air_rows(own, above, below, from_left, from_right, 1, store)
         run(512, 720, 4, lambda place: slope[:, row_span(place)])
         rows = []
         for r in range(ROWS):
             rows.append(second(80, 512, r))
         spread_rows(product, rows)
 
-    @pl.when(flags[0] != 0)
+    @pl.when(is_sea())
     def _():
         def store(field, place, rows):
             stack[:128, place * PITCH : (place + 1) * PITCH] = rows
 
-        sea_rows(flags, own, above, below, from_left, from_right, 1, store)
+        sea_rows(own, above, below, from_left, from_right, 1, store)
 
         def slope_slice(place):
             upper = slope[:256, row_span(jnp.minimum(place, 3))]
@@ -414,19 +461,19 @@
         spread_rows(product, rows)
 
 
-def call(kernel, name, out_shape, inputs, scratch=(), limit=8):
-    smem = pl.BlockSpec(memory_space=pltpu.SMEM)
+def call(kernel, name, out_shape, inputs, scratch=(), limit=8, loads=False):
     vmem = pl.BlockSpec(memory_space=pltpu.VMEM)
-    flagged = inputs[0].ndim == 1
-    specs = [smem if flagged and i == 0 else vmem for i in range(len(inputs))]
-    out_specs = tuple(vmem for _ in out_shape)
+    source = vmem
+    if loads:
+        source = pl.BlockSpec(memory_space=pltpu.HBM)
+        inputs = [pltpu.with_memory_space_constraint(array, pltpu.HBM) for array in inputs]
     return pl.pallas_call(
         kernel,
         name=name,
         out_shape=tuple(jax.ShapeDtypeStruct(shape, dtype) for shape, dtype in out_shape),
-        in_specs=specs,
-        out_specs=out_specs,
-        scratch_shapes=[pltpu.VMEM(shape, dtype) for shape, dtype in scratch],
+        in_specs=[source] * len(inputs),
+        out_specs=tuple(vmem for _ in out_shape),
+        scratch_shapes=list(scratch),
         compiler_params=pltpu.CompilerParams(vmem_limit_bytes=limit << 20),
     )(*inputs)
 
@@ -471,10 +518,29 @@
     regrid_weight,
     land_mask,
 ):
-    comp = lax.axis_index("comp")
-    flags = jnp.stack([comp, lax.axis_index("lat"), jnp.int32(lax.axis_size("lat"))]).astype(jnp.int32)
-    (own,) = call(pack_kernel, "pack", [((160, CELLS), BF16)], [state, direction])
+    (own,) = call(
+        pack_kernel,
+        "pack",
+        [((160, CELLS), BF16)],
+        [state, direction],
+        [pltpu.VMEM((2, 80, ROWS, COLS), BF16), pltpu.SemaphoreType.DMA((2,))],
+        loads=True,
+    )
     above, below = lat_pair(own)
+    raw = [
+        air_first.transpose(0, 2, 1),
+        air_second,
+        sea_first.transpose(0, 2, 1),
+        sea_second,
+        regrid_index,
+        regrid_weight,
+        land_mask,
+        air_bias.reshape(1, 512),
+        sea_bias.reshape(1, 256),
+        air_flux,
+        aloft_reaction_to_seawarmth.reshape(1, 80),
+        sea_forcing.T,
+    ]
     fwd1, fwd2, bwd1, bwd2, hot, share, line, mask, columns = call(
         prepare_kernel,
         "prepare",
@@ -483,24 +549,21 @@
             ((128, SLOTS * CELLS), BF16), ((SLOTS, CELLS), F32), ((SLOTS, CELLS), jnp.int32),
             ((2, CELLS), F32), ((512, 8), F32),
         ],
-        [
-            flags, air_first.transpose(0, 2, 1), air_second, sea_first.transpose(0, 2, 1),
-            sea_second, regrid_index, regrid_weight, land_mask, air_bias.reshape(1, 512),
-            sea_bias.reshape(1, 256), air_flux, aloft_reaction_to_seawarmth.reshape(1, 80),
-            sea_forcing.T,
-        ],
-        limit=16,
+        raw,
+        [pltpu.VMEM(array.shape, array.dtype) for array in raw] + [pltpu.SemaphoreType.DMA((12,))],
+        limit=20,
+        loads=True,
     )
     to_left, to_right = call(
-        edge_kernel, "edges", [((160, 128), BF16)] * 2, [flags, own, above, below, columns]
+        edge_kernel, "edges", [((160, 128), BF16)] * 2, [own, above, below, columns]
     )
     from_left, from_right = lon_pair(to_left, to_right)
     y, slope, payload = call(
         tangent_kernel,
         "tangent",
         [((80, 2 * CELLS), F32), ((512, 4 * PITCH), BF16), ((8, 128), F32)],
-        [flags, own, above, below, from_left, from_right, fwd1, fwd2, columns],
-        [((480, 8 * PITCH), BF16), ((512, 6 * PITCH), BF16)],
+        [own, above, below, from_left, from_right, fwd1, fwd2, columns],
+        [pltpu.VMEM((480, 8 * PITCH), BF16), pltpu.VMEM((512, 6 * PITCH), BF16)],
         limit=20,
     )
     near, far = across(payload, payload, -1)
@@ -508,17 +571,17 @@
         couple_kernel,
         "couple",
         [((80, CELLS), BF16), ((8, 128), F32), ((8, 128), F32)],
-        [flags, y, near, far, hot, line, share, mask, columns],
+        [y, near, far, hot, line, share, mask, columns],
     )
     back_near, back_far = across(back_near, back_far, 1)
     (cotangent,) = call(
         cotangent_kernel, "cotangent", [((80, CELLS), BF16)],
-        [flags, image, back_near, back_far, columns],
+        [image, back_near, back_far, columns],
     )
     above, below = lat_pair(cotangent)
     to_left, to_right = call(
         edge_kernel, "edges_back", [((80, 128), BF16)] * 2,
-        [flags, cotangent, above, below, columns],
+        [cotangent, above, below, columns],
     )
     from_left, from_right = lon_pair(to_left, to_right)
     (product,) = call(
@@ -526,10 +589,10 @@
         "adjoint",
         [((1, 80, ROWS, COLS), BF16)],
         [
-            flags, cotangent, above, below, from_left, from_right, bwd1, bwd2, slope,
+            cotangent, above, below, from_left, from_right, bwd1, bwd2, slope,
             back_near, back_far,
         ],
-        [((240, 8 * PITCH), BF16), ((512, 6 * PITCH), BF16)],
+        [pltpu.VMEM((240, 8 * PITCH), BF16), pltpu.VMEM((512, 6 * PITCH), BF16)],
         limit=16,
     )
     return image.reshape(1, 80, ROWS, COLS), product

time: 75 us -> 62.4 us (0.83)
  local copies, waits for them, and re-layouts: 12.9 us -> 0.66 us
  waiting for transfers between devices: 21.7 us -> 23.3 us
  Pallas kernels: 17.4 us -> 16 us
    unnamed x32 -> x0, local copies, waits for them, and re-layouts: 12.2 us -> none
    ppermute x2, starting transfers between devices: 5.83 us -> 2.89 us  [lat_pair(): lax.ppermute(block, 'lat', [((i + 1) % count, i) for i in range(count)])]
    ppermute x2, starting transfers between devices: 0.01 us -> 1.46 us  [lat_pair(): lax.ppermute(block, 'lat', [(i, (i + 1) % count) for i in range(count)])]
    pallas_call x8, Pallas kernels: 17.4 us -> 16 us  [call(): pl.pallas_call(kernel, name=name, out_shape=tuple((jax.ShapeDtypeStruct(s...]
    ppermute x2, starting transfers between devices: 11.1 us -> 12.1 us  [lon_pair(): lax.ppermute(to_right, 'lon', [(i, (i + 1) % count) for i in range(count)])]
    ppermute x2, waiting for transfers between devices: 1.81 us -> 2.76 us  [lat_pair(): lax.ppermute(block, 'lat', [((i + 1) % count, i) for i in range(count)])]
    ppermute x2, waiting for transfers between devices: 3.52 us -> 4.33 us  [lat_pair(): lax.ppermute(block, 'lat', [(i, (i + 1) % count) for i in range(count)])]
  transfers between devices with their start and end apart: 12 -> 12, of which waited for: 8 -> 10; matrix products, arithmetic and copies ran while one was open for 1% -> 1% of each run, Pallas kernels for 2% -> 4%
where the time goes in v2:
time: 62.4 us; the launch traced here: 62.3 us
  waiting for transfers between devices  23.3 us (37%)
  starting transfers between devices  21.6 us (35%)
  Pallas kernels  16 us (26%)
  between operations  0.7 us (1%)
  local copies, waits for them, and re-layouts  0.66 us (1%)
    pallas_call x8, Pallas kernels, call(): pl.pallas_call(kernel, name=name, out_shape=tuple((jax.ShapeDtypeStruct(s...  16 us
    ppermute x2, starting transfers between devices, lon_pair(): lax.ppermute(to_right, 'lon', [(i, (i + 1) % count) for i in range(count)])  12.1 us
    ppermute x2, waiting for transfers between devices, lon_pair(): lax.ppermute(to_left, 'lon', [((i + 1) % count, i) for i in range(count)])  8.84 us
    ppermute x2, waiting for transfers between devices, across(): return (same, lax.ppermute(far, ('comp', 'lon'), route))  6.01 us
    ppermute x2, waiting for transfers between devices, lat_pair(): lax.ppermute(block, 'lat', [(i, (i + 1) % count) for i in range(count)])  4.33 us
    ppermute x2, starting transfers between devices, across(): return (same, lax.ppermute(far, ('comp', 'lon'), route))  3.52 us
    ppermute x2, starting transfers between devices, lat_pair(): lax.ppermute(block, 'lat', [((i + 1) % count, i) for i in range(count)])  2.89 us
    ppermute x2, waiting for transfers between devices, lat_pair(): lax.ppermute(block, 'lat', [((i + 1) % count, i) for i in range(count)])  2.76 us
  transfers between devices with their start and end apart: 12, of which 10 were waited for; matrix products, arithmetic and copies ran while one was open for 1% of the time, Pallas kernels for 4%

profile of v2, /device:TPU:99, one launch (start us, length us, event | category | flops | bytes accessed | tf_op | source)
XLA Modules:
  0.0 62.3 jit_solution(9540408551191323836)
XLA Ops:
  0.6 1.3 %pack.1.own = bf16[160,512]{1,0:T(8,128)(2,1)S(1)} custom-call(bf16[1,80,2,256]{3,2,1,0:T(2,128)(2,1)} %state.1, bf16[1,80,2,256]{3,2,1,0:T(2,128)(2,1)} %direction.1), custom_call_target="tpu_custom_call" | custom-call | tf_op jit(solution)/shard_map/pack/pallas_call | solution.py:470
  2.0 2.8 %collective-permute-start.1 = (bf16[160,512]{1,0:T(8,128)(2,1)S(1)}, bf16[160,512]{1,0:T(8,128)(2,1)S(1)}, u32[]{:S(2)}, u32[]{:S(2)}) collective-permute-start(bf16[160,512]{1,0:T(8,128)(2,1)S(1)} %pack.1.own), channel_id=1, source_target_pairs={{32,0},{64,32},{96,64},{0,96},{33,1},{65,33},{97,65},{1,97},{34,2}... | collective-permute-start | bytes 491528 | tf_op jit(solution)/shard_map/ppermute | solution.py:484
  4.8 0.0 collective-permute-start
  4.8 2.3 %prepare.1 = (bf16[512,720]{1,0:T(8,128)(2,1)S(1)}, bf16[240,1536]{1,0:T(8,128)(2,1)S(1)}, bf16[512,720]{1,0:T(8,128)(2,1)S(1)}, bf16[240,1536]{1,0:T(8,128)(2,1...) custom-call(bf16[9,80,512]{2,1,0:T(8,128)(2,1)} %bitcast.6, ...), custom_call_target="tpu_custom_call" | custom-call | tf_op jit(solution)/shard_map/prepare/pallas_call | solution.py:470
  7.1 0.5 collective-permute-done.1.below
  7.7 3.1 %collective-permute-done.above = bf16[160,512]{1,0:T(8,128)(2,1)S(1)} collective-permute-done((bf16[160,512]{1,0:T(8,128)(2,1)S(1)}, bf16[160,512]{1,0:T(8,128)(2,1)S(1)}, u32[]{:S(2)}, u32[]{:S(2)}) %collective-permute-start) | collective-permute-done | bytes 163872 | tf_op jit(solution)/shard_map/ppermute | solution.py:483
  10.8 0.2 edges.1
  11.0 4.6 %collective-permute-start.2 = (bf16[160,128]{1,0:T(8,128)(2,1)S(1)}, bf16[160,128]{1,0:T(8,128)(2,1)S(1)}, u32[]{:S(2)}, u32[]{:S(2)}) collective-permute-start(bf16[160,128]{1,0:T(8,128)(2,1)S(1)} %get-tuple-element.22), channel_id=1, source_target_pairs={{0,1},{1,2},{2,3},{3,4},{4,5},{5,6},{6,7},{7,8},{8,9},{9,10},{10,1... | collective-permute-start | bytes 122888 | tf_op jit(solution)/shard_map/ppermute | solution.py:490
  15.6 0.0 collective-permute-start.3
  15.6 1.1 %collective-permute-done.2.from_left = bf16[160,128]{1,0:T(8,128)(2,1)S(1)} collective-permute-done((bf16[160,128]{1,0:T(8,128)(2,1)S(1)}, bf16[160,128]{1,0:T(8,128)(2,1)S(1)}, u32[]{:S(2)}, u32[]{:S(2)}) %collective-permute-start.2) | collective-permute-done | bytes 40992 | tf_op jit(solution)/shard_map/ppermute | solution.py:490
  16.7 4.4 %collective-permute-done.3.from_right = bf16[160,128]{1,0:T(8,128)(2,1)S(1)} collective-permute-done((bf16[160,128]{1,0:T(8,128)(2,1)S(1)}, bf16[160,128]{1,0:T(8,128)(2,1)S(1)}, u32[]{:S(2)}, u32[]{:S(2)}) %collective-permute-start.3) | collective-permute-done | bytes 40992 | tf_op jit(solution)/shard_map/ppermute | solution.py:491
  21.1 6.5 %tangent.1 = (f32[80,1024]{1,0:T(8,128)S(1)}, bf16[512,1536]{1,0:T(8,128)(2,1)S(1)}, f32[8,128]{1,0:T(8,128)S(1)}) custom-call(bf16[160,512]{1,0:T(8,128)(2,1)S(1)} %pack.1.own, bf16[160,512]{1,0:T(8,128)(2,1)S(1)} %collective-permute-done.above, bf16[160,512]{1,0:T(8,128)(2,1)S(1)} %collective-permute-done.1.below, ...), custom_call_target="tpu_custom_call" | custom-call | tf_op jit(solution)/shard_map/tangent/pallas_call | solution.py:470
  27.6 0.1 collective-permute-start.5
  27.7 0.2 collective-permute-start.4
  27.9 4.9 %collective-permute-done.5.far = f32[8,128]{1,0:T(8,128)S(1)} collective-permute-done((f32[8,128]{1,0:T(8,128)S(1)}, f32[8,128]{1,0:T(8,128)S(1)}, u32[]{:S(2)}, u32[]{:S(2)}) %collective-permute-start.5) | collective-permute-done | bytes 4128 | tf_op jit(solution)/shard_map/ppermute | solution.py:502
  32.8 0.0 collective-permute-done.4.near
  32.8 0.8 %couple.1 = (bf16[80,512]{1,0:T(8,128)(2,1)S(1)}, f32[8,128]{1,0:T(8,128)S(1)}, f32[8,128]{1,0:T(8,128)S(1)}) custom-call(f32[80,1024]{1,0:T(8,128)S(1)} %get-tuple-element.26.y, f32[8,128]{1,0:T(8,128)S(1)} %collective-permute-done.4.near, f32[8,128]{1,0:T(8,128)S(1)} %collective-permute-done.5.far, bf16[128,4096]{1,0:T(8,128)(2,1)S(1)} %get-tuple-element.28.hot, ...), custom_call_target="tpu_custom_call" | custom-call | tf_op jit(solution)/shard_map/couple/pallas_call | solution.py:470
  33.6 1.4 %collective-permute-start.6 = (f32[8,128]{1,0:T(8,128)S(1)}, f32[8,128]{1,0:T(8,128)S(1)}, u32[]{:S(2)}, u32[]{:S(2)}) collective-permute-start(f32[8,128]{1,0:T(8,128)S(1)} %get-tuple-element.33), channel_id=1, source_target_pairs={{0,128},{128,0},{1,129},{129,1},{2,130},{130,2},{3,131},{131,3},{4... | collective-permute-start | bytes 12296 | tf_op jit(solution)/shard_map/ppermute | solution.py:497
  35.0 3.4 %collective-permute-start.7 = (f32[8,128]{1,0:T(8,128)S(1)}, f32[8,128]{1,0:T(8,128)S(1)}, u32[]{:S(2)}, u32[]{:S(2)}) collective-permute-start(f32[8,128]{1,0:T(8,128)S(1)} %get-tuple-element.34), channel_id=1, source_target_pairs={{0,129},{1,130},{2,131},{3,132},{4,133},{5,134},{6,135},{7,136},{8... | collective-permute-start | bytes 12296 | tf_op jit(solution)/shard_map/ppermute | solution.py:502
  38.5 0.0 collective-permute-done.6.near
  38.5 1.1 %collective-permute-done.7.far = f32[8,128]{1,0:T(8,128)S(1)} collective-permute-done((f32[8,128]{1,0:T(8,128)S(1)}, f32[8,128]{1,0:T(8,128)S(1)}, u32[]{:S(2)}, u32[]{:S(2)}) %collective-permute-start.7) | collective-permute-done | bytes 4128 | tf_op jit(solution)/shard_map/ppermute | solution.py:502
  39.6 0.1 cotangent.1.own
  39.7 0.1 collective-permute-start.9
  39.8 1.5 %collective-permute-start.8 = (bf16[80,512]{1,0:T(8,128)(2,1)S(1)}, bf16[80,512]{1,0:T(8,128)(2,1)S(1)}, u32[]{:S(2)}, u32[]{:S(2)}) collective-permute-start(bf16[80,512]{1,0:T(8,128)(2,1)S(1)} %cotangent.1.own), channel_id=1, source_target_pairs={{0,32},{32,64},{64,96},{96,0},{1,33},{33,65},{65,97},{97,1},{2,34}... | collective-permute-start | bytes 245768 | tf_op jit(solution)/shard_map/ppermute | solution.py:483
  41.2 2.2 %collective-permute-done.9.below = bf16[80,512]{1,0:T(8,128)(2,1)S(1)} collective-permute-done((bf16[80,512]{1,0:T(8,128)(2,1)S(1)}, bf16[80,512]{1,0:T(8,128)(2,1)S(1)}, u32[]{:S(2)}, u32[]{:S(2)}) %collective-permute-start.9) | collective-permute-done | bytes 81952 | tf_op jit(solution)/shard_map/ppermute | solution.py:484
  43.4 1.2 %collective-permute-done.8.above = bf16[80,512]{1,0:T(8,128)(2,1)S(1)} collective-permute-done((bf16[80,512]{1,0:T(8,128)(2,1)S(1)}, bf16[80,512]{1,0:T(8,128)(2,1)S(1)}, u32[]{:S(2)}, u32[]{:S(2)}) %collective-permute-start.8) | collective-permute-done | bytes 81952 | tf_op jit(solution)/shard_map/ppermute | solution.py:483
  44.6 0.1 edges_back.1
  44.8 7.5 %collective-permute-start.10 = (bf16[80,128]{1,0:T(8,128)(2,1)S(1)}, bf16[80,128]{1,0:T(8,128)(2,1)S(1)}, u32[]{:S(2)}, u32[]{:S(2)}) collective-permute-start(bf16[80,128]{1,0:T(8,128)(2,1)S(1)} %get-tuple-element.35), channel_id=1, source_target_pairs={{0,1},{1,2},{2,3},{3,4},{4,5},{5,6},{6,7},{7,8},{8,9},{9,10},{10,1... | collective-permute-start | bytes 61448 | tf_op jit(solution)/shard_map/ppermute | solution.py:490
  52.3 0.0 collective-permute-start.11
  52.3 0.7 %reshape.19 = bf16[1,80,2,256]{3,2,1,0:T(2,128)(2,1)} reshape(bf16[80,512]{1,0:T(8,128)(2,1)S(1)} %get-tuple-element.32.image) | data formatting | bytes 163840 | tf_op jit(solution)/shard_map/reshape | solution.py:598
  52.9 0.2 collective-permute-done.10.from_left
  53.2 4.4 %collective-permute-done.11.from_right = bf16[80,128]{1,0:T(8,128)(2,1)S(1)} collective-permute-done((bf16[80,128]{1,0:T(8,128)(2,1)S(1)}, bf16[80,128]{1,0:T(8,128)(2,1)S(1)}, u32[]{:S(2)}, u32[]{:S(2)}) %collective-permute-start.11) | collective-permute-done | bytes 20512 | tf_op jit(solution)/shard_map/ppermute | solution.py:491
  57.6 4.7 %adjoint.1 = bf16[1,80,2,256]{3,2,1,0:T(2,128)(2,1)} custom-call(bf16[80,512]{1,0:T(8,128)(2,1)S(1)} %cotangent.1.own, bf16[80,512]{1,0:T(8,128)(2,1)S(1)} %collective-permute-done.8.above, bf16[80,512]{1,0:T(8,128)(2,1)S(1)} %collective-permute-done.9.below, bf16[80,128]{1,0:T(8,128)(2,1)S(1)} %collective-permute-done.10.from_left, ...), custom_call_target="tpu_custom_call" | custom-call | tf_op jit(solution)/shard_map/adjoint/pallas_call | solution.py:470
Async XLA Ops:
  2.0 5.7 %collective-permute-start.1 = (bf16[160,512]{1,0:T(8,128)(2,1)S(1)}, bf16[160,512]{1,0:T(8,128)(2,1)S(1)}, u32[]{:S(2)}, u32[]{:S(2)}) collective-permute-start(bf16[160,512]{1,0:T(8,128)(2,1)S(1)} %pack.1.own), channel_id=1, source_target_pairs={{32,0},{64,32},{96,64},{0,96},{33,1},{65,33},{97,65},{1,97},{34,2}... | collective-permute-start | bytes 491528 | tf_op jit(solution)/shard_map/ppermute | solution.py:484
  4.8 6.0 %collective-permute-start = (bf16[160,512]{1,0:T(8,128)(2,1)S(1)}, bf16[160,512]{1,0:T(8,128)(2,1)S(1)}, u32[]{:S(2)}, u32[]{:S(2)}) collective-permute-start(bf16[160,512]{1,0:T(8,128)(2,1)S(1)} %pack.1.own), channel_id=1, source_target_pairs={{0,32},{32,64},{64,96},{96,0},{1,33},{33,65},{65,97},{97,1},{2,34}... | collective-permute-start | bytes 491528 | tf_op jit(solution)/shard_map/ppermute | solution.py:483
  11.0 5.7 %collective-permute-start.2 = (bf16[160,128]{1,0:T(8,128)(2,1)S(1)}, bf16[160,128]{1,0:T(8,128)(2,1)S(1)}, u32[]{:S(2)}, u32[]{:S(2)}) collective-permute-start(bf16[160,128]{1,0:T(8,128)(2,1)S(1)} %get-tuple-element.22), channel_id=1, source_target_pairs={{0,1},{1,2},{2,3},{3,4},{4,5},{5,6},{6,7},{7,8},{8,9},{9,10},{10,1... | collective-permute-start | bytes 122888 | tf_op jit(solution)/shard_map/ppermute | solution.py:490
  15.6 5.5 %collective-permute-start.3 = (bf16[160,128]{1,0:T(8,128)(2,1)S(1)}, bf16[160,128]{1,0:T(8,128)(2,1)S(1)}, u32[]{:S(2)}, u32[]{:S(2)}) collective-permute-start(bf16[160,128]{1,0:T(8,128)(2,1)S(1)} %get-tuple-element.23), channel_id=1, source_target_pairs={{1,0},{2,1},{3,2},{4,3},{5,4},{6,5},{7,6},{8,7},{9,8},{10,9},{11,1... | collective-permute-start | bytes 122888 | tf_op jit(solution)/shard_map/ppermute | solution.py:491
  27.6 5.2 %collective-permute-start.5 = (f32[8,128]{1,0:T(8,128)S(1)}, f32[8,128]{1,0:T(8,128)S(1)}, u32[]{:S(2)}, u32[]{:S(2)}) collective-permute-start(f32[8,128]{1,0:T(8,128)S(1)} %get-tuple-element.27), channel_id=1, source_target_pairs={{0,159},{1,128},{2,129},{3,130},{4,131},{5,132},{6,133},{7,134},{8... | collective-permute-start | bytes 12296 | tf_op jit(solution)/shard_map/ppermute | solution.py:502
  27.7 5.1 %collective-permute-start.4 = (f32[8,128]{1,0:T(8,128)S(1)}, f32[8,128]{1,0:T(8,128)S(1)}, u32[]{:S(2)}, u32[]{:S(2)}) collective-permute-start(f32[8,128]{1,0:T(8,128)S(1)} %get-tuple-element.27), channel_id=1, source_target_pairs={{0,128},{128,0},{1,129},{129,1},{2,130},{130,2},{3,131},{131,3},{4... | collective-permute-start | bytes 12296 | tf_op jit(solution)/shard_map/ppermute | solution.py:497
  33.6 4.9 %collective-permute-start.6 = (f32[8,128]{1,0:T(8,128)S(1)}, f32[8,128]{1,0:T(8,128)S(1)}, u32[]{:S(2)}, u32[]{:S(2)}) collective-permute-start(f32[8,128]{1,0:T(8,128)S(1)} %get-tuple-element.33), channel_id=1, source_target_pairs={{0,128},{128,0},{1,129},{129,1},{2,130},{130,2},{3,131},{131,3},{4... | collective-permute-start | bytes 12296 | tf_op jit(solution)/shard_map/ppermute | solution.py:497
  35.0 4.5 %collective-permute-start.7 = (f32[8,128]{1,0:T(8,128)S(1)}, f32[8,128]{1,0:T(8,128)S(1)}, u32[]{:S(2)}, u32[]{:S(2)}) collective-permute-start(f32[8,128]{1,0:T(8,128)S(1)} %get-tuple-element.34), channel_id=1, source_target_pairs={{0,129},{1,130},{2,131},{3,132},{4,133},{5,134},{6,135},{7,136},{8... | collective-permute-start | bytes 12296 | tf_op jit(solution)/shard_map/ppermute | solution.py:502
  39.7 3.8 %collective-permute-start.9 = (bf16[80,512]{1,0:T(8,128)(2,1)S(1)}, bf16[80,512]{1,0:T(8,128)(2,1)S(1)}, u32[]{:S(2)}, u32[]{:S(2)}) collective-permute-start(bf16[80,512]{1,0:T(8,128)(2,1)S(1)} %cotangent.1.own), channel_id=1, source_target_pairs={{32,0},{64,32},{96,64},{0,96},{33,1},{65,33},{97,65},{1,97},{34,2}... | collective-permute-start | bytes 245768 | tf_op jit(solution)/shard_map/ppermute | solution.py:484
  39.8 4.9 %collective-permute-start.8 = (bf16[80,512]{1,0:T(8,128)(2,1)S(1)}, bf16[80,512]{1,0:T(8,128)(2,1)S(1)}, u32[]{:S(2)}, u32[]{:S(2)}) collective-permute-start(bf16[80,512]{1,0:T(8,128)(2,1)S(1)} %cotangent.1.own), channel_id=1, source_target_pairs={{0,32},{32,64},{64,96},{96,0},{1,33},{33,65},{65,97},{97,1},{2,34}... | collective-permute-start | bytes 245768 | tf_op jit(solution)/shard_map/ppermute | solution.py:483
  44.8 8.4 %collective-permute-start.10 = (bf16[80,128]{1,0:T(8,128)(2,1)S(1)}, bf16[80,128]{1,0:T(8,128)(2,1)S(1)}, u32[]{:S(2)}, u32[]{:S(2)}) collective-permute-start(bf16[80,128]{1,0:T(8,128)(2,1)S(1)} %get-tuple-element.35), channel_id=1, source_target_pairs={{0,1},{1,2},{2,3},{3,4},{4,5},{5,6},{6,7},{7,8},{8,9},{9,10},{10,1... | collective-permute-start | bytes 61448 | tf_op jit(solution)/shard_map/ppermute | solution.py:490
  52.3 5.3 %collective-permute-start.11 = (bf16[80,128]{1,0:T(8,128)(2,1)S(1)}, bf16[80,128]{1,0:T(8,128)(2,1)S(1)}, u32[]{:S(2)}, u32[]{:S(2)}) collective-permute-start(bf16[80,128]{1,0:T(8,128)(2,1)S(1)} %get-tuple-element.36), channel_id=1, source_target_pairs={{1,0},{2,1},{3,2},{4,3},{5,4},{6,5},{7,6},{8,7},{9,8},{10,9},{11,1... | collective-permute-start | bytes 61448 | tf_op jit(solution)/shard_map/ppermute | solution.py:491

commit v3 on v2

--- a/solution.py
+++ b/solution.py
@@ -11,7 +11,6 @@
 BF16 = jnp.bfloat16
 ROWS = 2
 COLS = 256
-PITCH = COLS + 128
 CELLS = ROWS * COLS
 SLOTS = 8
 
@@ -174,109 +173,171 @@
     left = jnp.zeros((channels, 128), F32)
     right = jnp.zeros((channels, 128), F32)
     for place, (read, r) in enumerate(sources(own, above, below)):
-        initial = read(slice(0, channels), 0, 128)
-        last = read(slice(0, channels), 128, COLS)
-        here = (lanes >> 1) == place
-        if place:
-            initial = pltpu.roll(initial, 2 * place, 1)
-        left = jnp.where(here, initial, left)
-        right = jnp.where(here, pltpu.roll(last, 2 * place + 2, 1), right)
+        initial = pltpu.roll(read(slice(0, channels), 0, 128), 4 * place + 2, 1)
+        last = pltpu.roll(read(slice(0, channels), 128, COLS), 4 * place + 2, 1)
+        left = jnp.where((lanes >> 1) == 2 * place + 1, initial, left)
+        right = jnp.where((lanes >> 1) == 2 * place, last, right)
     to_left[...] = left.astype(BF16)
     to_right[...] = right.astype(BF16)
 
 
-def shifted_rows(main, place, from_left, from_right, fill):
-    lanes = lane_iota(from_left.shape)
-    after = pltpu.roll(from_right, (128 - 2 * place) % 128, 1) if place else from_right
-    before = pltpu.roll(from_left, 126 - 2 * place, 1)
-    edge = jnp.where(lanes < 2, after, jnp.where(lanes >= 126, before, 0.0))
-    full = jnp.concatenate([main, edge], axis=1)
-    pieces = [pltpu.roll(full, 1, 1), full, pltpu.roll(full, PITCH - 1, 1)]
+def shifted_rows(main, fill):
+    pieces = [pltpu.roll(main, 1, 1), main, pltpu.roll(main, COLS - 1, 1)]
     if fill:
-        pieces.append(jnp.zeros((fill, PITCH), F32))
+        pieces.append(jnp.zeros((fill, COLS), F32))
     return jnp.concatenate(pieces, axis=0).astype(BF16)
 
 
-def air_rows(own, above, below, from_left, from_right, fields, store):
+def air_rows(own, above, below, fields, store):
     for field in range(fields):
         part = slice(field * 80, (field + 1) * 80)
-        left = from_left[part, :].astype(F32)
-        right = from_right[part, :].astype(F32)
         for place, (read, r) in enumerate(sources(own, above, below)):
-            main = read(part, 0, COLS)
-            store(field, place, shifted_rows(main, place, left, right, 0))
-
-
-def sea_rows(own, above, below, from_left, from_right, fields, store):
+            store(field, place, shifted_rows(read(part, 0, COLS), 0))
+
+
+def sea_rows(own, above, below, fields, store):
     for field in range(fields):
         part = slice(field * 80, (field + 1) * 80)
-        left = from_left[part, :].astype(F32)
-        right = from_right[part, :].astype(F32)
         for place, (read, r) in enumerate(sources(own, above, below)):
             main = read(part, 0, COLS)
             for half in range(2):
                 fine = 2 * (2 * (place // 2) + half - 1) + r
                 if 0 <= fine < 8:
-                    cut = slice(half * 40, half * 40 + 40)
-                    rows = shifted_rows(main[cut], place, left[cut], right[cut], 8)
-                    store(field, fine, rows)
-
-
-def row_span(place):
-    return pl.ds(pl.multiple_of(place * PITCH, 128), PITCH)
-
-
-def tap_stack(ref, first_row, depth, place):
-    pieces = [ref[first_row : first_row + depth, row_span(place + a)] for a in range(3)]
-    return jnp.concatenate(pieces, axis=0)
-
-
-def joined_taps(product, channels):
-    total = pltpu.roll(product[:channels], 1, 1) + product[channels : 2 * channels]
-    total = total + pltpu.roll(product[2 * channels : 3 * channels], PITCH - 1, 1)
-    return total[:, :COLS]
-
-
-def pole_scale(place, count):
-    outside = (at_top() & (place == 0)) | (at_bottom() & (place == count - 1))
-    return jnp.where(outside, 0.0, 1.0).astype(F32)
-
-
-def tangent_kernel(
-    own, above, below, from_left, from_right, fwd1, fwd2, columns,
-    y, slope, payload, stack, hidden,
+                    store(field, fine, shifted_rows(main[half * 40 : half * 40 + 40], 8))
+
+
+def kept(rows, count, first_row):
+    lanes = lane_iota((1, rows * COLS))
+    row = first_row + lanes // COLS
+    column = lanes % COLS
+    drop = (column == 0) | (column == COLS - 1)
+    drop = drop | (at_top() & (row == 0)) | (at_bottom() & (row == count - 1))
+    return jnp.where(drop, 0.0, 1.0).astype(F32)
+
+
+def edge_kept(count):
+    lanes = lane_iota((1, 128))
+    row = lanes >> 2
+    drop = (row >= count) | (at_top() & (row == 0)) | (at_bottom() & (row == count - 1))
+    return jnp.where(drop, 0.0, 1.0).astype(F32)
+
+
+def edge_sides(to_left, to_right, from_left, from_right, part):
+    lanes = lane_iota((80, 128))
+    head = (lanes & 3) < 2
+    before = jnp.where(
+        head, from_left[part, :].astype(F32), pltpu.roll(to_right[part, :].astype(F32), 2, 1)
+    )
+    after = jnp.where(
+        head, pltpu.roll(to_left[part, :].astype(F32), 126, 1), from_right[part, :].astype(F32)
+    )
+    return before, after
+
+
+def fine_lanes(rows):
+    lanes = lane_iota((40, 128)) >> 3
+    upper, lower = rows[:40], rows[40:]
+    result = jnp.where(lanes == 0, lower, upper)
+    result = jnp.where(lanes == 2, pltpu.roll(lower, 8, 1), result)
+    return jnp.where(lanes == 3, pltpu.roll(upper, 8, 1), result)
+
+
+def edge_stack(to_left, to_right, from_left, from_right, fields, fine):
+    merged = None
+    for field in range(fields):
+        part = slice(field * 80, (field + 1) * 80)
+        sides = edge_sides(to_left, to_right, from_left, from_right, part)
+        if fine:
+            sides = [fine_lanes(side) for side in sides]
+        if merged is None:
+            merged = sides
+        else:
+            low = lane_iota(sides[0].shape) < 64
+            merged = [jnp.where(low, m, pltpu.roll(s, 64, 1)) for m, s in zip(merged, sides)]
+    before, after = merged
+    even = (lane_iota(before.shape) & 1) == 0
+    middle = jnp.where(even, pltpu.roll(before, 127, 1), pltpu.roll(after, 1, 1))
+    pieces = []
+    for a in range(3):
+        for rows in (before, middle, after):
+            pieces.append(pltpu.roll(rows, 128 - 4 * a, 1) if a else rows)
+        if fine:
+            pieces.append(jnp.zeros((8, 128), F32))
+    return jnp.concatenate(pieces, axis=0).astype(BF16)
+
+
+def second_rows(weights, main, edge, channels, width, count):
+    shifted = [edge] + [pltpu.roll(edge, 128 - 4 * a, 1) for a in (1, 2)]
+    taps = jnp.concatenate(shifted, axis=0).astype(BF16)
+    matrix = weights[: 3 * channels, : 3 * width]
+    block = dot(matrix, taps)
+    first, middle, last = [block[e * channels : (e + 1) * channels] for e in range(3)]
+    lanes = lane_iota((channels, 128))
+    left = first + jnp.where((lanes & 3) == 0, pltpu.roll(middle, 127, 1), 0.0)
+    right = last + jnp.where((lanes & 3) == 3, pltpu.roll(middle, 1, 1), 0.0)
+    result = []
+    for pair in range(0, count, 2):
+        pieces = [main[:width, (pair + a) * COLS : (pair + a + 2) * COLS] for a in range(3)]
+        whole = dot(matrix, jnp.concatenate(pieces, axis=0))
+        for row in (pair, pair + 1):
+            cut = whole[:, (row - pair) * COLS : (row - pair + 1) * COLS]
+            total = pltpu.roll(cut[:channels], 1, 1) + cut[channels : 2 * channels]
+            total = total + pltpu.roll(cut[2 * channels :], COLS - 1, 1)
+            head = pltpu.roll(left, 128 - 4 * row, 1) if row else left
+            head = jnp.where(lanes < 2, head, 0.0)
+            tail = jnp.where(lanes >= 126, pltpu.roll(right, 124 - 4 * row, 1), 0.0)
+            result.append(total + jnp.concatenate([head, tail], axis=1))
+    return result
+
+
+def tangent_main_kernel(own, above, below, fwd1, columns, hidden, slope, stack):
+    def run(width, depth, count):
+        padded = depth // 3
+
+        def one_row(place, unused):
+            pieces = []
+            for a in range(3):
+                span = pl.ds(pl.multiple_of((place + a) * 2 * COLS, 128), 2 * COLS)
+                pieces.append(stack[:padded, span])
+            both = dot(fwd1[:width, :depth], jnp.concatenate(pieces, axis=0))
+            steep = 1.0 - jnp.tanh(both[:, :COLS] + columns[:width, 0:1]) ** 2
+            span = pl.ds(pl.multiple_of(place * COLS, 128), COLS)
+            hidden[:width, span] = (steep * both[:, COLS:] * kept(1, count, place)).astype(BF16)
+            slope[:width, span] = steep.astype(BF16)
+            return unused
+
+        lax.fori_loop(0, count, one_row, 0)
+
+    def store(field, place, rows):
+        start = place * 2 * COLS + field * COLS
+        stack[: rows.shape[0], start : start + COLS] = rows
+
+    @pl.when(is_air())
+    def _():
+        air_rows(own, above, below, 2, store)
+        run(512, 720, 4)
+
+    @pl.when(is_sea())
+    def _():
+        sea_rows(own, above, below, 2, store)
+        run(256, 384, 6)
+
+
+def tangent_edge_kernel(
+    own, to_left, to_right, from_left, from_right, hidden, fwd1, fwd2, columns,
+    y, slope, payload,
 ):
-    def run(channels, width, depth, count, slope_slice):
-        padded = depth // 3
-
-        def one_row(place, unused):
-            scale = pole_scale(place, count)
-            base = dot(fwd1[:width, :depth], tap_stack(stack, 0, padded, place))
-            tangent = dot(fwd1[:width, :depth], tap_stack(stack, padded, padded, place))
-            steep = 1.0 - jnp.tanh(base + columns[:width, 0:1]) ** 2
-            hidden[:width, row_span(place)] = (steep * tangent * scale).astype(BF16)
-            slope_slice(place, steep.astype(BF16))
-            return unused
-
-        lax.fori_loop(0, count, one_row, 0)
-
-    def second(channels, width, place):
-        taps = tap_stack(hidden, 0, width, place)
-        return joined_taps(dot(fwd2[: 3 * channels, : 3 * width], taps), channels)
-
-    @pl.when(is_air())
-    def _():
-        def store(field, place, rows):
-            stack[field * 240 : field * 240 + 240, place * PITCH : (place + 1) * PITCH] = rows
-
-        air_rows(own, above, below, from_left, from_right, 2, store)
-
-        def keep(place, rows):
-            slope[:, row_span(place)] = rows
-
-        run(80, 512, 720, 4, keep)
-        for r in range(ROWS):
-            result = second(80, 512, r)
+    def run(channels, width, depth, count):
+        stack = edge_stack(to_left, to_right, from_left, from_right, 2, channels == 40)
+        both = dot(fwd1[:width, :depth], stack)
+        steep = 1.0 - jnp.tanh(both + columns[:width, 0:1]) ** 2
+        slope[:width, :] = steep.astype(BF16)
+        edge = steep * pltpu.roll(both, 64, 1) * edge_kept(count)
+        return second_rows(fwd2, hidden, edge, channels, width, count - 2)
+
+    @pl.when(is_air())
+    def _():
+        for r, result in enumerate(run(80, 512, 720, 4)):
             y[:, r * COLS : (r + 1) * COLS] = result
             for f in range(2):
                 flux = jnp.sum(columns[:80, 1 + f : 2 + f] * result, axis=0, keepdims=True)
@@ -286,23 +347,8 @@
 
     @pl.when(is_sea())
     def _():
-        def store(field, place, rows):
-            stack[field * 128 : field * 128 + 128, place * PITCH : (place + 1) * PITCH] = rows
-
-        sea_rows(own, above, below, from_left, from_right, 2, store)
-
-        def keep(place, rows):
-            @pl.when(place < 4)
-            def _():
-                slope[:256, row_span(place)] = rows
-
-            @pl.when(place >= 4)
-            def _():
-                slope[256:, row_span(place - 4)] = rows
-
-        run(40, 256, 384, 6, keep)
-        for fine in range(2 * ROWS):
-            y[:40, fine * COLS : (fine + 1) * COLS] = second(40, 256, fine)
+        for fine, result in enumerate(run(40, 256, 384, 6)):
+            y[:40, fine * COLS : (fine + 1) * COLS] = result
             half, r = divmod(fine, 2)
             line = own[80 + 40 * half : 88 + 40 * half, r * COLS : (r + 1) * COLS].astype(F32)
             for part in range(2):
@@ -401,51 +447,57 @@
     target[0] = jnp.stack(rows, axis=1).astype(BF16)
 
 
-def adjoint_kernel(
-    own, above, below, from_left, from_right, bwd1, bwd2, slope, near, far,
-    product, stack, hidden,
+def adjoint_main_kernel(own, above, below, bwd1, slope, packed, hidden, image, stack):
+    wide = packed[...].astype(F32)
+    spread_rows(image, [wide[:, r * COLS : (r + 1) * COLS] for r in range(ROWS)])
+
+    def run(width, depth, count):
+        padded = depth // 3
+
+        def two_rows(pair, unused):
+            pieces = []
+            for a in range(3):
+                span = pl.ds(pl.multiple_of((2 * pair + a) * COLS, 128), 2 * COLS)
+                pieces.append(stack[:padded, span])
+            back = dot(bwd1[:width, :depth], jnp.concatenate(pieces, axis=0))
+            span = pl.ds(pl.multiple_of(2 * pair * COLS, 128), 2 * COLS)
+            back = back * slope[:width, span].astype(F32) * kept(2, count, 2 * pair)
+            hidden[:width, span] = back.astype(BF16)
+            return unused
+
+        lax.fori_loop(0, count // 2, two_rows, 0)
+
+    def store(field, place, rows):
+        stack[: rows.shape[0], place * COLS : (place + 1) * COLS] = rows
+
+    @pl.when(is_air())
+    def _():
+        air_rows(own, above, below, 1, store)
+        run(512, 720, 4)
+
+    @pl.when(is_sea())
+    def _():
+        sea_rows(own, above, below, 1, store)
+        run(256, 384, 6)
+
+
+def adjoint_edge_kernel(
+    to_left, to_right, from_left, from_right, hidden, slope, bwd1, bwd2, near, far, product
 ):
-    def run(width, depth, count, slope_slice):
-        padded = depth // 3
-
-        def one_row(place, unused):
-            scale = pole_scale(place, count)
-            back = dot(bwd1[:width, :depth], tap_stack(stack, 0, padded, place))
-            back = back * slope_slice(place).astype(F32) * scale
-            hidden[:width, row_span(place)] = back.astype(BF16)
-            return unused
-
-        lax.fori_loop(0, count, one_row, 0)
-
-    def second(channels, width, place):
-        taps = tap_stack(hidden, 0, width, place)
-        return joined_taps(dot(bwd2[: 3 * channels, : 3 * width], taps), channels)
-
-    @pl.when(is_air())
-    def _():
-        def store(field, place, rows):
-            stack[:240, place * PITCH : (place + 1) * PITCH] = rows
-
-        air_rows(own, above, below, from_left, from_right, 1, store)
-        run(512, 720, 4, lambda place: slope[:, row_span(place)])
-        rows = []
-        for r in range(ROWS):
-            rows.append(second(80, 512, r))
-        spread_rows(product, rows)
-
-    @pl.when(is_sea())
-    def _():
-        def store(field, place, rows):
-            stack[:128, place * PITCH : (place + 1) * PITCH] = rows
-
-        sea_rows(own, above, below, from_left, from_right, 1, store)
-
-        def slope_slice(place):
-            upper = slope[:256, row_span(jnp.minimum(place, 3))]
-            lower = slope[256:, row_span(jnp.maximum(place - 4, 0))]
-            return jnp.where(place < 4, upper, lower)
-
-        run(256, 384, 6, slope_slice)
+    def run(channels, width, depth, count):
+        stack = edge_stack(to_left, to_right, from_left, from_right, 1, channels == 40)
+        edge = dot(bwd1[:width, :depth], stack)
+        edge = edge * slope[:width, :].astype(F32)
+        edge = jnp.where(edge_kept(count) > 0.0, edge, 0.0)
+        return second_rows(bwd2, hidden, edge, channels, width, count - 2)
+
+    @pl.when(is_air())
+    def _():
+        spread_rows(product, run(80, 512, 720, 4))
+
+    @pl.when(is_sea())
+    def _():
+        results = run(40, 256, 384, 6)
         arrived = near[...] + far[...]
         channel = lax.broadcasted_iota(jnp.int32, (40, COLS), 0)
         rows = []
@@ -456,7 +508,7 @@
                 row = jnp.concatenate(
                     [arrived[2 * fine + q : 2 * fine + q + 1, :] for q in range(2)], axis=1
                 )
-                halves.append(second(40, 256, fine) + jnp.where(channel == 0, row, 0.0))
+                halves.append(results[fine] + jnp.where(channel == 0, row, 0.0))
             rows.append(jnp.concatenate(halves, axis=0))
         spread_rows(product, rows)
 
@@ -558,13 +610,20 @@
         edge_kernel, "edges", [((160, 128), BF16)] * 2, [own, above, below, columns]
     )
     from_left, from_right = lon_pair(to_left, to_right)
-    y, slope, payload = call(
-        tangent_kernel,
-        "tangent",
-        [((80, 2 * CELLS), F32), ((512, 4 * PITCH), BF16), ((8, 128), F32)],
-        [own, above, below, from_left, from_right, fwd1, fwd2, columns],
-        [pltpu.VMEM((480, 8 * PITCH), BF16), pltpu.VMEM((512, 6 * PITCH), BF16)],
-        limit=20,
+    hidden, slope = call(
+        tangent_main_kernel,
+        "tangent_main",
+        [((512, 6 * COLS), BF16), ((512, 6 * COLS), BF16)],
+        [own, above, below, fwd1, columns],
+        [pltpu.VMEM((240, 16 * COLS), BF16)],
+        limit=16,
+    )
+    y, edge_slope, payload = call(
+        tangent_edge_kernel,
+        "tangent_edge",
+        [((80, 2 * CELLS), F32), ((512, 128), BF16), ((8, 128), F32)],
+        [own, to_left, to_right, from_left, from_right, hidden, fwd1, fwd2, columns],
+        limit=16,
     )
     near, far = across(payload, payload, -1)
     image, back_near, back_far = call(
@@ -584,18 +643,25 @@
         [cotangent, above, below, columns],
     )
     from_left, from_right = lon_pair(to_left, to_right)
+    hidden, result = call(
+        adjoint_main_kernel,
+        "adjoint_main",
+        [((512, 6 * COLS), BF16), ((1, 80, ROWS, COLS), BF16)],
+        [cotangent, above, below, bwd1, slope, image],
+        [pltpu.VMEM((240, 8 * COLS), BF16)],
+        limit=16,
+    )
     (product,) = call(
-        adjoint_kernel,
-        "adjoint",
+        adjoint_edge_kernel,
+        "adjoint_edge",
         [((1, 80, ROWS, COLS), BF16)],
         [
-            cotangent, above, below, from_left, from_right, bwd1, bwd2, slope,
+            to_left, to_right, from_left, from_right, hidden, edge_slope, bwd1, bwd2,
             back_near, back_far,
         ],
-        [pltpu.VMEM((240, 8 * PITCH), BF16), pltpu.VMEM((512, 6 * PITCH), BF16)],
         limit=16,
     )
-    return image.reshape(1, 80, ROWS, COLS), product
+    return result, product
 
 
 def solution(mesh):

time: 62.4 us -> 53.6 us (0.86)
  the two profiles are of different devices: /device:TPU:99 before, /device:TPU:8 now
where the time goes in v3:
time: 53.6 us; the launch traced here: 53.4 us
  waiting for transfers between devices  21.6 us (40%)
  starting transfers between devices  17.3 us (32%)
  Pallas kernels  13.8 us (26%)
  between operations  0.71 us (1%)
    pallas_call x10, Pallas kernels, call(): pl.pallas_call(kernel, name=name, out_shape=tuple((jax.ShapeDtypeStruct(s...  13.8 us
    ppermute x2, waiting for transfers between devices, lon_pair(): lax.ppermute(to_right, 'lon', [(i, (i + 1) % count) for i in range(count)])  5.57 us
    ppermute x2, starting transfers between devices, lon_pair(): lax.ppermute(to_left, 'lon', [((i + 1) % count, i) for i in range(count)])  5.43 us
    ppermute x2, starting transfers between devices, lat_pair(): lax.ppermute(block, 'lat', [((i + 1) % count, i) for i in range(count)])  5.16 us
    ppermute x2, waiting for transfers between devices, across(): return (same, lax.ppermute(far, ('comp', 'lon'), route))  4.63 us
    ppermute x2, starting transfers between devices, across(): same = lax.ppermute(near, 'comp', [(0, 1), (1, 0)])  3.93 us
    ppermute x2, waiting for transfers between devices, across(): same = lax.ppermute(near, 'comp', [(0, 1), (1, 0)])  3.92 us
    ppermute x2, waiting for transfers between devices, lat_pair(): lax.ppermute(block, 'lat', [(i, (i + 1) % count) for i in range(count)])  3.92 us
  transfers between devices with their start and end apart: 12, of which 10 were waited for; matrix products, arithmetic and copies ran while one was open for 0% of the time, Pallas kernels for 13%

profile of v3, /device:TPU:8, one launch (start us, length us, event | category | flops | bytes accessed | tf_op | source)
XLA Modules:
  0.0 53.4 jit_solution(6473433752795476348)
XLA Ops:
  0.6 1.3 %pack.1.own = bf16[160,512]{1,0:T(8,128)(2,1)S(1)} custom-call(bf16[1,80,2,256]{3,2,1,0:T(2,128)(2,1)} %state.1, bf16[1,80,2,256]{3,2,1,0:T(2,128)(2,1)} %direction.1), custom_call_target="tpu_custom_call" | custom-call | tf_op jit(solution)/shard_map/pack/pallas_call | solution.py:522
  2.0 2.2 %collective-permute-start.1 = (bf16[160,512]{1,0:T(8,128)(2,1)S(1)}, bf16[160,512]{1,0:T(8,128)(2,1)S(1)}, u32[]{:S(2)}, u32[]{:S(2)}) collective-permute-start(bf16[160,512]{1,0:T(8,128)(2,1)S(1)} %pack.1.own), channel_id=1, source_target_pairs={{32,0},{64,32},{96,64},{0,96},{33,1},{65,33},{97,65},{1,97},{34,2}... | collective-permute-start | bytes 491528 | tf_op jit(solution)/shard_map/ppermute | solution.py:536
  4.2 0.0 collective-permute-start
  4.2 2.3 %prepare.1 = (bf16[512,720]{1,0:T(8,128)(2,1)S(1)}, bf16[240,1536]{1,0:T(8,128)(2,1)S(1)}, bf16[512,720]{1,0:T(8,128)(2,1)S(1)}, bf16[240,1536]{1,0:T(8,128)(2,1...) custom-call(bf16[9,80,512]{2,1,0:T(8,128)(2,1)} %bitcast.6, ...), custom_call_target="tpu_custom_call" | custom-call | tf_op jit(solution)/shard_map/prepare/pallas_call | solution.py:522
  6.5 1.4 %collective-permute-done.1.below = bf16[160,512]{1,0:T(8,128)(2,1)S(1)} collective-permute-done((bf16[160,512]{1,0:T(8,128)(2,1)S(1)}, bf16[160,512]{1,0:T(8,128)(2,1)S(1)}, u32[]{:S(2)}, u32[]{:S(2)}) %collective-permute-start.1) | collective-permute-done | bytes 163872 | tf_op jit(solution)/shard_map/ppermute | solution.py:536
  8.0 1.5 %collective-permute-done.above = bf16[160,512]{1,0:T(8,128)(2,1)S(1)} collective-permute-done((bf16[160,512]{1,0:T(8,128)(2,1)S(1)}, bf16[160,512]{1,0:T(8,128)(2,1)S(1)}, u32[]{:S(2)}, u32[]{:S(2)}) %collective-permute-start) | collective-permute-done | bytes 163872 | tf_op jit(solution)/shard_map/ppermute | solution.py:535
  9.5 0.2 edges.1
  9.7 5.3 %collective-permute-start.3 = (bf16[160,128]{1,0:T(8,128)(2,1)S(1)}, bf16[160,128]{1,0:T(8,128)(2,1)S(1)}, u32[]{:S(2)}, u32[]{:S(2)}) collective-permute-start(bf16[160,128]{1,0:T(8,128)(2,1)S(1)} %get-tuple-element.26.to_left), channel_id=1, source_target_pairs={{1,0},{2,1},{3,2},{4,3},{5,4},{6,5},{7,6},{8,7},{9,8},{10,9},{11,1... | collective-permute-start | bytes 122888 | tf_op jit(solution)/shard_map/ppermute | solution.py:543
  15.1 0.0 collective-permute-start.2
  15.1 2.7 %tangent_main.1 = (bf16[512,1536]{1,0:T(8,128)(2,1)S(1)}, bf16[512,1536]{1,0:T(8,128)(2,1)S(1)}) custom-call(bf16[160,512]{1,0:T(8,128)(2,1)S(1)} %pack.1.own, bf16[160,512]{1,0:T(8,128)(2,1)S(1)} %collective-permute-done.above, bf16[160,512]{1,0:T(8,128)(2,1)S(1)} %collective-permute-done.1.below, bf16[512,720]{1,0:T(8,128)(2,1)S(1)} %get-tuple-element.28.fwd1, ...), custom_call_target="tpu_custom_call" | custom-call | tf_op jit(solution)/shard_map/tangent_main/pallas_call | solution.py:522
  17.8 0.0 collective-permute-done.3.from_right
  17.8 2.8 %collective-permute-done.2.from_left = bf16[160,128]{1,0:T(8,128)(2,1)S(1)} collective-permute-done((bf16[160,128]{1,0:T(8,128)(2,1)S(1)}, bf16[160,128]{1,0:T(8,128)(2,1)S(1)}, u32[]{:S(2)}, u32[]{:S(2)}) %collective-permute-start.2) | collective-permute-done | bytes 40992 | tf_op jit(solution)/shard_map/ppermute | solution.py:542
  20.6 1.8 %tangent_edge.1 = (f32[80,1024]{1,0:T(8,128)S(1)}, bf16[512,128]{1,0:T(8,128)(2,1)S(1)}, f32[8,128]{1,0:T(8,128)S(1)}) custom-call(bf16[160,512]{1,0:T(8,128)(2,1)S(1)} %pack.1.own, bf16[160,128]{1,0:T(8,128)(2,1)S(1)} %get-tuple-element.26.to_left, bf16[160,128]{1,0:T(8,128)(2,1)S(1)} %get-tuple-element.27.to_right, ...), custom_call_target="tpu_custom_call" | custom-call | tf_op jit(solution)/shard_map/tangent_edge/pallas_call | solution.py:522
  22.4 1.3 %collective-permute-start.5 = (f32[8,128]{1,0:T(8,128)S(1)}, f32[8,128]{1,0:T(8,128)S(1)}, u32[]{:S(2)}, u32[]{:S(2)}) collective-permute-start(f32[8,128]{1,0:T(8,128)S(1)} %get-tuple-element.32), channel_id=1, source_target_pairs={{0,159},{1,128},{2,129},{3,130},{4,131},{5,132},{6,133},{7,134},{8... | collective-permute-start | bytes 12296 | tf_op jit(solution)/shard_map/ppermute | solution.py:554
  23.7 1.9 %collective-permute-start.4 = (f32[8,128]{1,0:T(8,128)S(1)}, f32[8,128]{1,0:T(8,128)S(1)}, u32[]{:S(2)}, u32[]{:S(2)}) collective-permute-start(f32[8,128]{1,0:T(8,128)S(1)} %get-tuple-element.32), channel_id=1, source_target_pairs={{0,128},{128,0},{1,129},{129,1},{2,130},{130,2},{3,131},{131,3},{4... | collective-permute-start | bytes 12296 | tf_op jit(solution)/shard_map/ppermute | solution.py:549
  25.6 1.4 %collective-permute-done.5.far = f32[8,128]{1,0:T(8,128)S(1)} collective-permute-done((f32[8,128]{1,0:T(8,128)S(1)}, f32[8,128]{1,0:T(8,128)S(1)}, u32[]{:S(2)}, u32[]{:S(2)}) %collective-permute-start.5) | collective-permute-done | bytes 4128 | tf_op jit(solution)/shard_map/ppermute | solution.py:554
  27.0 1.8 %collective-permute-done.4.near = f32[8,128]{1,0:T(8,128)S(1)} collective-permute-done((f32[8,128]{1,0:T(8,128)S(1)}, f32[8,128]{1,0:T(8,128)S(1)}, u32[]{:S(2)}, u32[]{:S(2)}) %collective-permute-start.4) | collective-permute-done | bytes 4128 | tf_op jit(solution)/shard_map/ppermute | solution.py:549
  28.8 0.8 %couple.1 = (bf16[80,512]{1,0:T(8,128)(2,1)S(1)}, f32[8,128]{1,0:T(8,128)S(1)}, f32[8,128]{1,0:T(8,128)S(1)}) custom-call(f32[80,1024]{1,0:T(8,128)S(1)} %get-tuple-element.31.y, f32[8,128]{1,0:T(8,128)S(1)} %collective-permute-done.4.near, f32[8,128]{1,0:T(8,128)S(1)} %collective-permute-done.5.far, bf16[128,4096]{1,0:T(8,128)(2,1)S(1)} %get-tuple-element.33.hot, ...), custom_call_target="tpu_custom_call" | custom-call | tf_op jit(solution)/shard_map/couple/pallas_call | solution.py:522
  29.6 2.0 %collective-permute-start.6 = (f32[8,128]{1,0:T(8,128)S(1)}, f32[8,128]{1,0:T(8,128)S(1)}, u32[]{:S(2)}, u32[]{:S(2)}) collective-permute-start(f32[8,128]{1,0:T(8,128)S(1)} %get-tuple-element.38), channel_id=1, source_target_pairs={{0,128},{128,0},{1,129},{129,1},{2,130},{130,2},{3,131},{131,3},{4... | collective-permute-start | bytes 12296 | tf_op jit(solution)/shard_map/ppermute | solution.py:549
  31.6 1.0 %collective-permute-start.7 = (f32[8,128]{1,0:T(8,128)S(1)}, f32[8,128]{1,0:T(8,128)S(1)}, u32[]{:S(2)}, u32[]{:S(2)}) collective-permute-start(f32[8,128]{1,0:T(8,128)S(1)} %get-tuple-element.39), channel_id=1, source_target_pairs={{0,129},{1,130},{2,131},{3,132},{4,133},{5,134},{6,135},{7,136},{8... | collective-permute-start | bytes 12296 | tf_op jit(solution)/shard_map/ppermute | solution.py:554
  32.6 2.1 %collective-permute-done.6.near = f32[8,128]{1,0:T(8,128)S(1)} collective-permute-done((f32[8,128]{1,0:T(8,128)S(1)}, f32[8,128]{1,0:T(8,128)S(1)}, u32[]{:S(2)}, u32[]{:S(2)}) %collective-permute-start.6) | collective-permute-done | bytes 4128 | tf_op jit(solution)/shard_map/ppermute | solution.py:549
  34.7 3.2 %collective-permute-done.7.far = f32[8,128]{1,0:T(8,128)S(1)} collective-permute-done((f32[8,128]{1,0:T(8,128)S(1)}, f32[8,128]{1,0:T(8,128)S(1)}, u32[]{:S(2)}, u32[]{:S(2)}) %collective-permute-start.7) | collective-permute-done | bytes 4128 | tf_op jit(solution)/shard_map/ppermute | solution.py:554
  37.9 0.1 cotangent.1.own
  38.1 2.9 %collective-permute-start.9 = (bf16[80,512]{1,0:T(8,128)(2,1)S(1)}, bf16[80,512]{1,0:T(8,128)(2,1)S(1)}, u32[]{:S(2)}, u32[]{:S(2)}) collective-permute-start(bf16[80,512]{1,0:T(8,128)(2,1)S(1)} %cotangent.1.own), channel_id=1, source_target_pairs={{32,0},{64,32},{96,64},{0,96},{33,1},{65,33},{97,65},{1,97},{34,2}... | collective-permute-start | bytes 245768 | tf_op jit(solution)/shard_map/ppermute | solution.py:536
  41.0 0.0 collective-permute-start.8
  41.0 2.1 %collective-permute-done.9.below = bf16[80,512]{1,0:T(8,128)(2,1)S(1)} collective-permute-done((bf16[80,512]{1,0:T(8,128)(2,1)S(1)}, bf16[80,512]{1,0:T(8,128)(2,1)S(1)}, u32[]{:S(2)}, u32[]{:S(2)}) %collective-permute-start.9) | collective-permute-done | bytes 81952 | tf_op jit(solution)/shard_map/ppermute | solution.py:536
  43.0 2.4 %collective-permute-done.8.above = bf16[80,512]{1,0:T(8,128)(2,1)S(1)} collective-permute-done((bf16[80,512]{1,0:T(8,128)(2,1)S(1)}, bf16[80,512]{1,0:T(8,128)(2,1)S(1)}, u32[]{:S(2)}, u32[]{:S(2)}) %collective-permute-start.8) | collective-permute-done | bytes 81952 | tf_op jit(solution)/shard_map/ppermute | solution.py:535
  45.4 0.1 edges_back.1
  45.6 0.1 collective-permute-start.11
  45.7 0.5 collective-permute-start.10
  46.2 2.1 %adjoint_main.1 = (bf16[512,1536]{1,0:T(8,128)(2,1)S(1)}, bf16[1,80,2,256]{3,2,1,0:T(2,128)(2,1)}) custom-call(bf16[80,512]{1,0:T(8,128)(2,1)S(1)} %cotangent.1.own, bf16[80,512]{1,0:T(8,128)(2,1)S(1)} %collective-permute-done.8.above, bf16[80,512]{1,0:T(8,128)(2,1)S(1)} %collective-permute-done.9.below, bf16[512,720]{1,0:T(8,128)(2,1)S(1)} %get-tuple-element.40.bwd1, ...), custom_call_target="tpu_custom_call" | custom-call | tf_op jit(solution)/shard_map/adjoint_main/pallas_call | solution.py:522
  48.3 0.0 collective-permute-done.11.from_right
  48.3 2.8 %collective-permute-done.10.from_left = bf16[80,128]{1,0:T(8,128)(2,1)S(1)} collective-permute-done((bf16[80,128]{1,0:T(8,128)(2,1)S(1)}, bf16[80,128]{1,0:T(8,128)(2,1)S(1)}, u32[]{:S(2)}, u32[]{:S(2)}) %collective-permute-start.10) | collective-permute-done | bytes 20512 | tf_op jit(solution)/shard_map/ppermute | solution.py:542
  51.1 2.4 %adjoint_edge.1 = bf16[1,80,2,256]{3,2,1,0:T(2,128)(2,1)} custom-call(bf16[80,128]{1,0:T(8,128)(2,1)S(1)} %get-tuple-element.43.to_left, bf16[80,128]{1,0:T(8,128)(2,1)S(1)} %get-tuple-element.44.to_right, bf16[80,128]{1,0:T(8,128)(2,1)S(1)} %collective-permute-done.10.from_left, bf16[80,128]{1,0:T(8,128)(2,1)S(1)} %collective-permute-done.11.from_right, ...), custom_call_target="tpu_custom_call" | custom-call | tf_op jit(solution)/shard_map/adjoint_edge/pallas_call | solution.py:522
Async XLA Ops:
  2.0 6.0 %collective-permute-start.1 = (bf16[160,512]{1,0:T(8,128)(2,1)S(1)}, bf16[160,512]{1,0:T(8,128)(2,1)S(1)}, u32[]{:S(2)}, u32[]{:S(2)}) collective-permute-start(bf16[160,512]{1,0:T(8,128)(2,1)S(1)} %pack.1.own), channel_id=1, source_target_pairs={{32,0},{64,32},{96,64},{0,96},{33,1},{65,33},{97,65},{1,97},{34,2}... | collective-permute-start | bytes 491528 | tf_op jit(solution)/shard_map/ppermute | solution.py:536
  4.2 5.3 %collective-permute-start = (bf16[160,512]{1,0:T(8,128)(2,1)S(1)}, bf16[160,512]{1,0:T(8,128)(2,1)S(1)}, u32[]{:S(2)}, u32[]{:S(2)}) collective-permute-start(bf16[160,512]{1,0:T(8,128)(2,1)S(1)} %pack.1.own), channel_id=1, source_target_pairs={{0,32},{32,64},{64,96},{96,0},{1,33},{33,65},{65,97},{97,1},{2,34}... | collective-permute-start | bytes 491528 | tf_op jit(solution)/shard_map/ppermute | solution.py:535
  9.7 8.1 %collective-permute-start.3 = (bf16[160,128]{1,0:T(8,128)(2,1)S(1)}, bf16[160,128]{1,0:T(8,128)(2,1)S(1)}, u32[]{:S(2)}, u32[]{:S(2)}) collective-permute-start(bf16[160,128]{1,0:T(8,128)(2,1)S(1)} %get-tuple-element.26.to_left), channel_id=1, source_target_pairs={{1,0},{2,1},{3,2},{4,3},{5,4},{6,5},{7,6},{8,7},{9,8},{10,9},{11,1... | collective-permute-start | bytes 122888 | tf_op jit(solution)/shard_map/ppermute | solution.py:543
  15.1 5.5 %collective-permute-start.2 = (bf16[160,128]{1,0:T(8,128)(2,1)S(1)}, bf16[160,128]{1,0:T(8,128)(2,1)S(1)}, u32[]{:S(2)}, u32[]{:S(2)}) collective-permute-start(bf16[160,128]{1,0:T(8,128)(2,1)S(1)} %get-tuple-element.27.to_right), channel_id=1, source_target_pairs={{0,1},{1,2},{2,3},{3,4},{4,5},{5,6},{6,7},{7,8},{8,9},{9,10},{10,1... | collective-permute-start | bytes 122888 | tf_op jit(solution)/shard_map/ppermute | solution.py:542
  22.4 4.6 %collective-permute-start.5 = (f32[8,128]{1,0:T(8,128)S(1)}, f32[8,128]{1,0:T(8,128)S(1)}, u32[]{:S(2)}, u32[]{:S(2)}) collective-permute-start(f32[8,128]{1,0:T(8,128)S(1)} %get-tuple-element.32), channel_id=1, source_target_pairs={{0,159},{1,128},{2,129},{3,130},{4,131},{5,132},{6,133},{7,134},{8... | collective-permute-start | bytes 12296 | tf_op jit(solution)/shard_map/ppermute | solution.py:554
  23.7 5.1 %collective-permute-start.4 = (f32[8,128]{1,0:T(8,128)S(1)}, f32[8,128]{1,0:T(8,128)S(1)}, u32[]{:S(2)}, u32[]{:S(2)}) collective-permute-start(f32[8,128]{1,0:T(8,128)S(1)} %get-tuple-element.32), channel_id=1, source_target_pairs={{0,128},{128,0},{1,129},{129,1},{2,130},{130,2},{3,131},{131,3},{4... | collective-permute-start | bytes 12296 | tf_op jit(solution)/shard_map/ppermute | solution.py:549
  29.6 5.1 %collective-permute-start.6 = (f32[8,128]{1,0:T(8,128)S(1)}, f32[8,128]{1,0:T(8,128)S(1)}, u32[]{:S(2)}, u32[]{:S(2)}) collective-permute-start(f32[8,128]{1,0:T(8,128)S(1)} %get-tuple-element.38), channel_id=1, source_target_pairs={{0,128},{128,0},{1,129},{129,1},{2,130},{130,2},{3,131},{131,3},{4... | collective-permute-start | bytes 12296 | tf_op jit(solution)/shard_map/ppermute | solution.py:549
  31.6 6.4 %collective-permute-start.7 = (f32[8,128]{1,0:T(8,128)S(1)}, f32[8,128]{1,0:T(8,128)S(1)}, u32[]{:S(2)}, u32[]{:S(2)}) collective-permute-start(f32[8,128]{1,0:T(8,128)S(1)} %get-tuple-element.39), channel_id=1, source_target_pairs={{0,129},{1,130},{2,131},{3,132},{4,133},{5,134},{6,135},{7,136},{8... | collective-permute-start | bytes 12296 | tf_op jit(solution)/shard_map/ppermute | solution.py:554
  38.1 5.0 %collective-permute-start.9 = (bf16[80,512]{1,0:T(8,128)(2,1)S(1)}, bf16[80,512]{1,0:T(8,128)(2,1)S(1)}, u32[]{:S(2)}, u32[]{:S(2)}) collective-permute-start(bf16[80,512]{1,0:T(8,128)(2,1)S(1)} %cotangent.1.own), channel_id=1, source_target_pairs={{32,0},{64,32},{96,64},{0,96},{33,1},{65,33},{97,65},{1,97},{34,2}... | collective-permute-start | bytes 245768 | tf_op jit(solution)/shard_map/ppermute | solution.py:536
  41.0 4.4 %collective-permute-start.8 = (bf16[80,512]{1,0:T(8,128)(2,1)S(1)}, bf16[80,512]{1,0:T(8,128)(2,1)S(1)}, u32[]{:S(2)}, u32[]{:S(2)}) collective-permute-start(bf16[80,512]{1,0:T(8,128)(2,1)S(1)} %cotangent.1.own), channel_id=1, source_target_pairs={{0,32},{32,64},{64,96},{96,0},{1,33},{33,65},{65,97},{97,1},{2,34}... | collective-permute-start | bytes 245768 | tf_op jit(solution)/shard_map/ppermute | solution.py:535
  45.6 2.7 %collective-permute-start.11 = (bf16[80,128]{1,0:T(8,128)(2,1)S(1)}, bf16[80,128]{1,0:T(8,128)(2,1)S(1)}, u32[]{:S(2)}, u32[]{:S(2)}) collective-permute-start(bf16[80,128]{1,0:T(8,128)(2,1)S(1)} %get-tuple-element.43.to_left), channel_id=1, source_target_pairs={{1,0},{2,1},{3,2},{4,3},{5,4},{6,5},{7,6},{8,7},{9,8},{10,9},{11,1... | collective-permute-start | bytes 61448 | tf_op jit(solution)/shard_map/ppermute | solution.py:543
  45.7 5.4 %collective-permute-start.10 = (bf16[80,128]{1,0:T(8,128)(2,1)S(1)}, bf16[80,128]{1,0:T(8,128)(2,1)S(1)}, u32[]{:S(2)}, u32[]{:S(2)}) collective-permute-start(bf16[80,128]{1,0:T(8,128)(2,1)S(1)} %get-tuple-element.44.to_right), channel_id=1, source_target_pairs={{0,1},{1,2},{2,3},{3,4},{4,5},{5,6},{6,7},{7,8},{8,9},{9,10},{10,1... | collective-permute-start | bytes 61448 | tf_op jit(solution)/shard_map/ppermute | solution.py:542

commit v4 on v3

--- a/solution.py
+++ b/solution.py
@@ -168,15 +168,18 @@
 
 
 def edge_kernel(own, above, below, after, to_left, to_right):
-    channels = own.shape[0]
-    lanes = lane_iota((channels, 128))
-    left = jnp.zeros((channels, 128), F32)
-    right = jnp.zeros((channels, 128), F32)
-    for place, (read, r) in enumerate(sources(own, above, below)):
-        initial = pltpu.roll(read(slice(0, channels), 0, 128), 4 * place + 2, 1)
-        last = pltpu.roll(read(slice(0, channels), 128, COLS), 4 * place + 2, 1)
-        left = jnp.where((lanes >> 1) == 2 * place + 1, initial, left)
-        right = jnp.where((lanes >> 1) == 2 * place, last, right)
+    lanes = lane_iota((80, 128)) >> 1
+    left = jnp.zeros((80, 128), F32)
+    right = jnp.zeros((80, 128), F32)
+    for field in range(own.shape[0] // 80):
+        part = slice(field * 80, (field + 1) * 80)
+        for place, (read, r) in enumerate(sources(own, above, below)):
+            shift = 64 * field + 4 * place + 2
+            initial = pltpu.roll(read(part, 0, 128), shift, 1)
+            last = pltpu.roll(read(part, 128, COLS), shift, 1)
+            pair = 32 * field + 2 * place
+            left = jnp.where(lanes == pair + 1, initial, left)
+            right = jnp.where(lanes == pair, last, right)
     to_left[...] = left.astype(BF16)
     to_right[...] = right.astype(BF16)
 
@@ -222,39 +225,29 @@
     return jnp.where(drop, 0.0, 1.0).astype(F32)
 
 
-def edge_sides(to_left, to_right, from_left, from_right, part):
-    lanes = lane_iota((80, 128))
-    head = (lanes & 3) < 2
-    before = jnp.where(
-        head, from_left[part, :].astype(F32), pltpu.roll(to_right[part, :].astype(F32), 2, 1)
-    )
-    after = jnp.where(
-        head, pltpu.roll(to_left[part, :].astype(F32), 126, 1), from_right[part, :].astype(F32)
-    )
-    return before, after
-
-
 def fine_lanes(rows):
-    lanes = lane_iota((40, 128)) >> 3
+    lanes = (lane_iota((40, 128)) & 63) >> 3
     upper, lower = rows[:40], rows[40:]
     result = jnp.where(lanes == 0, lower, upper)
     result = jnp.where(lanes == 2, pltpu.roll(lower, 8, 1), result)
     return jnp.where(lanes == 3, pltpu.roll(upper, 8, 1), result)
 
 
-def edge_stack(to_left, to_right, from_left, from_right, fields, fine):
-    merged = None
-    for field in range(fields):
-        part = slice(field * 80, (field + 1) * 80)
-        sides = edge_sides(to_left, to_right, from_left, from_right, part)
+def own_sides(to_left, to_right, sides, fine):
+    for i, (ref, shift) in enumerate(((to_right, 2), (to_left, 126))):
+        rows = pltpu.roll(ref[...].astype(F32), shift, 1)
         if fine:
-            sides = [fine_lanes(side) for side in sides]
-        if merged is None:
-            merged = sides
+            sides[i, :40, :] = fine_lanes(rows)
         else:
-            low = lane_iota(sides[0].shape) < 64
-            merged = [jnp.where(low, m, pltpu.roll(s, 64, 1)) for m, s in zip(merged, sides)]
-    before, after = merged
+            sides[i] = rows
+
+
+def edge_stack(sides, from_left, from_right, fine):
+    both = []
+    for i, ref in enumerate((from_left, from_right)):
+        rows = ref[...].astype(F32)
+        both.append(fine_lanes(rows) + sides[i, :40, :] if fine else rows + sides[i])
+    before, after = both
     even = (lane_iota(before.shape) & 1) == 0
     middle = jnp.where(even, pltpu.roll(before, 127, 1), pltpu.roll(after, 1, 1))
     pieces = []
@@ -266,47 +259,60 @@
     return jnp.concatenate(pieces, axis=0).astype(BF16)
 
 
-def second_rows(weights, main, edge, channels, width, count):
-    shifted = [edge] + [pltpu.roll(edge, 128 - 4 * a, 1) for a in (1, 2)]
-    taps = jnp.concatenate(shifted, axis=0).astype(BF16)
+def halved_dot(matrix, taps):
+    half = matrix.shape[0] // 16 * 8
+    return jnp.concatenate([dot(matrix[:half], taps), dot(matrix[half:], taps)], axis=0)
+
+
+def inner_rows(weights, main, channels, width, count):
     matrix = weights[: 3 * channels, : 3 * width]
-    block = dot(matrix, taps)
+    result = []
+    for pair in range(0, count, 2):
+        pieces = [main[:width, (pair + a) * COLS : (pair + a + 2) * COLS] for a in range(3)]
+        whole = dot(matrix, jnp.concatenate(pieces, axis=0))
+        for row in range(2):
+            cut = whole[:, row * COLS : (row + 1) * COLS]
+            total = pltpu.roll(cut[:channels], 1, 1) + cut[channels : 2 * channels]
+            result.append(total + pltpu.roll(cut[2 * channels :], COLS - 1, 1))
+    return result
+
+
+def outer_rows(weights, edge, channels, width, count):
+    taps = edge.astype(BF16)
+    block = dot(weights[: 3 * channels, :width], taps)
+    for a in (1, 2):
+        part = dot(weights[: 3 * channels, a * width : (a + 1) * width], taps)
+        block = block + pltpu.roll(part, 128 - 4 * a, 1)
     first, middle, last = [block[e * channels : (e + 1) * channels] for e in range(3)]
     lanes = lane_iota((channels, 128))
     left = first + jnp.where((lanes & 3) == 0, pltpu.roll(middle, 127, 1), 0.0)
     right = last + jnp.where((lanes & 3) == 3, pltpu.roll(middle, 1, 1), 0.0)
     result = []
-    for pair in range(0, count, 2):
-        pieces = [main[:width, (pair + a) * COLS : (pair + a + 2) * COLS] for a in range(3)]
-        whole = dot(matrix, jnp.concatenate(pieces, axis=0))
-        for row in (pair, pair + 1):
-            cut = whole[:, (row - pair) * COLS : (row - pair + 1) * COLS]
-            total = pltpu.roll(cut[:channels], 1, 1) + cut[channels : 2 * channels]
-            total = total + pltpu.roll(cut[2 * channels :], COLS - 1, 1)
-            head = pltpu.roll(left, 128 - 4 * row, 1) if row else left
-            head = jnp.where(lanes < 2, head, 0.0)
-            tail = jnp.where(lanes >= 126, pltpu.roll(right, 124 - 4 * row, 1), 0.0)
-            result.append(total + jnp.concatenate([head, tail], axis=1))
+    for row in range(count):
+        head = pltpu.roll(left, 128 - 4 * row, 1) if row else left
+        head = jnp.where(lanes < 2, head, 0.0)
+        tail = jnp.where(lanes >= 126, pltpu.roll(right, 124 - 4 * row, 1), 0.0)
+        result.append(jnp.concatenate([head, tail], axis=1))
     return result
 
 
-def tangent_main_kernel(own, above, below, fwd1, columns, hidden, slope, stack):
-    def run(width, depth, count):
+def tangent_main_kernel(
+    own, above, below, to_left, to_right, fwd1, fwd2, columns, inner, slope, sides, stack, hidden
+):
+    def run(channels, width, depth, count):
         padded = depth // 3
-
-        def one_row(place, unused):
+        for place in range(count):
             pieces = []
             for a in range(3):
-                span = pl.ds(pl.multiple_of((place + a) * 2 * COLS, 128), 2 * COLS)
-                pieces.append(stack[:padded, span])
+                start = (place + a) * 2 * COLS
+                pieces.append(stack[:padded, start : start + 2 * COLS])
             both = dot(fwd1[:width, :depth], jnp.concatenate(pieces, axis=0))
             steep = 1.0 - jnp.tanh(both[:, :COLS] + columns[:width, 0:1]) ** 2
-            span = pl.ds(pl.multiple_of(place * COLS, 128), COLS)
+            span = slice(place * COLS, (place + 1) * COLS)
             hidden[:width, span] = (steep * both[:, COLS:] * kept(1, count, place)).astype(BF16)
             slope[:width, span] = steep.astype(BF16)
-            return unused
-
-        lax.fori_loop(0, count, one_row, 0)
+        for row, result in enumerate(inner_rows(fwd2, hidden, channels, width, count - 2)):
+            inner[:channels, row * COLS : (row + 1) * COLS] = result
 
     def store(field, place, rows):
         start = place * 2 * COLS + field * COLS
@@ -314,26 +320,31 @@
 
     @pl.when(is_air())
     def _():
+        own_sides(to_left, to_right, sides, False)
         air_rows(own, above, below, 2, store)
-        run(512, 720, 4)
+        run(80, 512, 720, 4)
 
     @pl.when(is_sea())
     def _():
+        own_sides(to_left, to_right, sides, True)
         sea_rows(own, above, below, 2, store)
-        run(256, 384, 6)
+        run(40, 256, 384, 6)
 
 
 def tangent_edge_kernel(
-    own, to_left, to_right, from_left, from_right, hidden, fwd1, fwd2, columns,
+    own, sides, from_left, from_right, inner, fwd1, fwd2, columns,
     y, slope, payload,
 ):
     def run(channels, width, depth, count):
-        stack = edge_stack(to_left, to_right, from_left, from_right, 2, channels == 40)
-        both = dot(fwd1[:width, :depth], stack)
+        stack = edge_stack(sides, from_left, from_right, channels == 40)
+        both = halved_dot(fwd1[:width, :depth], stack)
         steep = 1.0 - jnp.tanh(both + columns[:width, 0:1]) ** 2
         slope[:width, :] = steep.astype(BF16)
         edge = steep * pltpu.roll(both, 64, 1) * edge_kept(count)
-        return second_rows(fwd2, hidden, edge, channels, width, count - 2)
+        rows = outer_rows(fwd2, edge, channels, width, count - 2)
+        return [
+            inner[:channels, i * COLS : (i + 1) * COLS] + row for i, row in enumerate(rows)
+        ]
 
     @pl.when(is_air())
     def _():
@@ -447,49 +458,55 @@
     target[0] = jnp.stack(rows, axis=1).astype(BF16)
 
 
-def adjoint_main_kernel(own, above, below, bwd1, slope, packed, hidden, image, stack):
+def unpack_kernel(packed, image):
     wide = packed[...].astype(F32)
     spread_rows(image, [wide[:, r * COLS : (r + 1) * COLS] for r in range(ROWS)])
 
-    def run(width, depth, count):
+
+def adjoint_main_kernel(
+    own, above, below, to_left, to_right, bwd1, bwd2, slope, inner, sides, stack, hidden
+):
+    def run(channels, width, depth, count):
         padded = depth // 3
-
-        def two_rows(pair, unused):
+        for pair in range(0, count, 2):
             pieces = []
             for a in range(3):
-                span = pl.ds(pl.multiple_of((2 * pair + a) * COLS, 128), 2 * COLS)
-                pieces.append(stack[:padded, span])
+                pieces.append(stack[:padded, (pair + a) * COLS : (pair + a + 2) * COLS])
             back = dot(bwd1[:width, :depth], jnp.concatenate(pieces, axis=0))
-            span = pl.ds(pl.multiple_of(2 * pair * COLS, 128), 2 * COLS)
-            back = back * slope[:width, span].astype(F32) * kept(2, count, 2 * pair)
+            span = slice(pair * COLS, (pair + 2) * COLS)
+            back = back * slope[:width, span].astype(F32) * kept(2, count, pair)
             hidden[:width, span] = back.astype(BF16)
-            return unused
-
-        lax.fori_loop(0, count // 2, two_rows, 0)
+        for row, result in enumerate(inner_rows(bwd2, hidden, channels, width, count - 2)):
+            inner[:channels, row * COLS : (row + 1) * COLS] = result
 
     def store(field, place, rows):
         stack[: rows.shape[0], place * COLS : (place + 1) * COLS] = rows
 
     @pl.when(is_air())
     def _():
+        own_sides(to_left, to_right, sides, False)
         air_rows(own, above, below, 1, store)
-        run(512, 720, 4)
+        run(80, 512, 720, 4)
 
     @pl.when(is_sea())
     def _():
+        own_sides(to_left, to_right, sides, True)
         sea_rows(own, above, below, 1, store)
-        run(256, 384, 6)
+        run(40, 256, 384, 6)
 
 
 def adjoint_edge_kernel(
-    to_left, to_right, from_left, from_right, hidden, slope, bwd1, bwd2, near, far, product
+    sides, from_left, from_right, inner, slope, bwd1, bwd2, near, far, product
 ):
     def run(channels, width, depth, count):
-        stack = edge_stack(to_left, to_right, from_left, from_right, 1, channels == 40)
-        edge = dot(bwd1[:width, :depth], stack)
+        stack = edge_stack(sides, from_left, from_right, channels == 40)
+        edge = halved_dot(bwd1[:width, :depth], stack)
         edge = edge * slope[:width, :].astype(F32)
         edge = jnp.where(edge_kept(count) > 0.0, edge, 0.0)
-        return second_rows(bwd2, hidden, edge, channels, width, count - 2)
+        rows = outer_rows(bwd2, edge, channels, width, count - 2)
+        return [
+            inner[:channels, i * COLS : (i + 1) * COLS] + row for i, row in enumerate(rows)
+        ]
 
     @pl.when(is_air())
     def _():
@@ -513,17 +530,19 @@
         spread_rows(product, rows)
 
 
-def call(kernel, name, out_shape, inputs, scratch=(), limit=8, loads=False):
+def call(kernel, name, out_shape, inputs, scratch=(), limit=8, loads=False, idle=0):
     vmem = pl.BlockSpec(memory_space=pltpu.VMEM)
     source = vmem
     if loads:
         source = pl.BlockSpec(memory_space=pltpu.HBM)
         inputs = [pltpu.with_memory_space_constraint(array, pltpu.HBM) for array in inputs]
+    for i in range(len(inputs) - idle, len(inputs)):
+        inputs[i] = pltpu.with_memory_space_constraint(inputs[i], pltpu.HBM)
     return pl.pallas_call(
         kernel,
         name=name,
         out_shape=tuple(jax.ShapeDtypeStruct(shape, dtype) for shape, dtype in out_shape),
-        in_specs=[source] * len(inputs),
+        in_specs=[source] * (len(inputs) - idle) + [pl.BlockSpec(memory_space=pltpu.HBM)] * idle,
         out_specs=tuple(vmem for _ in out_shape),
         scratch_shapes=list(scratch),
         compiler_params=pltpu.CompilerParams(vmem_limit_bytes=limit << 20),
@@ -607,22 +626,22 @@
         loads=True,
     )
     to_left, to_right = call(
-        edge_kernel, "edges", [((160, 128), BF16)] * 2, [own, above, below, columns]
+        edge_kernel, "edges", [((80, 128), BF16)] * 2, [own, above, below, columns]
     )
     from_left, from_right = lon_pair(to_left, to_right)
-    hidden, slope = call(
+    inner, slope, sides = call(
         tangent_main_kernel,
         "tangent_main",
-        [((512, 6 * COLS), BF16), ((512, 6 * COLS), BF16)],
-        [own, above, below, fwd1, columns],
-        [pltpu.VMEM((240, 16 * COLS), BF16)],
+        [((80, 2 * CELLS), F32), ((512, 6 * COLS), BF16), ((2, 80, 128), F32)],
+        [own, above, below, to_left, to_right, fwd1, fwd2, columns],
+        [pltpu.VMEM((240, 16 * COLS), BF16), pltpu.VMEM((512, 6 * COLS), BF16)],
         limit=16,
     )
     y, edge_slope, payload = call(
         tangent_edge_kernel,
         "tangent_edge",
         [((80, 2 * CELLS), F32), ((512, 128), BF16), ((8, 128), F32)],
-        [own, to_left, to_right, from_left, from_right, hidden, fwd1, fwd2, columns],
+        [own, sides, from_left, from_right, inner, fwd1, fwd2, columns],
         limit=16,
     )
     near, far = across(payload, payload, -1)
@@ -633,6 +652,7 @@
         [y, near, far, hot, line, share, mask, columns],
     )
     back_near, back_far = across(back_near, back_far, 1)
+    (result,) = call(unpack_kernel, "unpack", [((1, 80, ROWS, COLS), BF16)], [image])
     (cotangent,) = call(
         cotangent_kernel, "cotangent", [((80, CELLS), BF16)],
         [image, back_near, back_far, columns],
@@ -640,15 +660,16 @@
     above, below = lat_pair(cotangent)
     to_left, to_right = call(
         edge_kernel, "edges_back", [((80, 128), BF16)] * 2,
-        [cotangent, above, below, columns],
+        [cotangent, above, below, result],
+        idle=1,
     )
     from_left, from_right = lon_pair(to_left, to_right)
-    hidden, result = call(
+    inner, sides = call(
         adjoint_main_kernel,
         "adjoint_main",
-        [((512, 6 * COLS), BF16), ((1, 80, ROWS, COLS), BF16)],
-        [cotangent, above, below, bwd1, slope, image],
-        [pltpu.VMEM((240, 8 * COLS), BF16)],
+        [((80, 2 * CELLS), F32), ((2, 80, 128), F32)],
+        [cotangent, above, below, to_left, to_right, bwd1, bwd2, slope],
+        [pltpu.VMEM((240, 8 * COLS), BF16), pltpu.VMEM((512, 6 * COLS), BF16)],
         limit=16,
     )
     (product,) = call(
@@ -656,7 +677,7 @@
         "adjoint_edge",
         [((1, 80, ROWS, COLS), BF16)],
         [
-            to_left, to_right, from_left, from_right, hidden, edge_slope, bwd1, bwd2,
+            sides, from_left, from_right, inner, edge_slope, bwd1, bwd2,
             back_near, back_far,
         ],
         limit=16,

time: 53.6 us -> 52 us (0.970)
  Pallas kernels: 13.8 us -> 12.5 us
    pallas_call x10 -> x11, Pallas kernels: 13.8 us -> 12.5 us  [call(): pl.pallas_call(kernel, name=name, out_shape=tuple((jax.ShapeDtypeStruct(s...]
    ppermute x2, waiting for transfers between devices: 3.5 us -> 2.74 us  [lat_pair(): lax.ppermute(block, 'lat', [((i + 1) % count, i) for i in range(count)])]
    ppermute x2, waiting for transfers between devices: 5.57 us -> 6.22 us  [lon_pair(): lax.ppermute(to_right, 'lon', [(i, (i + 1) % count) for i in range(count)])]
  transfers between devices with their start and end apart: 12 -> 12, of which waited for: 10 -> 10; matrix products, arithmetic and copies ran while one was open for 0% -> 0% of each run, Pallas kernels for 13% -> 14%
where the time goes in v4:
time: 52 us; the launch traced here: 51.8 us
  waiting for transfers between devices  21.1 us (41%)
  starting transfers between devices  17.5 us (34%)
  Pallas kernels  12.5 us (24%)
  between operations  0.73 us (1%)
    pallas_call x11, Pallas kernels, call(): pl.pallas_call(kernel, name=name, out_shape=tuple((jax.ShapeDtypeStruct(s...  12.5 us
    ppermute x2, waiting for transfers between devices, lon_pair(): lax.ppermute(to_right, 'lon', [(i, (i + 1) % count) for i in range(count)])  6.22 us
    ppermute x2, starting transfers between devices, lon_pair(): lax.ppermute(to_left, 'lon', [((i + 1) % count, i) for i in range(count)])  5.43 us
    ppermute x2, starting transfers between devices, lat_pair(): lax.ppermute(block, 'lat', [((i + 1) % count, i) for i in range(count)])  4.99 us
    ppermute x2, waiting for transfers between devices, across(): return (same, lax.ppermute(far, ('comp', 'lon'), route))  4.75 us
    ppermute x2, starting transfers between devices, across(): same = lax.ppermute(near, 'comp', [(0, 1), (1, 0)])  4.17 us
    ppermute x2, waiting for transfers between devices, lat_pair(): lax.ppermute(block, 'lat', [(i, (i + 1) % count) for i in range(count)])  3.92 us
    ppermute x2, waiting for transfers between devices, across(): same = lax.ppermute(near, 'comp', [(0, 1), (1, 0)])  3.47 us
  transfers between devices with their start and end apart: 12, of which 10 were waited for; matrix products, arithmetic and copies ran while one was open for 0% of the time, Pallas kernels for 14%

profile of v4, /device:TPU:8, one launch (start us, length us, event | category | flops | bytes accessed | tf_op | source)
XLA Modules:
  0.0 51.8 jit_solution(14065392606688067544)
XLA Ops:
  0.6 1.3 %pack.1.own = bf16[160,512]{1,0:T(8,128)(2,1)S(1)} custom-call(bf16[1,80,2,256]{3,2,1,0:T(2,128)(2,1)} %state.1, bf16[1,80,2,256]{3,2,1,0:T(2,128)(2,1)} %direction.1), custom_call_target="tpu_custom_call" | custom-call | tf_op jit(solution)/shard_map/pack/pallas_call | solution.py:541
  2.0 2.2 %collective-permute-start.1 = (bf16[160,512]{1,0:T(8,128)(2,1)S(1)}, bf16[160,512]{1,0:T(8,128)(2,1)S(1)}, u32[]{:S(2)}, u32[]{:S(2)}) collective-permute-start(bf16[160,512]{1,0:T(8,128)(2,1)S(1)} %pack.1.own), channel_id=1, source_target_pairs={{32,0},{64,32},{96,64},{0,96},{33,1},{65,33},{97,65},{1,97},{34,2}... | collective-permute-start | bytes 491528 | tf_op jit(solution)/shard_map/ppermute | solution.py:555
  4.2 0.0 collective-permute-start
  4.2 2.3 %prepare.1 = (bf16[512,720]{1,0:T(8,128)(2,1)S(1)}, bf16[240,1536]{1,0:T(8,128)(2,1)S(1)}, bf16[512,720]{1,0:T(8,128)(2,1)S(1)}, bf16[240,1536]{1,0:T(8,128)(2,1...) custom-call(bf16[9,80,512]{2,1,0:T(8,128)(2,1)} %bitcast.6, ...), custom_call_target="tpu_custom_call" | custom-call | tf_op jit(solution)/shard_map/prepare/pallas_call | solution.py:541
  6.5 1.4 %collective-permute-done.1.below = bf16[160,512]{1,0:T(8,128)(2,1)S(1)} collective-permute-done((bf16[160,512]{1,0:T(8,128)(2,1)S(1)}, bf16[160,512]{1,0:T(8,128)(2,1)S(1)}, u32[]{:S(2)}, u32[]{:S(2)}) %collective-permute-start.1) | collective-permute-done | bytes 163872 | tf_op jit(solution)/shard_map/ppermute | solution.py:555
  8.0 1.5 %collective-permute-done.above = bf16[160,512]{1,0:T(8,128)(2,1)S(1)} collective-permute-done((bf16[160,512]{1,0:T(8,128)(2,1)S(1)}, bf16[160,512]{1,0:T(8,128)(2,1)S(1)}, u32[]{:S(2)}, u32[]{:S(2)}) %collective-permute-start) | collective-permute-done | bytes 163872 | tf_op jit(solution)/shard_map/ppermute | solution.py:554
  9.5 0.2 edges.1
  9.7 5.3 %collective-permute-start.3 = (bf16[80,128]{1,0:T(8,128)(2,1)S(1)}, bf16[80,128]{1,0:T(8,128)(2,1)S(1)}, u32[]{:S(2)}, u32[]{:S(2)}) collective-permute-start(bf16[80,128]{1,0:T(8,128)(2,1)S(1)} %get-tuple-element.27.to_left), channel_id=1, source_target_pairs={{1,0},{2,1},{3,2},{4,3},{5,4},{6,5},{7,6},{8,7},{9,8},{10,9},{11,1... | collective-permute-start | bytes 61448 | tf_op jit(solution)/shard_map/ppermute | solution.py:562
  15.1 0.0 collective-permute-start.2
  15.1 2.4 %tangent_main.1 = (f32[80,1024]{1,0:T(8,128)S(1)}, bf16[512,1536]{1,0:T(8,128)(2,1)S(1)}, f32[2,80,128]{2,1,0:T(8,128)S(1)}) custom-call(bf16[160,512]{1,0:T(8,128)(2,1)S(1)} %pack.1.own, bf16[160,512]{1,0:T(8,128)(2,1)S(1)} %collective-permute-done.above, bf16[160,512]{1,0:T(8,128)(2,1)S(1)} %collective-permute-done.1.below, ...), custom_call_target="tpu_custom_call" | custom-call | tf_op jit(solution)/shard_map/tangent_main/pallas_call | solution.py:541
  17.5 0.0 collective-permute-done.3.from_right
  17.5 2.9 %collective-permute-done.2.from_left = bf16[80,128]{1,0:T(8,128)(2,1)S(1)} collective-permute-done((bf16[80,128]{1,0:T(8,128)(2,1)S(1)}, bf16[80,128]{1,0:T(8,128)(2,1)S(1)}, u32[]{:S(2)}, u32[]{:S(2)}) %collective-permute-start.2) | collective-permute-done | bytes 20512 | tf_op jit(solution)/shard_map/ppermute | solution.py:561
  20.4 1.1 %tangent_edge.1 = (f32[80,1024]{1,0:T(8,128)S(1)}, bf16[512,128]{1,0:T(8,128)(2,1)S(1)}, f32[8,128]{1,0:T(8,128)S(1)}) custom-call(bf16[160,512]{1,0:T(8,128)(2,1)S(1)} %pack.1.own, f32[2,80,128]{2,1,0:T(8,128)S(1)} %get-tuple-element.31.sides, bf16[80,128]{1,0:T(8,128)(2,1)S(1)} %collective-permute-done.2.from_left, ...), custom_call_target="tpu_custom_call" | custom-call | tf_op jit(solution)/shard_map/tangent_edge/pallas_call | solution.py:541
  21.5 1.1 %collective-permute-start.5 = (f32[8,128]{1,0:T(8,128)S(1)}, f32[8,128]{1,0:T(8,128)S(1)}, u32[]{:S(2)}, u32[]{:S(2)}) collective-permute-start(f32[8,128]{1,0:T(8,128)S(1)} %get-tuple-element.34), channel_id=1, source_target_pairs={{0,159},{1,128},{2,129},{3,130},{4,131},{5,132},{6,133},{7,134},{8... | collective-permute-start | bytes 12296 | tf_op jit(solution)/shard_map/ppermute | solution.py:573
  22.7 2.0 %collective-permute-start.4 = (f32[8,128]{1,0:T(8,128)S(1)}, f32[8,128]{1,0:T(8,128)S(1)}, u32[]{:S(2)}, u32[]{:S(2)}) collective-permute-start(f32[8,128]{1,0:T(8,128)S(1)} %get-tuple-element.34), channel_id=1, source_target_pairs={{0,128},{128,0},{1,129},{129,1},{2,130},{130,2},{3,131},{131,3},{4... | collective-permute-start | bytes 12296 | tf_op jit(solution)/shard_map/ppermute | solution.py:568
  24.7 1.5 %collective-permute-done.5.far = f32[8,128]{1,0:T(8,128)S(1)} collective-permute-done((f32[8,128]{1,0:T(8,128)S(1)}, f32[8,128]{1,0:T(8,128)S(1)}, u32[]{:S(2)}, u32[]{:S(2)}) %collective-permute-start.5) | collective-permute-done | bytes 4128 | tf_op jit(solution)/shard_map/ppermute | solution.py:573
  26.1 1.6 %collective-permute-done.4.near = f32[8,128]{1,0:T(8,128)S(1)} collective-permute-done((f32[8,128]{1,0:T(8,128)S(1)}, f32[8,128]{1,0:T(8,128)S(1)}, u32[]{:S(2)}, u32[]{:S(2)}) %collective-permute-start.4) | collective-permute-done | bytes 4128 | tf_op jit(solution)/shard_map/ppermute | solution.py:568
  27.8 0.8 %couple.1 = (bf16[80,512]{1,0:T(8,128)(2,1)S(1)}, f32[8,128]{1,0:T(8,128)S(1)}, f32[8,128]{1,0:T(8,128)S(1)}) custom-call(f32[80,1024]{1,0:T(8,128)S(1)} %get-tuple-element.33.y, f32[8,128]{1,0:T(8,128)S(1)} %collective-permute-done.4.near, f32[8,128]{1,0:T(8,128)S(1)} %collective-permute-done.5.far, bf16[128,4096]{1,0:T(8,128)(2,1)S(1)} %get-tuple-element.35.hot, ...), custom_call_target="tpu_custom_call" | custom-call | tf_op jit(solution)/shard_map/couple/pallas_call | solution.py:541
  28.6 2.2 %collective-permute-start.6 = (f32[8,128]{1,0:T(8,128)S(1)}, f32[8,128]{1,0:T(8,128)S(1)}, u32[]{:S(2)}, u32[]{:S(2)}) collective-permute-start(f32[8,128]{1,0:T(8,128)S(1)} %get-tuple-element.40), channel_id=1, source_target_pairs={{0,128},{128,0},{1,129},{129,1},{2,130},{130,2},{3,131},{131,3},{4... | collective-permute-start | bytes 12296 | tf_op jit(solution)/shard_map/ppermute | solution.py:568
  30.8 1.3 %collective-permute-start.7 = (f32[8,128]{1,0:T(8,128)S(1)}, f32[8,128]{1,0:T(8,128)S(1)}, u32[]{:S(2)}, u32[]{:S(2)}) collective-permute-start(f32[8,128]{1,0:T(8,128)S(1)} %get-tuple-element.41), channel_id=1, source_target_pairs={{0,129},{1,130},{2,131},{3,132},{4,133},{5,134},{6,135},{7,136},{8... | collective-permute-start | bytes 12296 | tf_op jit(solution)/shard_map/ppermute | solution.py:573
  32.0 1.8 %collective-permute-done.6.near = f32[8,128]{1,0:T(8,128)S(1)} collective-permute-done((f32[8,128]{1,0:T(8,128)S(1)}, f32[8,128]{1,0:T(8,128)S(1)}, u32[]{:S(2)}, u32[]{:S(2)}) %collective-permute-start.6) | collective-permute-done | bytes 4128 | tf_op jit(solution)/shard_map/ppermute | solution.py:568
  33.9 3.3 %collective-permute-done.7.far = f32[8,128]{1,0:T(8,128)S(1)} collective-permute-done((f32[8,128]{1,0:T(8,128)S(1)}, f32[8,128]{1,0:T(8,128)S(1)}, u32[]{:S(2)}, u32[]{:S(2)}) %collective-permute-start.7) | collective-permute-done | bytes 4128 | tf_op jit(solution)/shard_map/ppermute | solution.py:573
  37.1 0.1 cotangent.1.own
  37.2 2.8 %collective-permute-start.9 = (bf16[80,512]{1,0:T(8,128)(2,1)S(1)}, bf16[80,512]{1,0:T(8,128)(2,1)S(1)}, u32[]{:S(2)}, u32[]{:S(2)}) collective-permute-start(bf16[80,512]{1,0:T(8,128)(2,1)S(1)} %cotangent.1.own), channel_id=1, source_target_pairs={{32,0},{64,32},{96,64},{0,96},{33,1},{65,33},{97,65},{1,97},{34,2}... | collective-permute-start | bytes 245768 | tf_op jit(solution)/shard_map/ppermute | solution.py:555
  40.0 0.0 collective-permute-start.8
  40.0 0.8 %unpack.1.after = bf16[1,80,2,256]{3,2,1,0:T(2,128)(2,1)} custom-call(bf16[80,512]{1,0:T(8,128)(2,1)S(1)} %get-tuple-element.39.packed.image), custom_call_target="tpu_custom_call" | custom-call | tf_op jit(solution)/shard_map/unpack/pallas_call | solution.py:541
  40.8 1.3 %collective-permute-done.9.below = bf16[80,512]{1,0:T(8,128)(2,1)S(1)} collective-permute-done((bf16[80,512]{1,0:T(8,128)(2,1)S(1)}, bf16[80,512]{1,0:T(8,128)(2,1)S(1)}, u32[]{:S(2)}, u32[]{:S(2)}) %collective-permute-start.9) | collective-permute-done | bytes 81952 | tf_op jit(solution)/shard_map/ppermute | solution.py:555
  42.0 2.4 %collective-permute-done.8.above = bf16[80,512]{1,0:T(8,128)(2,1)S(1)} collective-permute-done((bf16[80,512]{1,0:T(8,128)(2,1)S(1)}, bf16[80,512]{1,0:T(8,128)(2,1)S(1)}, u32[]{:S(2)}, u32[]{:S(2)}) %collective-permute-start.8) | collective-permute-done | bytes 81952 | tf_op jit(solution)/shard_map/ppermute | solution.py:554
  44.4 0.1 edges_back.1
  44.6 0.1 collective-permute-start.11
  44.7 0.5 collective-permute-start.10
  45.2 1.6 %adjoint_main.1 = (f32[80,1024]{1,0:T(8,128)S(1)}, f32[2,80,128]{2,1,0:T(8,128)S(1)}) custom-call(bf16[80,512]{1,0:T(8,128)(2,1)S(1)} %cotangent.1.own, bf16[80,512]{1,0:T(8,128)(2,1)S(1)} %collective-permute-done.8.above, bf16[80,512]{1,0:T(8,128)(2,1)S(1)} %collective-permute-done.9.below, bf16[80,128]{1,0:T(8,128)(2,1)S(1)} %get-tuple-element.42.to_left, ...), custom_call_target="tpu_custom_call" | custom-call | tf_op jit(solution)/shard_map/adjoint_main/pallas_call | solution.py:541
  46.7 0.0 collective-permute-done.11.from_right
  46.7 3.3 %collective-permute-done.10.from_left = bf16[80,128]{1,0:T(8,128)(2,1)S(1)} collective-permute-done((bf16[80,128]{1,0:T(8,128)(2,1)S(1)}, bf16[80,128]{1,0:T(8,128)(2,1)S(1)}, u32[]{:S(2)}, u32[]{:S(2)}) %collective-permute-start.10) | collective-permute-done | bytes 20512 | tf_op jit(solution)/shard_map/ppermute | solution.py:561
  50.1 1.8 %adjoint_edge.1 = bf16[1,80,2,256]{3,2,1,0:T(2,128)(2,1)} custom-call(f32[2,80,128]{2,1,0:T(8,128)S(1)} %get-tuple-element.47.sides, bf16[80,128]{1,0:T(8,128)(2,1)S(1)} %collective-permute-done.10.from_left, bf16[80,128]{1,0:T(8,128)(2,1)S(1)} %collective-permute-done.11.from_right, f32[80,1024]{1,0:T(8,128)S(1)} %get-tuple-element.48.inner, ...), custom_call_target="tpu_custom_call" | custom-call | tf_op jit(solution)/shard_map/adjoint_edge/pallas_call | solution.py:541
Async XLA Ops:
  2.0 6.0 %collective-permute-start.1 = (bf16[160,512]{1,0:T(8,128)(2,1)S(1)}, bf16[160,512]{1,0:T(8,128)(2,1)S(1)}, u32[]{:S(2)}, u32[]{:S(2)}) collective-permute-start(bf16[160,512]{1,0:T(8,128)(2,1)S(1)} %pack.1.own), channel_id=1, source_target_pairs={{32,0},{64,32},{96,64},{0,96},{33,1},{65,33},{97,65},{1,97},{34,2}... | collective-permute-start | bytes 491528 | tf_op jit(solution)/shard_map/ppermute | solution.py:555
  4.2 5.3 %collective-permute-start = (bf16[160,512]{1,0:T(8,128)(2,1)S(1)}, bf16[160,512]{1,0:T(8,128)(2,1)S(1)}, u32[]{:S(2)}, u32[]{:S(2)}) collective-permute-start(bf16[160,512]{1,0:T(8,128)(2,1)S(1)} %pack.1.own), channel_id=1, source_target_pairs={{0,32},{32,64},{64,96},{96,0},{1,33},{33,65},{65,97},{97,1},{2,34}... | collective-permute-start | bytes 491528 | tf_op jit(solution)/shard_map/ppermute | solution.py:554
  9.7 7.8 %collective-permute-start.3 = (bf16[80,128]{1,0:T(8,128)(2,1)S(1)}, bf16[80,128]{1,0:T(8,128)(2,1)S(1)}, u32[]{:S(2)}, u32[]{:S(2)}) collective-permute-start(bf16[80,128]{1,0:T(8,128)(2,1)S(1)} %get-tuple-element.27.to_left), channel_id=1, source_target_pairs={{1,0},{2,1},{3,2},{4,3},{5,4},{6,5},{7,6},{8,7},{9,8},{10,9},{11,1... | collective-permute-start | bytes 61448 | tf_op jit(solution)/shard_map/ppermute | solution.py:562
  15.1 5.3 %collective-permute-start.2 = (bf16[80,128]{1,0:T(8,128)(2,1)S(1)}, bf16[80,128]{1,0:T(8,128)(2,1)S(1)}, u32[]{:S(2)}, u32[]{:S(2)}) collective-permute-start(bf16[80,128]{1,0:T(8,128)(2,1)S(1)} %get-tuple-element.28.to_right), channel_id=1, source_target_pairs={{0,1},{1,2},{2,3},{3,4},{4,5},{5,6},{6,7},{7,8},{8,9},{9,10},{10,1... | collective-permute-start | bytes 61448 | tf_op jit(solution)/shard_map/ppermute | solution.py:561
  21.5 4.6 %collective-permute-start.5 = (f32[8,128]{1,0:T(8,128)S(1)}, f32[8,128]{1,0:T(8,128)S(1)}, u32[]{:S(2)}, u32[]{:S(2)}) collective-permute-start(f32[8,128]{1,0:T(8,128)S(1)} %get-tuple-element.34), channel_id=1, source_target_pairs={{0,159},{1,128},{2,129},{3,130},{4,131},{5,132},{6,133},{7,134},{8... | collective-permute-start | bytes 12296 | tf_op jit(solution)/shard_map/ppermute | solution.py:573
  22.7 5.1 %collective-permute-start.4 = (f32[8,128]{1,0:T(8,128)S(1)}, f32[8,128]{1,0:T(8,128)S(1)}, u32[]{:S(2)}, u32[]{:S(2)}) collective-permute-start(f32[8,128]{1,0:T(8,128)S(1)} %get-tuple-element.34), channel_id=1, source_target_pairs={{0,128},{128,0},{1,129},{129,1},{2,130},{130,2},{3,131},{131,3},{4... | collective-permute-start | bytes 12296 | tf_op jit(solution)/shard_map/ppermute | solution.py:568
  28.6 5.3 %collective-permute-start.6 = (f32[8,128]{1,0:T(8,128)S(1)}, f32[8,128]{1,0:T(8,128)S(1)}, u32[]{:S(2)}, u32[]{:S(2)}) collective-permute-start(f32[8,128]{1,0:T(8,128)S(1)} %get-tuple-element.40), channel_id=1, source_target_pairs={{0,128},{128,0},{1,129},{129,1},{2,130},{130,2},{3,131},{131,3},{4... | collective-permute-start | bytes 12296 | tf_op jit(solution)/shard_map/ppermute | solution.py:568
  30.8 6.4 %collective-permute-start.7 = (f32[8,128]{1,0:T(8,128)S(1)}, f32[8,128]{1,0:T(8,128)S(1)}, u32[]{:S(2)}, u32[]{:S(2)}) collective-permute-start(f32[8,128]{1,0:T(8,128)S(1)} %get-tuple-element.41), channel_id=1, source_target_pairs={{0,129},{1,130},{2,131},{3,132},{4,133},{5,134},{6,135},{7,136},{8... | collective-permute-start | bytes 12296 | tf_op jit(solution)/shard_map/ppermute | solution.py:573
  37.2 4.8 %collective-permute-start.9 = (bf16[80,512]{1,0:T(8,128)(2,1)S(1)}, bf16[80,512]{1,0:T(8,128)(2,1)S(1)}, u32[]{:S(2)}, u32[]{:S(2)}) collective-permute-start(bf16[80,512]{1,0:T(8,128)(2,1)S(1)} %cotangent.1.own), channel_id=1, source_target_pairs={{32,0},{64,32},{96,64},{0,96},{33,1},{65,33},{97,65},{1,97},{34,2}... | collective-permute-start | bytes 245768 | tf_op jit(solution)/shard_map/ppermute | solution.py:555
  40.0 4.4 %collective-permute-start.8 = (bf16[80,512]{1,0:T(8,128)(2,1)S(1)}, bf16[80,512]{1,0:T(8,128)(2,1)S(1)}, u32[]{:S(2)}, u32[]{:S(2)}) collective-permute-start(bf16[80,512]{1,0:T(8,128)(2,1)S(1)} %cotangent.1.own), channel_id=1, source_target_pairs={{0,32},{32,64},{64,96},{96,0},{1,33},{33,65},{65,97},{97,1},{2,34}... | collective-permute-start | bytes 245768 | tf_op jit(solution)/shard_map/ppermute | solution.py:554
  44.6 2.2 %collective-permute-start.11 = (bf16[80,128]{1,0:T(8,128)(2,1)S(1)}, bf16[80,128]{1,0:T(8,128)(2,1)S(1)}, u32[]{:S(2)}, u32[]{:S(2)}) collective-permute-start(bf16[80,128]{1,0:T(8,128)(2,1)S(1)} %get-tuple-element.42.to_left), channel_id=1, source_target_pairs={{1,0},{2,1},{3,2},{4,3},{5,4},{6,5},{7,6},{8,7},{9,8},{10,9},{11,1... | collective-permute-start | bytes 61448 | tf_op jit(solution)/shard_map/ppermute | solution.py:562
  44.7 5.4 %collective-permute-start.10 = (bf16[80,128]{1,0:T(8,128)(2,1)S(1)}, bf16[80,128]{1,0:T(8,128)(2,1)S(1)}, u32[]{:S(2)}, u32[]{:S(2)}) collective-permute-start(bf16[80,128]{1,0:T(8,128)(2,1)S(1)} %get-tuple-element.43.to_right), channel_id=1, source_target_pairs={{0,1},{1,2},{2,3},{3,4},{4,5},{5,6},{6,7},{7,8},{8,9},{9,10},{10,1... | collective-permute-start | bytes 61448 | tf_op jit(solution)/shard_map/ppermute | solution.py:561

commit v5 on v4

--- a/solution.py
+++ b/solution.py
@@ -65,18 +65,22 @@
     for field, ref in enumerate((state, direction)):
         copies.append(pltpu.make_async_copy(ref.at[0], rows.at[field], sems.at[field]))
         copies[-1].start()
+    line = lax.broadcasted_iota(jnp.int32, (160, 160), 0)
+    place = lane_iota((160, 160))
+    source = jnp.where(line < 80, 2 * line, 2 * line - 159)
+    order = jnp.where(place == source, 1.0, 0.0).astype(BF16)
     for field, copy in enumerate(copies):
         copy.wait()
-        block = rows[field].astype(F32)
+        block = dot(order, rows[field].reshape(160, COLS)).astype(BF16)
         for r in range(ROWS):
-            packed[field * 80 : field * 80 + 80, r * COLS : (r + 1) * COLS] = block[:, r, :].astype(BF16)
+            packed[field * 80 : field * 80 + 80, r * COLS : (r + 1) * COLS] = block[r * 80 : (r + 1) * 80]
 
 
 def prepare_kernel(*refs):
     sources = refs[:12]
-    fwd1, fwd2, bwd1, bwd2, hot, share, line, mask, columns = refs[12:21]
-    held = refs[21:33]
-    sems = refs[33]
+    fwd1, fwd2, bwd1, bwd2, hot, picked, mask, columns = refs[12:20]
+    held = refs[20:32]
+    sems = refs[32]
     copies = [
         pltpu.make_async_copy(source, target, sems.at[i])
         for i, (source, target) in enumerate(zip(sources, held))
@@ -133,7 +137,14 @@
 
     table = jnp.concatenate([flat(weight[0, s]) for s in range(SLOTS)], axis=0).astype(F32)
     place = jnp.concatenate([flat(index[0, s]) for s in range(SLOTS)], axis=0)
-    line[...] = ((place >> 8) & 1) * 8 + (place >> 9) * 2 + ((place >> 7) & 1)
+    line = ((place >> 8) & 1) * 8 + (place >> 9) * 2 + ((place >> 7) & 1)
+    rows16 = lax.broadcasted_iota(jnp.int32, (16, CELLS), 0)
+
+    def select(share, folded):
+        for slot in range(SLOTS):
+            chosen = folded == line[slot : slot + 1]
+            part = jnp.where(chosen, share[slot : slot + 1], 0.0)
+            picked[:, slot * CELLS : (slot + 1) * CELLS] = part
     mask[...] = jnp.concatenate([flat(land[s]) for s in range(2)], axis=0).astype(F32)
     pad = jnp.zeros((1, 512 - 80), F32)
     bias = jnp.where(is_air(), bias_a[...], jnp.concatenate([bias_o[...]] * 2, axis=1))
@@ -149,7 +160,7 @@
         for copy in copies[:2]:
             copy.wait()
         weights(first_a, second_a, first_a.shape[1])
-        share[...] = table / jnp.sum(table, axis=0, keepdims=True)
+        select(table / jnp.sum(table, axis=0, keepdims=True), rows16)
 
     @pl.when(is_sea())
     def _():
@@ -159,7 +170,7 @@
         upper = jnp.sum(table[:4], axis=0, keepdims=True)
         lower = jnp.sum(table[4:], axis=0, keepdims=True)
         slot = lax.broadcasted_iota(jnp.int32, table.shape, 0)
-        share[...] = table / jnp.where(slot < 4, upper, lower)
+        select(table / jnp.where(slot < 4, upper, lower), rows16 & 11)
 
     lanes = lax.broadcasted_iota(jnp.int32, (128, CELLS), 0)
     for slot in range(SLOTS):
@@ -367,21 +378,22 @@
                 payload[place : place + 1, :] = line[:1, part * 128 : (part + 1) * 128]
 
 
-def couple_kernel(
-    y, near, far, hot, line, share, mask, columns, image, back_near, back_far
-):
+def couple_kernel(y, near, far, hot, picked, mask, columns, image, back_near, back_far):
     window = jnp.concatenate([near[...], far[...]], axis=0)
     parts = dot(split_parts(window), hot[...])
-    gathered = parts[:16] + parts[16:]
-    lines = lax.broadcasted_iota(jnp.int32, (16, CELLS), 0)
 
     def span(slot):
         return slice(slot * CELLS, (slot + 1) * CELLS)
 
-    def line_of(slot):
-        return line[slot : slot + 1, :]
-
-    def scatter(pieces):
+    def gather(slots):
+        total = None
+        for slot in slots:
+            chosen = (parts[:16, span(slot)] + parts[16:, span(slot)]) * picked[:, span(slot)]
+            total = chosen if total is None else total + chosen
+        return total[:8] + total[8:]
+
+    def scatter(values):
+        pieces = [picked[:, span(slot)] * values[slot // 4] for slot in range(SLOTS)]
         spread = split_parts(jnp.concatenate(pieces, axis=1))
         total = lax.dot_general(
             spread, hot[...], (((1,), (1,)), ((), ())), preferred_element_type=F32
@@ -390,53 +402,34 @@
         back_near[...] = total[:8]
         back_far[...] = total[8:]
 
-    def pick(slot, offset):
-        chosen = jnp.where(lines == line_of(slot) + offset, gathered[:, span(slot)], 0.0)
-        return share[slot : slot + 1, :] * jnp.sum(chosen, axis=0, keepdims=True)
-
     @pl.when(is_air())
     def _():
         aloft = columns[:80, 3:4]
-        lifted = pick(0, 0)
-        for slot in range(1, SLOTS):
-            lifted = lifted + pick(slot, 0)
+        lifted = jnp.sum(gather(range(SLOTS)), axis=0, keepdims=True)
         rounded = (y[:, :CELLS] + aloft * lifted).astype(BF16)
         image[...] = rounded
         surface = jnp.sum(aloft * rounded.astype(F32), axis=0, keepdims=True)
-        pieces = []
-        for slot in range(SLOTS):
-            value = share[slot : slot + 1, :] * surface
-            pieces.append(jnp.where(lines == line_of(slot), value, 0.0))
-        scatter(pieces)
+        scatter([surface, surface])
 
     @pl.when(is_sea())
     def _():
         forcing_weight = columns[:40, 4:6]
+        fields = (lax.broadcasted_iota(jnp.int32, (16, CELLS), 0) & 4) == 0
         halves = []
         pulled = []
         for half in range(2):
-            forcing = []
-            for f in range(2):
-                total = pick(4 * half, 4 * f)
-                for k in range(1, 4):
-                    total = total + pick(4 * half + k, 4 * f)
-                forcing.append(total)
+            folded = gather(range(4 * half, 4 * half + 4))
+            forcing = [jnp.sum(folded[4 * f : 4 * f + 4], axis=0, keepdims=True) for f in range(2)]
             added = forcing_weight[:, :1] * forcing[0] + forcing_weight[:, 1:] * forcing[1]
             fine = mask[half : half + 1, :] * (y[:40, span(half)] + added)
             rounded = fine.astype(BF16).astype(F32)
             halves.append(rounded)
-            pulled.append(
-                [jnp.sum(forcing_weight[:, f : f + 1] * rounded, axis=0, keepdims=True) for f in range(2)]
-            )
+            first, other = [
+                jnp.sum(forcing_weight[:, f : f + 1] * rounded, axis=0, keepdims=True) for f in range(2)
+            ]
+            pulled.append(jnp.where(fields, first, other))
         image[...] = jnp.concatenate(halves, axis=0).astype(BF16)
-        pieces = []
-        for slot in range(SLOTS):
-            lead = line_of(slot)
-            part = share[slot : slot + 1, :]
-            first = jnp.where(lines == lead, part * pulled[slot // 4][0], 0.0)
-            other = jnp.where(lines == lead + 4, part * pulled[slot // 4][1], 0.0)
-            pieces.append(first + other)
-        scatter(pieces)
+        scatter(pulled)
 
 
 def cotangent_kernel(image, near, far, columns, cotangent):
@@ -455,7 +448,11 @@
 
 
 def spread_rows(target, rows):
-    target[0] = jnp.stack(rows, axis=1).astype(BF16)
+    line = lax.broadcasted_iota(jnp.int32, (160, 160), 0)
+    place = lane_iota((160, 160))
+    order = jnp.where(place == (line & 1) * 80 + (line >> 1), 1.0, 0.0).astype(BF16)
+    stacked = jnp.concatenate(rows, axis=0).astype(BF16)
+    target[0] = dot(order, stacked).astype(BF16).reshape(80, ROWS, COLS)
 
 
 def unpack_kernel(packed, image):
@@ -612,12 +609,12 @@
         aloft_reaction_to_seawarmth.reshape(1, 80),
         sea_forcing.T,
     ]
-    fwd1, fwd2, bwd1, bwd2, hot, share, line, mask, columns = call(
+    fwd1, fwd2, bwd1, bwd2, hot, picked, mask, columns = call(
         prepare_kernel,
         "prepare",
         [
             ((512, 720), BF16), ((240, 1536), BF16), ((512, 720), BF16), ((240, 1536), BF16),
-            ((128, SLOTS * CELLS), BF16), ((SLOTS, CELLS), F32), ((SLOTS, CELLS), jnp.int32),
+            ((128, SLOTS * CELLS), BF16), ((16, SLOTS * CELLS), F32),
             ((2, CELLS), F32), ((512, 8), F32),
         ],
         raw,
@@ -649,7 +646,7 @@
         couple_kernel,
         "couple",
         [((80, CELLS), BF16), ((8, 128), F32), ((8, 128), F32)],
-        [y, near, far, hot, line, share, mask, columns],
+        [y, near, far, hot, picked, mask, columns],
     )
     back_near, back_far = across(back_near, back_far, 1)
     (result,) = call(unpack_kernel, "unpack", [((1, 80, ROWS, COLS), BF16)], [image])

time: 52 us -> 51.8 us (level)
  no operation moved by 1% of the time
where the time goes in v5:
time: 51.8 us; the launch traced here: 51.6 us
  waiting for transfers between devices  21 us (41%)
  starting transfers between devices  17.4 us (34%)
  Pallas kernels  12.5 us (24%)
  between operations  0.73 us (1%)
    pallas_call x11, Pallas kernels, call(): pl.pallas_call(kernel, name=name, out_shape=tuple((jax.ShapeDtypeStruct(s...  12.5 us
    ppermute x2, waiting for transfers between devices, lon_pair(): lax.ppermute(to_right, 'lon', [(i, (i + 1) % count) for i in range(count)])  6.22 us
    ppermute x2, starting transfers between devices, lon_pair(): lax.ppermute(to_left, 'lon', [((i + 1) % count, i) for i in range(count)])  5.43 us
    ppermute x2, starting transfers between devices, lat_pair(): lax.ppermute(block, 'lat', [((i + 1) % count, i) for i in range(count)])  4.99 us
    ppermute x2, waiting for transfers between devices, across(): return (same, lax.ppermute(far, ('comp', 'lon'), route))  4.71 us
    ppermute x2, starting transfers between devices, across(): same = lax.ppermute(near, 'comp', [(0, 1), (1, 0)])  3.97 us
    ppermute x2, waiting for transfers between devices, lat_pair(): lax.ppermute(block, 'lat', [(i, (i + 1) % count) for i in range(count)])  3.92 us
    ppermute x2, waiting for transfers between devices, across(): same = lax.ppermute(near, 'comp', [(0, 1), (1, 0)])  3.48 us
  transfers between devices with their start and end apart: 12, of which 10 were waited for; matrix products, arithmetic and copies ran while one was open for 0% of the time, Pallas kernels for 14%

profile of v5, /device:TPU:8, one launch (start us, length us, event | category | flops | bytes accessed | tf_op | source)
XLA Modules:
  0.0 51.6 jit_solution(619596964614222707)
XLA Ops:
  0.6 1.3 %pack.1.own = bf16[160,512]{1,0:T(8,128)(2,1)S(1)} custom-call(bf16[1,80,2,256]{3,2,1,0:T(2,128)(2,1)} %state.1, bf16[1,80,2,256]{3,2,1,0:T(2,128)(2,1)} %direction.1), custom_call_target="tpu_custom_call" | custom-call | tf_op jit(solution)/shard_map/pack/pallas_call | solution.py:538
  1.9 2.2 %collective-permute-start.1 = (bf16[160,512]{1,0:T(8,128)(2,1)S(1)}, bf16[160,512]{1,0:T(8,128)(2,1)S(1)}, u32[]{:S(2)}, u32[]{:S(2)}) collective-permute-start(bf16[160,512]{1,0:T(8,128)(2,1)S(1)} %pack.1.own), channel_id=1, source_target_pairs={{32,0},{64,32},{96,64},{0,96},{33,1},{65,33},{97,65},{1,97},{34,2}... | collective-permute-start | bytes 491528 | tf_op jit(solution)/shard_map/ppermute | solution.py:552
  4.1 0.0 collective-permute-start
  4.2 2.3 %prepare.1 = (bf16[512,720]{1,0:T(8,128)(2,1)S(1)}, bf16[240,1536]{1,0:T(8,128)(2,1)S(1)}, bf16[512,720]{1,0:T(8,128)(2,1)S(1)}, bf16[240,1536]{1,0:T(8,128)(2,1...) custom-call(bf16[9,80,512]{2,1,0:T(8,128)(2,1)} %bitcast.6, ...), custom_call_target="tpu_custom_call" | custom-call | tf_op jit(solution)/shard_map/prepare/pallas_call | solution.py:538
  6.5 1.4 %collective-permute-done.1.below = bf16[160,512]{1,0:T(8,128)(2,1)S(1)} collective-permute-done((bf16[160,512]{1,0:T(8,128)(2,1)S(1)}, bf16[160,512]{1,0:T(8,128)(2,1)S(1)}, u32[]{:S(2)}, u32[]{:S(2)}) %collective-permute-start.1) | collective-permute-done | bytes 163872 | tf_op jit(solution)/shard_map/ppermute | solution.py:552
  7.9 1.5 %collective-permute-done.above = bf16[160,512]{1,0:T(8,128)(2,1)S(1)} collective-permute-done((bf16[160,512]{1,0:T(8,128)(2,1)S(1)}, bf16[160,512]{1,0:T(8,128)(2,1)S(1)}, u32[]{:S(2)}, u32[]{:S(2)}) %collective-permute-start) | collective-permute-done | bytes 163872 | tf_op jit(solution)/shard_map/ppermute | solution.py:551
  9.5 0.2 edges.1
  9.7 5.4 %collective-permute-start.3 = (bf16[80,128]{1,0:T(8,128)(2,1)S(1)}, bf16[80,128]{1,0:T(8,128)(2,1)S(1)}, u32[]{:S(2)}, u32[]{:S(2)}) collective-permute-start(bf16[80,128]{1,0:T(8,128)(2,1)S(1)} %get-tuple-element.26.to_left), channel_id=1, source_target_pairs={{1,0},{2,1},{3,2},{4,3},{5,4},{6,5},{7,6},{8,7},{9,8},{10,9},{11,1... | collective-permute-start | bytes 61448 | tf_op jit(solution)/shard_map/ppermute | solution.py:559
  15.0 0.0 collective-permute-start.2
  15.0 2.4 %tangent_main.1 = (f32[80,1024]{1,0:T(8,128)S(1)}, bf16[512,1536]{1,0:T(8,128)(2,1)S(1)}, f32[2,80,128]{2,1,0:T(8,128)S(1)}) custom-call(bf16[160,512]{1,0:T(8,128)(2,1)S(1)} %pack.1.own, bf16[160,512]{1,0:T(8,128)(2,1)S(1)} %collective-permute-done.above, bf16[160,512]{1,0:T(8,128)(2,1)S(1)} %collective-permute-done.1.below, ...), custom_call_target="tpu_custom_call" | custom-call | tf_op jit(solution)/shard_map/tangent_main/pallas_call | solution.py:538
  17.4 0.0 collective-permute-done.3.from_right
  17.4 2.9 %collective-permute-done.2.from_left = bf16[80,128]{1,0:T(8,128)(2,1)S(1)} collective-permute-done((bf16[80,128]{1,0:T(8,128)(2,1)S(1)}, bf16[80,128]{1,0:T(8,128)(2,1)S(1)}, u32[]{:S(2)}, u32[]{:S(2)}) %collective-permute-start.2) | collective-permute-done | bytes 20512 | tf_op jit(solution)/shard_map/ppermute | solution.py:558
  20.3 1.1 %tangent_edge.1 = (f32[80,1024]{1,0:T(8,128)S(1)}, bf16[512,128]{1,0:T(8,128)(2,1)S(1)}, f32[8,128]{1,0:T(8,128)S(1)}) custom-call(bf16[160,512]{1,0:T(8,128)(2,1)S(1)} %pack.1.own, f32[2,80,128]{2,1,0:T(8,128)S(1)} %get-tuple-element.30.sides, bf16[80,128]{1,0:T(8,128)(2,1)S(1)} %collective-permute-done.2.from_left, ...), custom_call_target="tpu_custom_call" | custom-call | tf_op jit(solution)/shard_map/tangent_edge/pallas_call | solution.py:538
  21.5 1.1 %collective-permute-start.5 = (f32[8,128]{1,0:T(8,128)S(1)}, f32[8,128]{1,0:T(8,128)S(1)}, u32[]{:S(2)}, u32[]{:S(2)}) collective-permute-start(f32[8,128]{1,0:T(8,128)S(1)} %get-tuple-element.33), channel_id=1, source_target_pairs={{0,159},{1,128},{2,129},{3,130},{4,131},{5,132},{6,133},{7,134},{8... | collective-permute-start | bytes 12296 | tf_op jit(solution)/shard_map/ppermute | solution.py:570
  22.6 2.0 %collective-permute-start.4 = (f32[8,128]{1,0:T(8,128)S(1)}, f32[8,128]{1,0:T(8,128)S(1)}, u32[]{:S(2)}, u32[]{:S(2)}) collective-permute-start(f32[8,128]{1,0:T(8,128)S(1)} %get-tuple-element.33), channel_id=1, source_target_pairs={{0,128},{128,0},{1,129},{129,1},{2,130},{130,2},{3,131},{131,3},{4... | collective-permute-start | bytes 12296 | tf_op jit(solution)/shard_map/ppermute | solution.py:565
  24.6 1.5 %collective-permute-done.5.far = f32[8,128]{1,0:T(8,128)S(1)} collective-permute-done((f32[8,128]{1,0:T(8,128)S(1)}, f32[8,128]{1,0:T(8,128)S(1)}, u32[]{:S(2)}, u32[]{:S(2)}) %collective-permute-start.5) | collective-permute-done | bytes 4128 | tf_op jit(solution)/shard_map/ppermute | solution.py:570
  26.1 1.6 %collective-permute-done.4.near = f32[8,128]{1,0:T(8,128)S(1)} collective-permute-done((f32[8,128]{1,0:T(8,128)S(1)}, f32[8,128]{1,0:T(8,128)S(1)}, u32[]{:S(2)}, u32[]{:S(2)}) %collective-permute-start.4) | collective-permute-done | bytes 4128 | tf_op jit(solution)/shard_map/ppermute | solution.py:565
  27.7 0.8 %couple.1 = (bf16[80,512]{1,0:T(8,128)(2,1)S(1)}, f32[8,128]{1,0:T(8,128)S(1)}, f32[8,128]{1,0:T(8,128)S(1)}) custom-call(f32[80,1024]{1,0:T(8,128)S(1)} %get-tuple-element.32.y, f32[8,128]{1,0:T(8,128)S(1)} %collective-permute-done.4.near, f32[8,128]{1,0:T(8,128)S(1)} %collective-permute-done.5.far, bf16[128,4096]{1,0:T(8,128)(2,1)S(1)} %get-tuple-element.34.hot, ...), custom_call_target="tpu_custom_call" | custom-call | tf_op jit(solution)/shard_map/couple/pallas_call | solution.py:538
  28.5 2.0 %collective-permute-start.6 = (f32[8,128]{1,0:T(8,128)S(1)}, f32[8,128]{1,0:T(8,128)S(1)}, u32[]{:S(2)}, u32[]{:S(2)}) collective-permute-start(f32[8,128]{1,0:T(8,128)S(1)} %get-tuple-element.38), channel_id=1, source_target_pairs={{0,128},{128,0},{1,129},{129,1},{2,130},{130,2},{3,131},{131,3},{4... | collective-permute-start | bytes 12296 | tf_op jit(solution)/shard_map/ppermute | solution.py:565
  30.5 1.3 %collective-permute-start.7 = (f32[8,128]{1,0:T(8,128)S(1)}, f32[8,128]{1,0:T(8,128)S(1)}, u32[]{:S(2)}, u32[]{:S(2)}) collective-permute-start(f32[8,128]{1,0:T(8,128)S(1)} %get-tuple-element.39), channel_id=1, source_target_pairs={{0,129},{1,130},{2,131},{3,132},{4,133},{5,134},{6,135},{7,136},{8... | collective-permute-start | bytes 12296 | tf_op jit(solution)/shard_map/ppermute | solution.py:570
  31.8 1.8 %collective-permute-done.6.near = f32[8,128]{1,0:T(8,128)S(1)} collective-permute-done((f32[8,128]{1,0:T(8,128)S(1)}, f32[8,128]{1,0:T(8,128)S(1)}, u32[]{:S(2)}, u32[]{:S(2)}) %collective-permute-start.6) | collective-permute-done | bytes 4128 | tf_op jit(solution)/shard_map/ppermute | solution.py:565
  33.6 3.2 %collective-permute-done.7.far = f32[8,128]{1,0:T(8,128)S(1)} collective-permute-done((f32[8,128]{1,0:T(8,128)S(1)}, f32[8,128]{1,0:T(8,128)S(1)}, u32[]{:S(2)}, u32[]{:S(2)}) %collective-permute-start.7) | collective-permute-done | bytes 4128 | tf_op jit(solution)/shard_map/ppermute | solution.py:570
  36.9 0.1 cotangent.1.own
  37.0 2.8 %collective-permute-start.9 = (bf16[80,512]{1,0:T(8,128)(2,1)S(1)}, bf16[80,512]{1,0:T(8,128)(2,1)S(1)}, u32[]{:S(2)}, u32[]{:S(2)}) collective-permute-start(bf16[80,512]{1,0:T(8,128)(2,1)S(1)} %cotangent.1.own), channel_id=1, source_target_pairs={{32,0},{64,32},{96,64},{0,96},{33,1},{65,33},{97,65},{1,97},{34,2}... | collective-permute-start | bytes 245768 | tf_op jit(solution)/shard_map/ppermute | solution.py:552
  39.7 0.0 collective-permute-start.8
  39.7 0.8 %unpack.1.after = bf16[1,80,2,256]{3,2,1,0:T(2,128)(2,1)} custom-call(bf16[80,512]{1,0:T(8,128)(2,1)S(1)} %get-tuple-element.37.packed.image), custom_call_target="tpu_custom_call" | custom-call | tf_op jit(solution)/shard_map/unpack/pallas_call | solution.py:538
  40.5 1.3 %collective-permute-done.9.below = bf16[80,512]{1,0:T(8,128)(2,1)S(1)} collective-permute-done((bf16[80,512]{1,0:T(8,128)(2,1)S(1)}, bf16[80,512]{1,0:T(8,128)(2,1)S(1)}, u32[]{:S(2)}, u32[]{:S(2)}) %collective-permute-start.9) | collective-permute-done | bytes 81952 | tf_op jit(solution)/shard_map/ppermute | solution.py:552
  41.8 2.4 %collective-permute-done.8.above = bf16[80,512]{1,0:T(8,128)(2,1)S(1)} collective-permute-done((bf16[80,512]{1,0:T(8,128)(2,1)S(1)}, bf16[80,512]{1,0:T(8,128)(2,1)S(1)}, u32[]{:S(2)}, u32[]{:S(2)}) %collective-permute-start.8) | collective-permute-done | bytes 81952 | tf_op jit(solution)/shard_map/ppermute | solution.py:551
  44.2 0.1 edges_back.1
  44.3 0.1 collective-permute-start.11
  44.4 0.5 collective-permute-start.10
  44.9 1.6 %adjoint_main.1 = (f32[80,1024]{1,0:T(8,128)S(1)}, f32[2,80,128]{2,1,0:T(8,128)S(1)}) custom-call(bf16[80,512]{1,0:T(8,128)(2,1)S(1)} %cotangent.1.own, bf16[80,512]{1,0:T(8,128)(2,1)S(1)} %collective-permute-done.8.above, bf16[80,512]{1,0:T(8,128)(2,1)S(1)} %collective-permute-done.9.below, bf16[80,128]{1,0:T(8,128)(2,1)S(1)} %get-tuple-element.40.to_left, ...), custom_call_target="tpu_custom_call" | custom-call | tf_op jit(solution)/shard_map/adjoint_main/pallas_call | solution.py:538
  46.5 0.0 collective-permute-done.11.from_right
  46.5 3.3 %collective-permute-done.10.from_left = bf16[80,128]{1,0:T(8,128)(2,1)S(1)} collective-permute-done((bf16[80,128]{1,0:T(8,128)(2,1)S(1)}, bf16[80,128]{1,0:T(8,128)(2,1)S(1)}, u32[]{:S(2)}, u32[]{:S(2)}) %collective-permute-start.10) | collective-permute-done | bytes 20512 | tf_op jit(solution)/shard_map/ppermute | solution.py:558
  49.8 1.8 %adjoint_edge.1 = bf16[1,80,2,256]{3,2,1,0:T(2,128)(2,1)} custom-call(f32[2,80,128]{2,1,0:T(8,128)S(1)} %get-tuple-element.45.sides, bf16[80,128]{1,0:T(8,128)(2,1)S(1)} %collective-permute-done.10.from_left, bf16[80,128]{1,0:T(8,128)(2,1)S(1)} %collective-permute-done.11.from_right, f32[80,1024]{1,0:T(8,128)S(1)} %get-tuple-element.46.inner, ...), custom_call_target="tpu_custom_call" | custom-call | tf_op jit(solution)/shard_map/adjoint_edge/pallas_call | solution.py:538
Async XLA Ops:
  1.9 6.0 %collective-permute-start.1 = (bf16[160,512]{1,0:T(8,128)(2,1)S(1)}, bf16[160,512]{1,0:T(8,128)(2,1)S(1)}, u32[]{:S(2)}, u32[]{:S(2)}) collective-permute-start(bf16[160,512]{1,0:T(8,128)(2,1)S(1)} %pack.1.own), channel_id=1, source_target_pairs={{32,0},{64,32},{96,64},{0,96},{33,1},{65,33},{97,65},{1,97},{34,2}... | collective-permute-start | bytes 491528 | tf_op jit(solution)/shard_map/ppermute | solution.py:552
  4.1 5.3 %collective-permute-start = (bf16[160,512]{1,0:T(8,128)(2,1)S(1)}, bf16[160,512]{1,0:T(8,128)(2,1)S(1)}, u32[]{:S(2)}, u32[]{:S(2)}) collective-permute-start(bf16[160,512]{1,0:T(8,128)(2,1)S(1)} %pack.1.own), channel_id=1, source_target_pairs={{0,32},{32,64},{64,96},{96,0},{1,33},{33,65},{65,97},{97,1},{2,34}... | collective-permute-start | bytes 491528 | tf_op jit(solution)/shard_map/ppermute | solution.py:551
  9.7 7.8 %collective-permute-start.3 = (bf16[80,128]{1,0:T(8,128)(2,1)S(1)}, bf16[80,128]{1,0:T(8,128)(2,1)S(1)}, u32[]{:S(2)}, u32[]{:S(2)}) collective-permute-start(bf16[80,128]{1,0:T(8,128)(2,1)S(1)} %get-tuple-element.26.to_left), channel_id=1, source_target_pairs={{1,0},{2,1},{3,2},{4,3},{5,4},{6,5},{7,6},{8,7},{9,8},{10,9},{11,1... | collective-permute-start | bytes 61448 | tf_op jit(solution)/shard_map/ppermute | solution.py:559
  15.0 5.3 %collective-permute-start.2 = (bf16[80,128]{1,0:T(8,128)(2,1)S(1)}, bf16[80,128]{1,0:T(8,128)(2,1)S(1)}, u32[]{:S(2)}, u32[]{:S(2)}) collective-permute-start(bf16[80,128]{1,0:T(8,128)(2,1)S(1)} %get-tuple-element.27.to_right), channel_id=1, source_target_pairs={{0,1},{1,2},{2,3},{3,4},{4,5},{5,6},{6,7},{7,8},{8,9},{9,10},{10,1... | collective-permute-start | bytes 61448 | tf_op jit(solution)/shard_map/ppermute | solution.py:558
  21.5 4.6 %collective-permute-start.5 = (f32[8,128]{1,0:T(8,128)S(1)}, f32[8,128]{1,0:T(8,128)S(1)}, u32[]{:S(2)}, u32[]{:S(2)}) collective-permute-start(f32[8,128]{1,0:T(8,128)S(1)} %get-tuple-element.33), channel_id=1, source_target_pairs={{0,159},{1,128},{2,129},{3,130},{4,131},{5,132},{6,133},{7,134},{8... | collective-permute-start | bytes 12296 | tf_op jit(solution)/shard_map/ppermute | solution.py:570
  22.6 5.1 %collective-permute-start.4 = (f32[8,128]{1,0:T(8,128)S(1)}, f32[8,128]{1,0:T(8,128)S(1)}, u32[]{:S(2)}, u32[]{:S(2)}) collective-permute-start(f32[8,128]{1,0:T(8,128)S(1)} %get-tuple-element.33), channel_id=1, source_target_pairs={{0,128},{128,0},{1,129},{129,1},{2,130},{130,2},{3,131},{131,3},{4... | collective-permute-start | bytes 12296 | tf_op jit(solution)/shard_map/ppermute | solution.py:565
  28.5 5.1 %collective-permute-start.6 = (f32[8,128]{1,0:T(8,128)S(1)}, f32[8,128]{1,0:T(8,128)S(1)}, u32[]{:S(2)}, u32[]{:S(2)}) collective-permute-start(f32[8,128]{1,0:T(8,128)S(1)} %get-tuple-element.38), channel_id=1, source_target_pairs={{0,128},{128,0},{1,129},{129,1},{2,130},{130,2},{3,131},{131,3},{4... | collective-permute-start | bytes 12296 | tf_op jit(solution)/shard_map/ppermute | solution.py:565
  30.5 6.4 %collective-permute-start.7 = (f32[8,128]{1,0:T(8,128)S(1)}, f32[8,128]{1,0:T(8,128)S(1)}, u32[]{:S(2)}, u32[]{:S(2)}) collective-permute-start(f32[8,128]{1,0:T(8,128)S(1)} %get-tuple-element.39), channel_id=1, source_target_pairs={{0,129},{1,130},{2,131},{3,132},{4,133},{5,134},{6,135},{7,136},{8... | collective-permute-start | bytes 12296 | tf_op jit(solution)/shard_map/ppermute | solution.py:570
  37.0 4.8 %collective-permute-start.9 = (bf16[80,512]{1,0:T(8,128)(2,1)S(1)}, bf16[80,512]{1,0:T(8,128)(2,1)S(1)}, u32[]{:S(2)}, u32[]{:S(2)}) collective-permute-start(bf16[80,512]{1,0:T(8,128)(2,1)S(1)} %cotangent.1.own), channel_id=1, source_target_pairs={{32,0},{64,32},{96,64},{0,96},{33,1},{65,33},{97,65},{1,97},{34,2}... | collective-permute-start | bytes 245768 | tf_op jit(solution)/shard_map/ppermute | solution.py:552
  39.7 4.4 %collective-permute-start.8 = (bf16[80,512]{1,0:T(8,128)(2,1)S(1)}, bf16[80,512]{1,0:T(8,128)(2,1)S(1)}, u32[]{:S(2)}, u32[]{:S(2)}) collective-permute-start(bf16[80,512]{1,0:T(8,128)(2,1)S(1)} %cotangent.1.own), channel_id=1, source_target_pairs={{0,32},{32,64},{64,96},{96,0},{1,33},{33,65},{65,97},{97,1},{2,34}... | collective-permute-start | bytes 245768 | tf_op jit(solution)/shard_map/ppermute | solution.py:551
  44.3 2.2 %collective-permute-start.11 = (bf16[80,128]{1,0:T(8,128)(2,1)S(1)}, bf16[80,128]{1,0:T(8,128)(2,1)S(1)}, u32[]{:S(2)}, u32[]{:S(2)}) collective-permute-start(bf16[80,128]{1,0:T(8,128)(2,1)S(1)} %get-tuple-element.40.to_left), channel_id=1, source_target_pairs={{1,0},{2,1},{3,2},{4,3},{5,4},{6,5},{7,6},{8,7},{9,8},{10,9},{11,1... | collective-permute-start | bytes 61448 | tf_op jit(solution)/shard_map/ppermute | solution.py:559
  44.4 5.4 %collective-permute-start.10 = (bf16[80,128]{1,0:T(8,128)(2,1)S(1)}, bf16[80,128]{1,0:T(8,128)(2,1)S(1)}, u32[]{:S(2)}, u32[]{:S(2)}) collective-permute-start(bf16[80,128]{1,0:T(8,128)(2,1)S(1)} %get-tuple-element.41.to_right), channel_id=1, source_target_pairs={{0,1},{1,2},{2,3},{3,4},{4,5},{5,6},{6,7},{7,8},{8,9},{9,10},{10,1... | collective-permute-start | bytes 61448 | tf_op jit(solution)/shard_map/ppermute | solution.py:558

commit v6 on v5

--- a/solution.py
+++ b/solution.py
@@ -60,7 +60,7 @@
     return chosen
 
 
-def pack_kernel(state, direction, packed, rows, sems):
+def pack_kernel(state, direction, packed, edge, rows, sems):
     copies = []
     for field, ref in enumerate((state, direction)):
         copies.append(pltpu.make_async_copy(ref.at[0], rows.at[field], sems.at[field]))
@@ -74,78 +74,76 @@
         block = dot(order, rows[field].reshape(160, COLS)).astype(BF16)
         for r in range(ROWS):
             packed[field * 80 : field * 80 + 80, r * COLS : (r + 1) * COLS] = block[r * 80 : (r + 1) * 80]
-
-
-def prepare_kernel(*refs):
-    sources = refs[:12]
-    fwd1, fwd2, bwd1, bwd2, hot, picked, mask, columns = refs[12:20]
-    held = refs[20:32]
-    sems = refs[32]
-    copies = [
+    edge[...] = own_edges(packed, 2)
+
+
+def load_all(copies):
+    for copy in copies[4:]:
+        copy.start()
+
+    @pl.when(is_air())
+    def _():
+        for copy in copies[:2]:
+            copy.start()
+
+    @pl.when(is_sea())
+    def _():
+        for copy in copies[2:4]:
+            copy.start()
+
+    for copy in copies[4:]:
+        copy.wait()
+
+
+def make_weights(to, back, flip, to_target, back_target):
+    channels = to.shape[1]
+    padded = -(-3 * channels // 16) * 16
+    hidden = to.shape[2]
+    pieces = []
+    for a in range(3):
+        for e in range(3):
+            tap = 3 * a + e
+            pieces.append(to[8 - tap if flip else tap].astype(F32))
+        if padded > 3 * channels:
+            pieces.append(jnp.zeros((padded - 3 * channels, hidden), F32))
+    stacked = jnp.concatenate(pieces, axis=0)
+    to_target[:hidden, : 3 * padded] = stacked.T.astype(BF16)
+    for a in range(3):
+        pieces = []
+        for e in range(3):
+            tap = 3 * a + e
+            pieces.append(back[8 - tap if flip else tap].astype(F32))
+        stacked = jnp.concatenate(pieces, axis=0)
+        back_target[: 3 * channels, a * hidden : (a + 1) * hidden] = stacked.astype(BF16)
+
+
+def both_weights(copies, held, flip, to_target, back_target):
+    @pl.when(is_air())
+    def _():
+        for copy in copies[:2]:
+            copy.wait()
+        make_weights(held[0], held[1], flip, to_target, back_target)
+
+    @pl.when(is_sea())
+    def _():
+        for copy in copies[2:4]:
+            copy.wait()
+        make_weights(held[2], held[3], flip, to_target, back_target)
+
+
+def copies_of(sources, held, sems):
+    return [
         pltpu.make_async_copy(source, target, sems.at[i])
         for i, (source, target) in enumerate(zip(sources, held))
     ]
-    first_a, second_a, first_o, second_o, index, weight, land, bias_a, bias_o, flux, aloft, forcing = held
-    for copy in copies[4:]:
-        copy.start()
-
-    @pl.when(is_air())
-    def _():
-        for copy in copies[:2]:
-            copy.start()
-
-    @pl.when(is_sea())
-    def _():
-        for copy in copies[2:4]:
-            copy.start()
-
-    for copy in copies[4:]:
-        copy.wait()
-
-    def flat(rows):
-        return jnp.concatenate([rows[r : r + 1] for r in range(ROWS)], axis=1)
-
-    def weights(first, second, channels):
-        padded = -(-3 * channels // 16) * 16
-        hidden = first.shape[2]
-        fill = jnp.zeros((padded - 3 * channels, hidden), F32)
-
-        def to_hidden(source, flip, target):
-            pieces = []
-            for a in range(3):
-                for e in range(3):
-                    tap = 3 * a + e
-                    pieces.append(source[8 - tap if flip else tap].astype(F32))
-                if padded > 3 * channels:
-                    pieces.append(fill)
-            stacked = jnp.concatenate(pieces, axis=0)
-            target[:hidden, : 3 * padded] = stacked.T.astype(BF16)
-
-        def from_hidden(source, flip, target):
-            for a in range(3):
-                pieces = []
-                for e in range(3):
-                    tap = 3 * a + e
-                    pieces.append(source[8 - tap if flip else tap].astype(F32))
-                stacked = jnp.concatenate(pieces, axis=0)
-                target[: 3 * channels, a * hidden : (a + 1) * hidden] = stacked.astype(BF16)
-
-        to_hidden(first, False, fwd1)
-        from_hidden(second, False, fwd2)
-        to_hidden(second, True, bwd1)
-        from_hidden(first, True, bwd2)
-
-    table = jnp.concatenate([flat(weight[0, s]) for s in range(SLOTS)], axis=0).astype(F32)
-    place = jnp.concatenate([flat(index[0, s]) for s in range(SLOTS)], axis=0)
-    line = ((place >> 8) & 1) * 8 + (place >> 9) * 2 + ((place >> 7) & 1)
-    rows16 = lax.broadcasted_iota(jnp.int32, (16, CELLS), 0)
-
-    def select(share, folded):
-        for slot in range(SLOTS):
-            chosen = folded == line[slot : slot + 1]
-            part = jnp.where(chosen, share[slot : slot + 1], 0.0)
-            picked[:, slot * CELLS : (slot + 1) * CELLS] = part
-    mask[...] = jnp.concatenate([flat(land[s]) for s in range(2)], axis=0).astype(F32)
+
+
+def forward_kernel(*refs):
+    fwd1, fwd2, columns = refs[10:13]
+    held = refs[13:22]
+    copies = copies_of(refs[:9], held, refs[22])
+    load_all(copies)
+    bias_a, bias_o, flux, aloft, forcing = held[4:]
     pad = jnp.zeros((1, 512 - 80), F32)
     bias = jnp.where(is_air(), bias_a[...], jnp.concatenate([bias_o[...]] * 2, axis=1))
     rows = [bias] + [jnp.concatenate([flux[f : f + 1, :].astype(F32), pad], axis=1) for f in range(2)]
@@ -154,45 +152,58 @@
     rows += [jnp.concatenate([forcing[f : f + 1, :].astype(F32), pad], axis=1) for f in range(2)]
     rows.append(jnp.zeros((2, 512), F32))
     columns[...] = jnp.concatenate(rows, axis=0).T
-
-    @pl.when(is_air())
-    def _():
-        for copy in copies[:2]:
-            copy.wait()
-        weights(first_a, second_a, first_a.shape[1])
-        select(table / jnp.sum(table, axis=0, keepdims=True), rows16)
-
-    @pl.when(is_sea())
-    def _():
-        for copy in copies[2:4]:
-            copy.wait()
-        weights(first_o, second_o, first_o.shape[1])
-        upper = jnp.sum(table[:4], axis=0, keepdims=True)
-        lower = jnp.sum(table[4:], axis=0, keepdims=True)
-        slot = lax.broadcasted_iota(jnp.int32, table.shape, 0)
-        select(table / jnp.where(slot < 4, upper, lower), rows16 & 11)
-
+    both_weights(copies, held, False, fwd1, fwd2)
+
+
+def backward_kernel(*refs):
+    bwd1, bwd2, hot, picked, mask = refs[8:13]
+    held = refs[13:20]
+    copies = copies_of(refs[:7], held, refs[20])
+    load_all(copies)
+    index, weight, land = held[4:]
+
+    def flat(rows):
+        return jnp.concatenate([rows[r : r + 1] for r in range(ROWS)], axis=1)
+
+    table = jnp.concatenate([flat(weight[0, s]) for s in range(SLOTS)], axis=0).astype(F32)
+    place = jnp.concatenate([flat(index[0, s]) for s in range(SLOTS)], axis=0)
+    line = ((place >> 8) & 1) * 8 + (place >> 9) * 2 + ((place >> 7) & 1)
+    rows16 = lax.broadcasted_iota(jnp.int32, (16, CELLS), 0)
+    mask[...] = jnp.concatenate([flat(land[s]) for s in range(2)], axis=0).astype(F32)
+    whole = jnp.sum(table, axis=0, keepdims=True)
+    upper = jnp.sum(table[:4], axis=0, keepdims=True)
+    slot_row = lax.broadcasted_iota(jnp.int32, table.shape, 0)
+    grouped = jnp.where(slot_row < 4, upper, whole - upper)
+    share = table / jnp.where(is_air(), whole, grouped)
+    folded = jnp.where(is_air(), rows16, rows16 & 11)
     lanes = lax.broadcasted_iota(jnp.int32, (128, CELLS), 0)
     for slot in range(SLOTS):
+        span = slice(slot * CELLS, (slot + 1) * CELLS)
+        picked[:, span] = jnp.where(folded == line[slot : slot + 1], share[slot : slot + 1], 0.0)
         low = place[slot : slot + 1, :] & 127
-        hot[:, slot * CELLS : (slot + 1) * CELLS] = jnp.where(lanes == low, 1.0, 0.0).astype(BF16)
-
-
-def edge_kernel(own, above, below, after, to_left, to_right):
+        hot[:, span] = jnp.where(lanes == low, 1.0, 0.0).astype(BF16)
+    both_weights(copies, held, True, bwd1, bwd2)
+
+
+def own_edges(rows, fields):
     lanes = lane_iota((80, 128)) >> 1
-    left = jnp.zeros((80, 128), F32)
-    right = jnp.zeros((80, 128), F32)
-    for field in range(own.shape[0] // 80):
+    result = jnp.zeros((80, 128), F32)
+    for field in range(fields):
         part = slice(field * 80, (field + 1) * 80)
-        for place, (read, r) in enumerate(sources(own, above, below)):
-            shift = 64 * field + 4 * place + 2
-            initial = pltpu.roll(read(part, 0, 128), shift, 1)
-            last = pltpu.roll(read(part, 128, COLS), shift, 1)
-            pair = 32 * field + 2 * place
-            left = jnp.where(lanes == pair + 1, initial, left)
-            right = jnp.where(lanes == pair, last, right)
-    to_left[...] = left.astype(BF16)
-    to_right[...] = right.astype(BF16)
+        for r in range(ROWS):
+            shift = 64 * field + 4 * (ROWS + r) + 2
+            initial = rows[part, r * COLS : r * COLS + 128].astype(F32)
+            last = rows[part, r * COLS + 128 : (r + 1) * COLS].astype(F32)
+            result = jnp.where(lanes == shift // 2, pltpu.roll(initial, shift, 1), result)
+            result = jnp.where(lanes == shift // 2 - 1, pltpu.roll(last, shift, 1), result)
+    return result.astype(BF16)
+
+
+def edge_kernel(own, above, below, merged):
+    upper = jnp.where(at_top(), 0.0, 1.0).astype(F32)
+    lower = jnp.where(at_bottom(), 0.0, 1.0).astype(F32)
+    total = own[...].astype(F32) + pltpu.roll(above[...].astype(F32), 120, 1) * upper
+    merged[...] = (total + pltpu.roll(below[...].astype(F32), 8, 1) * lower).astype(BF16)
 
 
 def shifted_rows(main, fill):
@@ -244,20 +255,24 @@
     return jnp.where(lanes == 3, pltpu.roll(upper, 8, 1), result)
 
 
-def own_sides(to_left, to_right, sides, fine):
-    for i, (ref, shift) in enumerate(((to_right, 2), (to_left, 126))):
-        rows = pltpu.roll(ref[...].astype(F32), shift, 1)
+def own_sides(edges, sides, fine):
+    rows = edges[...].astype(F32)
+    for i, shift in enumerate((2, 126)):
+        side = pltpu.roll(rows, shift, 1)
         if fine:
-            sides[i, :40, :] = fine_lanes(rows)
+            sides[i, :40, :] = fine_lanes(side)
         else:
-            sides[i] = rows
+            sides[i] = side
 
 
 def edge_stack(sides, from_left, from_right, fine):
     both = []
     for i, ref in enumerate((from_left, from_right)):
         rows = ref[...].astype(F32)
-        both.append(fine_lanes(rows) + sides[i, :40, :] if fine else rows + sides[i])
+        rows = fine_lanes(rows) if fine else rows
+        side = sides[i, :40, :] if fine else sides[i]
+        head = (lane_iota(rows.shape) & 3) < 2
+        both.append(jnp.where(head, rows, side) if i == 0 else jnp.where(head, side, rows))
     before, after = both
     even = (lane_iota(before.shape) & 1) == 0
     middle = jnp.where(even, pltpu.roll(before, 127, 1), pltpu.roll(after, 1, 1))
@@ -308,7 +323,7 @@
 
 
 def tangent_main_kernel(
-    own, above, below, to_left, to_right, fwd1, fwd2, columns, inner, slope, sides, stack, hidden
+    own, above, below, edges, fwd1, fwd2, columns, inner, slope, sides, stack, hidden
 ):
     def run(channels, width, depth, count):
         padded = depth // 3
@@ -331,13 +346,13 @@
 
     @pl.when(is_air())
     def _():
-        own_sides(to_left, to_right, sides, False)
+        own_sides(edges, sides, False)
         air_rows(own, above, below, 2, store)
         run(80, 512, 720, 4)
 
     @pl.when(is_sea())
     def _():
-        own_sides(to_left, to_right, sides, True)
+        own_sides(edges, sides, True)
         sea_rows(own, above, below, 2, store)
         run(40, 256, 384, 6)
 
@@ -432,7 +447,7 @@
         scatter(pulled)
 
 
-def cotangent_kernel(image, near, far, columns, cotangent):
+def cotangent_kernel(image, near, far, columns, after, cotangent, edge):
     @pl.when(is_air())
     def _():
         arrived = near[...] + far[...]
@@ -446,6 +461,8 @@
     def _():
         cotangent[...] = image[...]
 
+    edge[...] = own_edges(cotangent, 1)
+
 
 def spread_rows(target, rows):
     line = lax.broadcasted_iota(jnp.int32, (160, 160), 0)
@@ -461,7 +478,7 @@
 
 
 def adjoint_main_kernel(
-    own, above, below, to_left, to_right, bwd1, bwd2, slope, inner, sides, stack, hidden
+    own, above, below, edges, bwd1, bwd2, slope, inner, sides, stack, hidden
 ):
     def run(channels, width, depth, count):
         padded = depth // 3
@@ -481,13 +498,13 @@
 
     @pl.when(is_air())
     def _():
-        own_sides(to_left, to_right, sides, False)
+        own_sides(edges, sides, False)
         air_rows(own, above, below, 1, store)
         run(80, 512, 720, 4)
 
     @pl.when(is_sea())
     def _():
-        own_sides(to_left, to_right, sides, True)
+        own_sides(edges, sides, True)
         sea_rows(own, above, below, 1, store)
         run(40, 256, 384, 6)
 
@@ -527,19 +544,18 @@
         spread_rows(product, rows)
 
 
-def call(kernel, name, out_shape, inputs, scratch=(), limit=8, loads=False, idle=0):
+def call(kernel, name, out_shape, inputs, scratch=(), limit=8, stay=()):
     vmem = pl.BlockSpec(memory_space=pltpu.VMEM)
-    source = vmem
-    if loads:
-        source = pl.BlockSpec(memory_space=pltpu.HBM)
-        inputs = [pltpu.with_memory_space_constraint(array, pltpu.HBM) for array in inputs]
-    for i in range(len(inputs) - idle, len(inputs)):
-        inputs[i] = pltpu.with_memory_space_constraint(inputs[i], pltpu.HBM)
+    hbm = pl.BlockSpec(memory_space=pltpu.HBM)
+    inputs = [
+        pltpu.with_memory_space_constraint(x, pltpu.HBM) if i in stay else x
+        for i, x in enumerate(inputs)
+    ]
     return pl.pallas_call(
         kernel,
         name=name,
         out_shape=tuple(jax.ShapeDtypeStruct(shape, dtype) for shape, dtype in out_shape),
-        in_specs=[source] * (len(inputs) - idle) + [pl.BlockSpec(memory_space=pltpu.HBM)] * idle,
+        in_specs=[hbm if i in stay else vmem for i in range(len(inputs))],
         out_specs=tuple(vmem for _ in out_shape),
         scratch_shapes=list(scratch),
         compiler_params=pltpu.CompilerParams(vmem_limit_bytes=limit << 20),
@@ -553,10 +569,10 @@
     return above, below
 
 
-def lon_pair(to_left, to_right):
+def lon_pair(block):
     count = lax.axis_size("lon")
-    from_left = lax.ppermute(to_right, "lon", [(i, (i + 1) % count) for i in range(count)])
-    from_right = lax.ppermute(to_left, "lon", [((i + 1) % count, i) for i in range(count)])
+    from_left = lax.ppermute(block, "lon", [(i, (i + 1) % count) for i in range(count)])
+    from_right = lax.ppermute(block, "lon", [((i + 1) % count, i) for i in range(count)])
     return from_left, from_right
 
 
@@ -586,51 +602,50 @@
     regrid_weight,
     land_mask,
 ):
-    (own,) = call(
+    def held(arrays):
+        buffers = [pltpu.VMEM(array.shape, array.dtype) for array in arrays]
+        return buffers + [pltpu.SemaphoreType.DMA((len(arrays),))]
+
+    block = ((80, 128), BF16)
+    own, edge = call(
         pack_kernel,
         "pack",
-        [((160, CELLS), BF16)],
+        [((160, CELLS), BF16), block],
         [state, direction],
         [pltpu.VMEM((2, 80, ROWS, COLS), BF16), pltpu.SemaphoreType.DMA((2,))],
-        loads=True,
-    )
+        stay=range(2),
+    )
+    edge_above, edge_below = lat_pair(edge)
     above, below = lat_pair(own)
+    (edges,) = call(edge_kernel, "edges", [block], [edge, edge_above, edge_below])
+    from_left, from_right = lon_pair(edges)
+    first_a = air_first.transpose(0, 2, 1)
+    first_o = sea_first.transpose(0, 2, 1)
     raw = [
-        air_first.transpose(0, 2, 1),
+        first_a,
         air_second,
-        sea_first.transpose(0, 2, 1),
+        first_o,
         sea_second,
-        regrid_index,
-        regrid_weight,
-        land_mask,
         air_bias.reshape(1, 512),
         sea_bias.reshape(1, 256),
         air_flux,
         aloft_reaction_to_seawarmth.reshape(1, 80),
         sea_forcing.T,
     ]
-    fwd1, fwd2, bwd1, bwd2, hot, picked, mask, columns = call(
-        prepare_kernel,
-        "prepare",
-        [
-            ((512, 720), BF16), ((240, 1536), BF16), ((512, 720), BF16), ((240, 1536), BF16),
-            ((128, SLOTS * CELLS), BF16), ((16, SLOTS * CELLS), F32),
-            ((2, CELLS), F32), ((512, 8), F32),
-        ],
-        raw,
-        [pltpu.VMEM(array.shape, array.dtype) for array in raw] + [pltpu.SemaphoreType.DMA((12,))],
-        limit=20,
-        loads=True,
-    )
-    to_left, to_right = call(
-        edge_kernel, "edges", [((80, 128), BF16)] * 2, [own, above, below, columns]
-    )
-    from_left, from_right = lon_pair(to_left, to_right)
+    fwd1, fwd2, columns = call(
+        forward_kernel,
+        "forward",
+        [((512, 720), BF16), ((240, 1536), BF16), ((512, 8), F32)],
+        raw + [edges],
+        held(raw),
+        limit=16,
+        stay=range(len(raw)),
+    )
     inner, slope, sides = call(
         tangent_main_kernel,
         "tangent_main",
         [((80, 2 * CELLS), F32), ((512, 6 * COLS), BF16), ((2, 80, 128), F32)],
-        [own, above, below, to_left, to_right, fwd1, fwd2, columns],
+        [own, above, below, edges, fwd1, fwd2, columns],
         [pltpu.VMEM((240, 16 * COLS), BF16), pltpu.VMEM((512, 6 * COLS), BF16)],
         limit=16,
     )
@@ -642,6 +657,19 @@
         limit=16,
     )
     near, far = across(payload, payload, -1)
+    raw = [air_second, first_a, sea_second, first_o, regrid_index, regrid_weight, land_mask]
+    bwd1, bwd2, hot, picked, mask = call(
+        backward_kernel,
+        "backward",
+        [
+            ((512, 720), BF16), ((240, 1536), BF16), ((128, SLOTS * CELLS), BF16),
+            ((16, SLOTS * CELLS), F32), ((2, CELLS), F32),
+        ],
+        raw + [payload],
+        held(raw),
+        limit=16,
+        stay=range(len(raw)),
+    )
     image, back_near, back_far = call(
         couple_kernel,
         "couple",
@@ -650,22 +678,22 @@
     )
     back_near, back_far = across(back_near, back_far, 1)
     (result,) = call(unpack_kernel, "unpack", [((1, 80, ROWS, COLS), BF16)], [image])
-    (cotangent,) = call(
-        cotangent_kernel, "cotangent", [((80, CELLS), BF16)],
-        [image, back_near, back_far, columns],
-    )
+    cotangent, edge = call(
+        cotangent_kernel,
+        "cotangent",
+        [((80, CELLS), BF16), block],
+        [image, back_near, back_far, columns, result],
+        stay=(4,),
+    )
+    edge_above, edge_below = lat_pair(edge)
     above, below = lat_pair(cotangent)
-    to_left, to_right = call(
-        edge_kernel, "edges_back", [((80, 128), BF16)] * 2,
-        [cotangent, above, below, result],
-        idle=1,
-    )
-    from_left, from_right = lon_pair(to_left, to_right)
+    (edges,) = call(edge_kernel, "edges_back", [block], [edge, edge_above, edge_below])
+    from_left, from_right = lon_pair(edges)
     inner, sides = call(
         adjoint_main_kernel,
         "adjoint_main",
         [((80, 2 * CELLS), F32), ((2, 80, 128), F32)],
-        [cotangent, above, below, to_left, to_right, bwd1, bwd2, slope],
+        [cotangent, above, below, edges, bwd1, bwd2, slope],
         [pltpu.VMEM((240, 8 * COLS), BF16), pltpu.VMEM((512, 6 * COLS), BF16)],
         limit=16,
     )
@@ -673,10 +701,7 @@
         adjoint_edge_kernel,
         "adjoint_edge",
         [((1, 80, ROWS, COLS), BF16)],
-        [
-            sides, from_left, from_right, inner, edge_slope, bwd1, bwd2,
-            back_near, back_far,
-        ],
+        [sides, from_left, from_right, inner, edge_slope, bwd1, bwd2, back_near, back_far],
         limit=16,
     )
     return result, product

time: 51.8 us -> 56.8 us (1.097); the launches traced: 51.6 us -> 56 us
  starting transfers between devices: 17.4 us -> 22.5 us
  waiting for transfers between devices: 21 us -> 18.8 us
  Pallas kernels: 12.5 us -> 14 us
    ppermute x2 -> x4, starting transfers between devices: 4.99 us -> 9.31 us  [lat_pair(): lax.ppermute(block, 'lat', [((i + 1) % count, i) for i in range(count)])]
    ppermute x4, waiting for transfers between devices: 6.22 us -> 4.33 us  [the longest x2 4.32 us: lon_pair(): lax.ppermute(block, 'lon', [(i, (i + 1) % count) for i in range(count)])]
    pallas_call x11 -> x12, Pallas kernels: 12.5 us -> 14 us  [call(): pl.pallas_call(kernel, name=name, out_shape=tuple((jax.ShapeDtypeStruct(s...]
    ppermute x2 -> x4, waiting for transfers between devices: 2.69 us -> 3.95 us  [lat_pair(): lax.ppermute(block, 'lat', [((i + 1) % count, i) for i in range(count)])]
    ppermute x2, starting transfers between devices: 3.97 us -> 4.97 us  [across(): same = lax.ppermute(near, 'comp', [(0, 1), (1, 0)])]
    ppermute x2, waiting for transfers between devices: 4.71 us -> 3.73 us  [across(): return (same, lax.ppermute(far, ('comp', 'lon'), route))]
    ppermute x2, waiting for transfers between devices: 3.48 us -> 2.67 us  [across(): same = lax.ppermute(near, 'comp', [(0, 1), (1, 0)])]
    ppermute x2 -> x4, waiting for transfers between devices: 3.92 us -> 4.11 us  [lat_pair(): lax.ppermute(block, 'lat', [(i, (i + 1) % count) for i in range(count)])]
  transfers between devices with their start and end apart: 12 -> 16, of which waited for: 10 -> 9; matrix products, arithmetic and copies ran while one was open for 0% -> 0% of each run, Pallas kernels for 14% -> 15%
where the time goes in v6:
time: 56.8 us; the launch traced here: 56 us
  starting transfers between devices  22.5 us (40%)
  waiting for transfers between devices  18.8 us (33%)
  Pallas kernels  14 us (25%)
  between operations  0.76 us (1%)
    pallas_call x12, Pallas kernels, call(): pl.pallas_call(kernel, name=name, out_shape=tuple((jax.ShapeDtypeStruct(s...  14 us
    ppermute x4, starting transfers between devices, lat_pair(): lax.ppermute(block, 'lat', [((i + 1) % count, i) for i in range(count)])  9.31 us
    ppermute x2, starting transfers between devices, lon_pair(): lax.ppermute(block, 'lon', [((i + 1) % count, i) for i in range(count)])  5.19 us
    ppermute x2, starting transfers between devices, across(): same = lax.ppermute(near, 'comp', [(0, 1), (1, 0)])  4.97 us
    ppermute x2, waiting for transfers between devices, lon_pair(): lax.ppermute(block, 'lon', [(i, (i + 1) % count) for i in range(count)])  4.32 us
    ppermute x4, waiting for transfers between devices, lat_pair(): lax.ppermute(block, 'lat', [(i, (i + 1) % count) for i in range(count)])  4.11 us
    ppermute x4, waiting for transfers between devices, lat_pair(): lax.ppermute(block, 'lat', [((i + 1) % count, i) for i in range(count)])  3.95 us
    ppermute x2, waiting for transfers between devices, across(): return (same, lax.ppermute(far, ('comp', 'lon'), route))  3.73 us
  transfers between devices with their start and end apart: 16, of which 9 were waited for; matrix products, arithmetic and copies ran while one was open for 0% of the time, Pallas kernels for 15%

profile of v6, /device:TPU:8, one launch (start us, length us, event | category | flops | bytes accessed | tf_op | source)
XLA Modules:
  0.0 56.0 jit_solution(14072577756342858889)
XLA Ops:
  0.6 1.4 %pack.1 = (bf16[160,512]{1,0:T(8,128)(2,1)S(1)}, bf16[80,128]{1,0:T(8,128)(2,1)S(1)}) custom-call(bf16[1,80,2,256]{3,2,1,0:T(2,128)(2,1)} %state.1, bf16[1,80,2,256]{3,2,1,0:T(2,128)(2,1)} %direction.1), custom_call_target="tpu_custom_call" | custom-call | tf_op jit(solution)/shard_map/pack/pallas_call | solution.py:554
  2.0 2.2 %collective-permute-start.1 = (bf16[160,512]{1,0:T(8,128)(2,1)S(1)}, bf16[160,512]{1,0:T(8,128)(2,1)S(1)}, u32[]{:S(2)}, u32[]{:S(2)}) collective-permute-start(bf16[160,512]{1,0:T(8,128)(2,1)S(1)} %get-tuple-element.25.own), channel_id=1, source_target_pairs={{32,0},{64,32},{96,64},{0,96},{33,1},{65,33},{97,65},{1,97},{34,2}... | collective-permute-start | bytes 491528 | tf_op jit(solution)/shard_map/ppermute | solution.py:568
  4.2 0.0 collective-permute-start
  4.2 2.0 %collective-permute-start.3 = (bf16[80,128]{1,0:T(8,128)(2,1)S(1)}, bf16[80,128]{1,0:T(8,128)(2,1)S(1)}, u32[]{:S(2)}, u32[]{:S(2)}) collective-permute-start(bf16[80,128]{1,0:T(8,128)(2,1)S(1)} %get-tuple-element.26.own), channel_id=1, source_target_pairs={{32,0},{64,32},{96,64},{0,96},{33,1},{65,33},{97,65},{1,97},{34,2}... | collective-permute-start | bytes 61448 | tf_op jit(solution)/shard_map/ppermute | solution.py:568
  6.3 0.0 collective-permute-start.2
  6.3 2.2 %collective-permute-done.3.below = bf16[80,128]{1,0:T(8,128)(2,1)S(1)} collective-permute-done((bf16[80,128]{1,0:T(8,128)(2,1)S(1)}, bf16[80,128]{1,0:T(8,128)(2,1)S(1)}, u32[]{:S(2)}, u32[]{:S(2)}) %collective-permute-start.3) | collective-permute-done | bytes 20512 | tf_op jit(solution)/shard_map/ppermute | solution.py:568
  8.5 2.1 %collective-permute-done.2.above = bf16[80,128]{1,0:T(8,128)(2,1)S(1)} collective-permute-done((bf16[80,128]{1,0:T(8,128)(2,1)S(1)}, bf16[80,128]{1,0:T(8,128)(2,1)S(1)}, u32[]{:S(2)}, u32[]{:S(2)}) %collective-permute-start.2) | collective-permute-done | bytes 20512 | tf_op jit(solution)/shard_map/ppermute | solution.py:567
  10.5 0.1 edges.1.refs_9_
  10.6 5.1 %collective-permute-start.5 = (bf16[80,128]{1,0:T(8,128)(2,1)S(1)}, bf16[80,128]{1,0:T(8,128)(2,1)S(1)}, u32[]{:S(2)}, u32[]{:S(2)}) collective-permute-start(bf16[80,128]{1,0:T(8,128)(2,1)S(1)} %edges.1.refs_9_), channel_id=1, source_target_pairs={{1,0},{2,1},{3,2},{4,3},{5,4},{6,5},{7,6},{8,7},{9,8},{10,9},{11,1... | collective-permute-start | bytes 61448 | tf_op jit(solution)/shard_map/ppermute | solution.py:575
  15.7 0.0 collective-permute-start.4
  15.7 1.8 %forward.1 = (bf16[512,720]{1,0:T(8,128)(2,1)S(1)}, bf16[240,1536]{1,0:T(8,128)(2,1)S(1)}, f32[512,8]{1,0:T(8,128)S(1)}) custom-call(bf16[9,80,512]{2,1,0:T(8,128)(2,1)} %bitcast.6, bf16[9,80,512]{2,1,0:T(8,128)(2,1)} %refs_0_.1, bf16[9,40,256]{2,1,0:T(8,128)(2,1)} %bitcast.8, bf16[9,40,256]{2,1,0:T(8,128)(2,1)} %refs_2_.1, f32[1,512]{1,0:T(1,128)} %bitcast.10, ...), custom_call_target="tpu_custom_call" | custom-call | tf_op jit(solution)/shard_map/forward/pallas_call | solution.py:554
  17.6 0.0 collective-permute-done.1.below
  17.6 0.0 collective-permute-done.above
  17.6 2.4 %tangent_main.1 = (f32[80,1024]{1,0:T(8,128)S(1)}, bf16[512,1536]{1,0:T(8,128)(2,1)S(1)}, f32[2,80,128]{2,1,0:T(8,128)S(1)}) custom-call(bf16[160,512]{1,0:T(8,128)(2,1)S(1)} %get-tuple-element.25.own, bf16[160,512]{1,0:T(8,128)(2,1)S(1)} %collective-permute-done.above, bf16[160,512]{1,0:T(8,128)(2,1)S(1)} %collective-permute-done.1.below, ...), custom_call_target="tpu_custom_call" | custom-call | tf_op jit(solution)/shard_map/tangent_main/pallas_call | solution.py:554
  20.0 0.0 collective-permute-done.5.from_right
  20.0 1.0 %collective-permute-done.4.from_left = bf16[80,128]{1,0:T(8,128)(2,1)S(1)} collective-permute-done((bf16[80,128]{1,0:T(8,128)(2,1)S(1)}, bf16[80,128]{1,0:T(8,128)(2,1)S(1)}, u32[]{:S(2)}, u32[]{:S(2)}) %collective-permute-start.4) | collective-permute-done | bytes 20512 | tf_op jit(solution)/shard_map/ppermute | solution.py:574
  21.1 1.1 %tangent_edge.1 = (f32[80,1024]{1,0:T(8,128)S(1)}, bf16[512,128]{1,0:T(8,128)(2,1)S(1)}, f32[8,128]{1,0:T(8,128)S(1)}) custom-call(bf16[160,512]{1,0:T(8,128)(2,1)S(1)} %get-tuple-element.25.own, f32[2,80,128]{2,1,0:T(8,128)S(1)} %get-tuple-element.30.sides, bf16[80,128]{1,0:T(8,128)(2,1)S(1)} %collective-permute-done.4.from_left, ...), custom_call_target="tpu_custom_call" | custom-call | tf_op jit(solution)/shard_map/tangent_edge/pallas_call | solution.py:554
  22.2 2.5 %collective-permute-start.7 = (f32[8,128]{1,0:T(8,128)S(1)}, f32[8,128]{1,0:T(8,128)S(1)}, u32[]{:S(2)}, u32[]{:S(2)}) collective-permute-start(f32[8,128]{1,0:T(8,128)S(1)} %get-tuple-element.33.refs_7_), channel_id=1, source_target_pairs={{0,159},{1,128},{2,129},{3,130},{4,131},{5,132},{6,133},{7,134},{8... | collective-permute-start | bytes 12296 | tf_op jit(solution)/shard_map/ppermute | solution.py:586
  24.7 2.5 %collective-permute-start.6 = (f32[8,128]{1,0:T(8,128)S(1)}, f32[8,128]{1,0:T(8,128)S(1)}, u32[]{:S(2)}, u32[]{:S(2)}) collective-permute-start(f32[8,128]{1,0:T(8,128)S(1)} %get-tuple-element.33.refs_7_), channel_id=1, source_target_pairs={{0,128},{128,0},{1,129},{129,1},{2,130},{130,2},{3,131},{131,3},{4... | collective-permute-start | bytes 12296 | tf_op jit(solution)/shard_map/ppermute | solution.py:581
  27.2 1.8 %backward.1 = (bf16[512,720]{1,0:T(8,128)(2,1)S(1)}, bf16[240,1536]{1,0:T(8,128)(2,1)S(1)}, bf16[128,4096]{1,0:T(8,128)(2,1)S(1)}, f32[16,4096]{1,0:T(8,128)S(1)}, f32[2,512]{1,0:T(2,128)S(1)}) custom-call(bf16[9,80,512]{2,1,0:T(8,128)(2,1)} %refs_0_.1, bf16[9,80,512]{2,1,0:T(8,128)(2,1)} %bitcast.7, bf16[9,40,256]{2,1,0:T(8,128)(2,1)} %refs_2_.1, ...), custom_call_target="tpu_custom_call" | custom-call | tf_op jit(solution)/shard_map/backward/pallas_call | solution.py:554
  28.9 0.0 collective-permute-done.7.far
  29.0 0.9 %collective-permute-done.6.near = f32[8,128]{1,0:T(8,128)S(1)} collective-permute-done((f32[8,128]{1,0:T(8,128)S(1)}, f32[8,128]{1,0:T(8,128)S(1)}, u32[]{:S(2)}, u32[]{:S(2)}) %collective-permute-start.6) | collective-permute-done | bytes 4128 | tf_op jit(solution)/shard_map/ppermute | solution.py:581
  29.8 0.9 %couple.1 = (bf16[80,512]{1,0:T(8,128)(2,1)S(1)}, f32[8,128]{1,0:T(8,128)S(1)}, f32[8,128]{1,0:T(8,128)S(1)}) custom-call(f32[80,1024]{1,0:T(8,128)S(1)} %get-tuple-element.32.y, f32[8,128]{1,0:T(8,128)S(1)} %collective-permute-done.6.near, f32[8,128]{1,0:T(8,128)S(1)} %collective-permute-done.7.far, bf16[128,4096]{1,0:T(8,128)(2,1)S(1)} %get-tuple-element.34.hot, ...), custom_call_target="tpu_custom_call" | custom-call | tf_op jit(solution)/shard_map/couple/pallas_call | solution.py:554
  30.8 2.5 %collective-permute-start.8 = (f32[8,128]{1,0:T(8,128)S(1)}, f32[8,128]{1,0:T(8,128)S(1)}, u32[]{:S(2)}, u32[]{:S(2)}) collective-permute-start(f32[8,128]{1,0:T(8,128)S(1)} %get-tuple-element.38), channel_id=1, source_target_pairs={{0,128},{128,0},{1,129},{129,1},{2,130},{130,2},{3,131},{131,3},{4... | collective-permute-start | bytes 12296 | tf_op jit(solution)/shard_map/ppermute | solution.py:581
  33.3 0.0 collective-permute-start.9
  33.3 0.8 %unpack.1.after = bf16[1,80,2,256]{3,2,1,0:T(2,128)(2,1)} custom-call(bf16[80,512]{1,0:T(8,128)(2,1)S(1)} %get-tuple-element.37.packed.image), custom_call_target="tpu_custom_call" | custom-call | tf_op jit(solution)/shard_map/unpack/pallas_call | solution.py:554
  34.1 1.8 %collective-permute-done.8.near = f32[8,128]{1,0:T(8,128)S(1)} collective-permute-done((f32[8,128]{1,0:T(8,128)S(1)}, f32[8,128]{1,0:T(8,128)S(1)}, u32[]{:S(2)}, u32[]{:S(2)}) %collective-permute-start.8) | collective-permute-done | bytes 4128 | tf_op jit(solution)/shard_map/ppermute | solution.py:581
  35.9 3.7 %collective-permute-done.9.far = f32[8,128]{1,0:T(8,128)S(1)} collective-permute-done((f32[8,128]{1,0:T(8,128)S(1)}, f32[8,128]{1,0:T(8,128)S(1)}, u32[]{:S(2)}, u32[]{:S(2)}) %collective-permute-start.9) | collective-permute-done | bytes 4128 | tf_op jit(solution)/shard_map/ppermute | solution.py:586
  39.6 0.2 cotangent.1
  39.8 3.0 %collective-permute-start.11 = (bf16[80,512]{1,0:T(8,128)(2,1)S(1)}, bf16[80,512]{1,0:T(8,128)(2,1)S(1)}, u32[]{:S(2)}, u32[]{:S(2)}) collective-permute-start(bf16[80,512]{1,0:T(8,128)(2,1)S(1)} %get-tuple-element.40.own), channel_id=1, source_target_pairs={{32,0},{64,32},{96,64},{0,96},{33,1},{65,33},{97,65},{1,97},{34,2}... | collective-permute-start | bytes 245768 | tf_op jit(solution)/shard_map/ppermute | solution.py:568
  42.8 0.0 collective-permute-start.10
  42.9 2.0 %collective-permute-start.13 = (bf16[80,128]{1,0:T(8,128)(2,1)S(1)}, bf16[80,128]{1,0:T(8,128)(2,1)S(1)}, u32[]{:S(2)}, u32[]{:S(2)}) collective-permute-start(bf16[80,128]{1,0:T(8,128)(2,1)S(1)} %get-tuple-element.41.own), channel_id=1, source_target_pairs={{32,0},{64,32},{96,64},{0,96},{33,1},{65,33},{97,65},{1,97},{34,2}... | collective-permute-start | bytes 61448 | tf_op jit(solution)/shard_map/ppermute | solution.py:568
  44.9 0.0 collective-permute-start.12
  44.9 1.8 %collective-permute-done.13.below = bf16[80,128]{1,0:T(8,128)(2,1)S(1)} collective-permute-done((bf16[80,128]{1,0:T(8,128)(2,1)S(1)}, bf16[80,128]{1,0:T(8,128)(2,1)S(1)}, u32[]{:S(2)}, u32[]{:S(2)}) %collective-permute-start.13) | collective-permute-done | bytes 20512 | tf_op jit(solution)/shard_map/ppermute | solution.py:568
  46.6 2.0 %collective-permute-done.12.above = bf16[80,128]{1,0:T(8,128)(2,1)S(1)} collective-permute-done((bf16[80,128]{1,0:T(8,128)(2,1)S(1)}, bf16[80,128]{1,0:T(8,128)(2,1)S(1)}, u32[]{:S(2)}, u32[]{:S(2)}) %collective-permute-start.12) | collective-permute-done | bytes 20512 | tf_op jit(solution)/shard_map/ppermute | solution.py:567
  48.7 0.1 edges_back.1.edges
  48.7 0.1 collective-permute-start.15
  48.8 0.5 collective-permute-start.14
  49.3 0.0 collective-permute-done.11.below
  49.3 0.0 collective-permute-done.10.above
  49.3 1.6 %adjoint_main.1 = (f32[80,1024]{1,0:T(8,128)S(1)}, f32[2,80,128]{2,1,0:T(8,128)S(1)}) custom-call(bf16[80,512]{1,0:T(8,128)(2,1)S(1)} %get-tuple-element.40.own, bf16[80,512]{1,0:T(8,128)(2,1)S(1)} %collective-permute-done.10.above, bf16[80,512]{1,0:T(8,128)(2,1)S(1)} %collective-permute-done.11.below, bf16[80,128]{1,0:T(8,128)(2,1)S(1)} %edges_back.1.edges, ...), custom_call_target="tpu_custom_call" | custom-call | tf_op jit(solution)/shard_map/adjoint_main/pallas_call | solution.py:554
  50.9 0.0 collective-permute-done.15.from_right
  50.9 3.3 %collective-permute-done.14.from_left = bf16[80,128]{1,0:T(8,128)(2,1)S(1)} collective-permute-done((bf16[80,128]{1,0:T(8,128)(2,1)S(1)}, bf16[80,128]{1,0:T(8,128)(2,1)S(1)}, u32[]{:S(2)}, u32[]{:S(2)}) %collective-permute-start.14) | collective-permute-done | bytes 20512 | tf_op jit(solution)/shard_map/ppermute | solution.py:574
  54.2 1.8 %adjoint_edge.1 = bf16[1,80,2,256]{3,2,1,0:T(2,128)(2,1)} custom-call(f32[2,80,128]{2,1,0:T(8,128)S(1)} %get-tuple-element.45.sides, bf16[80,128]{1,0:T(8,128)(2,1)S(1)} %collective-permute-done.14.from_left, bf16[80,128]{1,0:T(8,128)(2,1)S(1)} %collective-permute-done.15.from_right, f32[80,1024]{1,0:T(8,128)S(1)} %get-tuple-element.46.inner, ...), custom_call_target="tpu_custom_call" | custom-call | tf_op jit(solution)/shard_map/adjoint_edge/pallas_call | solution.py:554
Async XLA Ops:
  2.0 15.6 %collective-permute-start.1 = (bf16[160,512]{1,0:T(8,128)(2,1)S(1)}, bf16[160,512]{1,0:T(8,128)(2,1)S(1)}, u32[]{:S(2)}, u32[]{:S(2)}) collective-permute-start(bf16[160,512]{1,0:T(8,128)(2,1)S(1)} %get-tuple-element.25.own), channel_id=1, source_target_pairs={{32,0},{64,32},{96,64},{0,96},{33,1},{65,33},{97,65},{1,97},{34,2}... | collective-permute-start | bytes 491528 | tf_op jit(solution)/shard_map/ppermute | solution.py:568
  4.2 13.3 %collective-permute-start = (bf16[160,512]{1,0:T(8,128)(2,1)S(1)}, bf16[160,512]{1,0:T(8,128)(2,1)S(1)}, u32[]{:S(2)}, u32[]{:S(2)}) collective-permute-start(bf16[160,512]{1,0:T(8,128)(2,1)S(1)} %get-tuple-element.25.own), channel_id=1, source_target_pairs={{0,32},{32,64},{64,96},{96,0},{1,33},{33,65},{65,97},{97,1},{2,34}... | collective-permute-start | bytes 491528 | tf_op jit(solution)/shard_map/ppermute | solution.py:567
  4.2 4.2 %collective-permute-start.3 = (bf16[80,128]{1,0:T(8,128)(2,1)S(1)}, bf16[80,128]{1,0:T(8,128)(2,1)S(1)}, u32[]{:S(2)}, u32[]{:S(2)}) collective-permute-start(bf16[80,128]{1,0:T(8,128)(2,1)S(1)} %get-tuple-element.26.own), channel_id=1, source_target_pairs={{32,0},{64,32},{96,64},{0,96},{33,1},{65,33},{97,65},{1,97},{34,2}... | collective-permute-start | bytes 61448 | tf_op jit(solution)/shard_map/ppermute | solution.py:568
  6.3 4.3 %collective-permute-start.2 = (bf16[80,128]{1,0:T(8,128)(2,1)S(1)}, bf16[80,128]{1,0:T(8,128)(2,1)S(1)}, u32[]{:S(2)}, u32[]{:S(2)}) collective-permute-start(bf16[80,128]{1,0:T(8,128)(2,1)S(1)} %get-tuple-element.26.own), channel_id=1, source_target_pairs={{0,32},{32,64},{64,96},{96,0},{1,33},{33,65},{65,97},{97,1},{2,34}... | collective-permute-start | bytes 61448 | tf_op jit(solution)/shard_map/ppermute | solution.py:567
  10.6 9.4 %collective-permute-start.5 = (bf16[80,128]{1,0:T(8,128)(2,1)S(1)}, bf16[80,128]{1,0:T(8,128)(2,1)S(1)}, u32[]{:S(2)}, u32[]{:S(2)}) collective-permute-start(bf16[80,128]{1,0:T(8,128)(2,1)S(1)} %edges.1.refs_9_), channel_id=1, source_target_pairs={{1,0},{2,1},{3,2},{4,3},{5,4},{6,5},{7,6},{8,7},{9,8},{10,9},{11,1... | collective-permute-start | bytes 61448 | tf_op jit(solution)/shard_map/ppermute | solution.py:575
  15.7 5.3 %collective-permute-start.4 = (bf16[80,128]{1,0:T(8,128)(2,1)S(1)}, bf16[80,128]{1,0:T(8,128)(2,1)S(1)}, u32[]{:S(2)}, u32[]{:S(2)}) collective-permute-start(bf16[80,128]{1,0:T(8,128)(2,1)S(1)} %edges.1.refs_9_), channel_id=1, source_target_pairs={{0,1},{1,2},{2,3},{3,4},{4,5},{5,6},{6,7},{7,8},{8,9},{9,10},{10,1... | collective-permute-start | bytes 61448 | tf_op jit(solution)/shard_map/ppermute | solution.py:574
  22.2 6.8 %collective-permute-start.7 = (f32[8,128]{1,0:T(8,128)S(1)}, f32[8,128]{1,0:T(8,128)S(1)}, u32[]{:S(2)}, u32[]{:S(2)}) collective-permute-start(f32[8,128]{1,0:T(8,128)S(1)} %get-tuple-element.33.refs_7_), channel_id=1, source_target_pairs={{0,159},{1,128},{2,129},{3,130},{4,131},{5,132},{6,133},{7,134},{8... | collective-permute-start | bytes 12296 | tf_op jit(solution)/shard_map/ppermute | solution.py:586
  24.7 5.1 %collective-permute-start.6 = (f32[8,128]{1,0:T(8,128)S(1)}, f32[8,128]{1,0:T(8,128)S(1)}, u32[]{:S(2)}, u32[]{:S(2)}) collective-permute-start(f32[8,128]{1,0:T(8,128)S(1)} %get-tuple-element.33.refs_7_), channel_id=1, source_target_pairs={{0,128},{128,0},{1,129},{129,1},{2,130},{130,2},{3,131},{131,3},{4... | collective-permute-start | bytes 12296 | tf_op jit(solution)/shard_map/ppermute | solution.py:581
  30.8 5.1 %collective-permute-start.8 = (f32[8,128]{1,0:T(8,128)S(1)}, f32[8,128]{1,0:T(8,128)S(1)}, u32[]{:S(2)}, u32[]{:S(2)}) collective-permute-start(f32[8,128]{1,0:T(8,128)S(1)} %get-tuple-element.38), channel_id=1, source_target_pairs={{0,128},{128,0},{1,129},{129,1},{2,130},{130,2},{3,131},{131,3},{4... | collective-permute-start | bytes 12296 | tf_op jit(solution)/shard_map/ppermute | solution.py:581
  33.3 6.4 %collective-permute-start.9 = (f32[8,128]{1,0:T(8,128)S(1)}, f32[8,128]{1,0:T(8,128)S(1)}, u32[]{:S(2)}, u32[]{:S(2)}) collective-permute-start(f32[8,128]{1,0:T(8,128)S(1)} %get-tuple-element.39), channel_id=1, source_target_pairs={{0,129},{1,130},{2,131},{3,132},{4,133},{5,134},{6,135},{7,136},{8... | collective-permute-start | bytes 12296 | tf_op jit(solution)/shard_map/ppermute | solution.py:586
  39.8 9.5 %collective-permute-start.11 = (bf16[80,512]{1,0:T(8,128)(2,1)S(1)}, bf16[80,512]{1,0:T(8,128)(2,1)S(1)}, u32[]{:S(2)}, u32[]{:S(2)}) collective-permute-start(bf16[80,512]{1,0:T(8,128)(2,1)S(1)} %get-tuple-element.40.own), channel_id=1, source_target_pairs={{32,0},{64,32},{96,64},{0,96},{33,1},{65,33},{97,65},{1,97},{34,2}... | collective-permute-start | bytes 245768 | tf_op jit(solution)/shard_map/ppermute | solution.py:568
  42.8 6.5 %collective-permute-start.10 = (bf16[80,512]{1,0:T(8,128)(2,1)S(1)}, bf16[80,512]{1,0:T(8,128)(2,1)S(1)}, u32[]{:S(2)}, u32[]{:S(2)}) collective-permute-start(bf16[80,512]{1,0:T(8,128)(2,1)S(1)} %get-tuple-element.40.own), channel_id=1, source_target_pairs={{0,32},{32,64},{64,96},{96,0},{1,33},{33,65},{65,97},{97,1},{2,34}... | collective-permute-start | bytes 245768 | tf_op jit(solution)/shard_map/ppermute | solution.py:567
  42.9 3.8 %collective-permute-start.13 = (bf16[80,128]{1,0:T(8,128)(2,1)S(1)}, bf16[80,128]{1,0:T(8,128)(2,1)S(1)}, u32[]{:S(2)}, u32[]{:S(2)}) collective-permute-start(bf16[80,128]{1,0:T(8,128)(2,1)S(1)} %get-tuple-element.41.own), channel_id=1, source_target_pairs={{32,0},{64,32},{96,64},{0,96},{33,1},{65,33},{97,65},{1,97},{34,2}... | collective-permute-start | bytes 61448 | tf_op jit(solution)/shard_map/ppermute | solution.py:568
  44.9 3.8 %collective-permute-start.12 = (bf16[80,128]{1,0:T(8,128)(2,1)S(1)}, bf16[80,128]{1,0:T(8,128)(2,1)S(1)}, u32[]{:S(2)}, u32[]{:S(2)}) collective-permute-start(bf16[80,128]{1,0:T(8,128)(2,1)S(1)} %get-tuple-element.41.own), channel_id=1, source_target_pairs={{0,32},{32,64},{64,96},{96,0},{1,33},{33,65},{65,97},{97,1},{2,34}... | collective-permute-start | bytes 61448 | tf_op jit(solution)/shard_map/ppermute | solution.py:567
  48.7 2.2 %collective-permute-start.15 = (bf16[80,128]{1,0:T(8,128)(2,1)S(1)}, bf16[80,128]{1,0:T(8,128)(2,1)S(1)}, u32[]{:S(2)}, u32[]{:S(2)}) collective-permute-start(bf16[80,128]{1,0:T(8,128)(2,1)S(1)} %edges_back.1.edges), channel_id=1, source_target_pairs={{1,0},{2,1},{3,2},{4,3},{5,4},{6,5},{7,6},{8,7},{9,8},{10,9},{11,1... | collective-permute-start | bytes 61448 | tf_op jit(solution)/shard_map/ppermute | solution.py:575
  48.8 5.4 %collective-permute-start.14 = (bf16[80,128]{1,0:T(8,128)(2,1)S(1)}, bf16[80,128]{1,0:T(8,128)(2,1)S(1)}, u32[]{:S(2)}, u32[]{:S(2)}) collective-permute-start(bf16[80,128]{1,0:T(8,128)(2,1)S(1)} %edges_back.1.edges), channel_id=1, source_target_pairs={{0,1},{1,2},{2,3},{3,4},{4,5},{5,6},{6,7},{7,8},{8,9},{9,10},{10,1... | collective-permute-start | bytes 61448 | tf_op jit(solution)/shard_map/ppermute | solution.py:574

commit v7 on v6

--- a/solution.py
+++ b/solution.py
@@ -1,11 +1,10 @@
-import functools
-
 import jax
 import jax.numpy as jnp
 from jax import lax
 from jax.experimental import pallas as pl
 from jax.experimental.pallas import tpu as pltpu
 from jax.sharding import PartitionSpec as P
+
 
 F32 = jnp.float32
 BF16 = jnp.bfloat16
@@ -544,7 +543,7 @@
         spread_rows(product, rows)
 
 
-def call(kernel, name, out_shape, inputs, scratch=(), limit=8, stay=()):
+def call(kernel, out_shape, inputs, scratch=(), limit=8, stay=()):
     vmem = pl.BlockSpec(memory_space=pltpu.VMEM)
     hbm = pl.BlockSpec(memory_space=pltpu.HBM)
     inputs = [
@@ -553,7 +552,6 @@
     ]
     return pl.pallas_call(
         kernel,
-        name=name,
         out_shape=tuple(jax.ShapeDtypeStruct(shape, dtype) for shape, dtype in out_shape),
         in_specs=[hbm if i in stay else vmem for i in range(len(inputs))],
         out_specs=tuple(vmem for _ in out_shape),
@@ -609,7 +607,6 @@
     block = ((80, 128), BF16)
     own, edge = call(
         pack_kernel,
-        "pack",
         [((160, CELLS), BF16), block],
         [state, direction],
         [pltpu.VMEM((2, 80, ROWS, COLS), BF16), pltpu.SemaphoreType.DMA((2,))],
@@ -617,7 +614,7 @@
     )
     edge_above, edge_below = lat_pair(edge)
     above, below = lat_pair(own)
-    (edges,) = call(edge_kernel, "edges", [block], [edge, edge_above, edge_below])
+    (edges,) = call(edge_kernel, [block], [edge, edge_above, edge_below])
     from_left, from_right = lon_pair(edges)
     first_a = air_first.transpose(0, 2, 1)
     first_o = sea_first.transpose(0, 2, 1)
@@ -634,7 +631,6 @@
     ]
     fwd1, fwd2, columns = call(
         forward_kernel,
-        "forward",
         [((512, 720), BF16), ((240, 1536), BF16), ((512, 8), F32)],
         raw + [edges],
         held(raw),
@@ -643,7 +639,6 @@
     )
     inner, slope, sides = call(
         tangent_main_kernel,
-        "tangent_main",
         [((80, 2 * CELLS), F32), ((512, 6 * COLS), BF16), ((2, 80, 128), F32)],
         [own, above, below, edges, fwd1, fwd2, columns],
         [pltpu.VMEM((240, 16 * COLS), BF16), pltpu.VMEM((512, 6 * COLS), BF16)],
@@ -651,7 +646,6 @@
     )
     y, edge_slope, payload = call(
         tangent_edge_kernel,
-        "tangent_edge",
         [((80, 2 * CELLS), F32), ((512, 128), BF16), ((8, 128), F32)],
         [own, sides, from_left, from_right, inner, fwd1, fwd2, columns],
         limit=16,
@@ -660,7 +654,6 @@
     raw = [air_second, first_a, sea_second, first_o, regrid_index, regrid_weight, land_mask]
     bwd1, bwd2, hot, picked, mask = call(
         backward_kernel,
-        "backward",
         [
             ((512, 720), BF16), ((240, 1536), BF16), ((128, SLOTS * CELLS), BF16),
             ((16, SLOTS * CELLS), F32), ((2, CELLS), F32),
@@ -672,26 +665,23 @@
     )
     image, back_near, back_far = call(
         couple_kernel,
-        "couple",
         [((80, CELLS), BF16), ((8, 128), F32), ((8, 128), F32)],
         [y, near, far, hot, picked, mask, columns],
     )
     back_near, back_far = across(back_near, back_far, 1)
-    (result,) = call(unpack_kernel, "unpack", [((1, 80, ROWS, COLS), BF16)], [image])
+    (result,) = call(unpack_kernel, [((1, 80, ROWS, COLS), BF16)], [image])
     cotangent, edge = call(
         cotangent_kernel,
-        "cotangent",
         [((80, CELLS), BF16), block],
         [image, back_near, back_far, columns, result],
         stay=(4,),
     )
     edge_above, edge_below = lat_pair(edge)
     above, below = lat_pair(cotangent)
-    (edges,) = call(edge_kernel, "edges_back", [block], [edge, edge_above, edge_below])
+    (edges,) = call(edge_kernel, [block], [edge, edge_above, edge_below])
     from_left, from_right = lon_pair(edges)
     inner, sides = call(
         adjoint_main_kernel,
-        "adjoint_main",
         [((80, 2 * CELLS), F32), ((2, 80, 128), F32)],
         [cotangent, above, below, edges, bwd1, bwd2, slope],
         [pltpu.VMEM((240, 8 * COLS), BF16), pltpu.VMEM((512, 6 * COLS), BF16)],
@@ -699,7 +689,6 @@
     )
     (product,) = call(
         adjoint_edge_kernel,
-        "adjoint_edge",
         [((1, 80, ROWS, COLS), BF16)],
         [sides, from_left, from_right, inner, edge_slope, bwd1, bwd2, back_near, back_far],
         limit=16,

time: 56.8 us -> 56.8 us (level)
  no operation moved by 1% of the time
where the time goes in v7:
time: 56.8 us; the launch traced here: 56 us
  starting transfers between devices  22.5 us (40%)
  waiting for transfers between devices  18.8 us (33%)
  Pallas kernels  14 us (25%)
  between operations  0.76 us (1%)
    pallas_call x12, Pallas kernels, call(): pl.pallas_call(kernel, out_shape=tuple((jax.ShapeDtypeStruct(shape, dtype...  14 us
    ppermute x4, starting transfers between devices, lat_pair(): lax.ppermute(block, 'lat', [((i + 1) % count, i) for i in range(count)])  9.31 us
    ppermute x2, starting transfers between devices, lon_pair(): lax.ppermute(block, 'lon', [((i + 1) % count, i) for i in range(count)])  5.19 us
    ppermute x2, starting transfers between devices, across(): same = lax.ppermute(near, 'comp', [(0, 1), (1, 0)])  4.97 us
    ppermute x2, waiting for transfers between devices, lon_pair(): lax.ppermute(block, 'lon', [(i, (i + 1) % count) for i in range(count)])  4.32 us
    ppermute x4, waiting for transfers between devices, lat_pair(): lax.ppermute(block, 'lat', [(i, (i + 1) % count) for i in range(count)])  4.11 us
    ppermute x4, waiting for transfers between devices, lat_pair(): lax.ppermute(block, 'lat', [((i + 1) % count, i) for i in range(count)])  3.95 us
    ppermute x2, waiting for transfers between devices, across(): return (same, lax.ppermute(far, ('comp', 'lon'), route))  3.73 us
  transfers between devices with their start and end apart: 16, of which 9 were waited for; matrix products, arithmetic and copies ran while one was open for 0% of the time, Pallas kernels for 15%

profile of v7, /device:TPU:8, one launch (start us, length us, event | category | flops | bytes accessed | tf_op | source)
XLA Modules:
  0.0 56.0 jit_solution(14072577756342858889)
XLA Ops:
  0.6 1.4 %shard_map.149 = (bf16[160,512]{1,0:T(8,128)(2,1)S(1)}, bf16[80,128]{1,0:T(8,128)(2,1)S(1)}) custom-call(bf16[1,80,2,256]{3,2,1,0:T(2,128)(2,1)} %state.1, bf16[1,80,2,256]{3,2,1,0:T(2,128)(2,1)} %direction.1), custom_call_target="tpu_custom_call" | custom-call | tf_op jit(solution)/shard_map/pallas_call | solution.py:553
  2.0 2.2 %collective-permute-start.1 = (bf16[160,512]{1,0:T(8,128)(2,1)S(1)}, bf16[160,512]{1,0:T(8,128)(2,1)S(1)}, u32[]{:S(2)}, u32[]{:S(2)}) collective-permute-start(bf16[160,512]{1,0:T(8,128)(2,1)S(1)} %get-tuple-element.25.own), channel_id=1, source_target_pairs={{32,0},{64,32},{96,64},{0,96},{33,1},{65,33},{97,65},{1,97},{34,2}... | collective-permute-start | bytes 491528 | tf_op jit(solution)/shard_map/ppermute | solution.py:566
  4.2 0.0 collective-permute-start
  4.2 2.0 %collective-permute-start.3 = (bf16[80,128]{1,0:T(8,128)(2,1)S(1)}, bf16[80,128]{1,0:T(8,128)(2,1)S(1)}, u32[]{:S(2)}, u32[]{:S(2)}) collective-permute-start(bf16[80,128]{1,0:T(8,128)(2,1)S(1)} %get-tuple-element.26.own), channel_id=1, source_target_pairs={{32,0},{64,32},{96,64},{0,96},{33,1},{65,33},{97,65},{1,97},{34,2}... | collective-permute-start | bytes 61448 | tf_op jit(solution)/shard_map/ppermute | solution.py:566
  6.3 0.0 collective-permute-start.2
  6.3 2.2 %collective-permute-done.3.below = bf16[80,128]{1,0:T(8,128)(2,1)S(1)} collective-permute-done((bf16[80,128]{1,0:T(8,128)(2,1)S(1)}, bf16[80,128]{1,0:T(8,128)(2,1)S(1)}, u32[]{:S(2)}, u32[]{:S(2)}) %collective-permute-start.3) | collective-permute-done | bytes 20512 | tf_op jit(solution)/shard_map/ppermute | solution.py:566
  8.5 2.1 %collective-permute-done.2.above = bf16[80,128]{1,0:T(8,128)(2,1)S(1)} collective-permute-done((bf16[80,128]{1,0:T(8,128)(2,1)S(1)}, bf16[80,128]{1,0:T(8,128)(2,1)S(1)}, u32[]{:S(2)}, u32[]{:S(2)}) %collective-permute-start.2) | collective-permute-done | bytes 20512 | tf_op jit(solution)/shard_map/ppermute | solution.py:565
  10.5 0.1 shard_map.150.refs_9_.edges
  10.6 5.1 %collective-permute-start.5 = (bf16[80,128]{1,0:T(8,128)(2,1)S(1)}, bf16[80,128]{1,0:T(8,128)(2,1)S(1)}, u32[]{:S(2)}, u32[]{:S(2)}) collective-permute-start(bf16[80,128]{1,0:T(8,128)(2,1)S(1)} %shard_map.150.refs_9_.edges), channel_id=1, source_target_pairs={{1,0},{2,1},{3,2},{4,3},{5,4},{6,5},{7,6},{8,7},{9,8},{10,9},{11,1... | collective-permute-start | bytes 61448 | tf_op jit(solution)/shard_map/ppermute | solution.py:573
  15.7 0.0 collective-permute-start.4
  15.7 1.8 %shard_map.151 = (bf16[512,720]{1,0:T(8,128)(2,1)S(1)}, bf16[240,1536]{1,0:T(8,128)(2,1)S(1)}, f32[512,8]{1,0:T(8,128)S(1)}) custom-call(bf16[9,80,512]{2,1,0:T(8,128)(2,1)} %bitcast.6, bf16[9,80,512]{2,1,0:T(8,128)(2,1)} %refs_0_.1, bf16[9,40,256]{2,1,0:T(8,128)(2,1)} %bitcast.8, bf16[9,40,256]{2,1,0:T(8,128)(2,1)} %refs_2_.1, f32[1,512]{1,0:T(1,128)} %bitcast.10, ...), custom_call_target="tpu_custom_call" | custom-call | tf_op jit(solution)/shard_map/pallas_call | solution.py:553
  17.6 0.0 collective-permute-done.1.below
  17.6 0.0 collective-permute-done.above
  17.6 2.4 %shard_map.152 = (f32[80,1024]{1,0:T(8,128)S(1)}, bf16[512,1536]{1,0:T(8,128)(2,1)S(1)}, f32[2,80,128]{2,1,0:T(8,128)S(1)}) custom-call(bf16[160,512]{1,0:T(8,128)(2,1)S(1)} %get-tuple-element.25.own, bf16[160,512]{1,0:T(8,128)(2,1)S(1)} %collective-permute-done.above, bf16[160,512]{1,0:T(8,128)(2,1)S(1)} %collective-permute-done.1.below, ...), custom_call_target="tpu_custom_call" | custom-call | tf_op jit(solution)/shard_map/pallas_call | solution.py:553
  20.0 0.0 collective-permute-done.5.from_right
  20.0 1.0 %collective-permute-done.4.from_left = bf16[80,128]{1,0:T(8,128)(2,1)S(1)} collective-permute-done((bf16[80,128]{1,0:T(8,128)(2,1)S(1)}, bf16[80,128]{1,0:T(8,128)(2,1)S(1)}, u32[]{:S(2)}, u32[]{:S(2)}) %collective-permute-start.4) | collective-permute-done | bytes 20512 | tf_op jit(solution)/shard_map/ppermute | solution.py:572
  21.1 1.1 %shard_map.153 = (f32[80,1024]{1,0:T(8,128)S(1)}, bf16[512,128]{1,0:T(8,128)(2,1)S(1)}, f32[8,128]{1,0:T(8,128)S(1)}) custom-call(bf16[160,512]{1,0:T(8,128)(2,1)S(1)} %get-tuple-element.25.own, f32[2,80,128]{2,1,0:T(8,128)S(1)} %get-tuple-element.30.sides, bf16[80,128]{1,0:T(8,128)(2,1)S(1)} %collective-permute-done.4.from_left, ...), custom_call_target="tpu_custom_call" | custom-call | tf_op jit(solution)/shard_map/pallas_call | solution.py:553
  22.2 2.5 %collective-permute-start.7 = (f32[8,128]{1,0:T(8,128)S(1)}, f32[8,128]{1,0:T(8,128)S(1)}, u32[]{:S(2)}, u32[]{:S(2)}) collective-permute-start(f32[8,128]{1,0:T(8,128)S(1)} %get-tuple-element.33.refs_7_), channel_id=1, source_target_pairs={{0,159},{1,128},{2,129},{3,130},{4,131},{5,132},{6,133},{7,134},{8... | collective-permute-start | bytes 12296 | tf_op jit(solution)/shard_map/ppermute | solution.py:584
  24.7 2.5 %collective-permute-start.6 = (f32[8,128]{1,0:T(8,128)S(1)}, f32[8,128]{1,0:T(8,128)S(1)}, u32[]{:S(2)}, u32[]{:S(2)}) collective-permute-start(f32[8,128]{1,0:T(8,128)S(1)} %get-tuple-element.33.refs_7_), channel_id=1, source_target_pairs={{0,128},{128,0},{1,129},{129,1},{2,130},{130,2},{3,131},{131,3},{4... | collective-permute-start | bytes 12296 | tf_op jit(solution)/shard_map/ppermute | solution.py:579
  27.2 1.8 %shard_map.154 = (bf16[512,720]{1,0:T(8,128)(2,1)S(1)}, bf16[240,1536]{1,0:T(8,128)(2,1)S(1)}, bf16[128,4096]{1,0:T(8,128)(2,1)S(1)}, f32[16,4096]{1,0:T(8,128)S(1)}, f32[2,512]{1,0:T(2,128)S(1)}) custom-call(bf16[9,80,512]{2,1,0:T(8,128)(2,1)} %refs_0_.1, bf16[9,80,512]{2,1,0:T(8,128)(2,1)} %bitcast.7, bf16[9,40,256]{2,1,0:T(8,128)(2,1)} %refs_2_.1, ...), custom_call_target="tpu_custom_call" | custom-call | tf_op jit(solution)/shard_map/pallas_call | solution.py:553
  28.9 0.0 collective-permute-done.7.far
  29.0 0.9 %collective-permute-done.6.near = f32[8,128]{1,0:T(8,128)S(1)} collective-permute-done((f32[8,128]{1,0:T(8,128)S(1)}, f32[8,128]{1,0:T(8,128)S(1)}, u32[]{:S(2)}, u32[]{:S(2)}) %collective-permute-start.6) | collective-permute-done | bytes 4128 | tf_op jit(solution)/shard_map/ppermute | solution.py:579
  29.8 0.9 %shard_map.155 = (bf16[80,512]{1,0:T(8,128)(2,1)S(1)}, f32[8,128]{1,0:T(8,128)S(1)}, f32[8,128]{1,0:T(8,128)S(1)}) custom-call(f32[80,1024]{1,0:T(8,128)S(1)} %get-tuple-element.32.y, f32[8,128]{1,0:T(8,128)S(1)} %collective-permute-done.6.near, f32[8,128]{1,0:T(8,128)S(1)} %collective-permute-done.7.far, bf16[128,4096]{1,0:T(8,128)(2,1)S(1)} %get-tuple-element.34.hot, ...), custom_call_target="tpu_custom_call" | custom-call | tf_op jit(solution)/shard_map/pallas_call | solution.py:553
  30.8 2.5 %collective-permute-start.8 = (f32[8,128]{1,0:T(8,128)S(1)}, f32[8,128]{1,0:T(8,128)S(1)}, u32[]{:S(2)}, u32[]{:S(2)}) collective-permute-start(f32[8,128]{1,0:T(8,128)S(1)} %get-tuple-element.38), channel_id=1, source_target_pairs={{0,128},{128,0},{1,129},{129,1},{2,130},{130,2},{3,131},{131,3},{4... | collective-permute-start | bytes 12296 | tf_op jit(solution)/shard_map/ppermute | solution.py:579
  33.3 0.0 collective-permute-start.9
  33.3 0.8 %shard_map.156.after = bf16[1,80,2,256]{3,2,1,0:T(2,128)(2,1)} custom-call(bf16[80,512]{1,0:T(8,128)(2,1)S(1)} %get-tuple-element.37.packed.image), custom_call_target="tpu_custom_call" | custom-call | tf_op jit(solution)/shard_map/pallas_call | solution.py:553
  34.1 1.8 %collective-permute-done.8.near = f32[8,128]{1,0:T(8,128)S(1)} collective-permute-done((f32[8,128]{1,0:T(8,128)S(1)}, f32[8,128]{1,0:T(8,128)S(1)}, u32[]{:S(2)}, u32[]{:S(2)}) %collective-permute-start.8) | collective-permute-done | bytes 4128 | tf_op jit(solution)/shard_map/ppermute | solution.py:579
  35.9 3.7 %collective-permute-done.9.far = f32[8,128]{1,0:T(8,128)S(1)} collective-permute-done((f32[8,128]{1,0:T(8,128)S(1)}, f32[8,128]{1,0:T(8,128)S(1)}, u32[]{:S(2)}, u32[]{:S(2)}) %collective-permute-start.9) | collective-permute-done | bytes 4128 | tf_op jit(solution)/shard_map/ppermute | solution.py:584
  39.6 0.2 shard_map.157
  39.8 3.0 %collective-permute-start.11 = (bf16[80,512]{1,0:T(8,128)(2,1)S(1)}, bf16[80,512]{1,0:T(8,128)(2,1)S(1)}, u32[]{:S(2)}, u32[]{:S(2)}) collective-permute-start(bf16[80,512]{1,0:T(8,128)(2,1)S(1)} %get-tuple-element.40.own), channel_id=1, source_target_pairs={{32,0},{64,32},{96,64},{0,96},{33,1},{65,33},{97,65},{1,97},{34,2}... | collective-permute-start | bytes 245768 | tf_op jit(solution)/shard_map/ppermute | solution.py:566
  42.8 0.0 collective-permute-start.10
  42.9 2.0 %collective-permute-start.13 = (bf16[80,128]{1,0:T(8,128)(2,1)S(1)}, bf16[80,128]{1,0:T(8,128)(2,1)S(1)}, u32[]{:S(2)}, u32[]{:S(2)}) collective-permute-start(bf16[80,128]{1,0:T(8,128)(2,1)S(1)} %get-tuple-element.41.own), channel_id=1, source_target_pairs={{32,0},{64,32},{96,64},{0,96},{33,1},{65,33},{97,65},{1,97},{34,2}... | collective-permute-start | bytes 61448 | tf_op jit(solution)/shard_map/ppermute | solution.py:566
  44.9 0.0 collective-permute-start.12
  44.9 1.8 %collective-permute-done.13.below = bf16[80,128]{1,0:T(8,128)(2,1)S(1)} collective-permute-done((bf16[80,128]{1,0:T(8,128)(2,1)S(1)}, bf16[80,128]{1,0:T(8,128)(2,1)S(1)}, u32[]{:S(2)}, u32[]{:S(2)}) %collective-permute-start.13) | collective-permute-done | bytes 20512 | tf_op jit(solution)/shard_map/ppermute | solution.py:566
  46.6 2.0 %collective-permute-done.12.above = bf16[80,128]{1,0:T(8,128)(2,1)S(1)} collective-permute-done((bf16[80,128]{1,0:T(8,128)(2,1)S(1)}, bf16[80,128]{1,0:T(8,128)(2,1)S(1)}, u32[]{:S(2)}, u32[]{:S(2)}) %collective-permute-start.12) | collective-permute-done | bytes 20512 | tf_op jit(solution)/shard_map/ppermute | solution.py:565
  48.7 0.1 shard_map.158.edges
  48.7 0.1 collective-permute-start.15
  48.8 0.5 collective-permute-start.14
  49.3 0.0 collective-permute-done.11.below
  49.3 0.0 collective-permute-done.10.above
  49.3 1.6 %shard_map.159 = (f32[80,1024]{1,0:T(8,128)S(1)}, f32[2,80,128]{2,1,0:T(8,128)S(1)}) custom-call(bf16[80,512]{1,0:T(8,128)(2,1)S(1)} %get-tuple-element.40.own, bf16[80,512]{1,0:T(8,128)(2,1)S(1)} %collective-permute-done.10.above, bf16[80,512]{1,0:T(8,128)(2,1)S(1)} %collective-permute-done.11.below, bf16[80,128]{1,0:T(8,128)(2,1)S(1)} %shard_map.158.edges, ...), custom_call_target="tpu_custom_call" | custom-call | tf_op jit(solution)/shard_map/pallas_call | solution.py:553
  50.9 0.0 collective-permute-done.15.from_right
  50.9 3.3 %collective-permute-done.14.from_left = bf16[80,128]{1,0:T(8,128)(2,1)S(1)} collective-permute-done((bf16[80,128]{1,0:T(8,128)(2,1)S(1)}, bf16[80,128]{1,0:T(8,128)(2,1)S(1)}, u32[]{:S(2)}, u32[]{:S(2)}) %collective-permute-start.14) | collective-permute-done | bytes 20512 | tf_op jit(solution)/shard_map/ppermute | solution.py:572
  54.2 1.8 %shard_map.160 = bf16[1,80,2,256]{3,2,1,0:T(2,128)(2,1)} custom-call(f32[2,80,128]{2,1,0:T(8,128)S(1)} %get-tuple-element.45.sides, bf16[80,128]{1,0:T(8,128)(2,1)S(1)} %collective-permute-done.14.from_left, bf16[80,128]{1,0:T(8,128)(2,1)S(1)} %collective-permute-done.15.from_right, f32[80,1024]{1,0:T(8,128)S(1)} %get-tuple-element.46.inner, ...), custom_call_target="tpu_custom_call" | custom-call | tf_op jit(solution)/shard_map/pallas_call | solution.py:553
Async XLA Ops:
  2.0 15.6 %collective-permute-start.1 = (bf16[160,512]{1,0:T(8,128)(2,1)S(1)}, bf16[160,512]{1,0:T(8,128)(2,1)S(1)}, u32[]{:S(2)}, u32[]{:S(2)}) collective-permute-start(bf16[160,512]{1,0:T(8,128)(2,1)S(1)} %get-tuple-element.25.own), channel_id=1, source_target_pairs={{32,0},{64,32},{96,64},{0,96},{33,1},{65,33},{97,65},{1,97},{34,2}... | collective-permute-start | bytes 491528 | tf_op jit(solution)/shard_map/ppermute | solution.py:566
  4.2 13.3 %collective-permute-start = (bf16[160,512]{1,0:T(8,128)(2,1)S(1)}, bf16[160,512]{1,0:T(8,128)(2,1)S(1)}, u32[]{:S(2)}, u32[]{:S(2)}) collective-permute-start(bf16[160,512]{1,0:T(8,128)(2,1)S(1)} %get-tuple-element.25.own), channel_id=1, source_target_pairs={{0,32},{32,64},{64,96},{96,0},{1,33},{33,65},{65,97},{97,1},{2,34}... | collective-permute-start | bytes 491528 | tf_op jit(solution)/shard_map/ppermute | solution.py:565
  4.2 4.2 %collective-permute-start.3 = (bf16[80,128]{1,0:T(8,128)(2,1)S(1)}, bf16[80,128]{1,0:T(8,128)(2,1)S(1)}, u32[]{:S(2)}, u32[]{:S(2)}) collective-permute-start(bf16[80,128]{1,0:T(8,128)(2,1)S(1)} %get-tuple-element.26.own), channel_id=1, source_target_pairs={{32,0},{64,32},{96,64},{0,96},{33,1},{65,33},{97,65},{1,97},{34,2}... | collective-permute-start | bytes 61448 | tf_op jit(solution)/shard_map/ppermute | solution.py:566
  6.3 4.3 %collective-permute-start.2 = (bf16[80,128]{1,0:T(8,128)(2,1)S(1)}, bf16[80,128]{1,0:T(8,128)(2,1)S(1)}, u32[]{:S(2)}, u32[]{:S(2)}) collective-permute-start(bf16[80,128]{1,0:T(8,128)(2,1)S(1)} %get-tuple-element.26.own), channel_id=1, source_target_pairs={{0,32},{32,64},{64,96},{96,0},{1,33},{33,65},{65,97},{97,1},{2,34}... | collective-permute-start | bytes 61448 | tf_op jit(solution)/shard_map/ppermute | solution.py:565
  10.6 9.4 %collective-permute-start.5 = (bf16[80,128]{1,0:T(8,128)(2,1)S(1)}, bf16[80,128]{1,0:T(8,128)(2,1)S(1)}, u32[]{:S(2)}, u32[]{:S(2)}) collective-permute-start(bf16[80,128]{1,0:T(8,128)(2,1)S(1)} %shard_map.150.refs_9_.edges), channel_id=1, source_target_pairs={{1,0},{2,1},{3,2},{4,3},{5,4},{6,5},{7,6},{8,7},{9,8},{10,9},{11,1... | collective-permute-start | bytes 61448 | tf_op jit(solution)/shard_map/ppermute | solution.py:573
  15.7 5.3 %collective-permute-start.4 = (bf16[80,128]{1,0:T(8,128)(2,1)S(1)}, bf16[80,128]{1,0:T(8,128)(2,1)S(1)}, u32[]{:S(2)}, u32[]{:S(2)}) collective-permute-start(bf16[80,128]{1,0:T(8,128)(2,1)S(1)} %shard_map.150.refs_9_.edges), channel_id=1, source_target_pairs={{0,1},{1,2},{2,3},{3,4},{4,5},{5,6},{6,7},{7,8},{8,9},{9,10},{10,1... | collective-permute-start | bytes 61448 | tf_op jit(solution)/shard_map/ppermute | solution.py:572
  22.2 6.8 %collective-permute-start.7 = (f32[8,128]{1,0:T(8,128)S(1)}, f32[8,128]{1,0:T(8,128)S(1)}, u32[]{:S(2)}, u32[]{:S(2)}) collective-permute-start(f32[8,128]{1,0:T(8,128)S(1)} %get-tuple-element.33.refs_7_), channel_id=1, source_target_pairs={{0,159},{1,128},{2,129},{3,130},{4,131},{5,132},{6,133},{7,134},{8... | collective-permute-start | bytes 12296 | tf_op jit(solution)/shard_map/ppermute | solution.py:584
  24.7 5.1 %collective-permute-start.6 = (f32[8,128]{1,0:T(8,128)S(1)}, f32[8,128]{1,0:T(8,128)S(1)}, u32[]{:S(2)}, u32[]{:S(2)}) collective-permute-start(f32[8,128]{1,0:T(8,128)S(1)} %get-tuple-element.33.refs_7_), channel_id=1, source_target_pairs={{0,128},{128,0},{1,129},{129,1},{2,130},{130,2},{3,131},{131,3},{4... | collective-permute-start | bytes 12296 | tf_op jit(solution)/shard_map/ppermute | solution.py:579
  30.8 5.1 %collective-permute-start.8 = (f32[8,128]{1,0:T(8,128)S(1)}, f32[8,128]{1,0:T(8,128)S(1)}, u32[]{:S(2)}, u32[]{:S(2)}) collective-permute-start(f32[8,128]{1,0:T(8,128)S(1)} %get-tuple-element.38), channel_id=1, source_target_pairs={{0,128},{128,0},{1,129},{129,1},{2,130},{130,2},{3,131},{131,3},{4... | collective-permute-start | bytes 12296 | tf_op jit(solution)/shard_map/ppermute | solution.py:579
  33.3 6.4 %collective-permute-start.9 = (f32[8,128]{1,0:T(8,128)S(1)}, f32[8,128]{1,0:T(8,128)S(1)}, u32[]{:S(2)}, u32[]{:S(2)}) collective-permute-start(f32[8,128]{1,0:T(8,128)S(1)} %get-tuple-element.39), channel_id=1, source_target_pairs={{0,129},{1,130},{2,131},{3,132},{4,133},{5,134},{6,135},{7,136},{8... | collective-permute-start | bytes 12296 | tf_op jit(solution)/shard_map/ppermute | solution.py:584
  39.8 9.5 %collective-permute-start.11 = (bf16[80,512]{1,0:T(8,128)(2,1)S(1)}, bf16[80,512]{1,0:T(8,128)(2,1)S(1)}, u32[]{:S(2)}, u32[]{:S(2)}) collective-permute-start(bf16[80,512]{1,0:T(8,128)(2,1)S(1)} %get-tuple-element.40.own), channel_id=1, source_target_pairs={{32,0},{64,32},{96,64},{0,96},{33,1},{65,33},{97,65},{1,97},{34,2}... | collective-permute-start | bytes 245768 | tf_op jit(solution)/shard_map/ppermute | solution.py:566
  42.8 6.5 %collective-permute-start.10 = (bf16[80,512]{1,0:T(8,128)(2,1)S(1)}, bf16[80,512]{1,0:T(8,128)(2,1)S(1)}, u32[]{:S(2)}, u32[]{:S(2)}) collective-permute-start(bf16[80,512]{1,0:T(8,128)(2,1)S(1)} %get-tuple-element.40.own), channel_id=1, source_target_pairs={{0,32},{32,64},{64,96},{96,0},{1,33},{33,65},{65,97},{97,1},{2,34}... | collective-permute-start | bytes 245768 | tf_op jit(solution)/shard_map/ppermute | solution.py:565
  42.9 3.8 %collective-permute-start.13 = (bf16[80,128]{1,0:T(8,128)(2,1)S(1)}, bf16[80,128]{1,0:T(8,128)(2,1)S(1)}, u32[]{:S(2)}, u32[]{:S(2)}) collective-permute-start(bf16[80,128]{1,0:T(8,128)(2,1)S(1)} %get-tuple-element.41.own), channel_id=1, source_target_pairs={{32,0},{64,32},{96,64},{0,96},{33,1},{65,33},{97,65},{1,97},{34,2}... | collective-permute-start | bytes 61448 | tf_op jit(solution)/shard_map/ppermute | solution.py:566
  44.9 3.8 %collective-permute-start.12 = (bf16[80,128]{1,0:T(8,128)(2,1)S(1)}, bf16[80,128]{1,0:T(8,128)(2,1)S(1)}, u32[]{:S(2)}, u32[]{:S(2)}) collective-permute-start(bf16[80,128]{1,0:T(8,128)(2,1)S(1)} %get-tuple-element.41.own), channel_id=1, source_target_pairs={{0,32},{32,64},{64,96},{96,0},{1,33},{33,65},{65,97},{97,1},{2,34}... | collective-permute-start | bytes 61448 | tf_op jit(solution)/shard_map/ppermute | solution.py:565
  48.7 2.2 %collective-permute-start.15 = (bf16[80,128]{1,0:T(8,128)(2,1)S(1)}, bf16[80,128]{1,0:T(8,128)(2,1)S(1)}, u32[]{:S(2)}, u32[]{:S(2)}) collective-permute-start(bf16[80,128]{1,0:T(8,128)(2,1)S(1)} %shard_map.158.edges), channel_id=1, source_target_pairs={{1,0},{2,1},{3,2},{4,3},{5,4},{6,5},{7,6},{8,7},{9,8},{10,9},{11,1... | collective-permute-start | bytes 61448 | tf_op jit(solution)/shard_map/ppermute | solution.py:573
  48.8 5.4 %collective-permute-start.14 = (bf16[80,128]{1,0:T(8,128)(2,1)S(1)}, bf16[80,128]{1,0:T(8,128)(2,1)S(1)}, u32[]{:S(2)}, u32[]{:S(2)}) collective-permute-start(bf16[80,128]{1,0:T(8,128)(2,1)S(1)} %shard_map.158.edges), channel_id=1, source_target_pairs={{0,1},{1,2},{2,3},{3,4},{4,5},{5,6},{6,7},{7,8},{8,9},{9,10},{10,1... | collective-permute-start | bytes 61448 | tf_op jit(solution)/shard_map/ppermute | solution.py:572

commit v8 on v7

--- a/solution.py
+++ b/solution.py
@@ -198,7 +198,7 @@
     return result.astype(BF16)
 
 
-def edge_kernel(own, above, below, merged):
+def edge_kernel(own, above, below, after, merged):
     upper = jnp.where(at_top(), 0.0, 1.0).astype(F32)
     lower = jnp.where(at_bottom(), 0.0, 1.0).astype(F32)
     total = own[...].astype(F32) + pltpu.roll(above[...].astype(F32), 120, 1) * upper
@@ -614,8 +614,6 @@
     )
     edge_above, edge_below = lat_pair(edge)
     above, below = lat_pair(own)
-    (edges,) = call(edge_kernel, [block], [edge, edge_above, edge_below])
-    from_left, from_right = lon_pair(edges)
     first_a = air_first.transpose(0, 2, 1)
     first_o = sea_first.transpose(0, 2, 1)
     raw = [
@@ -632,11 +630,13 @@
     fwd1, fwd2, columns = call(
         forward_kernel,
         [((512, 720), BF16), ((240, 1536), BF16), ((512, 8), F32)],
-        raw + [edges],
+        raw + [edge],
         held(raw),
         limit=16,
         stay=range(len(raw)),
     )
+    (edges,) = call(edge_kernel, [block], [edge, edge_above, edge_below, columns])
+    from_left, from_right = lon_pair(edges)
     inner, slope, sides = call(
         tangent_main_kernel,
         [((80, 2 * CELLS), F32), ((512, 6 * COLS), BF16), ((2, 80, 128), F32)],
@@ -678,7 +678,7 @@
     )
     edge_above, edge_below = lat_pair(edge)
     above, below = lat_pair(cotangent)
-    (edges,) = call(edge_kernel, [block], [edge, edge_above, edge_below])
+    (edges,) = call(edge_kernel, [block], [edge, edge_above, edge_below, columns])
     from_left, from_right = lon_pair(edges)
     inner, sides = call(
         adjoint_main_kernel,

time: 56.8 us -> 55.1 us (0.970)
  starting transfers between devices: 22.5 us -> 21.4 us
  waiting for transfers between devices: 18.8 us -> 18.1 us
    ppermute x2, waiting for transfers between devices: 4.32 us -> 6.18 us  [lon_pair(): lax.ppermute(block, 'lon', [(i, (i + 1) % count) for i in range(count)])]
    ppermute x4, waiting for transfers between devices: 3.95 us -> 2.13 us  [lat_pair(): lax.ppermute(block, 'lat', [((i + 1) % count, i) for i in range(count)])]
    ppermute x2, starting transfers between devices: 4.97 us -> 3.98 us  [across(): same = lax.ppermute(near, 'comp', [(0, 1), (1, 0)])]
  transfers between devices with their start and end apart: 16 -> 16, of which waited for: 9 -> 9; matrix products, arithmetic and copies ran while one was open for 0% -> 0% of each run, Pallas kernels for 15% -> 16%
where the time goes in v8:
time: 55.1 us; the launch traced here: 54.2 us
  starting transfers between devices  21.4 us (39%)
  waiting for transfers between devices  18.1 us (33%)
  Pallas kernels  14 us (25%)
  between operations  0.75 us (1%)
    pallas_call x12, Pallas kernels, call(): pl.pallas_call(kernel, out_shape=tuple((jax.ShapeDtypeStruct(shape, dtype...  14 us
    ppermute x4, starting transfers between devices, lat_pair(): lax.ppermute(block, 'lat', [((i + 1) % count, i) for i in range(count)])  9.32 us
    ppermute x2, waiting for transfers between devices, lon_pair(): lax.ppermute(block, 'lon', [(i, (i + 1) % count) for i in range(count)])  6.18 us
    ppermute x2, starting transfers between devices, lon_pair(): lax.ppermute(block, 'lon', [((i + 1) % count, i) for i in range(count)])  5.19 us
    ppermute x4, waiting for transfers between devices, lat_pair(): lax.ppermute(block, 'lat', [(i, (i + 1) % count) for i in range(count)])  4.11 us
    ppermute x2, starting transfers between devices, across(): same = lax.ppermute(near, 'comp', [(0, 1), (1, 0)])  3.98 us
    ppermute x2, waiting for transfers between devices, across(): return (same, lax.ppermute(far, ('comp', 'lon'), route))  3.23 us
    ppermute x2, starting transfers between devices, across(): return (same, lax.ppermute(far, ('comp', 'lon'), route))  2.43 us
  transfers between devices with their start and end apart: 16, of which 9 were waited for; matrix products, arithmetic and copies ran while one was open for 0% of the time, Pallas kernels for 16%

profile of v8, /device:TPU:8, one launch (start us, length us, event | category | flops | bytes accessed | tf_op | source)
XLA Modules:
  0.0 54.2 jit_solution(257858881828958300)
XLA Ops:
  0.6 1.4 %shard_map.149 = (bf16[160,512]{1,0:T(8,128)(2,1)S(1)}, bf16[80,128]{1,0:T(8,128)(2,1)S(1)}) custom-call(bf16[1,80,2,256]{3,2,1,0:T(2,128)(2,1)} %state.1, bf16[1,80,2,256]{3,2,1,0:T(2,128)(2,1)} %direction.1), custom_call_target="tpu_custom_call" | custom-call | tf_op jit(solution)/shard_map/pallas_call | solution.py:553
  2.0 2.2 %collective-permute-start.1 = (bf16[160,512]{1,0:T(8,128)(2,1)S(1)}, bf16[160,512]{1,0:T(8,128)(2,1)S(1)}, u32[]{:S(2)}, u32[]{:S(2)}) collective-permute-start(bf16[160,512]{1,0:T(8,128)(2,1)S(1)} %get-tuple-element.25.own), channel_id=1, source_target_pairs={{32,0},{64,32},{96,64},{0,96},{33,1},{65,33},{97,65},{1,97},{34,2}... | collective-permute-start | bytes 491528 | tf_op jit(solution)/shard_map/ppermute | solution.py:566
  4.2 0.0 collective-permute-start
  4.2 2.0 %collective-permute-start.3 = (bf16[80,128]{1,0:T(8,128)(2,1)S(1)}, bf16[80,128]{1,0:T(8,128)(2,1)S(1)}, u32[]{:S(2)}, u32[]{:S(2)}) collective-permute-start(bf16[80,128]{1,0:T(8,128)(2,1)S(1)} %get-tuple-element.26.refs_9_.own), channel_id=1, source_target_pairs={{32,0},{64,32},{96,64},{0,96},{33,1},{65,33},{97,65},{1,97},{34,2}... | collective-permute-start | bytes 61448 | tf_op jit(solution)/shard_map/ppermute | solution.py:566
  6.3 0.0 collective-permute-start.2
  6.3 1.8 %shard_map.150 = (bf16[512,720]{1,0:T(8,128)(2,1)S(1)}, bf16[240,1536]{1,0:T(8,128)(2,1)S(1)}, f32[512,8]{1,0:T(8,128)S(1)}) custom-call(bf16[9,80,512]{2,1,0:T(8,128)(2,1)} %bitcast.6, bf16[9,80,512]{2,1,0:T(8,128)(2,1)} %refs_0_.1, bf16[9,40,256]{2,1,0:T(8,128)(2,1)} %bitcast.8, bf16[9,40,256]{2,1,0:T(8,128)(2,1)} %refs_2_.1, f32[1,512]{1,0:T(1,128)} %bitcast.10, ...), custom_call_target="tpu_custom_call" | custom-call | tf_op jit(solution)/shard_map/pallas_call | solution.py:553
  8.1 0.4 collective-permute-done.3.below
  8.5 2.1 %collective-permute-done.2.above = bf16[80,128]{1,0:T(8,128)(2,1)S(1)} collective-permute-done((bf16[80,128]{1,0:T(8,128)(2,1)S(1)}, bf16[80,128]{1,0:T(8,128)(2,1)S(1)}, u32[]{:S(2)}, u32[]{:S(2)}) %collective-permute-start.2) | collective-permute-done | bytes 20512 | tf_op jit(solution)/shard_map/ppermute | solution.py:565
  10.5 0.1 shard_map.151.edges
  10.6 5.1 %collective-permute-start.5 = (bf16[80,128]{1,0:T(8,128)(2,1)S(1)}, bf16[80,128]{1,0:T(8,128)(2,1)S(1)}, u32[]{:S(2)}, u32[]{:S(2)}) collective-permute-start(bf16[80,128]{1,0:T(8,128)(2,1)S(1)} %shard_map.151.edges), channel_id=1, source_target_pairs={{1,0},{2,1},{3,2},{4,3},{5,4},{6,5},{7,6},{8,7},{9,8},{10,9},{11,1... | collective-permute-start | bytes 61448 | tf_op jit(solution)/shard_map/ppermute | solution.py:573
  15.7 0.0 collective-permute-start.4
  15.7 0.0 collective-permute-done.1.below
  15.7 0.0 collective-permute-done.above
  15.8 2.4 %shard_map.152 = (f32[80,1024]{1,0:T(8,128)S(1)}, bf16[512,1536]{1,0:T(8,128)(2,1)S(1)}, f32[2,80,128]{2,1,0:T(8,128)S(1)}) custom-call(bf16[160,512]{1,0:T(8,128)(2,1)S(1)} %get-tuple-element.25.own, bf16[160,512]{1,0:T(8,128)(2,1)S(1)} %collective-permute-done.above, bf16[160,512]{1,0:T(8,128)(2,1)S(1)} %collective-permute-done.1.below, ...), custom_call_target="tpu_custom_call" | custom-call | tf_op jit(solution)/shard_map/pallas_call | solution.py:553
  18.2 0.0 collective-permute-done.5.from_right
  18.2 2.9 %collective-permute-done.4.from_left = bf16[80,128]{1,0:T(8,128)(2,1)S(1)} collective-permute-done((bf16[80,128]{1,0:T(8,128)(2,1)S(1)}, bf16[80,128]{1,0:T(8,128)(2,1)S(1)}, u32[]{:S(2)}, u32[]{:S(2)}) %collective-permute-start.4) | collective-permute-done | bytes 20512 | tf_op jit(solution)/shard_map/ppermute | solution.py:572
  21.1 1.1 %shard_map.153 = (f32[80,1024]{1,0:T(8,128)S(1)}, bf16[512,128]{1,0:T(8,128)(2,1)S(1)}, f32[8,128]{1,0:T(8,128)S(1)}) custom-call(bf16[160,512]{1,0:T(8,128)(2,1)S(1)} %get-tuple-element.25.own, f32[2,80,128]{2,1,0:T(8,128)S(1)} %get-tuple-element.30.sides, bf16[80,128]{1,0:T(8,128)(2,1)S(1)} %collective-permute-done.4.from_left, ...), custom_call_target="tpu_custom_call" | custom-call | tf_op jit(solution)/shard_map/pallas_call | solution.py:553
  22.2 1.2 %collective-permute-start.7 = (f32[8,128]{1,0:T(8,128)S(1)}, f32[8,128]{1,0:T(8,128)S(1)}, u32[]{:S(2)}, u32[]{:S(2)}) collective-permute-start(f32[8,128]{1,0:T(8,128)S(1)} %get-tuple-element.33.refs_7_), channel_id=1, source_target_pairs={{0,159},{1,128},{2,129},{3,130},{4,131},{5,132},{6,133},{7,134},{8... | collective-permute-start | bytes 12296 | tf_op jit(solution)/shard_map/ppermute | solution.py:584
  23.3 2.0 %collective-permute-start.6 = (f32[8,128]{1,0:T(8,128)S(1)}, f32[8,128]{1,0:T(8,128)S(1)}, u32[]{:S(2)}, u32[]{:S(2)}) collective-permute-start(f32[8,128]{1,0:T(8,128)S(1)} %get-tuple-element.33.refs_7_), channel_id=1, source_target_pairs={{0,128},{128,0},{1,129},{129,1},{2,130},{130,2},{3,131},{131,3},{4... | collective-permute-start | bytes 12296 | tf_op jit(solution)/shard_map/ppermute | solution.py:579
  25.3 1.8 %shard_map.154 = (bf16[512,720]{1,0:T(8,128)(2,1)S(1)}, bf16[240,1536]{1,0:T(8,128)(2,1)S(1)}, bf16[128,4096]{1,0:T(8,128)(2,1)S(1)}, f32[16,4096]{1,0:T(8,128)S(1)}, f32[2,512]{1,0:T(2,128)S(1)}) custom-call(bf16[9,80,512]{2,1,0:T(8,128)(2,1)} %refs_0_.1, bf16[9,80,512]{2,1,0:T(8,128)(2,1)} %bitcast.7, bf16[9,40,256]{2,1,0:T(8,128)(2,1)} %refs_2_.1, ...), custom_call_target="tpu_custom_call" | custom-call | tf_op jit(solution)/shard_map/pallas_call | solution.py:553
  27.1 0.0 collective-permute-done.7.far
  27.1 1.4 %collective-permute-done.6.near = f32[8,128]{1,0:T(8,128)S(1)} collective-permute-done((f32[8,128]{1,0:T(8,128)S(1)}, f32[8,128]{1,0:T(8,128)S(1)}, u32[]{:S(2)}, u32[]{:S(2)}) %collective-permute-start.6) | collective-permute-done | bytes 4128 | tf_op jit(solution)/shard_map/ppermute | solution.py:579
  28.5 0.9 %shard_map.155 = (bf16[80,512]{1,0:T(8,128)(2,1)S(1)}, f32[8,128]{1,0:T(8,128)S(1)}, f32[8,128]{1,0:T(8,128)S(1)}) custom-call(f32[80,1024]{1,0:T(8,128)S(1)} %get-tuple-element.32.y, f32[8,128]{1,0:T(8,128)S(1)} %collective-permute-done.6.near, f32[8,128]{1,0:T(8,128)S(1)} %collective-permute-done.7.far, bf16[128,4096]{1,0:T(8,128)(2,1)S(1)} %get-tuple-element.34.hot, ...), custom_call_target="tpu_custom_call" | custom-call | tf_op jit(solution)/shard_map/pallas_call | solution.py:553
  29.4 2.0 %collective-permute-start.8 = (f32[8,128]{1,0:T(8,128)S(1)}, f32[8,128]{1,0:T(8,128)S(1)}, u32[]{:S(2)}, u32[]{:S(2)}) collective-permute-start(f32[8,128]{1,0:T(8,128)S(1)} %get-tuple-element.38), channel_id=1, source_target_pairs={{0,128},{128,0},{1,129},{129,1},{2,130},{130,2},{3,131},{131,3},{4... | collective-permute-start | bytes 12296 | tf_op jit(solution)/shard_map/ppermute | solution.py:579
  31.4 1.3 %collective-permute-start.9 = (f32[8,128]{1,0:T(8,128)S(1)}, f32[8,128]{1,0:T(8,128)S(1)}, u32[]{:S(2)}, u32[]{:S(2)}) collective-permute-start(f32[8,128]{1,0:T(8,128)S(1)} %get-tuple-element.39), channel_id=1, source_target_pairs={{0,129},{1,130},{2,131},{3,132},{4,133},{5,134},{6,135},{7,136},{8... | collective-permute-start | bytes 12296 | tf_op jit(solution)/shard_map/ppermute | solution.py:584
  32.7 0.8 %shard_map.156.after = bf16[1,80,2,256]{3,2,1,0:T(2,128)(2,1)} custom-call(bf16[80,512]{1,0:T(8,128)(2,1)S(1)} %get-tuple-element.37.packed.image), custom_call_target="tpu_custom_call" | custom-call | tf_op jit(solution)/shard_map/pallas_call | solution.py:553
  33.5 1.0 %collective-permute-done.8.near = f32[8,128]{1,0:T(8,128)S(1)} collective-permute-done((f32[8,128]{1,0:T(8,128)S(1)}, f32[8,128]{1,0:T(8,128)S(1)}, u32[]{:S(2)}, u32[]{:S(2)}) %collective-permute-start.8) | collective-permute-done | bytes 4128 | tf_op jit(solution)/shard_map/ppermute | solution.py:579
  34.5 3.2 %collective-permute-done.9.far = f32[8,128]{1,0:T(8,128)S(1)} collective-permute-done((f32[8,128]{1,0:T(8,128)S(1)}, f32[8,128]{1,0:T(8,128)S(1)}, u32[]{:S(2)}, u32[]{:S(2)}) %collective-permute-start.9) | collective-permute-done | bytes 4128 | tf_op jit(solution)/shard_map/ppermute | solution.py:584
  37.8 0.2 shard_map.157
  38.0 3.0 %collective-permute-start.11 = (bf16[80,512]{1,0:T(8,128)(2,1)S(1)}, bf16[80,512]{1,0:T(8,128)(2,1)S(1)}, u32[]{:S(2)}, u32[]{:S(2)}) collective-permute-start(bf16[80,512]{1,0:T(8,128)(2,1)S(1)} %get-tuple-element.40.own), channel_id=1, source_target_pairs={{32,0},{64,32},{96,64},{0,96},{33,1},{65,33},{97,65},{1,97},{34,2}... | collective-permute-start | bytes 245768 | tf_op jit(solution)/shard_map/ppermute | solution.py:566
  41.0 0.0 collective-permute-start.10
  41.0 2.0 %collective-permute-start.13 = (bf16[80,128]{1,0:T(8,128)(2,1)S(1)}, bf16[80,128]{1,0:T(8,128)(2,1)S(1)}, u32[]{:S(2)}, u32[]{:S(2)}) collective-permute-start(bf16[80,128]{1,0:T(8,128)(2,1)S(1)} %get-tuple-element.41.own), channel_id=1, source_target_pairs={{32,0},{64,32},{96,64},{0,96},{33,1},{65,33},{97,65},{1,97},{34,2}... | collective-permute-start | bytes 61448 | tf_op jit(solution)/shard_map/ppermute | solution.py:566
  43.0 0.0 collective-permute-start.12
  43.0 1.8 %collective-permute-done.13.below = bf16[80,128]{1,0:T(8,128)(2,1)S(1)} collective-permute-done((bf16[80,128]{1,0:T(8,128)(2,1)S(1)}, bf16[80,128]{1,0:T(8,128)(2,1)S(1)}, u32[]{:S(2)}, u32[]{:S(2)}) %collective-permute-start.13) | collective-permute-done | bytes 20512 | tf_op jit(solution)/shard_map/ppermute | solution.py:566
  44.8 2.0 %collective-permute-done.12.above = bf16[80,128]{1,0:T(8,128)(2,1)S(1)} collective-permute-done((bf16[80,128]{1,0:T(8,128)(2,1)S(1)}, bf16[80,128]{1,0:T(8,128)(2,1)S(1)}, u32[]{:S(2)}, u32[]{:S(2)}) %collective-permute-start.12) | collective-permute-done | bytes 20512 | tf_op jit(solution)/shard_map/ppermute | solution.py:565
  46.8 0.1 shard_map.158.edges
  46.9 0.1 collective-permute-start.15
  47.0 0.5 collective-permute-start.14
  47.5 0.0 collective-permute-done.11.below
  47.5 0.0 collective-permute-done.10.above
  47.5 1.6 %shard_map.159 = (f32[80,1024]{1,0:T(8,128)S(1)}, f32[2,80,128]{2,1,0:T(8,128)S(1)}) custom-call(bf16[80,512]{1,0:T(8,128)(2,1)S(1)} %get-tuple-element.40.own, bf16[80,512]{1,0:T(8,128)(2,1)S(1)} %collective-permute-done.10.above, bf16[80,512]{1,0:T(8,128)(2,1)S(1)} %collective-permute-done.11.below, bf16[80,128]{1,0:T(8,128)(2,1)S(1)} %shard_map.158.edges, ...), custom_call_target="tpu_custom_call" | custom-call | tf_op jit(solution)/shard_map/pallas_call | solution.py:553
  49.1 0.0 collective-permute-done.15.from_right
  49.1 3.3 %collective-permute-done.14.from_left = bf16[80,128]{1,0:T(8,128)(2,1)S(1)} collective-permute-done((bf16[80,128]{1,0:T(8,128)(2,1)S(1)}, bf16[80,128]{1,0:T(8,128)(2,1)S(1)}, u32[]{:S(2)}, u32[]{:S(2)}) %collective-permute-start.14) | collective-permute-done | bytes 20512 | tf_op jit(solution)/shard_map/ppermute | solution.py:572
  52.4 1.8 %shard_map.160 = bf16[1,80,2,256]{3,2,1,0:T(2,128)(2,1)} custom-call(f32[2,80,128]{2,1,0:T(8,128)S(1)} %get-tuple-element.45.sides, bf16[80,128]{1,0:T(8,128)(2,1)S(1)} %collective-permute-done.14.from_left, bf16[80,128]{1,0:T(8,128)(2,1)S(1)} %collective-permute-done.15.from_right, f32[80,1024]{1,0:T(8,128)S(1)} %get-tuple-element.46.inner, ...), custom_call_target="tpu_custom_call" | custom-call | tf_op jit(solution)/shard_map/pallas_call | solution.py:553
Async XLA Ops:
  2.0 13.7 %collective-permute-start.1 = (bf16[160,512]{1,0:T(8,128)(2,1)S(1)}, bf16[160,512]{1,0:T(8,128)(2,1)S(1)}, u32[]{:S(2)}, u32[]{:S(2)}) collective-permute-start(bf16[160,512]{1,0:T(8,128)(2,1)S(1)} %get-tuple-element.25.own), channel_id=1, source_target_pairs={{32,0},{64,32},{96,64},{0,96},{33,1},{65,33},{97,65},{1,97},{34,2}... | collective-permute-start | bytes 491528 | tf_op jit(solution)/shard_map/ppermute | solution.py:566
  4.2 11.5 %collective-permute-start = (bf16[160,512]{1,0:T(8,128)(2,1)S(1)}, bf16[160,512]{1,0:T(8,128)(2,1)S(1)}, u32[]{:S(2)}, u32[]{:S(2)}) collective-permute-start(bf16[160,512]{1,0:T(8,128)(2,1)S(1)} %get-tuple-element.25.own), channel_id=1, source_target_pairs={{0,32},{32,64},{64,96},{96,0},{1,33},{33,65},{65,97},{97,1},{2,34}... | collective-permute-start | bytes 491528 | tf_op jit(solution)/shard_map/ppermute | solution.py:565
  4.2 4.2 %collective-permute-start.3 = (bf16[80,128]{1,0:T(8,128)(2,1)S(1)}, bf16[80,128]{1,0:T(8,128)(2,1)S(1)}, u32[]{:S(2)}, u32[]{:S(2)}) collective-permute-start(bf16[80,128]{1,0:T(8,128)(2,1)S(1)} %get-tuple-element.26.refs_9_.own), channel_id=1, source_target_pairs={{32,0},{64,32},{96,64},{0,96},{33,1},{65,33},{97,65},{1,97},{34,2}... | collective-permute-start | bytes 61448 | tf_op jit(solution)/shard_map/ppermute | solution.py:566
  6.3 4.3 %collective-permute-start.2 = (bf16[80,128]{1,0:T(8,128)(2,1)S(1)}, bf16[80,128]{1,0:T(8,128)(2,1)S(1)}, u32[]{:S(2)}, u32[]{:S(2)}) collective-permute-start(bf16[80,128]{1,0:T(8,128)(2,1)S(1)} %get-tuple-element.26.refs_9_.own), channel_id=1, source_target_pairs={{0,32},{32,64},{64,96},{96,0},{1,33},{33,65},{65,97},{97,1},{2,34}... | collective-permute-start | bytes 61448 | tf_op jit(solution)/shard_map/ppermute | solution.py:565
  10.6 7.5 %collective-permute-start.5 = (bf16[80,128]{1,0:T(8,128)(2,1)S(1)}, bf16[80,128]{1,0:T(8,128)(2,1)S(1)}, u32[]{:S(2)}, u32[]{:S(2)}) collective-permute-start(bf16[80,128]{1,0:T(8,128)(2,1)S(1)} %shard_map.151.edges), channel_id=1, source_target_pairs={{1,0},{2,1},{3,2},{4,3},{5,4},{6,5},{7,6},{8,7},{9,8},{10,9},{11,1... | collective-permute-start | bytes 61448 | tf_op jit(solution)/shard_map/ppermute | solution.py:573
  15.7 5.3 %collective-permute-start.4 = (bf16[80,128]{1,0:T(8,128)(2,1)S(1)}, bf16[80,128]{1,0:T(8,128)(2,1)S(1)}, u32[]{:S(2)}, u32[]{:S(2)}) collective-permute-start(bf16[80,128]{1,0:T(8,128)(2,1)S(1)} %shard_map.151.edges), channel_id=1, source_target_pairs={{0,1},{1,2},{2,3},{3,4},{4,5},{5,6},{6,7},{7,8},{8,9},{9,10},{10,1... | collective-permute-start | bytes 61448 | tf_op jit(solution)/shard_map/ppermute | solution.py:572
  22.2 4.9 %collective-permute-start.7 = (f32[8,128]{1,0:T(8,128)S(1)}, f32[8,128]{1,0:T(8,128)S(1)}, u32[]{:S(2)}, u32[]{:S(2)}) collective-permute-start(f32[8,128]{1,0:T(8,128)S(1)} %get-tuple-element.33.refs_7_), channel_id=1, source_target_pairs={{0,159},{1,128},{2,129},{3,130},{4,131},{5,132},{6,133},{7,134},{8... | collective-permute-start | bytes 12296 | tf_op jit(solution)/shard_map/ppermute | solution.py:584
  23.3 5.1 %collective-permute-start.6 = (f32[8,128]{1,0:T(8,128)S(1)}, f32[8,128]{1,0:T(8,128)S(1)}, u32[]{:S(2)}, u32[]{:S(2)}) collective-permute-start(f32[8,128]{1,0:T(8,128)S(1)} %get-tuple-element.33.refs_7_), channel_id=1, source_target_pairs={{0,128},{128,0},{1,129},{129,1},{2,130},{130,2},{3,131},{131,3},{4... | collective-permute-start | bytes 12296 | tf_op jit(solution)/shard_map/ppermute | solution.py:579
  29.4 5.1 %collective-permute-start.8 = (f32[8,128]{1,0:T(8,128)S(1)}, f32[8,128]{1,0:T(8,128)S(1)}, u32[]{:S(2)}, u32[]{:S(2)}) collective-permute-start(f32[8,128]{1,0:T(8,128)S(1)} %get-tuple-element.38), channel_id=1, source_target_pairs={{0,128},{128,0},{1,129},{129,1},{2,130},{130,2},{3,131},{131,3},{4... | collective-permute-start | bytes 12296 | tf_op jit(solution)/shard_map/ppermute | solution.py:579
  31.4 6.4 %collective-permute-start.9 = (f32[8,128]{1,0:T(8,128)S(1)}, f32[8,128]{1,0:T(8,128)S(1)}, u32[]{:S(2)}, u32[]{:S(2)}) collective-permute-start(f32[8,128]{1,0:T(8,128)S(1)} %get-tuple-element.39), channel_id=1, source_target_pairs={{0,129},{1,130},{2,131},{3,132},{4,133},{5,134},{6,135},{7,136},{8... | collective-permute-start | bytes 12296 | tf_op jit(solution)/shard_map/ppermute | solution.py:584
  38.0 9.5 %collective-permute-start.11 = (bf16[80,512]{1,0:T(8,128)(2,1)S(1)}, bf16[80,512]{1,0:T(8,128)(2,1)S(1)}, u32[]{:S(2)}, u32[]{:S(2)}) collective-permute-start(bf16[80,512]{1,0:T(8,128)(2,1)S(1)} %get-tuple-element.40.own), channel_id=1, source_target_pairs={{32,0},{64,32},{96,64},{0,96},{33,1},{65,33},{97,65},{1,97},{34,2}... | collective-permute-start | bytes 245768 | tf_op jit(solution)/shard_map/ppermute | solution.py:566
  41.0 6.5 %collective-permute-start.10 = (bf16[80,512]{1,0:T(8,128)(2,1)S(1)}, bf16[80,512]{1,0:T(8,128)(2,1)S(1)}, u32[]{:S(2)}, u32[]{:S(2)}) collective-permute-start(bf16[80,512]{1,0:T(8,128)(2,1)S(1)} %get-tuple-element.40.own), channel_id=1, source_target_pairs={{0,32},{32,64},{64,96},{96,0},{1,33},{33,65},{65,97},{97,1},{2,34}... | collective-permute-start | bytes 245768 | tf_op jit(solution)/shard_map/ppermute | solution.py:565
  41.0 3.8 %collective-permute-start.13 = (bf16[80,128]{1,0:T(8,128)(2,1)S(1)}, bf16[80,128]{1,0:T(8,128)(2,1)S(1)}, u32[]{:S(2)}, u32[]{:S(2)}) collective-permute-start(bf16[80,128]{1,0:T(8,128)(2,1)S(1)} %get-tuple-element.41.own), channel_id=1, source_target_pairs={{32,0},{64,32},{96,64},{0,96},{33,1},{65,33},{97,65},{1,97},{34,2}... | collective-permute-start | bytes 61448 | tf_op jit(solution)/shard_map/ppermute | solution.py:566
  43.0 3.8 %collective-permute-start.12 = (bf16[80,128]{1,0:T(8,128)(2,1)S(1)}, bf16[80,128]{1,0:T(8,128)(2,1)S(1)}, u32[]{:S(2)}, u32[]{:S(2)}) collective-permute-start(bf16[80,128]{1,0:T(8,128)(2,1)S(1)} %get-tuple-element.41.own), channel_id=1, source_target_pairs={{0,32},{32,64},{64,96},{96,0},{1,33},{33,65},{65,97},{97,1},{2,34}... | collective-permute-start | bytes 61448 | tf_op jit(solution)/shard_map/ppermute | solution.py:565
  46.9 2.2 %collective-permute-start.15 = (bf16[80,128]{1,0:T(8,128)(2,1)S(1)}, bf16[80,128]{1,0:T(8,128)(2,1)S(1)}, u32[]{:S(2)}, u32[]{:S(2)}) collective-permute-start(bf16[80,128]{1,0:T(8,128)(2,1)S(1)} %shard_map.158.edges), channel_id=1, source_target_pairs={{1,0},{2,1},{3,2},{4,3},{5,4},{6,5},{7,6},{8,7},{9,8},{10,9},{11,1... | collective-permute-start | bytes 61448 | tf_op jit(solution)/shard_map/ppermute | solution.py:573
  47.0 5.4 %collective-permute-start.14 = (bf16[80,128]{1,0:T(8,128)(2,1)S(1)}, bf16[80,128]{1,0:T(8,128)(2,1)S(1)}, u32[]{:S(2)}, u32[]{:S(2)}) collective-permute-start(bf16[80,128]{1,0:T(8,128)(2,1)S(1)} %shard_map.158.edges), channel_id=1, source_target_pairs={{0,1},{1,2},{2,3},{3,4},{4,5},{5,6},{6,7},{7,8},{8,9},{9,10},{10,1... | collective-permute-start | bytes 61448 | tf_op jit(solution)/shard_map/ppermute | solution.py:572

commit v9 on v8

--- a/solution.py
+++ b/solution.py
@@ -264,10 +264,13 @@
             sides[i] = side
 
 
-def edge_stack(sides, from_left, from_right, fine):
+def edge_stack(sides, near, far, fine):
     both = []
-    for i, ref in enumerate((from_left, from_right)):
-        rows = ref[...].astype(F32)
+    even = lax.axis_index("lon") % 2 == 0
+    near, far = near[...].astype(F32), far[...].astype(F32)
+    from_left = jnp.where(even, far, near)
+    from_right = jnp.where(even, near, far)
+    for i, rows in enumerate((from_left, from_right)):
         rows = fine_lanes(rows) if fine else rows
         side = sides[i, :40, :] if fine else sides[i]
         head = (lane_iota(rows.shape) & 3) < 2
@@ -569,9 +572,10 @@
 
 def lon_pair(block):
     count = lax.axis_size("lon")
-    from_left = lax.ppermute(block, "lon", [(i, (i + 1) % count) for i in range(count)])
-    from_right = lax.ppermute(block, "lon", [((i + 1) % count, i) for i in range(count)])
-    return from_left, from_right
+    near = lax.ppermute(block, "lon", [(i, i ^ 1) for i in range(count)])
+    route = [(i, (i + (1 if i % 2 else -1)) % count) for i in range(count)]
+    far = lax.ppermute(block, "lon", route)
+    return near, far
 
 
 def across(near, far, shift):

time: 55.1 us -> 54.1 us (0.982)
  starting transfers between devices: 21.4 us -> 20.7 us
    ppermute x2, waiting for transfers between devices: 2.39 us -> 5.61 us  [across(): same = lax.ppermute(near, 'comp', [(0, 1), (1, 0)])]
    ppermute x4, waiting for transfers between devices: 6.18 us -> 3.59 us  [the longest x2 3.58 us: lon_pair(): far = lax.ppermute(block, 'lon', route)]
    ppermute x2, starting transfers between devices: 3.98 us -> 2.1 us  [across(): same = lax.ppermute(near, 'comp', [(0, 1), (1, 0)])]
    ppermute x2, starting transfers between devices: 2.43 us -> 4.01 us  [across(): return (same, lax.ppermute(far, ('comp', 'lon'), route))]
    ppermute x2, waiting for transfers between devices: 3.23 us -> 2.27 us  [across(): return (same, lax.ppermute(far, ('comp', 'lon'), route))]
  transfers between devices with their start and end apart: 16 -> 16, of which waited for: 9 -> 8; matrix products, arithmetic and copies ran while one was open for 0% -> 0% of each run, Pallas kernels for 16% -> 16%
where the time goes in v9:
time: 54.1 us; the launch traced here: 53.2 us
  starting transfers between devices  20.7 us (38%)
  waiting for transfers between devices  17.7 us (33%)
  Pallas kernels  13.9 us (26%)
  between operations  0.78 us (1%)
    pallas_call x12, Pallas kernels, call(): pl.pallas_call(kernel, out_shape=tuple((jax.ShapeDtypeStruct(shape, dtype...  13.9 us
    ppermute x4, starting transfers between devices, lat_pair(): lax.ppermute(block, 'lat', [((i + 1) % count, i) for i in range(count)])  9.31 us
    ppermute x2, waiting for transfers between devices, across(): same = lax.ppermute(near, 'comp', [(0, 1), (1, 0)])  5.61 us
    ppermute x2, starting transfers between devices, lon_pair(): far = lax.ppermute(block, 'lon', route)  5.21 us
    ppermute x4, waiting for transfers between devices, lat_pair(): lax.ppermute(block, 'lat', [(i, (i + 1) % count) for i in range(count)])  4.11 us
    ppermute x2, starting transfers between devices, across(): return (same, lax.ppermute(far, ('comp', 'lon'), route))  4.01 us
    ppermute x2, waiting for transfers between devices, lon_pair(): far = lax.ppermute(block, 'lon', route)  3.58 us
    ppermute x2, waiting for transfers between devices, across(): return (same, lax.ppermute(far, ('comp', 'lon'), route))  2.27 us
  transfers between devices with their start and end apart: 16, of which 8 were waited for; matrix products, arithmetic and copies ran while one was open for 0% of the time, Pallas kernels for 16%

profile of v9, /device:TPU:8, one launch (start us, length us, event | category | flops | bytes accessed | tf_op | source)
XLA Modules:
  0.0 53.2 jit_solution(4418065519295863453)
XLA Ops:
  0.6 1.4 %shard_map.149 = (bf16[160,512]{1,0:T(8,128)(2,1)S(1)}, bf16[80,128]{1,0:T(8,128)(2,1)S(1)}) custom-call(bf16[1,80,2,256]{3,2,1,0:T(2,128)(2,1)} %state.1, bf16[1,80,2,256]{3,2,1,0:T(2,128)(2,1)} %direction.1), custom_call_target="tpu_custom_call" | custom-call | tf_op jit(solution)/shard_map/pallas_call | solution.py:556
  2.0 2.2 %collective-permute-start.1 = (bf16[160,512]{1,0:T(8,128)(2,1)S(1)}, bf16[160,512]{1,0:T(8,128)(2,1)S(1)}, u32[]{:S(2)}, u32[]{:S(2)}) collective-permute-start(bf16[160,512]{1,0:T(8,128)(2,1)S(1)} %get-tuple-element.25.own), channel_id=1, source_target_pairs={{32,0},{64,32},{96,64},{0,96},{33,1},{65,33},{97,65},{1,97},{34,2}... | collective-permute-start | bytes 491528 | tf_op jit(solution)/shard_map/ppermute | solution.py:569
  4.2 0.0 collective-permute-start
  4.2 2.0 %collective-permute-start.3 = (bf16[80,128]{1,0:T(8,128)(2,1)S(1)}, bf16[80,128]{1,0:T(8,128)(2,1)S(1)}, u32[]{:S(2)}, u32[]{:S(2)}) collective-permute-start(bf16[80,128]{1,0:T(8,128)(2,1)S(1)} %get-tuple-element.26.refs_9_.own), channel_id=1, source_target_pairs={{32,0},{64,32},{96,64},{0,96},{33,1},{65,33},{97,65},{1,97},{34,2}... | collective-permute-start | bytes 61448 | tf_op jit(solution)/shard_map/ppermute | solution.py:569
  6.3 0.0 collective-permute-start.2
  6.3 1.8 %shard_map.150 = (bf16[512,720]{1,0:T(8,128)(2,1)S(1)}, bf16[240,1536]{1,0:T(8,128)(2,1)S(1)}, f32[512,8]{1,0:T(8,128)S(1)}) custom-call(bf16[9,80,512]{2,1,0:T(8,128)(2,1)} %bitcast.6, bf16[9,80,512]{2,1,0:T(8,128)(2,1)} %refs_0_.1, bf16[9,40,256]{2,1,0:T(8,128)(2,1)} %bitcast.8, bf16[9,40,256]{2,1,0:T(8,128)(2,1)} %refs_2_.1, f32[1,512]{1,0:T(1,128)} %bitcast.10, ...), custom_call_target="tpu_custom_call" | custom-call | tf_op jit(solution)/shard_map/pallas_call | solution.py:556
  8.1 0.4 collective-permute-done.3.below
  8.5 2.1 %collective-permute-done.2.above = bf16[80,128]{1,0:T(8,128)(2,1)S(1)} collective-permute-done((bf16[80,128]{1,0:T(8,128)(2,1)S(1)}, bf16[80,128]{1,0:T(8,128)(2,1)S(1)}, u32[]{:S(2)}, u32[]{:S(2)}) %collective-permute-start.2) | collective-permute-done | bytes 20512 | tf_op jit(solution)/shard_map/ppermute | solution.py:568
  10.5 0.1 shard_map.151.edges
  10.6 5.1 %collective-permute-start.5 = (bf16[80,128]{1,0:T(8,128)(2,1)S(1)}, bf16[80,128]{1,0:T(8,128)(2,1)S(1)}, u32[]{:S(2)}, u32[]{:S(2)}) collective-permute-start(bf16[80,128]{1,0:T(8,128)(2,1)S(1)} %shard_map.151.edges), channel_id=1, source_target_pairs={{0,31},{1,2},{2,1},{3,4},{4,3},{5,6},{6,5},{7,8},{8,7},{9,10},{10,... | collective-permute-start | bytes 61448 | tf_op jit(solution)/shard_map/ppermute | solution.py:577
  15.7 0.0 collective-permute-start.4
  15.8 0.0 collective-permute-done.1.below
  15.8 0.0 collective-permute-done.above
  15.8 2.4 %shard_map.152 = (f32[80,1024]{1,0:T(8,128)S(1)}, bf16[512,1536]{1,0:T(8,128)(2,1)S(1)}, f32[2,80,128]{2,1,0:T(8,128)S(1)}) custom-call(bf16[160,512]{1,0:T(8,128)(2,1)S(1)} %get-tuple-element.25.own, bf16[160,512]{1,0:T(8,128)(2,1)S(1)} %collective-permute-done.above, bf16[160,512]{1,0:T(8,128)(2,1)S(1)} %collective-permute-done.1.below, ...), custom_call_target="tpu_custom_call" | custom-call | tf_op jit(solution)/shard_map/pallas_call | solution.py:556
  18.2 0.0 collective-permute-done.5.from_right
  18.2 0.0 collective-permute-done.4.from_left
  18.2 1.1 %shard_map.153 = (f32[80,1024]{1,0:T(8,128)S(1)}, bf16[512,128]{1,0:T(8,128)(2,1)S(1)}, f32[8,128]{1,0:T(8,128)S(1)}) custom-call(bf16[160,512]{1,0:T(8,128)(2,1)S(1)} %get-tuple-element.25.own, f32[2,80,128]{2,1,0:T(8,128)S(1)} %get-tuple-element.30.sides, bf16[80,128]{1,0:T(8,128)(2,1)S(1)} %collective-permute-done.4.from_left, ...), custom_call_target="tpu_custom_call" | custom-call | tf_op jit(solution)/shard_map/pallas_call | solution.py:556
  19.3 4.0 %collective-permute-start.7 = (f32[8,128]{1,0:T(8,128)S(1)}, f32[8,128]{1,0:T(8,128)S(1)}, u32[]{:S(2)}, u32[]{:S(2)}) collective-permute-start(f32[8,128]{1,0:T(8,128)S(1)} %get-tuple-element.33.refs_7_), channel_id=1, source_target_pairs={{0,159},{1,128},{2,129},{3,130},{4,131},{5,132},{6,133},{7,134},{8... | collective-permute-start | bytes 12296 | tf_op jit(solution)/shard_map/ppermute | solution.py:588
  23.3 1.0 %collective-permute-start.6 = (f32[8,128]{1,0:T(8,128)S(1)}, f32[8,128]{1,0:T(8,128)S(1)}, u32[]{:S(2)}, u32[]{:S(2)}) collective-permute-start(f32[8,128]{1,0:T(8,128)S(1)} %get-tuple-element.33.refs_7_), channel_id=1, source_target_pairs={{0,128},{128,0},{1,129},{129,1},{2,130},{130,2},{3,131},{131,3},{4... | collective-permute-start | bytes 12296 | tf_op jit(solution)/shard_map/ppermute | solution.py:583
  24.3 1.8 %shard_map.154 = (bf16[512,720]{1,0:T(8,128)(2,1)S(1)}, bf16[240,1536]{1,0:T(8,128)(2,1)S(1)}, bf16[128,4096]{1,0:T(8,128)(2,1)S(1)}, f32[16,4096]{1,0:T(8,128)S(1)}, f32[2,512]{1,0:T(2,128)S(1)}) custom-call(bf16[9,80,512]{2,1,0:T(8,128)(2,1)} %refs_0_.1, bf16[9,80,512]{2,1,0:T(8,128)(2,1)} %bitcast.7, bf16[9,40,256]{2,1,0:T(8,128)(2,1)} %refs_2_.1, ...), custom_call_target="tpu_custom_call" | custom-call | tf_op jit(solution)/shard_map/pallas_call | solution.py:556
  26.1 0.0 collective-permute-done.7.far
  26.1 2.3 %collective-permute-done.6.near = f32[8,128]{1,0:T(8,128)S(1)} collective-permute-done((f32[8,128]{1,0:T(8,128)S(1)}, f32[8,128]{1,0:T(8,128)S(1)}, u32[]{:S(2)}, u32[]{:S(2)}) %collective-permute-start.6) | collective-permute-done | bytes 4128 | tf_op jit(solution)/shard_map/ppermute | solution.py:583
  28.5 0.9 %shard_map.155 = (bf16[80,512]{1,0:T(8,128)(2,1)S(1)}, f32[8,128]{1,0:T(8,128)S(1)}, f32[8,128]{1,0:T(8,128)S(1)}) custom-call(f32[80,1024]{1,0:T(8,128)S(1)} %get-tuple-element.32.y, f32[8,128]{1,0:T(8,128)S(1)} %collective-permute-done.6.near, f32[8,128]{1,0:T(8,128)S(1)} %collective-permute-done.7.far, bf16[128,4096]{1,0:T(8,128)(2,1)S(1)} %get-tuple-element.34.hot, ...), custom_call_target="tpu_custom_call" | custom-call | tf_op jit(solution)/shard_map/pallas_call | solution.py:556
  29.3 1.1 %collective-permute-start.8 = (f32[8,128]{1,0:T(8,128)S(1)}, f32[8,128]{1,0:T(8,128)S(1)}, u32[]{:S(2)}, u32[]{:S(2)}) collective-permute-start(f32[8,128]{1,0:T(8,128)S(1)} %get-tuple-element.38), channel_id=1, source_target_pairs={{0,128},{128,0},{1,129},{129,1},{2,130},{130,2},{3,131},{131,3},{4... | collective-permute-start | bytes 12296 | tf_op jit(solution)/shard_map/ppermute | solution.py:583
  30.4 0.0 collective-permute-start.9
  30.4 0.8 %shard_map.156.after = bf16[1,80,2,256]{3,2,1,0:T(2,128)(2,1)} custom-call(bf16[80,512]{1,0:T(8,128)(2,1)S(1)} %get-tuple-element.37.packed.image), custom_call_target="tpu_custom_call" | custom-call | tf_op jit(solution)/shard_map/pallas_call | solution.py:556
  31.3 3.3 %collective-permute-done.8.near = f32[8,128]{1,0:T(8,128)S(1)} collective-permute-done((f32[8,128]{1,0:T(8,128)S(1)}, f32[8,128]{1,0:T(8,128)S(1)}, u32[]{:S(2)}, u32[]{:S(2)}) %collective-permute-start.8) | collective-permute-done | bytes 4128 | tf_op jit(solution)/shard_map/ppermute | solution.py:583
  34.5 2.3 %collective-permute-done.9.far = f32[8,128]{1,0:T(8,128)S(1)} collective-permute-done((f32[8,128]{1,0:T(8,128)S(1)}, f32[8,128]{1,0:T(8,128)S(1)}, u32[]{:S(2)}, u32[]{:S(2)}) %collective-permute-start.9) | collective-permute-done | bytes 4128 | tf_op jit(solution)/shard_map/ppermute | solution.py:588
  36.8 0.2 shard_map.157
  37.0 3.0 %collective-permute-start.11 = (bf16[80,512]{1,0:T(8,128)(2,1)S(1)}, bf16[80,512]{1,0:T(8,128)(2,1)S(1)}, u32[]{:S(2)}, u32[]{:S(2)}) collective-permute-start(bf16[80,512]{1,0:T(8,128)(2,1)S(1)} %get-tuple-element.40.own), channel_id=1, source_target_pairs={{32,0},{64,32},{96,64},{0,96},{33,1},{65,33},{97,65},{1,97},{34,2}... | collective-permute-start | bytes 245768 | tf_op jit(solution)/shard_map/ppermute | solution.py:569
  40.0 0.0 collective-permute-start.10
  40.0 2.0 %collective-permute-start.13 = (bf16[80,128]{1,0:T(8,128)(2,1)S(1)}, bf16[80,128]{1,0:T(8,128)(2,1)S(1)}, u32[]{:S(2)}, u32[]{:S(2)}) collective-permute-start(bf16[80,128]{1,0:T(8,128)(2,1)S(1)} %get-tuple-element.41.own), channel_id=1, source_target_pairs={{32,0},{64,32},{96,64},{0,96},{33,1},{65,33},{97,65},{1,97},{34,2}... | collective-permute-start | bytes 61448 | tf_op jit(solution)/shard_map/ppermute | solution.py:569
  42.0 0.0 collective-permute-start.12
  42.1 1.8 %collective-permute-done.13.below = bf16[80,128]{1,0:T(8,128)(2,1)S(1)} collective-permute-done((bf16[80,128]{1,0:T(8,128)(2,1)S(1)}, bf16[80,128]{1,0:T(8,128)(2,1)S(1)}, u32[]{:S(2)}, u32[]{:S(2)}) %collective-permute-start.13) | collective-permute-done | bytes 20512 | tf_op jit(solution)/shard_map/ppermute | solution.py:569
  43.8 2.0 %collective-permute-done.12.above = bf16[80,128]{1,0:T(8,128)(2,1)S(1)} collective-permute-done((bf16[80,128]{1,0:T(8,128)(2,1)S(1)}, bf16[80,128]{1,0:T(8,128)(2,1)S(1)}, u32[]{:S(2)}, u32[]{:S(2)}) %collective-permute-start.12) | collective-permute-done | bytes 20512 | tf_op jit(solution)/shard_map/ppermute | solution.py:568
  45.8 0.1 shard_map.158.edges
  45.9 0.1 collective-permute-start.15
  46.0 0.1 collective-permute-start.14
  46.1 0.0 collective-permute-done.11.below
  46.1 0.0 collective-permute-done.10.above
  46.1 1.6 %shard_map.159 = (f32[80,1024]{1,0:T(8,128)S(1)}, f32[2,80,128]{2,1,0:T(8,128)S(1)}) custom-call(bf16[80,512]{1,0:T(8,128)(2,1)S(1)} %get-tuple-element.40.own, bf16[80,512]{1,0:T(8,128)(2,1)S(1)} %collective-permute-done.10.above, bf16[80,512]{1,0:T(8,128)(2,1)S(1)} %collective-permute-done.11.below, bf16[80,128]{1,0:T(8,128)(2,1)S(1)} %shard_map.158.edges, ...), custom_call_target="tpu_custom_call" | custom-call | tf_op jit(solution)/shard_map/pallas_call | solution.py:556
  47.7 3.6 %collective-permute-done.15.from_right = bf16[80,128]{1,0:T(8,128)(2,1)S(1)} collective-permute-done((bf16[80,128]{1,0:T(8,128)(2,1)S(1)}, bf16[80,128]{1,0:T(8,128)(2,1)S(1)}, u32[]{:S(2)}, u32[]{:S(2)}) %collective-permute-start.15) | collective-permute-done | bytes 20512 | tf_op jit(solution)/shard_map/ppermute | solution.py:577
  51.3 0.0 collective-permute-done.14.from_left
  51.3 1.8 %shard_map.160 = bf16[1,80,2,256]{3,2,1,0:T(2,128)(2,1)} custom-call(f32[2,80,128]{2,1,0:T(8,128)S(1)} %get-tuple-element.45.sides, bf16[80,128]{1,0:T(8,128)(2,1)S(1)} %collective-permute-done.14.from_left, bf16[80,128]{1,0:T(8,128)(2,1)S(1)} %collective-permute-done.15.from_right, f32[80,1024]{1,0:T(8,128)S(1)} %get-tuple-element.46.inner, ...), custom_call_target="tpu_custom_call" | custom-call | tf_op jit(solution)/shard_map/pallas_call | solution.py:556
Async XLA Ops:
  2.0 13.7 %collective-permute-start.1 = (bf16[160,512]{1,0:T(8,128)(2,1)S(1)}, bf16[160,512]{1,0:T(8,128)(2,1)S(1)}, u32[]{:S(2)}, u32[]{:S(2)}) collective-permute-start(bf16[160,512]{1,0:T(8,128)(2,1)S(1)} %get-tuple-element.25.own), channel_id=1, source_target_pairs={{32,0},{64,32},{96,64},{0,96},{33,1},{65,33},{97,65},{1,97},{34,2}... | collective-permute-start | bytes 491528 | tf_op jit(solution)/shard_map/ppermute | solution.py:569
  4.2 11.5 %collective-permute-start = (bf16[160,512]{1,0:T(8,128)(2,1)S(1)}, bf16[160,512]{1,0:T(8,128)(2,1)S(1)}, u32[]{:S(2)}, u32[]{:S(2)}) collective-permute-start(bf16[160,512]{1,0:T(8,128)(2,1)S(1)} %get-tuple-element.25.own), channel_id=1, source_target_pairs={{0,32},{32,64},{64,96},{96,0},{1,33},{33,65},{65,97},{97,1},{2,34}... | collective-permute-start | bytes 491528 | tf_op jit(solution)/shard_map/ppermute | solution.py:568
  4.2 4.2 %collective-permute-start.3 = (bf16[80,128]{1,0:T(8,128)(2,1)S(1)}, bf16[80,128]{1,0:T(8,128)(2,1)S(1)}, u32[]{:S(2)}, u32[]{:S(2)}) collective-permute-start(bf16[80,128]{1,0:T(8,128)(2,1)S(1)} %get-tuple-element.26.refs_9_.own), channel_id=1, source_target_pairs={{32,0},{64,32},{96,64},{0,96},{33,1},{65,33},{97,65},{1,97},{34,2}... | collective-permute-start | bytes 61448 | tf_op jit(solution)/shard_map/ppermute | solution.py:569
  6.3 4.3 %collective-permute-start.2 = (bf16[80,128]{1,0:T(8,128)(2,1)S(1)}, bf16[80,128]{1,0:T(8,128)(2,1)S(1)}, u32[]{:S(2)}, u32[]{:S(2)}) collective-permute-start(bf16[80,128]{1,0:T(8,128)(2,1)S(1)} %get-tuple-element.26.refs_9_.own), channel_id=1, source_target_pairs={{0,32},{32,64},{64,96},{96,0},{1,33},{33,65},{65,97},{97,1},{2,34}... | collective-permute-start | bytes 61448 | tf_op jit(solution)/shard_map/ppermute | solution.py:568
  10.6 7.5 %collective-permute-start.5 = (bf16[80,128]{1,0:T(8,128)(2,1)S(1)}, bf16[80,128]{1,0:T(8,128)(2,1)S(1)}, u32[]{:S(2)}, u32[]{:S(2)}) collective-permute-start(bf16[80,128]{1,0:T(8,128)(2,1)S(1)} %shard_map.151.edges), channel_id=1, source_target_pairs={{0,31},{1,2},{2,1},{3,4},{4,3},{5,6},{6,5},{7,8},{8,7},{9,10},{10,... | collective-permute-start | bytes 61448 | tf_op jit(solution)/shard_map/ppermute | solution.py:577
  15.7 2.4 %collective-permute-start.4 = (bf16[80,128]{1,0:T(8,128)(2,1)S(1)}, bf16[80,128]{1,0:T(8,128)(2,1)S(1)}, u32[]{:S(2)}, u32[]{:S(2)}) collective-permute-start(bf16[80,128]{1,0:T(8,128)(2,1)S(1)} %shard_map.151.edges), channel_id=1, source_target_pairs={{0,1},{1,0},{2,3},{3,2},{4,5},{5,4},{6,7},{7,6},{8,9},{9,8},{10,11... | collective-permute-start | bytes 61448 | tf_op jit(solution)/shard_map/ppermute | solution.py:575
  19.3 6.8 %collective-permute-start.7 = (f32[8,128]{1,0:T(8,128)S(1)}, f32[8,128]{1,0:T(8,128)S(1)}, u32[]{:S(2)}, u32[]{:S(2)}) collective-permute-start(f32[8,128]{1,0:T(8,128)S(1)} %get-tuple-element.33.refs_7_), channel_id=1, source_target_pairs={{0,159},{1,128},{2,129},{3,130},{4,131},{5,132},{6,133},{7,134},{8... | collective-permute-start | bytes 12296 | tf_op jit(solution)/shard_map/ppermute | solution.py:588
  23.3 5.1 %collective-permute-start.6 = (f32[8,128]{1,0:T(8,128)S(1)}, f32[8,128]{1,0:T(8,128)S(1)}, u32[]{:S(2)}, u32[]{:S(2)}) collective-permute-start(f32[8,128]{1,0:T(8,128)S(1)} %get-tuple-element.33.refs_7_), channel_id=1, source_target_pairs={{0,128},{128,0},{1,129},{129,1},{2,130},{130,2},{3,131},{131,3},{4... | collective-permute-start | bytes 12296 | tf_op jit(solution)/shard_map/ppermute | solution.py:583
  29.3 5.2 %collective-permute-start.8 = (f32[8,128]{1,0:T(8,128)S(1)}, f32[8,128]{1,0:T(8,128)S(1)}, u32[]{:S(2)}, u32[]{:S(2)}) collective-permute-start(f32[8,128]{1,0:T(8,128)S(1)} %get-tuple-element.38), channel_id=1, source_target_pairs={{0,128},{128,0},{1,129},{129,1},{2,130},{130,2},{3,131},{131,3},{4... | collective-permute-start | bytes 12296 | tf_op jit(solution)/shard_map/ppermute | solution.py:583
  30.4 6.4 %collective-permute-start.9 = (f32[8,128]{1,0:T(8,128)S(1)}, f32[8,128]{1,0:T(8,128)S(1)}, u32[]{:S(2)}, u32[]{:S(2)}) collective-permute-start(f32[8,128]{1,0:T(8,128)S(1)} %get-tuple-element.39), channel_id=1, source_target_pairs={{0,129},{1,130},{2,131},{3,132},{4,133},{5,134},{6,135},{7,136},{8... | collective-permute-start | bytes 12296 | tf_op jit(solution)/shard_map/ppermute | solution.py:588
  37.0 9.1 %collective-permute-start.11 = (bf16[80,512]{1,0:T(8,128)(2,1)S(1)}, bf16[80,512]{1,0:T(8,128)(2,1)S(1)}, u32[]{:S(2)}, u32[]{:S(2)}) collective-permute-start(bf16[80,512]{1,0:T(8,128)(2,1)S(1)} %get-tuple-element.40.own), channel_id=1, source_target_pairs={{32,0},{64,32},{96,64},{0,96},{33,1},{65,33},{97,65},{1,97},{34,2}... | collective-permute-start | bytes 245768 | tf_op jit(solution)/shard_map/ppermute | solution.py:569
  40.0 6.1 %collective-permute-start.10 = (bf16[80,512]{1,0:T(8,128)(2,1)S(1)}, bf16[80,512]{1,0:T(8,128)(2,1)S(1)}, u32[]{:S(2)}, u32[]{:S(2)}) collective-permute-start(bf16[80,512]{1,0:T(8,128)(2,1)S(1)} %get-tuple-element.40.own), channel_id=1, source_target_pairs={{0,32},{32,64},{64,96},{96,0},{1,33},{33,65},{65,97},{97,1},{2,34}... | collective-permute-start | bytes 245768 | tf_op jit(solution)/shard_map/ppermute | solution.py:568
  40.0 3.8 %collective-permute-start.13 = (bf16[80,128]{1,0:T(8,128)(2,1)S(1)}, bf16[80,128]{1,0:T(8,128)(2,1)S(1)}, u32[]{:S(2)}, u32[]{:S(2)}) collective-permute-start(bf16[80,128]{1,0:T(8,128)(2,1)S(1)} %get-tuple-element.41.own), channel_id=1, source_target_pairs={{32,0},{64,32},{96,64},{0,96},{33,1},{65,33},{97,65},{1,97},{34,2}... | collective-permute-start | bytes 61448 | tf_op jit(solution)/shard_map/ppermute | solution.py:569
  42.0 3.8 %collective-permute-start.12 = (bf16[80,128]{1,0:T(8,128)(2,1)S(1)}, bf16[80,128]{1,0:T(8,128)(2,1)S(1)}, u32[]{:S(2)}, u32[]{:S(2)}) collective-permute-start(bf16[80,128]{1,0:T(8,128)(2,1)S(1)} %get-tuple-element.41.own), channel_id=1, source_target_pairs={{0,32},{32,64},{64,96},{96,0},{1,33},{33,65},{65,97},{97,1},{2,34}... | collective-permute-start | bytes 61448 | tf_op jit(solution)/shard_map/ppermute | solution.py:568
  45.9 5.4 %collective-permute-start.15 = (bf16[80,128]{1,0:T(8,128)(2,1)S(1)}, bf16[80,128]{1,0:T(8,128)(2,1)S(1)}, u32[]{:S(2)}, u32[]{:S(2)}) collective-permute-start(bf16[80,128]{1,0:T(8,128)(2,1)S(1)} %shard_map.158.edges), channel_id=1, source_target_pairs={{0,31},{1,2},{2,1},{3,4},{4,3},{5,6},{6,5},{7,8},{8,7},{9,10},{10,... | collective-permute-start | bytes 61448 | tf_op jit(solution)/shard_map/ppermute | solution.py:577
  46.0 5.3 %collective-permute-start.14 = (bf16[80,128]{1,0:T(8,128)(2,1)S(1)}, bf16[80,128]{1,0:T(8,128)(2,1)S(1)}, u32[]{:S(2)}, u32[]{:S(2)}) collective-permute-start(bf16[80,128]{1,0:T(8,128)(2,1)S(1)} %shard_map.158.edges), channel_id=1, source_target_pairs={{0,1},{1,0},{2,3},{3,2},{4,5},{5,4},{6,7},{7,6},{8,9},{9,8},{10,11... | collective-permute-start | bytes 61448 | tf_op jit(solution)/shard_map/ppermute | solution.py:575

commit v10 on v8

--- a/solution.py
+++ b/solution.py
@@ -205,6 +205,14 @@
     merged[...] = (total + pltpu.roll(below[...].astype(F32), 8, 1) * lower).astype(BF16)
 
 
+def bulk_edge_kernel(own, above, below, merged):
+    upper = jnp.where(at_top(), 0.0, 1.0).astype(F32)
+    lower = jnp.where(at_bottom(), 0.0, 1.0).astype(F32)
+    sides = [own_edges(ref, 1).astype(F32) for ref in (own, above, below)]
+    total = sides[0] + pltpu.roll(sides[1], 120, 1) * upper
+    merged[...] = (total + pltpu.roll(sides[2], 8, 1) * lower).astype(BF16)
+
+
 def shifted_rows(main, fill):
     pieces = [pltpu.roll(main, 1, 1), main, pltpu.roll(main, COLS - 1, 1)]
     if fill:
@@ -446,7 +454,7 @@
         scatter(pulled)
 
 
-def cotangent_kernel(image, near, far, columns, after, cotangent, edge):
+def cotangent_kernel(image, near, far, columns, after, cotangent):
     @pl.when(is_air())
     def _():
         arrived = near[...] + far[...]
@@ -459,8 +467,6 @@
     @pl.when(is_sea())
     def _():
         cotangent[...] = image[...]
-
-    edge[...] = own_edges(cotangent, 1)
 
 
 def spread_rows(target, rows):
@@ -670,15 +676,14 @@
     )
     back_near, back_far = across(back_near, back_far, 1)
     (result,) = call(unpack_kernel, [((1, 80, ROWS, COLS), BF16)], [image])
-    cotangent, edge = call(
+    (cotangent,) = call(
         cotangent_kernel,
-        [((80, CELLS), BF16), block],
+        [((80, CELLS), BF16)],
         [image, back_near, back_far, columns, result],
         stay=(4,),
     )
-    edge_above, edge_below = lat_pair(edge)
     above, below = lat_pair(cotangent)
-    (edges,) = call(edge_kernel, [block], [edge, edge_above, edge_below, columns])
+    (edges,) = call(bulk_edge_kernel, [block], [cotangent, above, below])
     from_left, from_right = lon_pair(edges)
     inner, sides = call(
         adjoint_main_kernel,

time: 55.1 us -> 53.1 us (0.964); the launches traced: 54.2 us -> 52.9 us
  starting transfers between devices: 21.4 us -> 19.4 us
  waiting for transfers between devices: 18.1 us -> 18.7 us
    ppermute x4 -> x3, starting transfers between devices: 9.32 us -> 7.29 us  [lat_pair(): lax.ppermute(block, 'lat', [((i + 1) % count, i) for i in range(count)])]
    ppermute x4 -> x3, waiting for transfers between devices: 4.11 us -> 4.47 us  [lat_pair(): lax.ppermute(block, 'lat', [(i, (i + 1) % count) for i in range(count)])]
    ppermute x4 -> x3, waiting for transfers between devices: 2.13 us -> 2.43 us  [lat_pair(): lax.ppermute(block, 'lat', [((i + 1) % count, i) for i in range(count)])]
  transfers between devices with their start and end apart: 16 -> 14, of which waited for: 9 -> 9; matrix products, arithmetic and copies ran while one was open for 0% -> 0% of each run, Pallas kernels for 16% -> 16%
where the time goes in v10:
time: 53.1 us; the launch traced here: 52.9 us
  starting transfers between devices  19.4 us (37%)
  waiting for transfers between devices  18.7 us (35%)
  Pallas kernels  14 us (26%)
  between operations  0.74 us (1%)
    pallas_call x12, Pallas kernels, call(): pl.pallas_call(kernel, out_shape=tuple((jax.ShapeDtypeStruct(shape, dtype...  14 us
    ppermute x3, starting transfers between devices, lat_pair(): lax.ppermute(block, 'lat', [((i + 1) % count, i) for i in range(count)])  7.29 us
    ppermute x2, waiting for transfers between devices, lon_pair(): lax.ppermute(block, 'lon', [(i, (i + 1) % count) for i in range(count)])  6.19 us
    ppermute x2, starting transfers between devices, lon_pair(): lax.ppermute(block, 'lon', [((i + 1) % count, i) for i in range(count)])  5.19 us
    ppermute x3, waiting for transfers between devices, lat_pair(): lax.ppermute(block, 'lat', [(i, (i + 1) % count) for i in range(count)])  4.47 us
    ppermute x2, starting transfers between devices, across(): same = lax.ppermute(near, 'comp', [(0, 1), (1, 0)])  3.98 us
    ppermute x2, waiting for transfers between devices, across(): return (same, lax.ppermute(far, ('comp', 'lon'), route))  3.23 us
    ppermute x2, starting transfers between devices, across(): return (same, lax.ppermute(far, ('comp', 'lon'), route))  2.43 us
  transfers between devices with their start and end apart: 14, of which 9 were waited for; matrix products, arithmetic and copies ran while one was open for 0% of the time, Pallas kernels for 16%

profile of v10, /device:TPU:8, one launch (start us, length us, event | category | flops | bytes accessed | tf_op | source)
XLA Modules:
  0.0 52.9 jit_solution(3764943518680739088)
XLA Ops:
  0.6 1.4 %shard_map.149 = (bf16[160,512]{1,0:T(8,128)(2,1)S(1)}, bf16[80,128]{1,0:T(8,128)(2,1)S(1)}) custom-call(bf16[1,80,2,256]{3,2,1,0:T(2,128)(2,1)} %state.1, bf16[1,80,2,256]{3,2,1,0:T(2,128)(2,1)} %direction.1), custom_call_target="tpu_custom_call" | custom-call | tf_op jit(solution)/shard_map/pallas_call | solution.py:559
  2.0 2.2 %collective-permute-start.1 = (bf16[160,512]{1,0:T(8,128)(2,1)S(1)}, bf16[160,512]{1,0:T(8,128)(2,1)S(1)}, u32[]{:S(2)}, u32[]{:S(2)}) collective-permute-start(bf16[160,512]{1,0:T(8,128)(2,1)S(1)} %get-tuple-element.23.own), channel_id=1, source_target_pairs={{32,0},{64,32},{96,64},{0,96},{33,1},{65,33},{97,65},{1,97},{34,2}... | collective-permute-start | bytes 491528 | tf_op jit(solution)/shard_map/ppermute | solution.py:572
  4.2 0.0 collective-permute-start
  4.2 2.0 %collective-permute-start.3 = (bf16[80,128]{1,0:T(8,128)(2,1)S(1)}, bf16[80,128]{1,0:T(8,128)(2,1)S(1)}, u32[]{:S(2)}, u32[]{:S(2)}) collective-permute-start(bf16[80,128]{1,0:T(8,128)(2,1)S(1)} %get-tuple-element.24.refs_9_.own), channel_id=1, source_target_pairs={{32,0},{64,32},{96,64},{0,96},{33,1},{65,33},{97,65},{1,97},{34,2}... | collective-permute-start | bytes 61448 | tf_op jit(solution)/shard_map/ppermute | solution.py:572
  6.3 0.0 collective-permute-start.2
  6.3 1.8 %shard_map.150 = (bf16[512,720]{1,0:T(8,128)(2,1)S(1)}, bf16[240,1536]{1,0:T(8,128)(2,1)S(1)}, f32[512,8]{1,0:T(8,128)S(1)}) custom-call(bf16[9,80,512]{2,1,0:T(8,128)(2,1)} %bitcast.6, bf16[9,80,512]{2,1,0:T(8,128)(2,1)} %refs_0_.1, bf16[9,40,256]{2,1,0:T(8,128)(2,1)} %bitcast.8, bf16[9,40,256]{2,1,0:T(8,128)(2,1)} %refs_2_.1, f32[1,512]{1,0:T(1,128)} %bitcast.10, ...), custom_call_target="tpu_custom_call" | custom-call | tf_op jit(solution)/shard_map/pallas_call | solution.py:559
  8.1 0.4 collective-permute-done.3.below
  8.5 2.1 %collective-permute-done.2.above = bf16[80,128]{1,0:T(8,128)(2,1)S(1)} collective-permute-done((bf16[80,128]{1,0:T(8,128)(2,1)S(1)}, bf16[80,128]{1,0:T(8,128)(2,1)S(1)}, u32[]{:S(2)}, u32[]{:S(2)}) %collective-permute-start.2) | collective-permute-done | bytes 20512 | tf_op jit(solution)/shard_map/ppermute | solution.py:571
  10.5 0.1 shard_map.151.edges
  10.6 5.1 %collective-permute-start.5 = (bf16[80,128]{1,0:T(8,128)(2,1)S(1)}, bf16[80,128]{1,0:T(8,128)(2,1)S(1)}, u32[]{:S(2)}, u32[]{:S(2)}) collective-permute-start(bf16[80,128]{1,0:T(8,128)(2,1)S(1)} %shard_map.151.edges), channel_id=1, source_target_pairs={{1,0},{2,1},{3,2},{4,3},{5,4},{6,5},{7,6},{8,7},{9,8},{10,9},{11,1... | collective-permute-start | bytes 61448 | tf_op jit(solution)/shard_map/ppermute | solution.py:579
  15.7 0.0 collective-permute-start.4
  15.7 0.0 collective-permute-done.1.below
  15.7 0.0 collective-permute-done.above
  15.8 2.4 %shard_map.152 = (f32[80,1024]{1,0:T(8,128)S(1)}, bf16[512,1536]{1,0:T(8,128)(2,1)S(1)}, f32[2,80,128]{2,1,0:T(8,128)S(1)}) custom-call(bf16[160,512]{1,0:T(8,128)(2,1)S(1)} %get-tuple-element.23.own, bf16[160,512]{1,0:T(8,128)(2,1)S(1)} %collective-permute-done.above, bf16[160,512]{1,0:T(8,128)(2,1)S(1)} %collective-permute-done.1.below, ...), custom_call_target="tpu_custom_call" | custom-call | tf_op jit(solution)/shard_map/pallas_call | solution.py:559
  18.2 0.0 collective-permute-done.5.from_right
  18.2 2.9 %collective-permute-done.4.from_left = bf16[80,128]{1,0:T(8,128)(2,1)S(1)} collective-permute-done((bf16[80,128]{1,0:T(8,128)(2,1)S(1)}, bf16[80,128]{1,0:T(8,128)(2,1)S(1)}, u32[]{:S(2)}, u32[]{:S(2)}) %collective-permute-start.4) | collective-permute-done | bytes 20512 | tf_op jit(solution)/shard_map/ppermute | solution.py:578
  21.1 1.1 %shard_map.153 = (f32[80,1024]{1,0:T(8,128)S(1)}, bf16[512,128]{1,0:T(8,128)(2,1)S(1)}, f32[8,128]{1,0:T(8,128)S(1)}) custom-call(bf16[160,512]{1,0:T(8,128)(2,1)S(1)} %get-tuple-element.23.own, f32[2,80,128]{2,1,0:T(8,128)S(1)} %get-tuple-element.28.sides, bf16[80,128]{1,0:T(8,128)(2,1)S(1)} %collective-permute-done.4.from_left, ...), custom_call_target="tpu_custom_call" | custom-call | tf_op jit(solution)/shard_map/pallas_call | solution.py:559
  22.2 1.2 %collective-permute-start.7 = (f32[8,128]{1,0:T(8,128)S(1)}, f32[8,128]{1,0:T(8,128)S(1)}, u32[]{:S(2)}, u32[]{:S(2)}) collective-permute-start(f32[8,128]{1,0:T(8,128)S(1)} %get-tuple-element.31.refs_7_), channel_id=1, source_target_pairs={{0,159},{1,128},{2,129},{3,130},{4,131},{5,132},{6,133},{7,134},{8... | collective-permute-start | bytes 12296 | tf_op jit(solution)/shard_map/ppermute | solution.py:590
  23.3 2.0 %collective-permute-start.6 = (f32[8,128]{1,0:T(8,128)S(1)}, f32[8,128]{1,0:T(8,128)S(1)}, u32[]{:S(2)}, u32[]{:S(2)}) collective-permute-start(f32[8,128]{1,0:T(8,128)S(1)} %get-tuple-element.31.refs_7_), channel_id=1, source_target_pairs={{0,128},{128,0},{1,129},{129,1},{2,130},{130,2},{3,131},{131,3},{4... | collective-permute-start | bytes 12296 | tf_op jit(solution)/shard_map/ppermute | solution.py:585
  25.3 1.8 %shard_map.154 = (bf16[512,720]{1,0:T(8,128)(2,1)S(1)}, bf16[240,1536]{1,0:T(8,128)(2,1)S(1)}, bf16[128,4096]{1,0:T(8,128)(2,1)S(1)}, f32[16,4096]{1,0:T(8,128)S(1)}, f32[2,512]{1,0:T(2,128)S(1)}) custom-call(bf16[9,80,512]{2,1,0:T(8,128)(2,1)} %refs_0_.1, bf16[9,80,512]{2,1,0:T(8,128)(2,1)} %bitcast.7, bf16[9,40,256]{2,1,0:T(8,128)(2,1)} %refs_2_.1, ...), custom_call_target="tpu_custom_call" | custom-call | tf_op jit(solution)/shard_map/pallas_call | solution.py:559
  27.1 0.0 collective-permute-done.7.far
  27.1 1.4 %collective-permute-done.6.near = f32[8,128]{1,0:T(8,128)S(1)} collective-permute-done((f32[8,128]{1,0:T(8,128)S(1)}, f32[8,128]{1,0:T(8,128)S(1)}, u32[]{:S(2)}, u32[]{:S(2)}) %collective-permute-start.6) | collective-permute-done | bytes 4128 | tf_op jit(solution)/shard_map/ppermute | solution.py:585
  28.5 0.9 %shard_map.155 = (bf16[80,512]{1,0:T(8,128)(2,1)S(1)}, f32[8,128]{1,0:T(8,128)S(1)}, f32[8,128]{1,0:T(8,128)S(1)}) custom-call(f32[80,1024]{1,0:T(8,128)S(1)} %get-tuple-element.30.y, f32[8,128]{1,0:T(8,128)S(1)} %collective-permute-done.6.near, f32[8,128]{1,0:T(8,128)S(1)} %collective-permute-done.7.far, bf16[128,4096]{1,0:T(8,128)(2,1)S(1)} %get-tuple-element.32.hot, ...), custom_call_target="tpu_custom_call" | custom-call | tf_op jit(solution)/shard_map/pallas_call | solution.py:559
  29.4 2.0 %collective-permute-start.8 = (f32[8,128]{1,0:T(8,128)S(1)}, f32[8,128]{1,0:T(8,128)S(1)}, u32[]{:S(2)}, u32[]{:S(2)}) collective-permute-start(f32[8,128]{1,0:T(8,128)S(1)} %get-tuple-element.36), channel_id=1, source_target_pairs={{0,128},{128,0},{1,129},{129,1},{2,130},{130,2},{3,131},{131,3},{4... | collective-permute-start | bytes 12296 | tf_op jit(solution)/shard_map/ppermute | solution.py:585
  31.4 1.3 %collective-permute-start.9 = (f32[8,128]{1,0:T(8,128)S(1)}, f32[8,128]{1,0:T(8,128)S(1)}, u32[]{:S(2)}, u32[]{:S(2)}) collective-permute-start(f32[8,128]{1,0:T(8,128)S(1)} %get-tuple-element.37), channel_id=1, source_target_pairs={{0,129},{1,130},{2,131},{3,132},{4,133},{5,134},{6,135},{7,136},{8... | collective-permute-start | bytes 12296 | tf_op jit(solution)/shard_map/ppermute | solution.py:590
  32.7 0.8 %shard_map.156.after = bf16[1,80,2,256]{3,2,1,0:T(2,128)(2,1)} custom-call(bf16[80,512]{1,0:T(8,128)(2,1)S(1)} %get-tuple-element.35.packed.image), custom_call_target="tpu_custom_call" | custom-call | tf_op jit(solution)/shard_map/pallas_call | solution.py:559
  33.5 1.0 %collective-permute-done.8.near = f32[8,128]{1,0:T(8,128)S(1)} collective-permute-done((f32[8,128]{1,0:T(8,128)S(1)}, f32[8,128]{1,0:T(8,128)S(1)}, u32[]{:S(2)}, u32[]{:S(2)}) %collective-permute-start.8) | collective-permute-done | bytes 4128 | tf_op jit(solution)/shard_map/ppermute | solution.py:585
  34.5 3.2 %collective-permute-done.9.far = f32[8,128]{1,0:T(8,128)S(1)} collective-permute-done((f32[8,128]{1,0:T(8,128)S(1)}, f32[8,128]{1,0:T(8,128)S(1)}, u32[]{:S(2)}, u32[]{:S(2)}) %collective-permute-start.9) | collective-permute-done | bytes 4128 | tf_op jit(solution)/shard_map/ppermute | solution.py:590
  37.8 0.1 shard_map.157.own
  37.9 3.0 %collective-permute-start.11 = (bf16[80,512]{1,0:T(8,128)(2,1)S(1)}, bf16[80,512]{1,0:T(8,128)(2,1)S(1)}, u32[]{:S(2)}, u32[]{:S(2)}) collective-permute-start(bf16[80,512]{1,0:T(8,128)(2,1)S(1)} %shard_map.157.own), channel_id=1, source_target_pairs={{32,0},{64,32},{96,64},{0,96},{33,1},{65,33},{97,65},{1,97},{34,2}... | collective-permute-start | bytes 245768 | tf_op jit(solution)/shard_map/ppermute | solution.py:572
  40.9 0.0 collective-permute-start.10
  40.9 2.1 %collective-permute-done.11.below = bf16[80,512]{1,0:T(8,128)(2,1)S(1)} collective-permute-done((bf16[80,512]{1,0:T(8,128)(2,1)S(1)}, bf16[80,512]{1,0:T(8,128)(2,1)S(1)}, u32[]{:S(2)}, u32[]{:S(2)}) %collective-permute-start.11) | collective-permute-done | bytes 81952 | tf_op jit(solution)/shard_map/ppermute | solution.py:572
  43.0 2.4 %collective-permute-done.10.above = bf16[80,512]{1,0:T(8,128)(2,1)S(1)} collective-permute-done((bf16[80,512]{1,0:T(8,128)(2,1)S(1)}, bf16[80,512]{1,0:T(8,128)(2,1)S(1)}, u32[]{:S(2)}, u32[]{:S(2)}) %collective-permute-start.10) | collective-permute-done | bytes 81952 | tf_op jit(solution)/shard_map/ppermute | solution.py:571
  45.3 0.2 shard_map.158.edges
  45.5 0.1 collective-permute-start.13
  45.6 0.5 collective-permute-start.12
  46.1 1.6 %shard_map.159 = (f32[80,1024]{1,0:T(8,128)S(1)}, f32[2,80,128]{2,1,0:T(8,128)S(1)}) custom-call(bf16[80,512]{1,0:T(8,128)(2,1)S(1)} %shard_map.157.own, bf16[80,512]{1,0:T(8,128)(2,1)S(1)} %collective-permute-done.10.above, bf16[80,512]{1,0:T(8,128)(2,1)S(1)} %collective-permute-done.11.below, bf16[80,128]{1,0:T(8,128)(2,1)S(1)} %shard_map.158.edges, ...), custom_call_target="tpu_custom_call" | custom-call | tf_op jit(solution)/shard_map/pallas_call | solution.py:559
  47.7 0.0 collective-permute-done.13.from_right
  47.7 3.3 %collective-permute-done.12.from_left = bf16[80,128]{1,0:T(8,128)(2,1)S(1)} collective-permute-done((bf16[80,128]{1,0:T(8,128)(2,1)S(1)}, bf16[80,128]{1,0:T(8,128)(2,1)S(1)}, u32[]{:S(2)}, u32[]{:S(2)}) %collective-permute-start.12) | collective-permute-done | bytes 20512 | tf_op jit(solution)/shard_map/ppermute | solution.py:578
  51.0 1.8 %shard_map.160 = bf16[1,80,2,256]{3,2,1,0:T(2,128)(2,1)} custom-call(f32[2,80,128]{2,1,0:T(8,128)S(1)} %get-tuple-element.41.sides, bf16[80,128]{1,0:T(8,128)(2,1)S(1)} %collective-permute-done.12.from_left, bf16[80,128]{1,0:T(8,128)(2,1)S(1)} %collective-permute-done.13.from_right, f32[80,1024]{1,0:T(8,128)S(1)} %get-tuple-element.42.inner, ...), custom_call_target="tpu_custom_call" | custom-call | tf_op jit(solution)/shard_map/pallas_call | solution.py:559
Async XLA Ops:
  2.0 13.7 %collective-permute-start.1 = (bf16[160,512]{1,0:T(8,128)(2,1)S(1)}, bf16[160,512]{1,0:T(8,128)(2,1)S(1)}, u32[]{:S(2)}, u32[]{:S(2)}) collective-permute-start(bf16[160,512]{1,0:T(8,128)(2,1)S(1)} %get-tuple-element.23.own), channel_id=1, source_target_pairs={{32,0},{64,32},{96,64},{0,96},{33,1},{65,33},{97,65},{1,97},{34,2}... | collective-permute-start | bytes 491528 | tf_op jit(solution)/shard_map/ppermute | solution.py:572
  4.2 11.5 %collective-permute-start = (bf16[160,512]{1,0:T(8,128)(2,1)S(1)}, bf16[160,512]{1,0:T(8,128)(2,1)S(1)}, u32[]{:S(2)}, u32[]{:S(2)}) collective-permute-start(bf16[160,512]{1,0:T(8,128)(2,1)S(1)} %get-tuple-element.23.own), channel_id=1, source_target_pairs={{0,32},{32,64},{64,96},{96,0},{1,33},{33,65},{65,97},{97,1},{2,34}... | collective-permute-start | bytes 491528 | tf_op jit(solution)/shard_map/ppermute | solution.py:571
  4.2 4.2 %collective-permute-start.3 = (bf16[80,128]{1,0:T(8,128)(2,1)S(1)}, bf16[80,128]{1,0:T(8,128)(2,1)S(1)}, u32[]{:S(2)}, u32[]{:S(2)}) collective-permute-start(bf16[80,128]{1,0:T(8,128)(2,1)S(1)} %get-tuple-element.24.refs_9_.own), channel_id=1, source_target_pairs={{32,0},{64,32},{96,64},{0,96},{33,1},{65,33},{97,65},{1,97},{34,2}... | collective-permute-start | bytes 61448 | tf_op jit(solution)/shard_map/ppermute | solution.py:572
  6.3 4.3 %collective-permute-start.2 = (bf16[80,128]{1,0:T(8,128)(2,1)S(1)}, bf16[80,128]{1,0:T(8,128)(2,1)S(1)}, u32[]{:S(2)}, u32[]{:S(2)}) collective-permute-start(bf16[80,128]{1,0:T(8,128)(2,1)S(1)} %get-tuple-element.24.refs_9_.own), channel_id=1, source_target_pairs={{0,32},{32,64},{64,96},{96,0},{1,33},{33,65},{65,97},{97,1},{2,34}... | collective-permute-start | bytes 61448 | tf_op jit(solution)/shard_map/ppermute | solution.py:571
  10.6 7.5 %collective-permute-start.5 = (bf16[80,128]{1,0:T(8,128)(2,1)S(1)}, bf16[80,128]{1,0:T(8,128)(2,1)S(1)}, u32[]{:S(2)}, u32[]{:S(2)}) collective-permute-start(bf16[80,128]{1,0:T(8,128)(2,1)S(1)} %shard_map.151.edges), channel_id=1, source_target_pairs={{1,0},{2,1},{3,2},{4,3},{5,4},{6,5},{7,6},{8,7},{9,8},{10,9},{11,1... | collective-permute-start | bytes 61448 | tf_op jit(solution)/shard_map/ppermute | solution.py:579
  15.7 5.3 %collective-permute-start.4 = (bf16[80,128]{1,0:T(8,128)(2,1)S(1)}, bf16[80,128]{1,0:T(8,128)(2,1)S(1)}, u32[]{:S(2)}, u32[]{:S(2)}) collective-permute-start(bf16[80,128]{1,0:T(8,128)(2,1)S(1)} %shard_map.151.edges), channel_id=1, source_target_pairs={{0,1},{1,2},{2,3},{3,4},{4,5},{5,6},{6,7},{7,8},{8,9},{9,10},{10,1... | collective-permute-start | bytes 61448 | tf_op jit(solution)/shard_map/ppermute | solution.py:578
  22.2 4.9 %collective-permute-start.7 = (f32[8,128]{1,0:T(8,128)S(1)}, f32[8,128]{1,0:T(8,128)S(1)}, u32[]{:S(2)}, u32[]{:S(2)}) collective-permute-start(f32[8,128]{1,0:T(8,128)S(1)} %get-tuple-element.31.refs_7_), channel_id=1, source_target_pairs={{0,159},{1,128},{2,129},{3,130},{4,131},{5,132},{6,133},{7,134},{8... | collective-permute-start | bytes 12296 | tf_op jit(solution)/shard_map/ppermute | solution.py:590
  23.3 5.1 %collective-permute-start.6 = (f32[8,128]{1,0:T(8,128)S(1)}, f32[8,128]{1,0:T(8,128)S(1)}, u32[]{:S(2)}, u32[]{:S(2)}) collective-permute-start(f32[8,128]{1,0:T(8,128)S(1)} %get-tuple-element.31.refs_7_), channel_id=1, source_target_pairs={{0,128},{128,0},{1,129},{129,1},{2,130},{130,2},{3,131},{131,3},{4... | collective-permute-start | bytes 12296 | tf_op jit(solution)/shard_map/ppermute | solution.py:585
  29.4 5.1 %collective-permute-start.8 = (f32[8,128]{1,0:T(8,128)S(1)}, f32[8,128]{1,0:T(8,128)S(1)}, u32[]{:S(2)}, u32[]{:S(2)}) collective-permute-start(f32[8,128]{1,0:T(8,128)S(1)} %get-tuple-element.36), channel_id=1, source_target_pairs={{0,128},{128,0},{1,129},{129,1},{2,130},{130,2},{3,131},{131,3},{4... | collective-permute-start | bytes 12296 | tf_op jit(solution)/shard_map/ppermute | solution.py:585
  31.4 6.4 %collective-permute-start.9 = (f32[8,128]{1,0:T(8,128)S(1)}, f32[8,128]{1,0:T(8,128)S(1)}, u32[]{:S(2)}, u32[]{:S(2)}) collective-permute-start(f32[8,128]{1,0:T(8,128)S(1)} %get-tuple-element.37), channel_id=1, source_target_pairs={{0,129},{1,130},{2,131},{3,132},{4,133},{5,134},{6,135},{7,136},{8... | collective-permute-start | bytes 12296 | tf_op jit(solution)/shard_map/ppermute | solution.py:590
  37.9 5.1 %collective-permute-start.11 = (bf16[80,512]{1,0:T(8,128)(2,1)S(1)}, bf16[80,512]{1,0:T(8,128)(2,1)S(1)}, u32[]{:S(2)}, u32[]{:S(2)}) collective-permute-start(bf16[80,512]{1,0:T(8,128)(2,1)S(1)} %shard_map.157.own), channel_id=1, source_target_pairs={{32,0},{64,32},{96,64},{0,96},{33,1},{65,33},{97,65},{1,97},{34,2}... | collective-permute-start | bytes 245768 | tf_op jit(solution)/shard_map/ppermute | solution.py:572
  40.9 4.4 %collective-permute-start.10 = (bf16[80,512]{1,0:T(8,128)(2,1)S(1)}, bf16[80,512]{1,0:T(8,128)(2,1)S(1)}, u32[]{:S(2)}, u32[]{:S(2)}) collective-permute-start(bf16[80,512]{1,0:T(8,128)(2,1)S(1)} %shard_map.157.own), channel_id=1, source_target_pairs={{0,32},{32,64},{64,96},{96,0},{1,33},{33,65},{65,97},{97,1},{2,34}... | collective-permute-start | bytes 245768 | tf_op jit(solution)/shard_map/ppermute | solution.py:571
  45.5 2.2 %collective-permute-start.13 = (bf16[80,128]{1,0:T(8,128)(2,1)S(1)}, bf16[80,128]{1,0:T(8,128)(2,1)S(1)}, u32[]{:S(2)}, u32[]{:S(2)}) collective-permute-start(bf16[80,128]{1,0:T(8,128)(2,1)S(1)} %shard_map.158.edges), channel_id=1, source_target_pairs={{1,0},{2,1},{3,2},{4,3},{5,4},{6,5},{7,6},{8,7},{9,8},{10,9},{11,1... | collective-permute-start | bytes 61448 | tf_op jit(solution)/shard_map/ppermute | solution.py:579
  45.6 5.4 %collective-permute-start.12 = (bf16[80,128]{1,0:T(8,128)(2,1)S(1)}, bf16[80,128]{1,0:T(8,128)(2,1)S(1)}, u32[]{:S(2)}, u32[]{:S(2)}) collective-permute-start(bf16[80,128]{1,0:T(8,128)(2,1)S(1)} %shard_map.158.edges), channel_id=1, source_target_pairs={{0,1},{1,2},{2,3},{3,4},{4,5},{5,6},{6,7},{7,8},{8,9},{9,10},{10,1... | collective-permute-start | bytes 61448 | tf_op jit(solution)/shard_map/ppermute | solution.py:578

commit v11 on v5

--- a/solution.py
+++ b/solution.py
@@ -1,11 +1,10 @@
-import functools
-
 import jax
 import jax.numpy as jnp
 from jax import lax
 from jax.experimental import pallas as pl
 from jax.experimental.pallas import tpu as pltpu
 from jax.sharding import PartitionSpec as P
+
 
 F32 = jnp.float32
 BF16 = jnp.bfloat16
@@ -145,6 +144,7 @@
             chosen = folded == line[slot : slot + 1]
             part = jnp.where(chosen, share[slot : slot + 1], 0.0)
             picked[:, slot * CELLS : (slot + 1) * CELLS] = part
+
     mask[...] = jnp.concatenate([flat(land[s]) for s in range(2)], axis=0).astype(F32)
     pad = jnp.zeros((1, 512 - 80), F32)
     bias = jnp.where(is_air(), bias_a[...], jnp.concatenate([bias_o[...]] * 2, axis=1))
@@ -527,7 +527,7 @@
         spread_rows(product, rows)
 
 
-def call(kernel, name, out_shape, inputs, scratch=(), limit=8, loads=False, idle=0):
+def call(kernel, out_shape, inputs, scratch=(), limit=8, loads=False, idle=0):
     vmem = pl.BlockSpec(memory_space=pltpu.VMEM)
     source = vmem
     if loads:
@@ -537,7 +537,6 @@
         inputs[i] = pltpu.with_memory_space_constraint(inputs[i], pltpu.HBM)
     return pl.pallas_call(
         kernel,
-        name=name,
         out_shape=tuple(jax.ShapeDtypeStruct(shape, dtype) for shape, dtype in out_shape),
         in_specs=[source] * (len(inputs) - idle) + [pl.BlockSpec(memory_space=pltpu.HBM)] * idle,
         out_specs=tuple(vmem for _ in out_shape),
@@ -562,12 +561,13 @@
 
 def across(near, far, shift):
     count = lax.axis_size("lon")
-    same = lax.ppermute(near, "comp", [(0, 1), (1, 0)])
     route = []
     for part in range(2):
         for i in range(count):
             route.append((part * count + i, (1 - part) * count + (i + shift) % count))
-    return same, lax.ppermute(far, ("comp", "lon"), route)
+    same = lax.ppermute(near, "comp", [(0, 1), (1, 0)])
+    moved = lax.ppermute(far, ("comp", "lon"), route)
+    return same, moved
 
 
 def shards(
@@ -588,7 +588,6 @@
 ):
     (own,) = call(
         pack_kernel,
-        "pack",
         [((160, CELLS), BF16)],
         [state, direction],
         [pltpu.VMEM((2, 80, ROWS, COLS), BF16), pltpu.SemaphoreType.DMA((2,))],
@@ -611,7 +610,6 @@
     ]
     fwd1, fwd2, bwd1, bwd2, hot, picked, mask, columns = call(
         prepare_kernel,
-        "prepare",
         [
             ((512, 720), BF16), ((240, 1536), BF16), ((512, 720), BF16), ((240, 1536), BF16),
             ((128, SLOTS * CELLS), BF16), ((16, SLOTS * CELLS), F32),
@@ -622,13 +620,10 @@
         limit=20,
         loads=True,
     )
-    to_left, to_right = call(
-        edge_kernel, "edges", [((80, 128), BF16)] * 2, [own, above, below, columns]
-    )
+    to_left, to_right = call(edge_kernel, [((80, 128), BF16)] * 2, [own, above, below, columns])
     from_left, from_right = lon_pair(to_left, to_right)
     inner, slope, sides = call(
         tangent_main_kernel,
-        "tangent_main",
         [((80, 2 * CELLS), F32), ((512, 6 * COLS), BF16), ((2, 80, 128), F32)],
         [own, above, below, to_left, to_right, fwd1, fwd2, columns],
         [pltpu.VMEM((240, 16 * COLS), BF16), pltpu.VMEM((512, 6 * COLS), BF16)],
@@ -636,7 +631,6 @@
     )
     y, edge_slope, payload = call(
         tangent_edge_kernel,
-        "tangent_edge",
         [((80, 2 * CELLS), F32), ((512, 128), BF16), ((8, 128), F32)],
         [own, sides, from_left, from_right, inner, fwd1, fwd2, columns],
         limit=16,
@@ -644,26 +638,24 @@
     near, far = across(payload, payload, -1)
     image, back_near, back_far = call(
         couple_kernel,
-        "couple",
         [((80, CELLS), BF16), ((8, 128), F32), ((8, 128), F32)],
         [y, near, far, hot, picked, mask, columns],
     )
     back_near, back_far = across(back_near, back_far, 1)
-    (result,) = call(unpack_kernel, "unpack", [((1, 80, ROWS, COLS), BF16)], [image])
+    (result,) = call(unpack_kernel, [((1, 80, ROWS, COLS), BF16)], [image])
     (cotangent,) = call(
-        cotangent_kernel, "cotangent", [((80, CELLS), BF16)],
+        cotangent_kernel, [((80, CELLS), BF16)],
         [image, back_near, back_far, columns],
     )
     above, below = lat_pair(cotangent)
     to_left, to_right = call(
-        edge_kernel, "edges_back", [((80, 128), BF16)] * 2,
+        edge_kernel, [((80, 128), BF16)] * 2,
         [cotangent, above, below, result],
         idle=1,
     )
     from_left, from_right = lon_pair(to_left, to_right)
     inner, sides = call(
         adjoint_main_kernel,
-        "adjoint_main",
         [((80, 2 * CELLS), F32), ((2, 80, 128), F32)],
         [cotangent, above, below, to_left, to_right, bwd1, bwd2, slope],
         [pltpu.VMEM((240, 8 * COLS), BF16), pltpu.VMEM((512, 6 * COLS), BF16)],
@@ -671,7 +663,6 @@
     )
     (product,) = call(
         adjoint_edge_kernel,
-        "adjoint_edge",
         [((1, 80, ROWS, COLS), BF16)],
         [
             sides, from_left, from_right, inner, edge_slope, bwd1, bwd2,

time: 51.8 us -> 51.8 us (level)
  no operation moved by 1% of the time
where the time goes in v11:
time: 51.8 us; the launch traced here: 51.6 us
  waiting for transfers between devices  21 us (41%)
  starting transfers between devices  17.4 us (34%)
  Pallas kernels  12.5 us (24%)
  between operations  0.73 us (1%)
    pallas_call x11, Pallas kernels, call(): pl.pallas_call(kernel, out_shape=tuple((jax.ShapeDtypeStruct(shape, dtype...  12.5 us
    ppermute x2, waiting for transfers between devices, lon_pair(): lax.ppermute(to_right, 'lon', [(i, (i + 1) % count) for i in range(count)])  6.22 us
    ppermute x2, starting transfers between devices, lon_pair(): lax.ppermute(to_left, 'lon', [((i + 1) % count, i) for i in range(count)])  5.43 us
    ppermute x2, starting transfers between devices, lat_pair(): lax.ppermute(block, 'lat', [((i + 1) % count, i) for i in range(count)])  4.99 us
    ppermute x2, waiting for transfers between devices, across(): moved = lax.ppermute(far, ('comp', 'lon'), route)  4.71 us
    ppermute x2, starting transfers between devices, across(): same = lax.ppermute(near, 'comp', [(0, 1), (1, 0)])  3.97 us
    ppermute x2, waiting for transfers between devices, lat_pair(): lax.ppermute(block, 'lat', [(i, (i + 1) % count) for i in range(count)])  3.92 us
    ppermute x2, waiting for transfers between devices, across(): same = lax.ppermute(near, 'comp', [(0, 1), (1, 0)])  3.48 us
  transfers between devices with their start and end apart: 12, of which 10 were waited for; matrix products, arithmetic and copies ran while one was open for 0% of the time, Pallas kernels for 14%

profile of v11, /device:TPU:8, one launch (start us, length us, event | category | flops | bytes accessed | tf_op | source)
XLA Modules:
  0.0 51.6 jit_solution(619596964614222707)
XLA Ops:
  0.6 1.3 %shard_map.149.own = bf16[160,512]{1,0:T(8,128)(2,1)S(1)} custom-call(bf16[1,80,2,256]{3,2,1,0:T(2,128)(2,1)} %state.1, bf16[1,80,2,256]{3,2,1,0:T(2,128)(2,1)} %direction.1), custom_call_target="tpu_custom_call" | custom-call | tf_op jit(solution)/shard_map/pallas_call | solution.py:538
  1.9 2.2 %collective-permute-start.1 = (bf16[160,512]{1,0:T(8,128)(2,1)S(1)}, bf16[160,512]{1,0:T(8,128)(2,1)S(1)}, u32[]{:S(2)}, u32[]{:S(2)}) collective-permute-start(bf16[160,512]{1,0:T(8,128)(2,1)S(1)} %shard_map.149.own), channel_id=1, source_target_pairs={{32,0},{64,32},{96,64},{0,96},{33,1},{65,33},{97,65},{1,97},{34,2}... | collective-permute-start | bytes 491528 | tf_op jit(solution)/shard_map/ppermute | solution.py:551
  4.1 0.0 collective-permute-start
  4.2 2.3 %shard_map.150 = (bf16[512,720]{1,0:T(8,128)(2,1)S(1)}, bf16[240,1536]{1,0:T(8,128)(2,1)S(1)}, bf16[512,720]{1,0:T(8,128)(2,1)S(1)}, bf16[240,1536]{1,0:T(8,128)...) custom-call(bf16[9,80,512]{2,1,0:T(8,128)(2,1)} %bitcast.6, ...), custom_call_target="tpu_custom_call" | custom-call | tf_op jit(solution)/shard_map/pallas_call | solution.py:538
  6.5 1.4 %collective-permute-done.1.below = bf16[160,512]{1,0:T(8,128)(2,1)S(1)} collective-permute-done((bf16[160,512]{1,0:T(8,128)(2,1)S(1)}, bf16[160,512]{1,0:T(8,128)(2,1)S(1)}, u32[]{:S(2)}, u32[]{:S(2)}) %collective-permute-start.1) | collective-permute-done | bytes 163872 | tf_op jit(solution)/shard_map/ppermute | solution.py:551
  7.9 1.5 %collective-permute-done.above = bf16[160,512]{1,0:T(8,128)(2,1)S(1)} collective-permute-done((bf16[160,512]{1,0:T(8,128)(2,1)S(1)}, bf16[160,512]{1,0:T(8,128)(2,1)S(1)}, u32[]{:S(2)}, u32[]{:S(2)}) %collective-permute-start) | collective-permute-done | bytes 163872 | tf_op jit(solution)/shard_map/ppermute | solution.py:550
  9.5 0.2 shard_map.151
  9.7 5.4 %collective-permute-start.3 = (bf16[80,128]{1,0:T(8,128)(2,1)S(1)}, bf16[80,128]{1,0:T(8,128)(2,1)S(1)}, u32[]{:S(2)}, u32[]{:S(2)}) collective-permute-start(bf16[80,128]{1,0:T(8,128)(2,1)S(1)} %get-tuple-element.26.to_left), channel_id=1, source_target_pairs={{1,0},{2,1},{3,2},{4,3},{5,4},{6,5},{7,6},{8,7},{9,8},{10,9},{11,1... | collective-permute-start | bytes 61448 | tf_op jit(solution)/shard_map/ppermute | solution.py:558
  15.0 0.0 collective-permute-start.2
  15.0 2.4 %shard_map.152 = (f32[80,1024]{1,0:T(8,128)S(1)}, bf16[512,1536]{1,0:T(8,128)(2,1)S(1)}, f32[2,80,128]{2,1,0:T(8,128)S(1)}) custom-call(bf16[160,512]{1,0:T(8,128)(2,1)S(1)} %shard_map.149.own, bf16[160,512]{1,0:T(8,128)(2,1)S(1)} %collective-permute-done.above, bf16[160,512]{1,0:T(8,128)(2,1)S(1)} %collective-permute-done.1.below, ...), custom_call_target="tpu_custom_call" | custom-call | tf_op jit(solution)/shard_map/pallas_call | solution.py:538
  17.4 0.0 collective-permute-done.3.from_right
  17.4 2.9 %collective-permute-done.2.from_left = bf16[80,128]{1,0:T(8,128)(2,1)S(1)} collective-permute-done((bf16[80,128]{1,0:T(8,128)(2,1)S(1)}, bf16[80,128]{1,0:T(8,128)(2,1)S(1)}, u32[]{:S(2)}, u32[]{:S(2)}) %collective-permute-start.2) | collective-permute-done | bytes 20512 | tf_op jit(solution)/shard_map/ppermute | solution.py:557
  20.3 1.1 %shard_map.153 = (f32[80,1024]{1,0:T(8,128)S(1)}, bf16[512,128]{1,0:T(8,128)(2,1)S(1)}, f32[8,128]{1,0:T(8,128)S(1)}) custom-call(bf16[160,512]{1,0:T(8,128)(2,1)S(1)} %shard_map.149.own, f32[2,80,128]{2,1,0:T(8,128)S(1)} %get-tuple-element.30.sides, bf16[80,128]{1,0:T(8,128)(2,1)S(1)} %collective-permute-done.2.from_left, ...), custom_call_target="tpu_custom_call" | custom-call | tf_op jit(solution)/shard_map/pallas_call | solution.py:538
  21.5 1.1 %collective-permute-start.5 = (f32[8,128]{1,0:T(8,128)S(1)}, f32[8,128]{1,0:T(8,128)S(1)}, u32[]{:S(2)}, u32[]{:S(2)}) collective-permute-start(f32[8,128]{1,0:T(8,128)S(1)} %get-tuple-element.33), channel_id=1, source_target_pairs={{0,159},{1,128},{2,129},{3,130},{4,131},{5,132},{6,133},{7,134},{8... | collective-permute-start | bytes 12296 | tf_op jit(solution)/shard_map/ppermute | solution.py:569
  22.6 2.0 %collective-permute-start.4 = (f32[8,128]{1,0:T(8,128)S(1)}, f32[8,128]{1,0:T(8,128)S(1)}, u32[]{:S(2)}, u32[]{:S(2)}) collective-permute-start(f32[8,128]{1,0:T(8,128)S(1)} %get-tuple-element.33), channel_id=1, source_target_pairs={{0,128},{128,0},{1,129},{129,1},{2,130},{130,2},{3,131},{131,3},{4... | collective-permute-start | bytes 12296 | tf_op jit(solution)/shard_map/ppermute | solution.py:568
  24.6 1.5 %collective-permute-done.5.far = f32[8,128]{1,0:T(8,128)S(1)} collective-permute-done((f32[8,128]{1,0:T(8,128)S(1)}, f32[8,128]{1,0:T(8,128)S(1)}, u32[]{:S(2)}, u32[]{:S(2)}) %collective-permute-start.5) | collective-permute-done | bytes 4128 | tf_op jit(solution)/shard_map/ppermute | solution.py:569
  26.1 1.6 %collective-permute-done.4.near = f32[8,128]{1,0:T(8,128)S(1)} collective-permute-done((f32[8,128]{1,0:T(8,128)S(1)}, f32[8,128]{1,0:T(8,128)S(1)}, u32[]{:S(2)}, u32[]{:S(2)}) %collective-permute-start.4) | collective-permute-done | bytes 4128 | tf_op jit(solution)/shard_map/ppermute | solution.py:568
  27.7 0.8 %shard_map.154 = (bf16[80,512]{1,0:T(8,128)(2,1)S(1)}, f32[8,128]{1,0:T(8,128)S(1)}, f32[8,128]{1,0:T(8,128)S(1)}) custom-call(f32[80,1024]{1,0:T(8,128)S(1)} %get-tuple-element.32.y, f32[8,128]{1,0:T(8,128)S(1)} %collective-permute-done.4.near, f32[8,128]{1,0:T(8,128)S(1)} %collective-permute-done.5.far, bf16[128,4096]{1,0:T(8,128)(2,1)S(1)} %get-tuple-element.34.hot, ...), custom_call_target="tpu_custom_call" | custom-call | tf_op jit(solution)/shard_map/pallas_call | solution.py:538
  28.5 2.0 %collective-permute-start.6 = (f32[8,128]{1,0:T(8,128)S(1)}, f32[8,128]{1,0:T(8,128)S(1)}, u32[]{:S(2)}, u32[]{:S(2)}) collective-permute-start(f32[8,128]{1,0:T(8,128)S(1)} %get-tuple-element.38), channel_id=1, source_target_pairs={{0,128},{128,0},{1,129},{129,1},{2,130},{130,2},{3,131},{131,3},{4... | collective-permute-start | bytes 12296 | tf_op jit(solution)/shard_map/ppermute | solution.py:568
  30.5 1.3 %collective-permute-start.7 = (f32[8,128]{1,0:T(8,128)S(1)}, f32[8,128]{1,0:T(8,128)S(1)}, u32[]{:S(2)}, u32[]{:S(2)}) collective-permute-start(f32[8,128]{1,0:T(8,128)S(1)} %get-tuple-element.39), channel_id=1, source_target_pairs={{0,129},{1,130},{2,131},{3,132},{4,133},{5,134},{6,135},{7,136},{8... | collective-permute-start | bytes 12296 | tf_op jit(solution)/shard_map/ppermute | solution.py:569
  31.8 1.8 %collective-permute-done.6.near = f32[8,128]{1,0:T(8,128)S(1)} collective-permute-done((f32[8,128]{1,0:T(8,128)S(1)}, f32[8,128]{1,0:T(8,128)S(1)}, u32[]{:S(2)}, u32[]{:S(2)}) %collective-permute-start.6) | collective-permute-done | bytes 4128 | tf_op jit(solution)/shard_map/ppermute | solution.py:568
  33.6 3.2 %collective-permute-done.7.far = f32[8,128]{1,0:T(8,128)S(1)} collective-permute-done((f32[8,128]{1,0:T(8,128)S(1)}, f32[8,128]{1,0:T(8,128)S(1)}, u32[]{:S(2)}, u32[]{:S(2)}) %collective-permute-start.7) | collective-permute-done | bytes 4128 | tf_op jit(solution)/shard_map/ppermute | solution.py:569
  36.9 0.1 shard_map.156.own
  37.0 2.8 %collective-permute-start.9 = (bf16[80,512]{1,0:T(8,128)(2,1)S(1)}, bf16[80,512]{1,0:T(8,128)(2,1)S(1)}, u32[]{:S(2)}, u32[]{:S(2)}) collective-permute-start(bf16[80,512]{1,0:T(8,128)(2,1)S(1)} %shard_map.156.own), channel_id=1, source_target_pairs={{32,0},{64,32},{96,64},{0,96},{33,1},{65,33},{97,65},{1,97},{34,2}... | collective-permute-start | bytes 245768 | tf_op jit(solution)/shard_map/ppermute | solution.py:551
  39.7 0.0 collective-permute-start.8
  39.7 0.8 %shard_map.155.after = bf16[1,80,2,256]{3,2,1,0:T(2,128)(2,1)} custom-call(bf16[80,512]{1,0:T(8,128)(2,1)S(1)} %get-tuple-element.37.packed.image), custom_call_target="tpu_custom_call" | custom-call | tf_op jit(solution)/shard_map/pallas_call | solution.py:538
  40.5 1.3 %collective-permute-done.9.below = bf16[80,512]{1,0:T(8,128)(2,1)S(1)} collective-permute-done((bf16[80,512]{1,0:T(8,128)(2,1)S(1)}, bf16[80,512]{1,0:T(8,128)(2,1)S(1)}, u32[]{:S(2)}, u32[]{:S(2)}) %collective-permute-start.9) | collective-permute-done | bytes 81952 | tf_op jit(solution)/shard_map/ppermute | solution.py:551
  41.8 2.4 %collective-permute-done.8.above = bf16[80,512]{1,0:T(8,128)(2,1)S(1)} collective-permute-done((bf16[80,512]{1,0:T(8,128)(2,1)S(1)}, bf16[80,512]{1,0:T(8,128)(2,1)S(1)}, u32[]{:S(2)}, u32[]{:S(2)}) %collective-permute-start.8) | collective-permute-done | bytes 81952 | tf_op jit(solution)/shard_map/ppermute | solution.py:550
  44.2 0.1 shard_map.157
  44.3 0.1 collective-permute-start.11
  44.4 0.5 collective-permute-start.10
  44.9 1.6 %shard_map.158 = (f32[80,1024]{1,0:T(8,128)S(1)}, f32[2,80,128]{2,1,0:T(8,128)S(1)}) custom-call(bf16[80,512]{1,0:T(8,128)(2,1)S(1)} %shard_map.156.own, bf16[80,512]{1,0:T(8,128)(2,1)S(1)} %collective-permute-done.8.above, bf16[80,512]{1,0:T(8,128)(2,1)S(1)} %collective-permute-done.9.below, bf16[80,128]{1,0:T(8,128)(2,1)S(1)} %get-tuple-element.40.to_left, ...), custom_call_target="tpu_custom_call" | custom-call | tf_op jit(solution)/shard_map/pallas_call | solution.py:538
  46.5 0.0 collective-permute-done.11.from_right
  46.5 3.3 %collective-permute-done.10.from_left = bf16[80,128]{1,0:T(8,128)(2,1)S(1)} collective-permute-done((bf16[80,128]{1,0:T(8,128)(2,1)S(1)}, bf16[80,128]{1,0:T(8,128)(2,1)S(1)}, u32[]{:S(2)}, u32[]{:S(2)}) %collective-permute-start.10) | collective-permute-done | bytes 20512 | tf_op jit(solution)/shard_map/ppermute | solution.py:557
  49.8 1.8 %shard_map.159 = bf16[1,80,2,256]{3,2,1,0:T(2,128)(2,1)} custom-call(f32[2,80,128]{2,1,0:T(8,128)S(1)} %get-tuple-element.45.sides, bf16[80,128]{1,0:T(8,128)(2,1)S(1)} %collective-permute-done.10.from_left, bf16[80,128]{1,0:T(8,128)(2,1)S(1)} %collective-permute-done.11.from_right, f32[80,1024]{1,0:T(8,128)S(1)} %get-tuple-element.46.inner, ...), custom_call_target="tpu_custom_call" | custom-call | tf_op jit(solution)/shard_map/pallas_call | solution.py:538
Async XLA Ops:
  1.9 6.0 %collective-permute-start.1 = (bf16[160,512]{1,0:T(8,128)(2,1)S(1)}, bf16[160,512]{1,0:T(8,128)(2,1)S(1)}, u32[]{:S(2)}, u32[]{:S(2)}) collective-permute-start(bf16[160,512]{1,0:T(8,128)(2,1)S(1)} %shard_map.149.own), channel_id=1, source_target_pairs={{32,0},{64,32},{96,64},{0,96},{33,1},{65,33},{97,65},{1,97},{34,2}... | collective-permute-start | bytes 491528 | tf_op jit(solution)/shard_map/ppermute | solution.py:551
  4.1 5.3 %collective-permute-start = (bf16[160,512]{1,0:T(8,128)(2,1)S(1)}, bf16[160,512]{1,0:T(8,128)(2,1)S(1)}, u32[]{:S(2)}, u32[]{:S(2)}) collective-permute-start(bf16[160,512]{1,0:T(8,128)(2,1)S(1)} %shard_map.149.own), channel_id=1, source_target_pairs={{0,32},{32,64},{64,96},{96,0},{1,33},{33,65},{65,97},{97,1},{2,34}... | collective-permute-start | bytes 491528 | tf_op jit(solution)/shard_map/ppermute | solution.py:550
  9.7 7.8 %collective-permute-start.3 = (bf16[80,128]{1,0:T(8,128)(2,1)S(1)}, bf16[80,128]{1,0:T(8,128)(2,1)S(1)}, u32[]{:S(2)}, u32[]{:S(2)}) collective-permute-start(bf16[80,128]{1,0:T(8,128)(2,1)S(1)} %get-tuple-element.26.to_left), channel_id=1, source_target_pairs={{1,0},{2,1},{3,2},{4,3},{5,4},{6,5},{7,6},{8,7},{9,8},{10,9},{11,1... | collective-permute-start | bytes 61448 | tf_op jit(solution)/shard_map/ppermute | solution.py:558
  15.0 5.3 %collective-permute-start.2 = (bf16[80,128]{1,0:T(8,128)(2,1)S(1)}, bf16[80,128]{1,0:T(8,128)(2,1)S(1)}, u32[]{:S(2)}, u32[]{:S(2)}) collective-permute-start(bf16[80,128]{1,0:T(8,128)(2,1)S(1)} %get-tuple-element.27.to_right), channel_id=1, source_target_pairs={{0,1},{1,2},{2,3},{3,4},{4,5},{5,6},{6,7},{7,8},{8,9},{9,10},{10,1... | collective-permute-start | bytes 61448 | tf_op jit(solution)/shard_map/ppermute | solution.py:557
  21.5 4.6 %collective-permute-start.5 = (f32[8,128]{1,0:T(8,128)S(1)}, f32[8,128]{1,0:T(8,128)S(1)}, u32[]{:S(2)}, u32[]{:S(2)}) collective-permute-start(f32[8,128]{1,0:T(8,128)S(1)} %get-tuple-element.33), channel_id=1, source_target_pairs={{0,159},{1,128},{2,129},{3,130},{4,131},{5,132},{6,133},{7,134},{8... | collective-permute-start | bytes 12296 | tf_op jit(solution)/shard_map/ppermute | solution.py:569
  22.6 5.1 %collective-permute-start.4 = (f32[8,128]{1,0:T(8,128)S(1)}, f32[8,128]{1,0:T(8,128)S(1)}, u32[]{:S(2)}, u32[]{:S(2)}) collective-permute-start(f32[8,128]{1,0:T(8,128)S(1)} %get-tuple-element.33), channel_id=1, source_target_pairs={{0,128},{128,0},{1,129},{129,1},{2,130},{130,2},{3,131},{131,3},{4... | collective-permute-start | bytes 12296 | tf_op jit(solution)/shard_map/ppermute | solution.py:568
  28.5 5.1 %collective-permute-start.6 = (f32[8,128]{1,0:T(8,128)S(1)}, f32[8,128]{1,0:T(8,128)S(1)}, u32[]{:S(2)}, u32[]{:S(2)}) collective-permute-start(f32[8,128]{1,0:T(8,128)S(1)} %get-tuple-element.38), channel_id=1, source_target_pairs={{0,128},{128,0},{1,129},{129,1},{2,130},{130,2},{3,131},{131,3},{4... | collective-permute-start | bytes 12296 | tf_op jit(solution)/shard_map/ppermute | solution.py:568
  30.5 6.4 %collective-permute-start.7 = (f32[8,128]{1,0:T(8,128)S(1)}, f32[8,128]{1,0:T(8,128)S(1)}, u32[]{:S(2)}, u32[]{:S(2)}) collective-permute-start(f32[8,128]{1,0:T(8,128)S(1)} %get-tuple-element.39), channel_id=1, source_target_pairs={{0,129},{1,130},{2,131},{3,132},{4,133},{5,134},{6,135},{7,136},{8... | collective-permute-start | bytes 12296 | tf_op jit(solution)/shard_map/ppermute | solution.py:569
  37.0 4.8 %collective-permute-start.9 = (bf16[80,512]{1,0:T(8,128)(2,1)S(1)}, bf16[80,512]{1,0:T(8,128)(2,1)S(1)}, u32[]{:S(2)}, u32[]{:S(2)}) collective-permute-start(bf16[80,512]{1,0:T(8,128)(2,1)S(1)} %shard_map.156.own), channel_id=1, source_target_pairs={{32,0},{64,32},{96,64},{0,96},{33,1},{65,33},{97,65},{1,97},{34,2}... | collective-permute-start | bytes 245768 | tf_op jit(solution)/shard_map/ppermute | solution.py:551
  39.7 4.4 %collective-permute-start.8 = (bf16[80,512]{1,0:T(8,128)(2,1)S(1)}, bf16[80,512]{1,0:T(8,128)(2,1)S(1)}, u32[]{:S(2)}, u32[]{:S(2)}) collective-permute-start(bf16[80,512]{1,0:T(8,128)(2,1)S(1)} %shard_map.156.own), channel_id=1, source_target_pairs={{0,32},{32,64},{64,96},{96,0},{1,33},{33,65},{65,97},{97,1},{2,34}... | collective-permute-start | bytes 245768 | tf_op jit(solution)/shard_map/ppermute | solution.py:550
  44.3 2.2 %collective-permute-start.11 = (bf16[80,128]{1,0:T(8,128)(2,1)S(1)}, bf16[80,128]{1,0:T(8,128)(2,1)S(1)}, u32[]{:S(2)}, u32[]{:S(2)}) collective-permute-start(bf16[80,128]{1,0:T(8,128)(2,1)S(1)} %get-tuple-element.40.to_left), channel_id=1, source_target_pairs={{1,0},{2,1},{3,2},{4,3},{5,4},{6,5},{7,6},{8,7},{9,8},{10,9},{11,1... | collective-permute-start | bytes 61448 | tf_op jit(solution)/shard_map/ppermute | solution.py:558
  44.4 5.4 %collective-permute-start.10 = (bf16[80,128]{1,0:T(8,128)(2,1)S(1)}, bf16[80,128]{1,0:T(8,128)(2,1)S(1)}, u32[]{:S(2)}, u32[]{:S(2)}) collective-permute-start(bf16[80,128]{1,0:T(8,128)(2,1)S(1)} %get-tuple-element.41.to_right), channel_id=1, source_target_pairs={{0,1},{1,2},{2,3},{3,4},{4,5},{5,6},{6,7},{7,8},{8,9},{9,10},{10,1... | collective-permute-start | bytes 61448 | tf_op jit(solution)/shard_map/ppermute | solution.py:557
